TPU v7x, 32 devices: a whole 2x2x4 slice. The times are simulated.
32 devices in a mesh: seq: 8 (over y, x, core), mp: 4 (over z).
Axes of the slice: x: 2, y: 2, z: 4, core: 2. Of those that a mesh axis runs over, the one named last changes fastest.
Arguments:
- coarse: bfloat16 [768, 1024], P('mp', 'seq'), may hold values from -6 to 6
- skip: bfloat16 [768, 2048], P('mp', 'seq'), may hold values from -6 to 6
- conv_weight: bfloat16 [3, 768, 768], P(None, 'mp'), may hold values from -0.125 to 0.125
- conv_bias: float32 [768], P('mp'), may hold values from -3 to 3
- head_weight: bfloat16 [768, 512], P(None, 'mp'), may hold values from -0.21875 to 0.21875
- head_bias: float32 [512], P('mp'), may hold values from -3 to 3
- counts: int32 [2048, 512], P('seq', 'mp'), may hold values from 0 to 3
- seg_mask: int32 [1, 512], P(None, 'mp'), may hold values 0 or 1
Outputs:
- grad_skip: bfloat16 [768, 2048], P('mp', 'seq')
- grad_coarse: bfloat16 [768, 1024], P('mp', 'seq')
- grad_head: float32 [768, 512], P('seq', 'mp')
- grad_conv: float32 [768, 3, 768], P('seq', None, 'mp')
All inputs are finite; a program needn't handle non-finite values. No bound on the sum of `seg_mask` on one device may be relied on, other than what follows from the above.
Results may differ from a plain program's by a relative error of at most 0.0068.
Values may be sent and summed in bfloat16 or wider, within the bound.
No kernel may reach another device: no remote copies, remote signals or barrier semaphores. Data moves between devices by JAX's collectives and lax.ppermute only.
A program may use at most 64 MiB of HBM per device.

v0:
```python
import functools
import math

import jax
import jax.numpy as jnp
from jax import lax
from jax.experimental import pallas as pl
from jax.experimental.pallas import tpu as pltpu
from jax.sharding import PartitionSpec as P


root_two_pi = 0.7978845608028654
cubic_coef = 0.044715
multi_weight = 5.0
pseudo_count = 0.5
edge_rows = 16
edge_lanes = 128
bf16, f32 = jnp.bfloat16, jnp.float32


def swap(block, axis, mask):
    count = lax.axis_size(axis)
    return lax.ppermute(block, axis, [(i, i ^ mask) for i in range(count)])


def shifted(block, axis, step):
    count = lax.axis_size(axis)
    pairs = [(i, i + step) for i in range(count) if 0 <= i + step < count]
    return lax.ppermute(block, axis, pairs)


def gathered(block, axis):
    parts = [block]
    for j in range(1, lax.axis_size(axis)):
        parts.append(swap(block, axis, j))
    return parts


def staged(low, bits):
    while low < bits:
        wide = 1 if low == 0 else min(2, bits - low)
        yield low, wide
        low += wide


def scattered(parts, axis):
    bits = lax.axis_size(axis).bit_length() - 1
    mine = lax.axis_index(axis)
    for low, wide in staged(0, bits):
        size = 1 << wide
        parts = parts.reshape((parts.shape[0] // size, size) + parts.shape[1:])
        at = (mine >> low) & (size - 1)
        small = parts.astype(bf16)
        kept = lax.dynamic_index_in_dim(parts, at, 1, keepdims=False)
        for step in range(1, size):
            piece = lax.dynamic_index_in_dim(small, at ^ step, 1, keepdims=False)
            kept = kept + swap(piece, axis, step << low).astype(f32)
        parts = kept
    return parts[0]


def totalled(block, axis, span):
    for low, wide in staged(0, span.bit_length() - 1):
        block = sum([swap(block, axis, step << low) for step in range(1, 1 << wide)], block)
    return block


def dot(left, right, dims, precision=None):
    return lax.dot_general(
        left, right, (dims, ((), ())), preferred_element_type=f32, precision=precision
    )


nn, nt, tn = ((1,), (0,)), ((1,), (1,)), ((0,), (0,))


def iota(shape, axis):
    return lax.broadcasted_iota(jnp.int32, shape, axis)


def chosen(shape, pairs):
    rows, columns = iota(shape, 0), iota(shape, 1)
    hit = functools.reduce(jnp.logical_or, [(rows == r) & (columns == c) for r, c in pairs])
    return jnp.where(hit, 1.0, 0.0).astype(bf16)


def call(body, outs, *args, scratch=(), grant=16 << 20, outside=(), last=False):
    spaces = [pltpu.HBM if i in outside else pltpu.VMEM for i in range(len(args))]
    return pl.pallas_call(
        body,
        out_shape=[
            jax.ShapeDtypeStruct(shape, kind) if last else pltpu.VMEM(shape, kind)
            for shape, kind in outs
        ],
        in_specs=[pl.BlockSpec(memory_space=space) for space in spaces],
        out_specs=[pl.BlockSpec(memory_space=pltpu.VMEM)] * len(outs),
        scratch_shapes=[
            pltpu.SemaphoreType.DMA(shape) if kind is None else pltpu.VMEM(shape, kind)
            for shape, kind in scratch
        ],
        compiler_params=pltpu.CompilerParams(vmem_limit_bytes=grant),
    )(*[pltpu.with_memory_space_constraint(arg, space) for arg, space in zip(args, spaces)])


def block_rows(column, j, size):
    return pl.ds(pl.multiple_of((column ^ j) * size, size), size)


def prepare(coarse_in, skip_in, counts_in, summed, ahead, behind, own, coarse, skip, top, bottom, done):
    width, length = skip.shape
    rows, tracks = top.shape
    copies = [
        pltpu.make_async_copy(source, target, done.at[i])
        for i, (source, target) in enumerate(
            (
                (coarse_in, coarse),
                (skip_in, skip),
                (counts_in.at[pl.ds(0, rows)], top),
                (counts_in.at[pl.ds(length - rows, rows)], bottom),
            )
        )
    ]
    for copy in copies:
        copy.start()
    for copy in copies:
        copy.wait()
    pairs = jnp.where(
        iota((coarse.shape[1], length), 0) == iota((coarse.shape[1], length), 1) // 2, 1.0, 0.0
    ).astype(bf16)
    total = (dot(coarse[...], pairs, nn) + skip[...].astype(f32)).astype(bf16)
    summed[...] = total
    for out, picks, slot, line in (
        (ahead, ((0, length - 2), (1, length - 1)), 6, bottom[rows - 1 : rows, :]),
        (behind, ((4, 0), (5, 1)), 7, top[0:1, :]),
        (own, ((2, 0), (3, length - 1)), None, None),
    ):
        picked = dot(chosen((edge_rows, length), picks), total, nt).astype(bf16)
        out[...] = jnp.zeros(out.shape, bf16)
        out[:, :width] = picked
        if slot is not None:
            line = jnp.broadcast_to(line.astype(f32), (edge_rows, tracks))
            held = picked[:, :tracks].astype(f32)
            out[:, :tracks] = jnp.where(iota(held.shape, 0) == slot, line, held).astype(bf16)


def stage(after, weight_in, weight, done):
    copy = pltpu.make_async_copy(weight_in, weight, done.at[0])
    copy.start()
    copy.wait()


def gelu_parts(inputs):
    inner = root_two_pi * (inputs + cubic_coef * inputs * inputs * inputs)
    tangent = jnp.tanh(inner)
    value = 0.5 * inputs * (1.0 + tangent)
    slope = 0.5 * (1.0 + tangent) + 0.5 * inputs * (1.0 - tangent * tangent) * root_two_pi * (
        1.0 + 3.0 * cubic_coef * inputs * inputs
    )
    return value, slope


def assembled(pieces, whole, column, width, length):
    spread = jnp.where(
        iota((edge_rows, edge_lanes), 0) == iota((edge_rows, edge_lanes), 1), 1.0, 0.0
    ).astype(bf16)
    for j, piece in enumerate(pieces):
        rows = block_rows(column, j, width)
        whole[rows, :length] = piece[:width, :]
        whole[rows, length:] = dot(piece[width:, :width], spread, tn).astype(bf16)


def convolve(mp_count, *refs):
    pieces, (weight, bias, message, slopes, full, whole) = refs[:mp_count], refs[mp_count:]
    width = weight.shape[0] // 3
    length = message.shape[1]
    column = lax.axis_index("mp")
    assembled(pieces, whole, column, width, length)
    full[...] = whole[:, :length]
    taps = [dot(weight[k * width : (k + 1) * width, :], whole[...], nn) for k in range(3)]
    lanes = iota((width, length), 1)
    edge = iota((width, edge_lanes), 1)
    inner = (
        taps[1][:, :length]
        + jnp.where(lanes == 0, taps[0][:, length + 1 : length + 2], pltpu.roll(taps[0][:, :length], 1, 1))
        + jnp.where(
            lanes == length - 1,
            taps[2][:, length + 4 : length + 5],
            pltpu.roll(taps[2][:, :length], length - 1, 1),
        )
        + bias[...]
    )
    outer = [
        sum(taps[k][:, length + first + k : length + first + k + 1] for k in range(3)) + bias[...]
        for first in (0, 3)
    ]
    outer = jnp.where(edge == 0, outer[0], jnp.where(edge == 1, outer[1], 0.0))
    own = whole[block_rows(column, 0, width), :].astype(f32)
    beside = jnp.where(edge == 0, own[:, length + 1 : length + 2], own[:, length + 4 : length + 5])
    value, slope = gelu_parts(inner)
    message[:width, :] = (own[:, :length] + value).astype(bf16)
    slopes[:, :length] = slope
    value, slope = gelu_parts(outer)
    hidden = (beside + value).astype(bf16)
    message[width:, :] = jnp.zeros((edge_rows, length), bf16)
    message[width:, :width] = dot(chosen((edge_rows, edge_lanes), ((0, 0), (1, 1))), hidden, nt).astype(bf16)
    slopes[:, length:] = slope


def predict(logits):
    return jnp.maximum(logits, 0.0) + jnp.log1p(jnp.exp(-jnp.abs(logits))) + pseudo_count


def score(mp_count, *refs):
    pieces, (head, bias, counts, logits, sums, full, whole) = refs[:mp_count], refs[mp_count:]
    width = head.shape[0] // mp_count
    length = counts.shape[0]
    assembled(pieces, whole, lax.axis_index("mp"), width, length)
    full[...] = whole[:, :length]
    scores = dot(whole[...], head[...], tn) + bias[...]
    logits[...] = scores[: length + edge_rows, :]
    tracks = head.shape[1]
    pred = jnp.sum(predict(scores[:length, :]), axis=0, keepdims=True)
    seen = jnp.sum(counts[...].astype(f32), axis=0, keepdims=True)
    row = iota((8, tracks), 0)
    sums[...] = jnp.where(row == 0, pred, jnp.where(row == 1, seen, 0.0))


def differentiate(logits, counts, edges, totals, mask, slope):
    length, tracks = counts.shape
    pred_total, count_total = totals[0:1, :], totals[1:2, :]
    ratio = (multi_weight - 1.0) * count_total / pred_total

    def slope_of(scores, observed):
        inner = 1.0 + ratio - multi_weight * observed / predict(scores)
        return (mask[...] * inner * jax.nn.sigmoid(scores)).astype(bf16)

    slope[:length, :] = slope_of(logits[:length, :], counts[...].astype(f32))
    row = iota((edge_rows, tracks), 0)
    beside = edges[...].astype(f32)
    beside = jnp.where(row == 0, beside[6:7, :tracks], jnp.where(row == 1, beside[7:8, :tracks], 0.0))
    slope[length:, :] = slope_of(logits[length:, :], beside)


def packed(out, base, source, start, chunk, both):
    tiles, half = both // 128, chunk // 2
    for t in range(tiles):
        rows = source[pl.ds(start, chunk), t * 128 : (t + 1) * 128]
        out[base + t * chunk : base + (t + 1) * chunk, :] = rows.astype(out.dtype)
    if both % 128:
        pair = [source[pl.ds(start + i * half, half), tiles * 128 :] for i in range(2)]
        at = base + tiles * chunk
        out[at : at + half, :] = jnp.concatenate(pair, axis=1).astype(out.dtype)


def packed_rows(chunk, both):
    return chunk * both // 128


def backward(mp_count, seq_count, split, *refs):
    slopes, heads = refs[:mp_count], refs[mp_count : 2 * mp_count]
    gelu, full, hidden, weight, *outs = refs[2 * mp_count :]
    own, *outs = outs
    carry, outs = outs[: mp_count - 1], outs[mp_count - 1 :]
    width, length = heads[0].shape[0], full.shape[1]
    tracks = heads[0].shape[1]
    place, column = lax.axis_index("seq"), lax.axis_index("mp")
    inner = sum(dot(head[...], part[:length, :], nt) for head, part in zip(heads, slopes))
    outer = sum(dot(head[...], part[length:, :], nt) for head, part in zip(heads, slopes))
    middle = (inner * gelu[:, :length]).astype(bf16).astype(f32)
    outer = (outer * gelu[:, length : length + edge_rows]).astype(bf16).astype(f32)
    low = jnp.where(place == 0, 0.0, outer[:, 0:1])
    high = jnp.where(place == seq_count - 1, 0.0, outer[:, 1:2])
    lanes = iota((width, length), 1)
    stacked = outs[-1]
    stacked[:width, :] = jnp.where(lanes == length - 1, high, pltpu.roll(middle, length - 1, 1)).astype(bf16)
    stacked[width : 2 * width, :] = middle.astype(bf16)
    stacked[2 * width :, :] = jnp.where(lanes == 0, low, pltpu.roll(middle, 1, 1)).astype(bf16)
    grads, total = outs[-3], outs[-2]
    grads[:, :tracks] = dot(hidden[...], slopes[0][:length, :], nn)
    grads[:, tracks:] = dot(full[...], stacked[...], nt)
    if split:
        kept, sent = outs[:2]
        both = grads.shape[1]
        chunk = full.shape[0] // seq_count
        mine = place & 1
        for q in range(seq_count // 2):
            base = q * packed_rows(chunk, both)
            packed(kept, base, grads, pl.multiple_of((2 * q + mine) * chunk, 8), chunk, both)
            packed(sent, base, grads, pl.multiple_of((2 * q + 1 - mine) * chunk, 8), chunk, both)
    total[...] = dot(weight[...], stacked[...], tn)
    own[...] = inner + total[block_rows(column, 0, width), :]
    for j, out in zip(range(1, mp_count), carry):
        out[...] = total[block_rows(column, j, width), :].astype(bf16)


def quartered(count, kept, got, own, *outs):
    rows = own.shape[0]
    at = lax.axis_index("seq") >> 1
    total = outs[-1]
    total[...] = kept[...] + got[...].astype(f32)
    own[...] = total[pl.ds(pl.multiple_of(at * rows, 8), rows), :]
    for j, out in zip(range(1, count), outs):
        out[...] = total[pl.ds(pl.multiple_of((at ^ j) * rows, 8), rows), :].astype(bf16)


def summed_up(scale, own, *refs):
    *parts, grad_head, grad_conv, whole = refs
    total = own[...]
    for part in parts:
        total = total + part[...].astype(f32)
    total = total * scale
    chunk, both = whole.shape
    if total.shape == whole.shape:
        whole[...] = total
    else:
        tiles, half = both // 128, chunk // 2
        for t in range(tiles):
            whole[:, t * 128 : (t + 1) * 128] = total[t * chunk : (t + 1) * chunk, :]
        for i in range(2 if both % 128 else 0):
            at = tiles * chunk
            whole[i * half : (i + 1) * half, tiles * 128 :] = total[at : at + half, i * 64 : (i + 1) * 64]
    tracks, wide = grad_head.shape[1], grad_conv.shape[2]
    grad_head[...] = whole[:, :tracks]
    for k in range(grad_conv.shape[0]):
        grad_conv[k] = whole[:, tracks + k * wide : tracks + (k + 1) * wide]


def finish(mp_count, *refs):
    own, parts, (grad_skip, grad_coarse) = refs[0], refs[1:mp_count], refs[mp_count:]
    total = own[...]
    for part in parts:
        total = total + part[...].astype(f32)
    grad_skip[...] = total.astype(bf16)
    length, half = grad_skip.shape[1], grad_coarse.shape[1]
    pairs = jnp.where(iota((length, half), 0) // 2 == iota((length, half), 1), 1.0, 0.0)
    grad_coarse[...] = dot(total, pairs, nn, lax.Precision.HIGHEST).astype(bf16)


def shards(coarse, skip, conv_weight, conv_bias, head_weight, head_bias, counts, seg_mask):
    width, length = skip.shape
    taps = conv_weight.shape[0]
    seq_count, mp_count = lax.axis_size("seq"), lax.axis_size("mp")
    channels, tracks = head_weight.shape
    scale_back = 1.0 / math.sqrt(length * seq_count)
    place, column = lax.axis_index("seq"), lax.axis_index("mp")
    weight = conv_weight.reshape(taps * width, channels)
    tall = width + edge_rows

    tile = ((edge_rows, length), bf16)
    summed, ahead, behind, own = call(
        prepare, [((width, length), bf16), tile, tile, tile], coarse, skip, counts,
        scratch=[
            (coarse.shape, bf16), (skip.shape, bf16), ((8, tracks), jnp.int32), ((8, tracks), jnp.int32), ((4,), None),
        ],
        outside=(0, 1, 2),
    )
    low = shifted(ahead, "seq", 1)
    high = shifted(behind, "seq", -1)
    edges = low + high + own
    head_rows = head_weight.reshape(mp_count, width, tracks)
    heads = [lax.dynamic_index_in_dim(head_rows, column, 0, keepdims=False)]
    for j in range(1, mp_count):
        heads.append(swap(lax.dynamic_index_in_dim(head_rows, column ^ j, 0, keepdims=False), "mp", j))
    pieces = gathered(jnp.concatenate([summed, edges], axis=0), "mp")
    (weight,) = call(
        stage, [(weight.shape, bf16)], pieces[0], weight, scratch=[((1,), None)], outside=(1,)
    )
    wide = length + edge_lanes
    message, gelu, full_in = call(
        functools.partial(convolve, mp_count),
        [((tall, length), bf16), ((width, wide), f32), ((channels, length), bf16)],
        *pieces, weight, conv_bias[:, None],
        scratch=[((channels, wide), bf16)],
    )
    pieces = gathered(message, "mp")
    logits, sums, full = call(
        functools.partial(score, mp_count),
        [((length + edge_rows, tracks), f32), ((8, tracks), f32), ((channels, length), bf16)],
        *pieces, head_weight, head_bias[None, :], counts,
        scratch=[((channels, wide), bf16)],
    )
    span = seq_count // seg_mask.shape[0]
    totals = totalled(sums, "seq", span)
    mask_row = lax.dynamic_slice_in_dim(seg_mask, place // span, 1, 0).astype(f32)
    (slope,) = call(
        differentiate, [((length + edge_rows, tracks), bf16)], logits, counts, edges, totals, mask_row
    )
    slopes = gathered(slope, "mp")
    chunk = channels // seq_count
    both = tracks + taps * width
    split = chunk % (2 * edge_rows) == 0 and both % 64 == 0 and len(list(staged(0, seq_count.bit_length() - 1))) == 2
    quarter = (packed_rows(chunk, both), 128)
    half = (seq_count // 2 * quarter[0], 128)
    grads_at = ((channels, both), f32)
    scratch = [((channels, length), f32), ((taps * width, length), bf16)]
    own, *outs = call(
        functools.partial(backward, mp_count, seq_count, split),
        [((width, length), f32)]
        + [((width, length), bf16)] * (mp_count - 1)
        + ([(half, f32), (half, bf16)] if split else [grads_at]),
        *slopes, *heads, gelu, full_in, full, weight,
        scratch=([grads_at] if split else []) + scratch,
    )
    carry, grads = outs[: mp_count - 1], outs[mp_count - 1 :]
    if split:
        got = swap(grads[1], "seq", 1)
    parts = []
    for j in range(mp_count - 1, 0, -1):
        parts.append(swap(carry[j - 1], "mp", j))
    if split:
        count = seq_count // 2
        grad_own, *sends = call(
            functools.partial(quartered, count),
            [(quarter, f32)] + [(quarter, bf16)] * (count - 1),
            grads[0], got,
            scratch=[(half, f32)],
        )
        gots = []
        for j in range(count - 1, 0, -1):
            gots.append(swap(sends[j - 1], "seq", 2 * j))
    else:
        grad_own, gots = scattered(grads[0].reshape(seq_count, chunk, both), "seq"), []
    grad_skip, grad_coarse = call(
        functools.partial(finish, mp_count),
        [((width, length), bf16), ((width, length // 2), bf16)],
        own, *parts, last=True,
    )
    grad_head, grad_conv = call(
        functools.partial(summed_up, scale_back),
        [((chunk, tracks), f32), ((taps, chunk, width), f32)],
        grad_own, *gots, scratch=[((chunk, both), f32)], last=True,
    )
    return (grad_skip, grad_coarse, grad_head, grad_conv.transpose(1, 0, 2))


def solution(mesh):
    in_specs = (
        P("mp", "seq"),
        P("mp", "seq"),
        P(None, "mp", None),
        P("mp"),
        P(None, "mp"),
        P("mp"),
        P("seq", "mp"),
        P(None, "mp"),
    )
    out_specs = (P("mp", "seq"), P("mp", "seq"), P("seq", "mp"), P("seq", None, "mp"))

    return jax.shard_map(shards, mesh=mesh, in_specs=in_specs, out_specs=out_specs, check_vma=False)
```

profile of v0, /device:TPU:0, one launch (start us, length us, event | category | flops | bytes accessed | tf_op | source)
XLA Modules:
  0.0 72.7 jit_solution(5237909710817466699)
XLA Ops:
  0.6 1.3 %shard_map.111 = (bf16[192,256]{1,0:T(8,128)(2,1)S(1)}, bf16[16,256]{1,0:T(8,128)(2,1)S(1)}, bf16[16,256]{1,0:T(8,128)(2,1)S(1)}, bf16[16,256]{1,0:T(8,128)(2,1)S(1)}) custom-call(bf16[192,128]{1,0:T(8,128)(2,1)} %coarse_in.1, bf16[192,256]{1,0:T(8,128)(2,1)} %skip_in.1, s32[256,128]{1,0:T(8,128)} %counts.1), custom_call_target="tpu_custom_call" | custom-call | tf_op jit(solution)/shard_map/pallas_call | solution.py:89
  2.0 2.4 %collective-permute-start = (bf16[16,256]{1,0:T(8,128)(2,1)S(1)}, bf16[16,256]{1,0:T(8,128)(2,1)S(1)}, u32[]{:S(2)}, u32[]{:S(2)}) collective-permute-start(bf16[16,256]{1,0:T(8,128)(2,1)S(1)} %get-tuple-element.29), channel_id=1, source_target_pairs={{0,4},{4,8},{8,12},{12,16},{16,20},{20,24},{24,28},{1,5},{5,9},{9,... | collective-permute-start | bytes 24584 | tf_op jit(solution)/shard_map/ppermute | solution.py:29
  4.4 1.3 %collective-permute-start.1 = (bf16[16,256]{1,0:T(8,128)(2,1)S(1)}, bf16[16,256]{1,0:T(8,128)(2,1)S(1)}, u32[]{:S(2)}, u32[]{:S(2)}) collective-permute-start(bf16[16,256]{1,0:T(8,128)(2,1)S(1)} %get-tuple-element.30), channel_id=1, source_target_pairs={{4,0},{8,4},{12,8},{16,12},{20,16},{24,20},{28,24},{5,1},{9,5},{13... | collective-permute-start | bytes 24584 | tf_op jit(solution)/shard_map/ppermute | solution.py:29
  5.7 0.0 collective-permute-done
  5.7 3.9 %collective-permute-done.1 = bf16[16,256]{1,0:T(8,128)(2,1)S(1)} collective-permute-done((bf16[16,256]{1,0:T(8,128)(2,1)S(1)}, bf16[16,256]{1,0:T(8,128)(2,1)S(1)}, u32[]{:S(2)}, u32[]{:S(2)}) %collective-permute-start.1) | collective-permute-done | bytes 8224 | tf_op jit(solution)/shard_map/ppermute | solution.py:29
  9.5 3.7 %collective-permute-start.4 = (bf16[208,256]{1,0:T(8,128)(2,1)S(1)}, bf16[208,256]{1,0:T(8,128)(2,1)S(1)}, u32[]{:S(2)}, u32[]{:S(2)}) collective-permute-start(bf16[208,256]{1,0:T(8,128)(2,1)S(1)} %pad_maximum_fusion.after.refs_0_), channel_id=1, source_target_pairs={{0,3},{1,2},{2,1},{3,0},{4,7},{5,6},{6,5},{7,4},{8,11},{9,10},{10,... | collective-permute-start | bytes 319496 | tf_op jit(solution)/shard_map/ppermute | solution.py:23
  13.2 0.0 collective-permute-start.3
  13.2 0.8 %collective-permute-start.2 = (bf16[208,256]{1,0:T(8,128)(2,1)S(1)}, bf16[208,256]{1,0:T(8,128)(2,1)S(1)}, u32[]{:S(2)}, u32[]{:S(2)}) collective-permute-start(bf16[208,256]{1,0:T(8,128)(2,1)S(1)} %pad_maximum_fusion.after.refs_0_), channel_id=1, source_target_pairs={{0,1},{1,0},{2,3},{3,2},{4,5},{5,4},{6,7},{7,6},{8,9},{9,8},{10,11... | collective-permute-start | bytes 319496 | tf_op jit(solution)/shard_map/ppermute | solution.py:23
  14.0 0.8 %copy.12.refs_5_ = f32[192,1]{1,0:T(8,128)S(1)} copy(f32[192,1]{0,1:T(1,128)} %bitcast.16) | data formatting | bytes 1536 | tf_op jit(solution)/shard_map/broadcast_in_dim | solution.py:372
  14.8 1.2 %shard_map.112.refs_4_.refs_11_ = bf16[576,768]{1,0:T(8,128)(2,1)S(1)} custom-call(bf16[208,256]{1,0:T(8,128)(2,1)S(1)} %pad_maximum_fusion.after.refs_0_, bf16[576,768]{1,0:T(8,128)(2,1)} %bitcast.15), custom_call_target="tpu_custom_call" | custom-call | tf_op jit(solution)/shard_map/pallas_call | solution.py:89
  16.0 0.0 copy-start
  16.0 0.0 copy-start.1
  16.0 0.0 copy-start.2
  16.0 0.0 copy-start.3
  16.0 0.2 collective-permute-done.4.refs_3_
  16.2 6.2 %collective-permute-done.3.refs_2_ = bf16[208,256]{1,0:T(8,128)(2,1)S(1)} collective-permute-done((bf16[208,256]{1,0:T(8,128)(2,1)S(1)}, bf16[208,256]{1,0:T(8,128)(2,1)S(1)}, u32[]{:S(2)}, u32[]{:S(2)}) %collective-permute-start.3) | collective-permute-done | bytes 106528 | tf_op jit(solution)/shard_map/ppermute | solution.py:23
  22.4 0.0 collective-permute-done.2.refs_1_
  22.4 1.3 %shard_map.113 = (bf16[208,256]{1,0:T(8,128)(2,1)S(1)}, f32[192,384]{1,0:T(8,128)S(1)}, bf16[768,256]{1,0:T(8,128)(2,1)S(1)}) custom-call(bf16[208,256]{1,0:T(8,128)(2,1)S(1)} %pad_maximum_fusion.after.refs_0_, bf16[208,256]{1,0:T(8,128)(2,1)S(1)} %collective-permute-done.2.refs_1_, bf16[208,256]{1,0:T(8,128)(2,1)S(1)} %collective-permute-done.3.refs_2_, ...), custom_call_target="tpu_custom_call" | custom-call | tf_op jit(solution)/shard_map/pallas_call | solution.py:89
  23.7 2.1 %collective-permute-start.7 = (bf16[208,256]{1,0:T(8,128)(2,1)S(1)}, bf16[208,256]{1,0:T(8,128)(2,1)S(1)}, u32[]{:S(2)}, u32[]{:S(2)}) collective-permute-start(bf16[208,256]{1,0:T(8,128)(2,1)S(1)} %get-tuple-element.32.refs_0_), channel_id=1, source_target_pairs={{0,3},{1,2},{2,1},{3,0},{4,7},{5,6},{6,5},{7,4},{8,11},{9,10},{10,... | collective-permute-start | bytes 319496 | tf_op jit(solution)/shard_map/ppermute | solution.py:23
  25.8 0.0 collective-permute-start.6
  25.8 2.3 %collective-permute-start.5 = (bf16[208,256]{1,0:T(8,128)(2,1)S(1)}, bf16[208,256]{1,0:T(8,128)(2,1)S(1)}, u32[]{:S(2)}, u32[]{:S(2)}) collective-permute-start(bf16[208,256]{1,0:T(8,128)(2,1)S(1)} %get-tuple-element.32.refs_0_), channel_id=1, source_target_pairs={{0,1},{1,0},{2,3},{3,2},{4,5},{5,4},{6,7},{7,6},{8,9},{9,8},{10,11... | collective-permute-start | bytes 319496 | tf_op jit(solution)/shard_map/ppermute | solution.py:23
  28.1 3.4 %collective-permute-done.7.refs_3_ = bf16[208,256]{1,0:T(8,128)(2,1)S(1)} collective-permute-done((bf16[208,256]{1,0:T(8,128)(2,1)S(1)}, bf16[208,256]{1,0:T(8,128)(2,1)S(1)}, u32[]{:S(2)}, u32[]{:S(2)}) %collective-permute-start.7) | collective-permute-done | bytes 106528 | tf_op jit(solution)/shard_map/ppermute | solution.py:23
  31.5 4.2 %collective-permute-done.6.refs_2_ = bf16[208,256]{1,0:T(8,128)(2,1)S(1)} collective-permute-done((bf16[208,256]{1,0:T(8,128)(2,1)S(1)}, bf16[208,256]{1,0:T(8,128)(2,1)S(1)}, u32[]{:S(2)}, u32[]{:S(2)}) %collective-permute-start.6) | collective-permute-done | bytes 106528 | tf_op jit(solution)/shard_map/ppermute | solution.py:23
  35.7 0.0 collective-permute-done.5.refs_1_
  35.7 0.6 shard_map.114
  36.4 0.2 collective-permute-start.8
  36.6 1.0 %collective-permute-done.8 = f32[8,128]{1,0:T(8,128)S(1)} collective-permute-done((f32[8,128]{1,0:T(8,128)S(1)}, f32[8,128]{1,0:T(8,128)S(1)}, u32[]{:S(2)}, u32[]{:S(2)}) %collective-permute-start.8) | collective-permute-done | bytes 4128 | tf_op jit(solution)/shard_map/ppermute | solution.py:23
  37.6 0.0 collective-permute-start.11
  37.7 3.7 %collective-permute-start.10 = (f32[8,128]{1,0:T(8,128)S(1)}, f32[8,128]{1,0:T(8,128)S(1)}, u32[]{:S(2)}, u32[]{:S(2)}) collective-permute-start(f32[8,128]{1,0:T(8,128)S(1)} %add.35), channel_id=1, source_target_pairs={{0,16},{4,20},{8,24},{12,28},{16,0},{20,4},{24,8},{28,12},{1,17},{... | collective-permute-start | bytes 12296 | tf_op jit(solution)/shard_map/ppermute | solution.py:23
  41.4 0.9 %collective-permute-start.9 = (f32[8,128]{1,0:T(8,128)S(1)}, f32[8,128]{1,0:T(8,128)S(1)}, u32[]{:S(2)}, u32[]{:S(2)}) collective-permute-start(f32[8,128]{1,0:T(8,128)S(1)} %add.35), channel_id=1, source_target_pairs={{0,8},{4,12},{8,0},{12,4},{16,24},{20,28},{24,16},{28,20},{1,9},{5... | collective-permute-start | bytes 12296 | tf_op jit(solution)/shard_map/ppermute | solution.py:23
  42.3 2.3 %collective-permute-start.17 = (bf16[192,128]{1,0:T(8,128)(2,1)S(1)}, bf16[192,128]{1,0:T(8,128)(2,1)S(1)}, u32[]{:S(2)}, u32[]{:S(2)}) collective-permute-start(bf16[192,128]{1,0:T(8,128)(2,1)S(1)} %get-tuple-element.52), channel_id=1, source_target_pairs={{0,3},{1,2},{2,1},{3,0},{4,7},{5,6},{6,5},{7,4},{8,11},{9,10},{10,... | collective-permute-start | bytes 147464 | tf_op jit(solution)/shard_map/ppermute | solution.py:23
  44.6 0.0 collective-permute-done.11
  44.6 0.0 collective-permute-done.10
  44.6 0.4 collective-permute-done.9
  45.0 0.1 shard_map.115.refs_0_
  45.1 2.4 %collective-permute-start.14 = (bf16[272,128]{1,0:T(8,128)(2,1)S(1)}, bf16[272,128]{1,0:T(8,128)(2,1)S(1)}, u32[]{:S(2)}, u32[]{:S(2)}) collective-permute-start(bf16[272,128]{1,0:T(8,128)(2,1)S(1)} %shard_map.115.refs_0_), channel_id=1, source_target_pairs={{0,3},{1,2},{2,1},{3,0},{4,7},{5,6},{6,5},{7,4},{8,11},{9,10},{10,... | collective-permute-start | bytes 208904 | tf_op jit(solution)/shard_map/ppermute | solution.py:23
  47.5 0.0 collective-permute-start.13
  47.5 2.1 %collective-permute-start.12 = (bf16[272,128]{1,0:T(8,128)(2,1)S(1)}, bf16[272,128]{1,0:T(8,128)(2,1)S(1)}, u32[]{:S(2)}, u32[]{:S(2)}) collective-permute-start(bf16[272,128]{1,0:T(8,128)(2,1)S(1)} %shard_map.115.refs_0_), channel_id=1, source_target_pairs={{0,1},{1,0},{2,3},{3,2},{4,5},{5,4},{6,7},{7,6},{8,9},{9,8},{10,11... | collective-permute-start | bytes 208904 | tf_op jit(solution)/shard_map/ppermute | solution.py:23
  49.6 0.9 %collective-permute-start.16 = (bf16[192,128]{1,0:T(8,128)(2,1)S(1)}, bf16[192,128]{1,0:T(8,128)(2,1)S(1)}, u32[]{:S(2)}, u32[]{:S(2)}) collective-permute-start(bf16[192,128]{1,0:T(8,128)(2,1)S(1)} %get-tuple-element.53), channel_id=1, source_target_pairs={{0,2},{1,3},{2,0},{3,1},{4,6},{5,7},{6,4},{7,5},{8,10},{9,11},{10,... | collective-permute-start | bytes 147464 | tf_op jit(solution)/shard_map/ppermute | solution.py:23
  50.4 0.0 collective-permute-done.17.refs_7_
  50.5 2.0 %collective-permute-start.15 = (bf16[192,128]{1,0:T(8,128)(2,1)S(1)}, bf16[192,128]{1,0:T(8,128)(2,1)S(1)}, u32[]{:S(2)}, u32[]{:S(2)}) collective-permute-start(bf16[192,128]{1,0:T(8,128)(2,1)S(1)} %get-tuple-element.54), channel_id=1, source_target_pairs={{0,1},{1,0},{2,3},{3,2},{4,5},{5,4},{6,7},{7,6},{8,9},{9,8},{10,11... | collective-permute-start | bytes 147464 | tf_op jit(solution)/shard_map/ppermute | solution.py:23
  52.5 3.3 %collective-permute-done.16.refs_6_ = bf16[192,128]{1,0:T(8,128)(2,1)S(1)} collective-permute-done((bf16[192,128]{1,0:T(8,128)(2,1)S(1)}, bf16[192,128]{1,0:T(8,128)(2,1)S(1)}, u32[]{:S(2)}, u32[]{:S(2)}) %collective-permute-start.16) | collective-permute-done | bytes 49184 | tf_op jit(solution)/shard_map/ppermute | solution.py:23
  55.8 0.0 collective-permute-done.15.refs_5_
  55.8 0.0 collective-permute-done.14.refs_3_
  55.8 0.0 collective-permute-done.13.refs_2_
  55.8 0.0 collective-permute-done.12.refs_1_
  55.8 1.6 %shard_map.116 = (f32[192,256]{1,0:T(8,128)S(1)}, bf16[192,256]{1,0:T(8,128)(2,1)S(1)}, bf16[192,256]{1,0:T(8,128)(2,1)S(1)}, bf16[192,256]{1,0:T(8,128)(2,1)S(1...) custom-call(bf16[272,128]{1,0:T(8,128)(2,1)S(1)} %shard_map.115.refs_0_, ...), custom_call_target="tpu_custom_call" | custom-call | tf_op jit(solution)/shard_map/pallas_call | solution.py:89
  57.5 0.1 collective-permute-start.21
  57.6 2.0 %collective-permute-start.18 = (bf16[192,256]{1,0:T(8,128)(2,1)S(1)}, bf16[192,256]{1,0:T(8,128)(2,1)S(1)}, u32[]{:S(2)}, u32[]{:S(2)}) collective-permute-start(bf16[192,256]{1,0:T(8,128)(2,1)S(1)} %get-tuple-element.39), channel_id=1, source_target_pairs={{0,3},{1,2},{2,1},{3,0},{4,7},{5,6},{6,5},{7,4},{8,11},{9,10},{10,... | collective-permute-start | bytes 294920 | tf_op jit(solution)/shard_map/ppermute | solution.py:23
  59.6 0.0 collective-permute-done.21.got
  59.6 0.2 shard_map.118
  59.8 1.9 %collective-permute-start.22 = (bf16[528,128]{1,0:T(8,128)(2,1)S(1)}, bf16[528,128]{1,0:T(8,128)(2,1)S(1)}, u32[]{:S(2)}, u32[]{:S(2)}) collective-permute-start(bf16[528,128]{1,0:T(8,128)(2,1)S(1)} %get-tuple-element.47), channel_id=1, source_target_pairs={{0,24},{4,28},{8,16},{12,20},{16,8},{20,12},{24,0},{28,4},{1,25},{... | collective-permute-start | bytes 405512 | tf_op jit(solution)/shard_map/ppermute | solution.py:23
  61.8 0.5 collective-permute-start.23
  62.3 1.1 %collective-permute-start.24 = (bf16[528,128]{1,0:T(8,128)(2,1)S(1)}, bf16[528,128]{1,0:T(8,128)(2,1)S(1)}, u32[]{:S(2)}, u32[]{:S(2)}) collective-permute-start(bf16[528,128]{1,0:T(8,128)(2,1)S(1)} %get-tuple-element.49), channel_id=1, source_target_pairs={{0,8},{4,12},{8,0},{12,4},{16,24},{20,28},{24,16},{28,20},{1,9},{5... | collective-permute-start | bytes 405512 | tf_op jit(solution)/shard_map/ppermute | solution.py:23
  63.4 0.6 collective-permute-start.19
  64.0 0.7 collective-permute-done.18.refs_1_
  64.7 1.1 %collective-permute-start.20 = (bf16[192,256]{1,0:T(8,128)(2,1)S(1)}, bf16[192,256]{1,0:T(8,128)(2,1)S(1)}, u32[]{:S(2)}, u32[]{:S(2)}) collective-permute-start(bf16[192,256]{1,0:T(8,128)(2,1)S(1)} %get-tuple-element.41), channel_id=1, source_target_pairs={{0,1},{1,0},{2,3},{3,2},{4,5},{5,4},{6,7},{7,6},{8,9},{9,8},{10,11... | collective-permute-start | bytes 294920 | tf_op jit(solution)/shard_map/ppermute | solution.py:23
  65.8 4.7 %collective-permute-done.19.refs_2_ = bf16[192,256]{1,0:T(8,128)(2,1)S(1)} collective-permute-done((bf16[192,256]{1,0:T(8,128)(2,1)S(1)}, bf16[192,256]{1,0:T(8,128)(2,1)S(1)}, u32[]{:S(2)}, u32[]{:S(2)}) %collective-permute-start.19) | collective-permute-done | bytes 98336 | tf_op jit(solution)/shard_map/ppermute | solution.py:23
  70.5 0.4 collective-permute-done.20.refs_3_
  70.9 1.0 %shard_map.117 = (bf16[192,256]{1,0:T(8,128)(2,1)}, bf16[192,128]{1,0:T(8,128)(2,1)}) custom-call(f32[192,256]{1,0:T(8,128)S(1)} %get-tuple-element.38.refs_0_, bf16[192,256]{1,0:T(8,128)(2,1)S(1)} %collective-permute-done.18.refs_1_, bf16[192,256]{1,0:T(8,128)(2,1)S(1)} %collective-permute-done.19.refs_2_, bf16[192,256]{1,0:T(8,128)(2,1)S(1)} %collective-permute-done.20.refs_3_), custom_call_target="tpu_custom_call" | custom-call | tf_op jit(solution)/shard_map/pallas_call | solution.py:89
  71.8 0.0 collective-permute-done.22.refs_0_
  71.8 0.0 collective-permute-done.23.refs_1_
  71.9 0.0 collective-permute-done.24.refs_2_
  71.9 0.8 %shard_map.119 = (f32[96,128]{1,0:T(8,128)}, f32[3,96,192]{2,1,0:T(8,128)}) custom-call(f32[528,128]{1,0:T(8,128)S(1)} %get-tuple-element.46.own, bf16[528,128]{1,0:T(8,128)(2,1)S(1)} %collective-permute-done.22.refs_0_, bf16[528,128]{1,0:T(8,128)(2,1)S(1)} %collective-permute-done.23.refs_1_, bf16[528,128]{1,0:T(8,128)(2,1)S(1)} %collective-permute-done.24.refs_2_), custom_call_target="tpu_custom_call" | custom-call | tf_op jit(solution)/shard_map/pallas_call | solution.py:89
  (10 shorter events, 0.0 us)
Async XLA Ops:
  2.0 3.7 %collective-permute-start = (bf16[16,256]{1,0:T(8,128)(2,1)S(1)}, bf16[16,256]{1,0:T(8,128)(2,1)S(1)}, u32[]{:S(2)}, u32[]{:S(2)}) collective-permute-start(bf16[16,256]{1,0:T(8,128)(2,1)S(1)} %get-tuple-element.29), channel_id=1, source_target_pairs={{0,4},{4,8},{8,12},{12,16},{16,20},{20,24},{24,28},{1,5},{5,9},{9,... | collective-permute-start | bytes 24584 | tf_op jit(solution)/shard_map/ppermute | solution.py:29
  4.4 5.2 %collective-permute-start.1 = (bf16[16,256]{1,0:T(8,128)(2,1)S(1)}, bf16[16,256]{1,0:T(8,128)(2,1)S(1)}, u32[]{:S(2)}, u32[]{:S(2)}) collective-permute-start(bf16[16,256]{1,0:T(8,128)(2,1)S(1)} %get-tuple-element.30), channel_id=1, source_target_pairs={{4,0},{8,4},{12,8},{16,12},{20,16},{24,20},{28,24},{5,1},{9,5},{13... | collective-permute-start | bytes 24584 | tf_op jit(solution)/shard_map/ppermute | solution.py:29
  9.5 6.7 %collective-permute-start.4 = (bf16[208,256]{1,0:T(8,128)(2,1)S(1)}, bf16[208,256]{1,0:T(8,128)(2,1)S(1)}, u32[]{:S(2)}, u32[]{:S(2)}) collective-permute-start(bf16[208,256]{1,0:T(8,128)(2,1)S(1)} %pad_maximum_fusion.after.refs_0_), channel_id=1, source_target_pairs={{0,3},{1,2},{2,1},{3,0},{4,7},{5,6},{6,5},{7,4},{8,11},{9,10},{10,... | collective-permute-start | bytes 319496 | tf_op jit(solution)/shard_map/ppermute | solution.py:23
  13.2 9.2 %collective-permute-start.3 = (bf16[208,256]{1,0:T(8,128)(2,1)S(1)}, bf16[208,256]{1,0:T(8,128)(2,1)S(1)}, u32[]{:S(2)}, u32[]{:S(2)}) collective-permute-start(bf16[208,256]{1,0:T(8,128)(2,1)S(1)} %pad_maximum_fusion.after.refs_0_), channel_id=1, source_target_pairs={{0,2},{1,3},{2,0},{3,1},{4,6},{5,7},{6,4},{7,5},{8,10},{9,11},{10,... | collective-permute-start | bytes 319496 | tf_op jit(solution)/shard_map/ppermute | solution.py:23
  13.2 9.2 %collective-permute-start.2 = (bf16[208,256]{1,0:T(8,128)(2,1)S(1)}, bf16[208,256]{1,0:T(8,128)(2,1)S(1)}, u32[]{:S(2)}, u32[]{:S(2)}) collective-permute-start(bf16[208,256]{1,0:T(8,128)(2,1)S(1)} %pad_maximum_fusion.after.refs_0_), channel_id=1, source_target_pairs={{0,1},{1,0},{2,3},{3,2},{4,5},{5,4},{6,7},{7,6},{8,9},{9,8},{10,11... | collective-permute-start | bytes 319496 | tf_op jit(solution)/shard_map/ppermute | solution.py:23
  16.0 19.8 %copy-start = (s32[256,128]{1,0:T(8,128)S(1)}, s32[256,128]{1,0:T(8,128)}, u32[]{:S(2)}) copy-start(s32[256,128]{1,0:T(8,128)} %counts.1) | copy-start | bytes 393220
  16.0 19.7 %copy-start.1 = (bf16[768,128]{1,0:T(8,128)(2,1)S(1)}, bf16[768,128]{1,0:T(8,128)(2,1)}, u32[]{:S(2)}) copy-start(bf16[768,128]{1,0:T(8,128)(2,1)} %refs_4_.1) | copy-start | bytes 589828
  16.0 19.7 %copy-start.2 = (f32[128]{0:T(128)S(1)}, f32[128]{0:T(128)}, u32[]{:S(2)}) copy-start(f32[128]{0:T(128)} %param.13) | copy-start | bytes 1540
  16.0 28.6 %copy-start.3 = (s32[1,128]{1,0:T(1,128)S(1)}, s32[1,128]{1,0:T(1,128)}, u32[]{:S(2)}) copy-start(s32[1,128]{1,0:T(1,128)} %param.15) | copy-start | bytes 1540
  23.7 7.8 %collective-permute-start.7 = (bf16[208,256]{1,0:T(8,128)(2,1)S(1)}, bf16[208,256]{1,0:T(8,128)(2,1)S(1)}, u32[]{:S(2)}, u32[]{:S(2)}) collective-permute-start(bf16[208,256]{1,0:T(8,128)(2,1)S(1)} %get-tuple-element.32.refs_0_), channel_id=1, source_target_pairs={{0,3},{1,2},{2,1},{3,0},{4,7},{5,6},{6,5},{7,4},{8,11},{9,10},{10,... | collective-permute-start | bytes 319496 | tf_op jit(solution)/shard_map/ppermute | solution.py:23
  25.8 9.9 %collective-permute-start.6 = (bf16[208,256]{1,0:T(8,128)(2,1)S(1)}, bf16[208,256]{1,0:T(8,128)(2,1)S(1)}, u32[]{:S(2)}, u32[]{:S(2)}) collective-permute-start(bf16[208,256]{1,0:T(8,128)(2,1)S(1)} %get-tuple-element.32.refs_0_), channel_id=1, source_target_pairs={{0,2},{1,3},{2,0},{3,1},{4,6},{5,7},{6,4},{7,5},{8,10},{9,11},{10,... | collective-permute-start | bytes 319496 | tf_op jit(solution)/shard_map/ppermute | solution.py:23
  25.8 9.9 %collective-permute-start.5 = (bf16[208,256]{1,0:T(8,128)(2,1)S(1)}, bf16[208,256]{1,0:T(8,128)(2,1)S(1)}, u32[]{:S(2)}, u32[]{:S(2)}) collective-permute-start(bf16[208,256]{1,0:T(8,128)(2,1)S(1)} %get-tuple-element.32.refs_0_), channel_id=1, source_target_pairs={{0,1},{1,0},{2,3},{3,2},{4,5},{5,4},{6,7},{7,6},{8,9},{9,8},{10,11... | collective-permute-start | bytes 319496 | tf_op jit(solution)/shard_map/ppermute | solution.py:23
  36.4 1.2 %collective-permute-start.8 = (f32[8,128]{1,0:T(8,128)S(1)}, f32[8,128]{1,0:T(8,128)S(1)}, u32[]{:S(2)}, u32[]{:S(2)}) collective-permute-start(f32[8,128]{1,0:T(8,128)S(1)} %get-tuple-element.34), channel_id=1, source_target_pairs={{0,4},{4,0},{8,12},{12,8},{16,20},{20,16},{24,28},{28,24},{1,5},{5... | collective-permute-start | bytes 12296 | tf_op jit(solution)/shard_map/ppermute | solution.py:23
  37.6 7.0 %collective-permute-start.11 = (f32[8,128]{1,0:T(8,128)S(1)}, f32[8,128]{1,0:T(8,128)S(1)}, u32[]{:S(2)}, u32[]{:S(2)}) collective-permute-start(f32[8,128]{1,0:T(8,128)S(1)} %add.35), channel_id=1, source_target_pairs={{0,24},{4,28},{8,16},{12,20},{16,8},{20,12},{24,0},{28,4},{1,25},{... | collective-permute-start | bytes 12296 | tf_op jit(solution)/shard_map/ppermute | solution.py:23
  37.7 7.0 %collective-permute-start.10 = (f32[8,128]{1,0:T(8,128)S(1)}, f32[8,128]{1,0:T(8,128)S(1)}, u32[]{:S(2)}, u32[]{:S(2)}) collective-permute-start(f32[8,128]{1,0:T(8,128)S(1)} %add.35), channel_id=1, source_target_pairs={{0,16},{4,20},{8,24},{12,28},{16,0},{20,4},{24,8},{28,12},{1,17},{... | collective-permute-start | bytes 12296 | tf_op jit(solution)/shard_map/ppermute | solution.py:23
  41.4 3.6 %collective-permute-start.9 = (f32[8,128]{1,0:T(8,128)S(1)}, f32[8,128]{1,0:T(8,128)S(1)}, u32[]{:S(2)}, u32[]{:S(2)}) collective-permute-start(f32[8,128]{1,0:T(8,128)S(1)} %add.35), channel_id=1, source_target_pairs={{0,8},{4,12},{8,0},{12,4},{16,24},{20,28},{24,16},{28,20},{1,9},{5... | collective-permute-start | bytes 12296 | tf_op jit(solution)/shard_map/ppermute | solution.py:23
  42.3 8.1 %collective-permute-start.17 = (bf16[192,128]{1,0:T(8,128)(2,1)S(1)}, bf16[192,128]{1,0:T(8,128)(2,1)S(1)}, u32[]{:S(2)}, u32[]{:S(2)}) collective-permute-start(bf16[192,128]{1,0:T(8,128)(2,1)S(1)} %get-tuple-element.52), channel_id=1, source_target_pairs={{0,3},{1,2},{2,1},{3,0},{4,7},{5,6},{6,5},{7,4},{8,11},{9,10},{10,... | collective-permute-start | bytes 147464 | tf_op jit(solution)/shard_map/ppermute | solution.py:23
  45.1 10.7 %collective-permute-start.14 = (bf16[272,128]{1,0:T(8,128)(2,1)S(1)}, bf16[272,128]{1,0:T(8,128)(2,1)S(1)}, u32[]{:S(2)}, u32[]{:S(2)}) collective-permute-start(bf16[272,128]{1,0:T(8,128)(2,1)S(1)} %shard_map.115.refs_0_), channel_id=1, source_target_pairs={{0,3},{1,2},{2,1},{3,0},{4,7},{5,6},{6,5},{7,4},{8,11},{9,10},{10,... | collective-permute-start | bytes 208904 | tf_op jit(solution)/shard_map/ppermute | solution.py:23
  47.5 8.3 %collective-permute-start.13 = (bf16[272,128]{1,0:T(8,128)(2,1)S(1)}, bf16[272,128]{1,0:T(8,128)(2,1)S(1)}, u32[]{:S(2)}, u32[]{:S(2)}) collective-permute-start(bf16[272,128]{1,0:T(8,128)(2,1)S(1)} %shard_map.115.refs_0_), channel_id=1, source_target_pairs={{0,2},{1,3},{2,0},{3,1},{4,6},{5,7},{6,4},{7,5},{8,10},{9,11},{10,... | collective-permute-start | bytes 208904 | tf_op jit(solution)/shard_map/ppermute | solution.py:23
  47.5 8.3 %collective-permute-start.12 = (bf16[272,128]{1,0:T(8,128)(2,1)S(1)}, bf16[272,128]{1,0:T(8,128)(2,1)S(1)}, u32[]{:S(2)}, u32[]{:S(2)}) collective-permute-start(bf16[272,128]{1,0:T(8,128)(2,1)S(1)} %shard_map.115.refs_0_), channel_id=1, source_target_pairs={{0,1},{1,0},{2,3},{3,2},{4,5},{5,4},{6,7},{7,6},{8,9},{9,8},{10,11... | collective-permute-start | bytes 208904 | tf_op jit(solution)/shard_map/ppermute | solution.py:23
  49.6 6.2 %collective-permute-start.16 = (bf16[192,128]{1,0:T(8,128)(2,1)S(1)}, bf16[192,128]{1,0:T(8,128)(2,1)S(1)}, u32[]{:S(2)}, u32[]{:S(2)}) collective-permute-start(bf16[192,128]{1,0:T(8,128)(2,1)S(1)} %get-tuple-element.53), channel_id=1, source_target_pairs={{0,2},{1,3},{2,0},{3,1},{4,6},{5,7},{6,4},{7,5},{8,10},{9,11},{10,... | collective-permute-start | bytes 147464 | tf_op jit(solution)/shard_map/ppermute | solution.py:23
  50.5 5.4 %collective-permute-start.15 = (bf16[192,128]{1,0:T(8,128)(2,1)S(1)}, bf16[192,128]{1,0:T(8,128)(2,1)S(1)}, u32[]{:S(2)}, u32[]{:S(2)}) collective-permute-start(bf16[192,128]{1,0:T(8,128)(2,1)S(1)} %get-tuple-element.54), channel_id=1, source_target_pairs={{0,1},{1,0},{2,3},{3,2},{4,5},{5,4},{6,7},{7,6},{8,9},{9,8},{10,11... | collective-permute-start | bytes 147464 | tf_op jit(solution)/shard_map/ppermute | solution.py:23
  57.5 2.1 %collective-permute-start.21 = (bf16[2112,128]{1,0:T(8,128)(2,1)S(1)}, bf16[2112,128]{1,0:T(8,128)(2,1)S(1)}, u32[]{:S(2)}, u32[]{:S(2)}) collective-permute-start(bf16[2112,128]{1,0:T(8,128)(2,1)S(1)} %get-tuple-element.45), channel_id=1, source_target_pairs={{0,4},{4,0},{8,12},{12,8},{16,20},{20,16},{24,28},{28,24},{1,5},{5... | collective-permute-start | bytes 1622024 | tf_op jit(solution)/shard_map/ppermute | solution.py:23
  57.6 7.1 %collective-permute-start.18 = (bf16[192,256]{1,0:T(8,128)(2,1)S(1)}, bf16[192,256]{1,0:T(8,128)(2,1)S(1)}, u32[]{:S(2)}, u32[]{:S(2)}) collective-permute-start(bf16[192,256]{1,0:T(8,128)(2,1)S(1)} %get-tuple-element.39), channel_id=1, source_target_pairs={{0,3},{1,2},{2,1},{3,0},{4,7},{5,6},{6,5},{7,4},{8,11},{9,10},{10,... | collective-permute-start | bytes 294920 | tf_op jit(solution)/shard_map/ppermute | solution.py:23
  59.8 12.0 %collective-permute-start.22 = (bf16[528,128]{1,0:T(8,128)(2,1)S(1)}, bf16[528,128]{1,0:T(8,128)(2,1)S(1)}, u32[]{:S(2)}, u32[]{:S(2)}) collective-permute-start(bf16[528,128]{1,0:T(8,128)(2,1)S(1)} %get-tuple-element.47), channel_id=1, source_target_pairs={{0,24},{4,28},{8,16},{12,20},{16,8},{20,12},{24,0},{28,4},{1,25},{... | collective-permute-start | bytes 405512 | tf_op jit(solution)/shard_map/ppermute | solution.py:23
  61.8 10.1 %collective-permute-start.23 = (bf16[528,128]{1,0:T(8,128)(2,1)S(1)}, bf16[528,128]{1,0:T(8,128)(2,1)S(1)}, u32[]{:S(2)}, u32[]{:S(2)}) collective-permute-start(bf16[528,128]{1,0:T(8,128)(2,1)S(1)} %get-tuple-element.48), channel_id=1, source_target_pairs={{0,16},{4,20},{8,24},{12,28},{16,0},{20,4},{24,8},{28,12},{1,17},{... | collective-permute-start | bytes 405512 | tf_op jit(solution)/shard_map/ppermute | solution.py:23
  62.3 9.6 %collective-permute-start.24 = (bf16[528,128]{1,0:T(8,128)(2,1)S(1)}, bf16[528,128]{1,0:T(8,128)(2,1)S(1)}, u32[]{:S(2)}, u32[]{:S(2)}) collective-permute-start(bf16[528,128]{1,0:T(8,128)(2,1)S(1)} %get-tuple-element.49), channel_id=1, source_target_pairs={{0,8},{4,12},{8,0},{12,4},{16,24},{20,28},{24,16},{28,20},{1,9},{5... | collective-permute-start | bytes 405512 | tf_op jit(solution)/shard_map/ppermute | solution.py:23
  63.4 7.1 %collective-permute-start.19 = (bf16[192,256]{1,0:T(8,128)(2,1)S(1)}, bf16[192,256]{1,0:T(8,128)(2,1)S(1)}, u32[]{:S(2)}, u32[]{:S(2)}) collective-permute-start(bf16[192,256]{1,0:T(8,128)(2,1)S(1)} %get-tuple-element.40), channel_id=1, source_target_pairs={{0,2},{1,3},{2,0},{3,1},{4,6},{5,7},{6,4},{7,5},{8,10},{9,11},{10,... | collective-permute-start | bytes 294920 | tf_op jit(solution)/shard_map/ppermute | solution.py:23
  64.7 6.2 %collective-permute-start.20 = (bf16[192,256]{1,0:T(8,128)(2,1)S(1)}, bf16[192,256]{1,0:T(8,128)(2,1)S(1)}, u32[]{:S(2)}, u32[]{:S(2)}) collective-permute-start(bf16[192,256]{1,0:T(8,128)(2,1)S(1)} %get-tuple-element.41), channel_id=1, source_target_pairs={{0,1},{1,0},{2,3},{3,2},{4,5},{5,4},{6,7},{7,6},{8,9},{9,8},{10,11... | collective-permute-start | bytes 294920 | tf_op jit(solution)/shard_map/ppermute | solution.py:23
where the time goes:
time: 72.9 us; the launch traced here: 72.7 us
  starting transfers between devices  34.4 us (47%)
  waiting for transfers between devices  28.4 us (39%)
  Pallas kernels  8.23 us (11%)
  local copies, waits for them, and re-layouts  0.83 us (1%)
  between operations  0.8 us (1%)
    ppermute x23, starting transfers between devices, swap(): return lax.ppermute(block, axis, [(i, i ^ mask) for i in range(count)])  30.7 us
    ppermute x23, waiting for transfers between devices, swap(): return lax.ppermute(block, axis, [(i, i ^ mask) for i in range(count)])  24.5 us
    pallas_call x9, Pallas kernels, call(): pl.pallas_call(body, out_shape=[jax.ShapeDtypeStruct(shape, kind) if last...  8.23 us
    ppermute x2, waiting for transfers between devices, shifted(): return lax.ppermute(block, axis, pairs)  3.86 us
    ppermute x2, starting transfers between devices, shifted(): return lax.ppermute(block, axis, pairs)  3.69 us
  transfers between devices with their start and end apart: 25, of which 11 were waited for; matrix products, arithmetic and copies ran while one was open for 1% of the time, Pallas kernels for 3%

commit v1 on v0

--- a/solution.py
+++ b/solution.py
@@ -13,7 +13,7 @@
 cubic_coef = 0.044715
 multi_weight = 5.0
 pseudo_count = 0.5
-edge_rows = 16
+edge_rows = 8
 edge_lanes = 128
 bf16, f32 = jnp.bfloat16, jnp.float32
 
@@ -23,10 +23,10 @@
     return lax.ppermute(block, axis, [(i, i ^ mask) for i in range(count)])
 
 
-def shifted(block, axis, step):
+def crossed(block, axis):
     count = lax.axis_size(axis)
-    pairs = [(i, i + step) for i in range(count) if 0 <= i + step < count]
-    return lax.ppermute(block, axis, pairs)
+    pairs = [(i, i + 1) for i in range(1, count - 1, 2)]
+    return lax.ppermute(block, axis, pairs + [(b, a) for a, b in pairs])
 
 
 def gathered(block, axis):
@@ -61,7 +61,10 @@
 
 def totalled(block, axis, span):
     for low, wide in staged(0, span.bit_length() - 1):
-        block = sum([swap(block, axis, step << low) for step in range(1, 1 << wide)], block)
+        parts = []
+        for step in range(1, 1 << wide):
+            parts.append(swap(block, axis, step << low))
+        block = sum(parts, block)
     return block
 
 
@@ -106,7 +109,7 @@
     return pl.ds(pl.multiple_of((column ^ j) * size, size), size)
 
 
-def prepare(coarse_in, skip_in, counts_in, summed, ahead, behind, own, coarse, skip, top, bottom, done):
+def prepare(coarse_in, skip_in, counts_in, summed, pair, cross, own, coarse, skip, top, bottom, done):
     width, length = skip.shape
     rows, tracks = top.shape
     copies = [
@@ -129,24 +132,34 @@
     ).astype(bf16)
     total = (dot(coarse[...], pairs, nn) + skip[...].astype(f32)).astype(bf16)
     summed[...] = total
-    for out, picks, slot, line in (
-        (ahead, ((0, length - 2), (1, length - 1)), 6, bottom[rows - 1 : rows, :]),
-        (behind, ((4, 0), (5, 1)), 7, top[0:1, :]),
-        (own, ((2, 0), (3, length - 1)), None, None),
+    slot = iota((edge_rows, tracks), 0)
+    ahead = dot(chosen((edge_rows, length), ((0, length - 2), (1, length - 1))), total, nt)
+    behind = dot(chosen((edge_rows, length), ((4, 0), (5, 1))), total, nt)
+    mine = dot(chosen((edge_rows, length), ((2, 0), (3, length - 1))), total, nt)
+    first = jnp.where(slot == 7, top[0:1, :].astype(f32), behind[:, :tracks])
+    last = jnp.where(slot == 6, bottom[rows - 1 : rows, :].astype(f32), ahead[:, :tracks])
+    even = lax.axis_index("seq") % 2 == 0
+    for out, (left, right) in (
+        (pair, (jnp.where(even, last, first), jnp.where(even, ahead, behind))),
+        (cross, (jnp.where(even, first, last), jnp.where(even, behind, ahead))),
+        (own, (mine[:, :tracks], mine)),
     ):
-        picked = dot(chosen((edge_rows, length), picks), total, nt).astype(bf16)
         out[...] = jnp.zeros(out.shape, bf16)
-        out[:, :width] = picked
-        if slot is not None:
-            line = jnp.broadcast_to(line.astype(f32), (edge_rows, tracks))
-            held = picked[:, :tracks].astype(f32)
-            out[:, :tracks] = jnp.where(iota(held.shape, 0) == slot, line, held).astype(bf16)
+        out[:, :tracks] = left.astype(bf16)
+        out[:, tracks:width] = right[:, tracks:].astype(bf16)
 
 
 def stage(after, weight_in, weight, done):
     copy = pltpu.make_async_copy(weight_in, weight, done.at[0])
     copy.start()
     copy.wait()
+
+
+def joined(after, *refs):
+    *parts, out = refs
+    rows = parts[0].shape[0]
+    for i, part in enumerate(parts):
+        out[i * rows : (i + 1) * rows, :] = part[...]
 
 
 def gelu_parts(inputs):
@@ -256,14 +269,21 @@
     return chunk * both // 128
 
 
-def backward(mp_count, seq_count, split, *refs):
-    slopes, heads = refs[:mp_count], refs[mp_count : 2 * mp_count]
-    gelu, full, hidden, weight, *outs = refs[2 * mp_count :]
+def backward(mp_count, seq_count, split, group, *refs):
+    slopes, head_own, bundles = refs[:mp_count], refs[mp_count], refs[mp_count + 1 : mp_count + 1 + group]
+    gelu, full, hidden, weight, *outs = refs[mp_count + 1 + group :]
+    head_rows = outs[-3]
     own, *outs = outs
     carry, outs = outs[: mp_count - 1], outs[mp_count - 1 :]
-    width, length = heads[0].shape[0], full.shape[1]
-    tracks = heads[0].shape[1]
+    width, length = head_own.shape[0], full.shape[1]
+    tracks = head_own.shape[1]
     place, column = lax.axis_index("seq"), lax.axis_index("mp")
+    part = width // group
+    for r, bundle in enumerate(bundles):
+        at = pl.multiple_of((((place >> 1) & (group - 1)) ^ r) * part, 16)
+        for j in range(mp_count - 1):
+            head_rows[j, pl.ds(at, part), :] = bundle[j * part : (j + 1) * part, :]
+    heads = [head_own] + [head_rows.at[j] for j in range(mp_count - 1)]
     inner = sum(dot(head[...], part[:length, :], nt) for head, part in zip(heads, slopes))
     outer = sum(dot(head[...], part[length:, :], nt) for head, part in zip(heads, slopes))
     middle = (inner * gelu[:, :length]).astype(bf16).astype(f32)
@@ -275,7 +295,7 @@
     stacked[:width, :] = jnp.where(lanes == length - 1, high, pltpu.roll(middle, length - 1, 1)).astype(bf16)
     stacked[width : 2 * width, :] = middle.astype(bf16)
     stacked[2 * width :, :] = jnp.where(lanes == 0, low, pltpu.roll(middle, 1, 1)).astype(bf16)
-    grads, total = outs[-3], outs[-2]
+    grads, total = outs[-4], outs[-2]
     grads[:, :tracks] = dot(hidden[...], slopes[0][:length, :], nn)
     grads[:, tracks:] = dot(full[...], stacked[...], nt)
     if split:
@@ -326,7 +346,7 @@
 
 
 def finish(mp_count, *refs):
-    own, parts, (grad_skip, grad_coarse) = refs[0], refs[1:mp_count], refs[mp_count:]
+    own, parts, (_, grad_skip, grad_coarse) = refs[0], refs[1:mp_count], refs[mp_count:]
     total = own[...]
     for part in parts:
         total = total + part[...].astype(f32)
@@ -347,20 +367,25 @@
     tall = width + edge_rows
 
     tile = ((edge_rows, length), bf16)
-    summed, ahead, behind, own = call(
+    summed, pair, cross, own = call(
         prepare, [((width, length), bf16), tile, tile, tile], coarse, skip, counts,
         scratch=[
             (coarse.shape, bf16), (skip.shape, bf16), ((8, tracks), jnp.int32), ((8, tracks), jnp.int32), ((4,), None),
         ],
         outside=(0, 1, 2),
     )
-    low = shifted(ahead, "seq", 1)
-    high = shifted(behind, "seq", -1)
-    edges = low + high + own
-    head_rows = head_weight.reshape(mp_count, width, tracks)
-    heads = [lax.dynamic_index_in_dim(head_rows, column, 0, keepdims=False)]
+    cross = crossed(cross, "seq")
+    pair = swap(pair, "seq", 1)
+    edges = cross + pair + own
+    group = min(4, seq_count // 2)
+    head_parts = head_weight.reshape(mp_count, group, width // group, tracks)
+    head_own = lax.dynamic_index_in_dim(head_weight.reshape(mp_count, width, tracks), column, 0, keepdims=False)
+    shares = []
     for j in range(1, mp_count):
-        heads.append(swap(lax.dynamic_index_in_dim(head_rows, column ^ j, 0, keepdims=False), "mp", j))
+        share = lax.dynamic_slice(
+            head_parts, (column ^ j, (place >> 1) & (group - 1), 0, 0), (1, 1, width // group, tracks)
+        )
+        shares.append(swap(share.reshape(width // group, tracks), "mp", j))
     pieces = gathered(jnp.concatenate([summed, edges], axis=0), "mp")
     (weight,) = call(
         stage, [(weight.shape, bf16)], pieces[0], weight, scratch=[((1,), None)], outside=(1,)
@@ -373,6 +398,10 @@
         scratch=[((channels, wide), bf16)],
     )
     pieces = gathered(message, "mp")
+    (share,) = call(joined, [((width // group * (mp_count - 1), tracks), bf16)], message, *shares)
+    bundles = [share]
+    for r in range(1, group):
+        bundles.append(swap(share, "seq", 2 * r))
     logits, sums, full = call(
         functools.partial(score, mp_count),
         [((length + edge_rows, tracks), f32), ((8, tracks), f32), ((channels, length), bf16)],
@@ -393,13 +422,14 @@
     half = (seq_count // 2 * quarter[0], 128)
     grads_at = ((channels, both), f32)
     scratch = [((channels, length), f32), ((taps * width, length), bf16)]
+    head_at = [((mp_count - 1, width, tracks), bf16)]
     own, *outs = call(
-        functools.partial(backward, mp_count, seq_count, split),
+        functools.partial(backward, mp_count, seq_count, split, group),
         [((width, length), f32)]
         + [((width, length), bf16)] * (mp_count - 1)
         + ([(half, f32), (half, bf16)] if split else [grads_at]),
-        *slopes, *heads, gelu, full_in, full, weight,
-        scratch=([grads_at] if split else []) + scratch,
+        *slopes, head_own, *bundles, gelu, full_in, full, weight,
+        scratch=([grads_at] if split else []) + head_at + scratch,
     )
     carry, grads = outs[: mp_count - 1], outs[mp_count - 1 :]
     if split:
@@ -420,15 +450,15 @@
             gots.append(swap(sends[j - 1], "seq", 2 * j))
     else:
         grad_own, gots = scattered(grads[0].reshape(seq_count, chunk, both), "seq"), []
-    grad_skip, grad_coarse = call(
-        functools.partial(finish, mp_count),
-        [((width, length), bf16), ((width, length // 2), bf16)],
-        own, *parts, last=True,
-    )
     grad_head, grad_conv = call(
         functools.partial(summed_up, scale_back),
         [((chunk, tracks), f32), ((taps, chunk, width), f32)],
         grad_own, *gots, scratch=[((chunk, both), f32)], last=True,
+    )
+    grad_skip, grad_coarse = call(
+        functools.partial(finish, mp_count),
+        [((width, length), bf16), ((width, length // 2), bf16)],
+        own, *parts, grad_head, outside=(mp_count,), last=True,
     )
     return (grad_skip, grad_coarse, grad_head, grad_conv.transpose(1, 0, 2))
 

time: 72.9 us -> 71.1 us (0.975)
  waiting for transfers between devices: 28.4 us -> 24.5 us
  starting transfers between devices: 34.4 us -> 36.5 us
    ppermute x23 -> x27, starting transfers between devices: 30.7 us -> 35.8 us  [swap(): return lax.ppermute(block, axis, [(i, i ^ mask) for i in range(count)])]
    ppermute x2 -> x1, waiting for transfers between devices: 3.86 us -> 0.01 us  [crossed(): return lax.ppermute(block, axis, pairs + [(b, a) for a, b in pairs])]
    ppermute x2 -> x1, starting transfers between devices: 3.69 us -> 0.66 us  [crossed(): return lax.ppermute(block, axis, pairs + [(b, a) for a, b in pairs])]
    pallas_call x9 -> x10, Pallas kernels: 8.23 us -> 8.23 us  [call(): pl.pallas_call(body, out_shape=[jax.ShapeDtypeStruct(shape, kind) if last...]
    ppermute x23 -> x27, waiting for transfers between devices: 24.5 us -> 24.5 us  [swap(): return lax.ppermute(block, axis, [(i, i ^ mask) for i in range(count)])]
  transfers between devices with their start and end apart: 25 -> 28, of which waited for: 11 -> 13; matrix products, arithmetic and copies ran while one was open for 1% -> 1% of each run, Pallas kernels for 3% -> 4%
where the time goes in v1:
time: 71.1 us; the launch traced here: 70.9 us
  starting transfers between devices  36.5 us (51%)
  waiting for transfers between devices  24.5 us (34%)
  Pallas kernels  8.23 us (12%)
  local copies, waits for them, and re-layouts  0.82 us (1%)
  between operations  0.82 us (1%)
    ppermute x27, starting transfers between devices, swap(): return lax.ppermute(block, axis, [(i, i ^ mask) for i in range(count)])  35.8 us
    ppermute x27, waiting for transfers between devices, swap(): return lax.ppermute(block, axis, [(i, i ^ mask) for i in range(count)])  24.5 us
    pallas_call x10, Pallas kernels, call(): pl.pallas_call(body, out_shape=[jax.ShapeDtypeStruct(shape, kind) if last...  8.23 us
  transfers between devices with their start and end apart: 28, of which 13 were waited for; matrix products, arithmetic and copies ran while one was open for 1% of the time, Pallas kernels for 4%

profile of v1, /device:TPU:0, one launch (start us, length us, event | category | flops | bytes accessed | tf_op | source)
XLA Modules:
  0.0 70.9 jit_solution(2343687400108092258)
XLA Ops:
  0.6 1.3 %shard_map.111 = (bf16[192,256]{1,0:T(8,128)(2,1)S(1)}, bf16[8,256]{1,0:T(8,128)(2,1)S(1)}, bf16[8,256]{1,0:T(8,128)(2,1)S(1)}, bf16[8,256]{1,0:T(8,128)(2,1)S(1)}) custom-call(bf16[192,128]{1,0:T(8,128)(2,1)} %coarse_in.1, bf16[192,256]{1,0:T(8,128)(2,1)} %skip_in.1, s32[256,128]{1,0:T(8,128)} %counts.1), custom_call_target="tpu_custom_call" | custom-call | tf_op jit(solution)/shard_map/pallas_call | solution.py:92
  2.0 0.7 collective-permute-start
  2.6 4.4 %collective-permute-start.1 = (bf16[8,256]{1,0:T(8,128)(2,1)S(1)}, bf16[8,256]{1,0:T(8,128)(2,1)S(1)}, u32[]{:S(2)}, u32[]{:S(2)}) collective-permute-start(bf16[8,256]{1,0:T(8,128)(2,1)S(1)} %get-tuple-element.30), channel_id=1, source_target_pairs={{0,4},{4,0},{8,12},{12,8},{16,20},{20,16},{24,28},{28,24},{1,5},{5... | collective-permute-start | bytes 12296 | tf_op jit(solution)/shard_map/ppermute | solution.py:23
  7.0 0.0 collective-permute-done
  7.0 0.8 %collective-permute-done.1 = bf16[8,256]{1,0:T(8,128)(2,1)S(1)} collective-permute-done((bf16[8,256]{1,0:T(8,128)(2,1)S(1)}, bf16[8,256]{1,0:T(8,128)(2,1)S(1)}, u32[]{:S(2)}, u32[]{:S(2)}) %collective-permute-start.1) | collective-permute-done | bytes 4128 | tf_op jit(solution)/shard_map/ppermute | solution.py:23
  7.9 3.7 %collective-permute-start.4 = (bf16[200,256]{1,0:T(8,128)(2,1)S(1)}, bf16[200,256]{1,0:T(8,128)(2,1)S(1)}, u32[]{:S(2)}, u32[]{:S(2)}) collective-permute-start(bf16[200,256]{1,0:T(8,128)(2,1)S(1)} %pad_maximum_fusion.after.refs_0_), channel_id=1, source_target_pairs={{0,3},{1,2},{2,1},{3,0},{4,7},{5,6},{6,5},{7,4},{8,11},{9,10},{10,... | collective-permute-start | bytes 307208 | tf_op jit(solution)/shard_map/ppermute | solution.py:23
  11.5 0.0 collective-permute-start.3
  11.5 0.8 %collective-permute-start.2 = (bf16[200,256]{1,0:T(8,128)(2,1)S(1)}, bf16[200,256]{1,0:T(8,128)(2,1)S(1)}, u32[]{:S(2)}, u32[]{:S(2)}) collective-permute-start(bf16[200,256]{1,0:T(8,128)(2,1)S(1)} %pad_maximum_fusion.after.refs_0_), channel_id=1, source_target_pairs={{0,1},{1,0},{2,3},{3,2},{4,5},{5,4},{6,7},{7,6},{8,9},{9,8},{10,11... | collective-permute-start | bytes 307208 | tf_op jit(solution)/shard_map/ppermute | solution.py:23
  12.3 0.8 %copy.12.refs_5_ = f32[192,1]{1,0:T(8,128)S(1)} copy(f32[192,1]{0,1:T(1,128)} %bitcast.18) | data formatting | bytes 1536 | tf_op jit(solution)/shard_map/broadcast_in_dim | solution.py:397
  13.1 1.2 %shard_map.112.refs_4_.refs_12_ = bf16[576,768]{1,0:T(8,128)(2,1)S(1)} custom-call(bf16[200,256]{1,0:T(8,128)(2,1)S(1)} %pad_maximum_fusion.after.refs_0_, bf16[576,768]{1,0:T(8,128)(2,1)} %bitcast.17), custom_call_target="tpu_custom_call" | custom-call | tf_op jit(solution)/shard_map/pallas_call | solution.py:92
  14.3 0.0 copy-start.1
  14.3 0.0 copy-start
  14.3 0.0 copy-start.2
  14.3 0.0 copy-start.3
  14.4 1.2 %collective-permute-done.4.refs_3_ = bf16[200,256]{1,0:T(8,128)(2,1)S(1)} collective-permute-done((bf16[200,256]{1,0:T(8,128)(2,1)S(1)}, bf16[200,256]{1,0:T(8,128)(2,1)S(1)}, u32[]{:S(2)}, u32[]{:S(2)}) %collective-permute-start.4) | collective-permute-done | bytes 102432 | tf_op jit(solution)/shard_map/ppermute | solution.py:23
  15.6 5.1 %collective-permute-done.3.refs_2_ = bf16[200,256]{1,0:T(8,128)(2,1)S(1)} collective-permute-done((bf16[200,256]{1,0:T(8,128)(2,1)S(1)}, bf16[200,256]{1,0:T(8,128)(2,1)S(1)}, u32[]{:S(2)}, u32[]{:S(2)}) %collective-permute-start.3) | collective-permute-done | bytes 102432 | tf_op jit(solution)/shard_map/ppermute | solution.py:23
  20.7 0.0 collective-permute-done.2.refs_1_
  20.7 1.3 %shard_map.113 = (bf16[200,256]{1,0:T(8,128)(2,1)S(1)}, f32[192,384]{1,0:T(8,128)S(1)}, bf16[768,256]{1,0:T(8,128)(2,1)S(1)}) custom-call(bf16[200,256]{1,0:T(8,128)(2,1)S(1)} %pad_maximum_fusion.after.refs_0_, bf16[200,256]{1,0:T(8,128)(2,1)S(1)} %collective-permute-done.2.refs_1_, bf16[200,256]{1,0:T(8,128)(2,1)S(1)} %collective-permute-done.3.refs_2_, ...), custom_call_target="tpu_custom_call" | custom-call | tf_op jit(solution)/shard_map/pallas_call | solution.py:92
  22.0 2.5 %collective-permute-start.7 = (bf16[200,256]{1,0:T(8,128)(2,1)S(1)}, bf16[200,256]{1,0:T(8,128)(2,1)S(1)}, u32[]{:S(2)}, u32[]{:S(2)}) collective-permute-start(bf16[200,256]{1,0:T(8,128)(2,1)S(1)} %get-tuple-element.32.refs_0_.after), channel_id=1, source_target_pairs={{0,3},{1,2},{2,1},{3,0},{4,7},{5,6},{6,5},{7,4},{8,11},{9,10},{10,... | collective-permute-start | bytes 307208 | tf_op jit(solution)/shard_map/ppermute | solution.py:23
  24.5 0.0 collective-permute-start.6
  24.5 1.9 %collective-permute-start.5 = (bf16[200,256]{1,0:T(8,128)(2,1)S(1)}, bf16[200,256]{1,0:T(8,128)(2,1)S(1)}, u32[]{:S(2)}, u32[]{:S(2)}) collective-permute-start(bf16[200,256]{1,0:T(8,128)(2,1)S(1)} %get-tuple-element.32.refs_0_.after), channel_id=1, source_target_pairs={{0,1},{1,0},{2,3},{3,2},{4,5},{5,4},{6,7},{7,6},{8,9},{9,8},{10,11... | collective-permute-start | bytes 307208 | tf_op jit(solution)/shard_map/ppermute | solution.py:23
  26.4 2.5 %collective-permute-start.17 = (bf16[48,128]{1,0:T(8,128)(2,1)S(1)}, bf16[48,128]{1,0:T(8,128)(2,1)S(1)}, u32[]{:S(2)}, u32[]{:S(2)}) collective-permute-start(bf16[48,128]{1,0:T(8,128)(2,1)S(1)} %get-tuple-element.52), channel_id=1, source_target_pairs={{0,3},{1,2},{2,1},{3,0},{4,7},{5,6},{6,5},{7,4},{8,11},{9,10},{10,... | collective-permute-start | bytes 36872 | tf_op jit(solution)/shard_map/ppermute | solution.py:23
  28.9 0.0 collective-permute-start.16
  28.9 0.7 collective-permute-done.7.refs_3_
  29.6 2.1 %collective-permute-start.15 = (bf16[48,128]{1,0:T(8,128)(2,1)S(1)}, bf16[48,128]{1,0:T(8,128)(2,1)S(1)}, u32[]{:S(2)}, u32[]{:S(2)}) collective-permute-start(bf16[48,128]{1,0:T(8,128)(2,1)S(1)} %get-tuple-element.54), channel_id=1, source_target_pairs={{0,1},{1,0},{2,3},{3,2},{4,5},{5,4},{6,7},{7,6},{8,9},{9,8},{10,11... | collective-permute-start | bytes 36872 | tf_op jit(solution)/shard_map/ppermute | solution.py:23
  31.7 2.2 %collective-permute-done.6.refs_2_ = bf16[200,256]{1,0:T(8,128)(2,1)S(1)} collective-permute-done((bf16[200,256]{1,0:T(8,128)(2,1)S(1)}, bf16[200,256]{1,0:T(8,128)(2,1)S(1)}, u32[]{:S(2)}, u32[]{:S(2)}) %collective-permute-start.6) | collective-permute-done | bytes 102432 | tf_op jit(solution)/shard_map/ppermute | solution.py:23
  33.9 0.0 collective-permute-done.5.refs_1_
  33.9 0.6 shard_map.114
  34.6 0.1 collective-permute-start.8
  34.7 1.2 %collective-permute-done.8 = f32[8,128]{1,0:T(8,128)S(1)} collective-permute-done((f32[8,128]{1,0:T(8,128)S(1)}, f32[8,128]{1,0:T(8,128)S(1)}, u32[]{:S(2)}, u32[]{:S(2)}) %collective-permute-start.8) | collective-permute-done | bytes 4128 | tf_op jit(solution)/shard_map/ppermute | solution.py:23
  35.8 0.0 collective-permute-start.11
  35.8 3.8 %collective-permute-start.10 = (f32[8,128]{1,0:T(8,128)S(1)}, f32[8,128]{1,0:T(8,128)S(1)}, u32[]{:S(2)}, u32[]{:S(2)}) collective-permute-start(f32[8,128]{1,0:T(8,128)S(1)} %add.40), channel_id=1, source_target_pairs={{0,16},{4,20},{8,24},{12,28},{16,0},{20,4},{24,8},{28,12},{1,17},{... | collective-permute-start | bytes 12296 | tf_op jit(solution)/shard_map/ppermute | solution.py:23
  39.6 0.0 collective-permute-done.17.refs_2_
  39.6 0.0 collective-permute-start.9
  39.6 0.0 collective-permute-done.16.refs_1_
  39.6 0.0 collective-permute-done.15.refs_0_
  39.7 1.5 %collective-permute-start.20 = (bf16[144,128]{1,0:T(8,128)(2,1)S(1)}, bf16[144,128]{1,0:T(8,128)(2,1)S(1)}, u32[]{:S(2)}, u32[]{:S(2)}) collective-permute-start(bf16[144,128]{1,0:T(8,128)(2,1)S(1)} %shard_map.116.refs_5_), channel_id=1, source_target_pairs={{0,24},{4,28},{8,16},{12,20},{16,8},{20,12},{24,0},{28,4},{1,25},{... | collective-permute-start | bytes 110600 | tf_op jit(solution)/shard_map/ppermute | solution.py:23
  41.2 2.0 %collective-permute-start.19 = (bf16[144,128]{1,0:T(8,128)(2,1)S(1)}, bf16[144,128]{1,0:T(8,128)(2,1)S(1)}, u32[]{:S(2)}, u32[]{:S(2)}) collective-permute-start(bf16[144,128]{1,0:T(8,128)(2,1)S(1)} %shard_map.116.refs_5_), channel_id=1, source_target_pairs={{0,16},{4,20},{8,24},{12,28},{16,0},{20,4},{24,8},{28,12},{1,17},{... | collective-permute-start | bytes 110600 | tf_op jit(solution)/shard_map/ppermute | solution.py:23
  43.2 0.0 collective-permute-start.18
  43.2 0.0 collective-permute-done.10
  43.2 0.0 collective-permute-done.9
  43.2 0.1 shard_map.115.refs_0_
  43.4 1.9 %collective-permute-start.14 = (bf16[264,128]{1,0:T(8,128)(2,1)S(1)}, bf16[264,128]{1,0:T(8,128)(2,1)S(1)}, u32[]{:S(2)}, u32[]{:S(2)}) collective-permute-start(bf16[264,128]{1,0:T(8,128)(2,1)S(1)} %shard_map.115.refs_0_), channel_id=1, source_target_pairs={{0,3},{1,2},{2,1},{3,0},{4,7},{5,6},{6,5},{7,4},{8,11},{9,10},{10,... | collective-permute-start | bytes 202760 | tf_op jit(solution)/shard_map/ppermute | solution.py:23
  45.3 0.0 collective-permute-start.13
  45.3 2.6 %collective-permute-start.12 = (bf16[264,128]{1,0:T(8,128)(2,1)S(1)}, bf16[264,128]{1,0:T(8,128)(2,1)S(1)}, u32[]{:S(2)}, u32[]{:S(2)}) collective-permute-start(bf16[264,128]{1,0:T(8,128)(2,1)S(1)} %shard_map.115.refs_0_), channel_id=1, source_target_pairs={{0,1},{1,0},{2,3},{3,2},{4,5},{5,4},{6,7},{7,6},{8,9},{9,8},{10,11... | collective-permute-start | bytes 202760 | tf_op jit(solution)/shard_map/ppermute | solution.py:23
  47.8 2.2 %collective-permute-done.14.refs_3_ = bf16[264,128]{1,0:T(8,128)(2,1)S(1)} collective-permute-done((bf16[264,128]{1,0:T(8,128)(2,1)S(1)}, bf16[264,128]{1,0:T(8,128)(2,1)S(1)}, u32[]{:S(2)}, u32[]{:S(2)}) %collective-permute-start.14) | collective-permute-done | bytes 67616 | tf_op jit(solution)/shard_map/ppermute | solution.py:23
  50.0 1.6 %collective-permute-done.13.refs_2_ = bf16[264,128]{1,0:T(8,128)(2,1)S(1)} collective-permute-done((bf16[264,128]{1,0:T(8,128)(2,1)S(1)}, bf16[264,128]{1,0:T(8,128)(2,1)S(1)}, u32[]{:S(2)}, u32[]{:S(2)}) %collective-permute-start.13) | collective-permute-done | bytes 67616 | tf_op jit(solution)/shard_map/ppermute | solution.py:23
  51.6 0.0 collective-permute-done.12.refs_1_
  51.6 1.7 %shard_map.117 = (f32[192,256]{1,0:T(8,128)S(1)}, bf16[192,256]{1,0:T(8,128)(2,1)S(1)}, bf16[192,256]{1,0:T(8,128)(2,1)S(1)}, bf16[192,256]{1,0:T(8,128)(2,1)S(1...) custom-call(bf16[264,128]{1,0:T(8,128)(2,1)S(1)} %shard_map.115.refs_0_, ...), custom_call_target="tpu_custom_call" | custom-call | tf_op jit(solution)/shard_map/pallas_call | solution.py:92
  53.3 0.1 collective-permute-start.24
  53.4 1.9 %collective-permute-done.24.got = bf16[2112,128]{1,0:T(8,128)(2,1)S(1)} collective-permute-done((bf16[2112,128]{1,0:T(8,128)(2,1)S(1)}, bf16[2112,128]{1,0:T(8,128)(2,1)S(1)}, u32[]{:S(2)}, u32[]{:S(2)}) %collective-permute-start.24) | collective-permute-done | bytes 540704 | tf_op jit(solution)/shard_map/ppermute | solution.py:23
  55.3 0.2 shard_map.118
  55.5 1.5 %collective-permute-start.25 = (bf16[528,128]{1,0:T(8,128)(2,1)S(1)}, bf16[528,128]{1,0:T(8,128)(2,1)S(1)}, u32[]{:S(2)}, u32[]{:S(2)}) collective-permute-start(bf16[528,128]{1,0:T(8,128)(2,1)S(1)} %get-tuple-element.45), channel_id=1, source_target_pairs={{0,24},{4,28},{8,16},{12,20},{16,8},{20,12},{24,0},{28,4},{1,25},{... | collective-permute-start | bytes 405512 | tf_op jit(solution)/shard_map/ppermute | solution.py:23
  57.0 1.8 %collective-permute-start.26 = (bf16[528,128]{1,0:T(8,128)(2,1)S(1)}, bf16[528,128]{1,0:T(8,128)(2,1)S(1)}, u32[]{:S(2)}, u32[]{:S(2)}) collective-permute-start(bf16[528,128]{1,0:T(8,128)(2,1)S(1)} %get-tuple-element.46), channel_id=1, source_target_pairs={{0,16},{4,20},{8,24},{12,28},{16,0},{20,4},{24,8},{28,12},{1,17},{... | collective-permute-start | bytes 405512 | tf_op jit(solution)/shard_map/ppermute | solution.py:23
  58.8 0.2 collective-permute-start.27
  59.0 1.7 %collective-permute-start.21 = (bf16[192,256]{1,0:T(8,128)(2,1)S(1)}, bf16[192,256]{1,0:T(8,128)(2,1)S(1)}, u32[]{:S(2)}, u32[]{:S(2)}) collective-permute-start(bf16[192,256]{1,0:T(8,128)(2,1)S(1)} %get-tuple-element.39), channel_id=1, source_target_pairs={{0,3},{1,2},{2,1},{3,0},{4,7},{5,6},{6,5},{7,4},{8,11},{9,10},{10,... | collective-permute-start | bytes 294920 | tf_op jit(solution)/shard_map/ppermute | solution.py:23
  60.7 0.3 collective-permute-start.22
  61.0 1.9 %collective-permute-done.25.refs_0_ = bf16[528,128]{1,0:T(8,128)(2,1)S(1)} collective-permute-done((bf16[528,128]{1,0:T(8,128)(2,1)S(1)}, bf16[528,128]{1,0:T(8,128)(2,1)S(1)}, u32[]{:S(2)}, u32[]{:S(2)}) %collective-permute-start.25) | collective-permute-done | bytes 135200 | tf_op jit(solution)/shard_map/ppermute | solution.py:23
  62.9 0.5 collective-permute-start.23
  63.4 1.5 %collective-permute-done.26.refs_1_ = bf16[528,128]{1,0:T(8,128)(2,1)S(1)} collective-permute-done((bf16[528,128]{1,0:T(8,128)(2,1)S(1)}, bf16[528,128]{1,0:T(8,128)(2,1)S(1)}, u32[]{:S(2)}, u32[]{:S(2)}) %collective-permute-start.26) | collective-permute-done | bytes 135200 | tf_op jit(solution)/shard_map/ppermute | solution.py:23
  65.0 0.8 %shard_map.119 = (f32[96,128]{1,0:T(8,128)}, f32[3,96,192]{2,1,0:T(8,128)}) custom-call(f32[528,128]{1,0:T(8,128)S(1)} %get-tuple-element.44.own, bf16[528,128]{1,0:T(8,128)(2,1)S(1)} %collective-permute-done.25.refs_0_, bf16[528,128]{1,0:T(8,128)(2,1)S(1)} %collective-permute-done.26.refs_1_, bf16[528,128]{1,0:T(8,128)(2,1)S(1)} %collective-permute-done.27.refs_2_), custom_call_target="tpu_custom_call" | custom-call | tf_op jit(solution)/shard_map/pallas_call | solution.py:92
  65.8 0.7 collective-permute-done.21.refs_1_
  66.5 3.4 %collective-permute-done.22.refs_2_ = bf16[192,256]{1,0:T(8,128)(2,1)S(1)} collective-permute-done((bf16[192,256]{1,0:T(8,128)(2,1)S(1)}, bf16[192,256]{1,0:T(8,128)(2,1)S(1)}, u32[]{:S(2)}, u32[]{:S(2)}) %collective-permute-start.22) | collective-permute-done | bytes 98336 | tf_op jit(solution)/shard_map/ppermute | solution.py:23
  69.9 1.0 %shard_map.120 = (bf16[192,256]{1,0:T(8,128)(2,1)}, bf16[192,128]{1,0:T(8,128)(2,1)}) custom-call(f32[192,256]{1,0:T(8,128)S(1)} %get-tuple-element.38.refs_0_, bf16[192,256]{1,0:T(8,128)(2,1)S(1)} %collective-permute-done.21.refs_1_, bf16[192,256]{1,0:T(8,128)(2,1)S(1)} %collective-permute-done.22.refs_2_, ...), custom_call_target="tpu_custom_call" | custom-call | tf_op jit(solution)/shard_map/pallas_call | solution.py:92
  (18 shorter events, 0.1 us)
Async XLA Ops:
  2.0 5.1 %collective-permute-start = (bf16[8,256]{1,0:T(8,128)(2,1)S(1)}, bf16[8,256]{1,0:T(8,128)(2,1)S(1)}, u32[]{:S(2)}, u32[]{:S(2)}) collective-permute-start(bf16[8,256]{1,0:T(8,128)(2,1)S(1)} %get-tuple-element.29), channel_id=1, source_target_pairs={{4,8},{12,16},{20,24},{8,4},{16,12},{24,20},{5,9},{13,17},{21,25},... | collective-permute-start | bytes 12296 | tf_op jit(solution)/shard_map/ppermute | solution.py:29
  2.6 5.2 %collective-permute-start.1 = (bf16[8,256]{1,0:T(8,128)(2,1)S(1)}, bf16[8,256]{1,0:T(8,128)(2,1)S(1)}, u32[]{:S(2)}, u32[]{:S(2)}) collective-permute-start(bf16[8,256]{1,0:T(8,128)(2,1)S(1)} %get-tuple-element.30), channel_id=1, source_target_pairs={{0,4},{4,0},{8,12},{12,8},{16,20},{20,16},{24,28},{28,24},{1,5},{5... | collective-permute-start | bytes 12296 | tf_op jit(solution)/shard_map/ppermute | solution.py:23
  7.9 7.7 %collective-permute-start.4 = (bf16[200,256]{1,0:T(8,128)(2,1)S(1)}, bf16[200,256]{1,0:T(8,128)(2,1)S(1)}, u32[]{:S(2)}, u32[]{:S(2)}) collective-permute-start(bf16[200,256]{1,0:T(8,128)(2,1)S(1)} %pad_maximum_fusion.after.refs_0_), channel_id=1, source_target_pairs={{0,3},{1,2},{2,1},{3,0},{4,7},{5,6},{6,5},{7,4},{8,11},{9,10},{10,... | collective-permute-start | bytes 307208 | tf_op jit(solution)/shard_map/ppermute | solution.py:23
  11.5 9.2 %collective-permute-start.3 = (bf16[200,256]{1,0:T(8,128)(2,1)S(1)}, bf16[200,256]{1,0:T(8,128)(2,1)S(1)}, u32[]{:S(2)}, u32[]{:S(2)}) collective-permute-start(bf16[200,256]{1,0:T(8,128)(2,1)S(1)} %pad_maximum_fusion.after.refs_0_), channel_id=1, source_target_pairs={{0,2},{1,3},{2,0},{3,1},{4,6},{5,7},{6,4},{7,5},{8,10},{9,11},{10,... | collective-permute-start | bytes 307208 | tf_op jit(solution)/shard_map/ppermute | solution.py:23
  11.5 9.2 %collective-permute-start.2 = (bf16[200,256]{1,0:T(8,128)(2,1)S(1)}, bf16[200,256]{1,0:T(8,128)(2,1)S(1)}, u32[]{:S(2)}, u32[]{:S(2)}) collective-permute-start(bf16[200,256]{1,0:T(8,128)(2,1)S(1)} %pad_maximum_fusion.after.refs_0_), channel_id=1, source_target_pairs={{0,1},{1,0},{2,3},{3,2},{4,5},{5,4},{6,7},{7,6},{8,9},{9,8},{10,11... | collective-permute-start | bytes 307208 | tf_op jit(solution)/shard_map/ppermute | solution.py:23
  14.3 12.1 %copy-start.1 = (bf16[768,128]{1,0:T(8,128)(2,1)S(1)}, bf16[768,128]{1,0:T(8,128)(2,1)}, u32[]{:S(2)}) copy-start(bf16[768,128]{1,0:T(8,128)(2,1)} %refs_4_.1) | copy-start | bytes 589828
  14.3 19.6 %copy-start = (s32[256,128]{1,0:T(8,128)S(1)}, s32[256,128]{1,0:T(8,128)}, u32[]{:S(2)}) copy-start(s32[256,128]{1,0:T(8,128)} %counts.1) | copy-start | bytes 393220
  14.3 19.6 %copy-start.2 = (f32[128]{0:T(128)S(1)}, f32[128]{0:T(128)}, u32[]{:S(2)}) copy-start(f32[128]{0:T(128)} %param.13) | copy-start | bytes 1540
  14.3 25.3 %copy-start.3 = (s32[1,128]{1,0:T(1,128)S(1)}, s32[1,128]{1,0:T(1,128)}, u32[]{:S(2)}) copy-start(s32[1,128]{1,0:T(1,128)} %param.15) | copy-start | bytes 1540
  22.0 7.6 %collective-permute-start.7 = (bf16[200,256]{1,0:T(8,128)(2,1)S(1)}, bf16[200,256]{1,0:T(8,128)(2,1)S(1)}, u32[]{:S(2)}, u32[]{:S(2)}) collective-permute-start(bf16[200,256]{1,0:T(8,128)(2,1)S(1)} %get-tuple-element.32.refs_0_.after), channel_id=1, source_target_pairs={{0,3},{1,2},{2,1},{3,0},{4,7},{5,6},{6,5},{7,4},{8,11},{9,10},{10,... | collective-permute-start | bytes 307208 | tf_op jit(solution)/shard_map/ppermute | solution.py:23
  24.5 9.4 %collective-permute-start.6 = (bf16[200,256]{1,0:T(8,128)(2,1)S(1)}, bf16[200,256]{1,0:T(8,128)(2,1)S(1)}, u32[]{:S(2)}, u32[]{:S(2)}) collective-permute-start(bf16[200,256]{1,0:T(8,128)(2,1)S(1)} %get-tuple-element.32.refs_0_.after), channel_id=1, source_target_pairs={{0,2},{1,3},{2,0},{3,1},{4,6},{5,7},{6,4},{7,5},{8,10},{9,11},{10,... | collective-permute-start | bytes 307208 | tf_op jit(solution)/shard_map/ppermute | solution.py:23
  24.5 9.4 %collective-permute-start.5 = (bf16[200,256]{1,0:T(8,128)(2,1)S(1)}, bf16[200,256]{1,0:T(8,128)(2,1)S(1)}, u32[]{:S(2)}, u32[]{:S(2)}) collective-permute-start(bf16[200,256]{1,0:T(8,128)(2,1)S(1)} %get-tuple-element.32.refs_0_.after), channel_id=1, source_target_pairs={{0,1},{1,0},{2,3},{3,2},{4,5},{5,4},{6,7},{7,6},{8,9},{9,8},{10,11... | collective-permute-start | bytes 307208 | tf_op jit(solution)/shard_map/ppermute | solution.py:23
  26.4 13.2 %collective-permute-start.17 = (bf16[48,128]{1,0:T(8,128)(2,1)S(1)}, bf16[48,128]{1,0:T(8,128)(2,1)S(1)}, u32[]{:S(2)}, u32[]{:S(2)}) collective-permute-start(bf16[48,128]{1,0:T(8,128)(2,1)S(1)} %get-tuple-element.52), channel_id=1, source_target_pairs={{0,3},{1,2},{2,1},{3,0},{4,7},{5,6},{6,5},{7,4},{8,11},{9,10},{10,... | collective-permute-start | bytes 36872 | tf_op jit(solution)/shard_map/ppermute | solution.py:23
  28.9 10.8 %collective-permute-start.16 = (bf16[48,128]{1,0:T(8,128)(2,1)S(1)}, bf16[48,128]{1,0:T(8,128)(2,1)S(1)}, u32[]{:S(2)}, u32[]{:S(2)}) collective-permute-start(bf16[48,128]{1,0:T(8,128)(2,1)S(1)} %get-tuple-element.53), channel_id=1, source_target_pairs={{0,2},{1,3},{2,0},{3,1},{4,6},{5,7},{6,4},{7,5},{8,10},{9,11},{10,... | collective-permute-start | bytes 36872 | tf_op jit(solution)/shard_map/ppermute | solution.py:23
  29.6 10.1 %collective-permute-start.15 = (bf16[48,128]{1,0:T(8,128)(2,1)S(1)}, bf16[48,128]{1,0:T(8,128)(2,1)S(1)}, u32[]{:S(2)}, u32[]{:S(2)}) collective-permute-start(bf16[48,128]{1,0:T(8,128)(2,1)S(1)} %get-tuple-element.54), channel_id=1, source_target_pairs={{0,1},{1,0},{2,3},{3,2},{4,5},{5,4},{6,7},{7,6},{8,9},{9,8},{10,11... | collective-permute-start | bytes 36872 | tf_op jit(solution)/shard_map/ppermute | solution.py:23
  34.6 1.2 %collective-permute-start.8 = (f32[8,128]{1,0:T(8,128)S(1)}, f32[8,128]{1,0:T(8,128)S(1)}, u32[]{:S(2)}, u32[]{:S(2)}) collective-permute-start(f32[8,128]{1,0:T(8,128)S(1)} %get-tuple-element.34), channel_id=1, source_target_pairs={{0,4},{4,0},{8,12},{12,8},{16,20},{20,16},{24,28},{28,24},{1,5},{5... | collective-permute-start | bytes 12296 | tf_op jit(solution)/shard_map/ppermute | solution.py:23
  35.8 7.4 %collective-permute-start.11 = (f32[8,128]{1,0:T(8,128)S(1)}, f32[8,128]{1,0:T(8,128)S(1)}, u32[]{:S(2)}, u32[]{:S(2)}) collective-permute-start(f32[8,128]{1,0:T(8,128)S(1)} %add.40), channel_id=1, source_target_pairs={{0,24},{4,28},{8,16},{12,20},{16,8},{20,12},{24,0},{28,4},{1,25},{... | collective-permute-start | bytes 12296 | tf_op jit(solution)/shard_map/ppermute | solution.py:23
  35.8 7.4 %collective-permute-start.10 = (f32[8,128]{1,0:T(8,128)S(1)}, f32[8,128]{1,0:T(8,128)S(1)}, u32[]{:S(2)}, u32[]{:S(2)}) collective-permute-start(f32[8,128]{1,0:T(8,128)S(1)} %add.40), channel_id=1, source_target_pairs={{0,16},{4,20},{8,24},{12,28},{16,0},{20,4},{24,8},{28,12},{1,17},{... | collective-permute-start | bytes 12296 | tf_op jit(solution)/shard_map/ppermute | solution.py:23
  39.6 3.6 %collective-permute-start.9 = (f32[8,128]{1,0:T(8,128)S(1)}, f32[8,128]{1,0:T(8,128)S(1)}, u32[]{:S(2)}, u32[]{:S(2)}) collective-permute-start(f32[8,128]{1,0:T(8,128)S(1)} %add.40), channel_id=1, source_target_pairs={{0,8},{4,12},{8,0},{12,4},{16,24},{20,28},{24,16},{28,20},{1,9},{5... | collective-permute-start | bytes 12296 | tf_op jit(solution)/shard_map/ppermute | solution.py:23
  39.7 5.6 %collective-permute-start.20 = (bf16[144,128]{1,0:T(8,128)(2,1)S(1)}, bf16[144,128]{1,0:T(8,128)(2,1)S(1)}, u32[]{:S(2)}, u32[]{:S(2)}) collective-permute-start(bf16[144,128]{1,0:T(8,128)(2,1)S(1)} %shard_map.116.refs_5_), channel_id=1, source_target_pairs={{0,24},{4,28},{8,16},{12,20},{16,8},{20,12},{24,0},{28,4},{1,25},{... | collective-permute-start | bytes 110600 | tf_op jit(solution)/shard_map/ppermute | solution.py:23
  41.2 6.7 %collective-permute-start.19 = (bf16[144,128]{1,0:T(8,128)(2,1)S(1)}, bf16[144,128]{1,0:T(8,128)(2,1)S(1)}, u32[]{:S(2)}, u32[]{:S(2)}) collective-permute-start(bf16[144,128]{1,0:T(8,128)(2,1)S(1)} %shard_map.116.refs_5_), channel_id=1, source_target_pairs={{0,16},{4,20},{8,24},{12,28},{16,0},{20,4},{24,8},{28,12},{1,17},{... | collective-permute-start | bytes 110600 | tf_op jit(solution)/shard_map/ppermute | solution.py:23
  43.2 4.6 %collective-permute-start.18 = (bf16[144,128]{1,0:T(8,128)(2,1)S(1)}, bf16[144,128]{1,0:T(8,128)(2,1)S(1)}, u32[]{:S(2)}, u32[]{:S(2)}) collective-permute-start(bf16[144,128]{1,0:T(8,128)(2,1)S(1)} %shard_map.116.refs_5_), channel_id=1, source_target_pairs={{0,8},{4,12},{8,0},{12,4},{16,24},{20,28},{24,16},{28,20},{1,9},{5... | collective-permute-start | bytes 110600 | tf_op jit(solution)/shard_map/ppermute | solution.py:23
  43.4 6.6 %collective-permute-start.14 = (bf16[264,128]{1,0:T(8,128)(2,1)S(1)}, bf16[264,128]{1,0:T(8,128)(2,1)S(1)}, u32[]{:S(2)}, u32[]{:S(2)}) collective-permute-start(bf16[264,128]{1,0:T(8,128)(2,1)S(1)} %shard_map.115.refs_0_), channel_id=1, source_target_pairs={{0,3},{1,2},{2,1},{3,0},{4,7},{5,6},{6,5},{7,4},{8,11},{9,10},{10,... | collective-permute-start | bytes 202760 | tf_op jit(solution)/shard_map/ppermute | solution.py:23
  45.3 6.3 %collective-permute-start.13 = (bf16[264,128]{1,0:T(8,128)(2,1)S(1)}, bf16[264,128]{1,0:T(8,128)(2,1)S(1)}, u32[]{:S(2)}, u32[]{:S(2)}) collective-permute-start(bf16[264,128]{1,0:T(8,128)(2,1)S(1)} %shard_map.115.refs_0_), channel_id=1, source_target_pairs={{0,2},{1,3},{2,0},{3,1},{4,6},{5,7},{6,4},{7,5},{8,10},{9,11},{10,... | collective-permute-start | bytes 202760 | tf_op jit(solution)/shard_map/ppermute | solution.py:23
  45.3 6.3 %collective-permute-start.12 = (bf16[264,128]{1,0:T(8,128)(2,1)S(1)}, bf16[264,128]{1,0:T(8,128)(2,1)S(1)}, u32[]{:S(2)}, u32[]{:S(2)}) collective-permute-start(bf16[264,128]{1,0:T(8,128)(2,1)S(1)} %shard_map.115.refs_0_), channel_id=1, source_target_pairs={{0,1},{1,0},{2,3},{3,2},{4,5},{5,4},{6,7},{7,6},{8,9},{9,8},{10,11... | collective-permute-start | bytes 202760 | tf_op jit(solution)/shard_map/ppermute | solution.py:23
  53.3 2.0 %collective-permute-start.24 = (bf16[2112,128]{1,0:T(8,128)(2,1)S(1)}, bf16[2112,128]{1,0:T(8,128)(2,1)S(1)}, u32[]{:S(2)}, u32[]{:S(2)}) collective-permute-start(bf16[2112,128]{1,0:T(8,128)(2,1)S(1)} %get-tuple-element.43), channel_id=1, source_target_pairs={{0,4},{4,0},{8,12},{12,8},{16,20},{20,16},{24,28},{28,24},{1,5},{5... | collective-permute-start | bytes 1622024 | tf_op jit(solution)/shard_map/ppermute | solution.py:23
  55.5 7.4 %collective-permute-start.25 = (bf16[528,128]{1,0:T(8,128)(2,1)S(1)}, bf16[528,128]{1,0:T(8,128)(2,1)S(1)}, u32[]{:S(2)}, u32[]{:S(2)}) collective-permute-start(bf16[528,128]{1,0:T(8,128)(2,1)S(1)} %get-tuple-element.45), channel_id=1, source_target_pairs={{0,24},{4,28},{8,16},{12,20},{16,8},{20,12},{24,0},{28,4},{1,25},{... | collective-permute-start | bytes 405512 | tf_op jit(solution)/shard_map/ppermute | solution.py:23
  57.0 8.0 %collective-permute-start.26 = (bf16[528,128]{1,0:T(8,128)(2,1)S(1)}, bf16[528,128]{1,0:T(8,128)(2,1)S(1)}, u32[]{:S(2)}, u32[]{:S(2)}) collective-permute-start(bf16[528,128]{1,0:T(8,128)(2,1)S(1)} %get-tuple-element.46), channel_id=1, source_target_pairs={{0,16},{4,20},{8,24},{12,28},{16,0},{20,4},{24,8},{28,12},{1,17},{... | collective-permute-start | bytes 405512 | tf_op jit(solution)/shard_map/ppermute | solution.py:23
  58.8 6.2 %collective-permute-start.27 = (bf16[528,128]{1,0:T(8,128)(2,1)S(1)}, bf16[528,128]{1,0:T(8,128)(2,1)S(1)}, u32[]{:S(2)}, u32[]{:S(2)}) collective-permute-start(bf16[528,128]{1,0:T(8,128)(2,1)S(1)} %get-tuple-element.47), channel_id=1, source_target_pairs={{0,8},{4,12},{8,0},{12,4},{16,24},{20,28},{24,16},{28,20},{1,9},{5... | collective-permute-start | bytes 405512 | tf_op jit(solution)/shard_map/ppermute | solution.py:23
  59.0 7.5 %collective-permute-start.21 = (bf16[192,256]{1,0:T(8,128)(2,1)S(1)}, bf16[192,256]{1,0:T(8,128)(2,1)S(1)}, u32[]{:S(2)}, u32[]{:S(2)}) collective-permute-start(bf16[192,256]{1,0:T(8,128)(2,1)S(1)} %get-tuple-element.39), channel_id=1, source_target_pairs={{0,3},{1,2},{2,1},{3,0},{4,7},{5,6},{6,5},{7,4},{8,11},{9,10},{10,... | collective-permute-start | bytes 294920 | tf_op jit(solution)/shard_map/ppermute | solution.py:23
  60.7 9.2 %collective-permute-start.22 = (bf16[192,256]{1,0:T(8,128)(2,1)S(1)}, bf16[192,256]{1,0:T(8,128)(2,1)S(1)}, u32[]{:S(2)}, u32[]{:S(2)}) collective-permute-start(bf16[192,256]{1,0:T(8,128)(2,1)S(1)} %get-tuple-element.40), channel_id=1, source_target_pairs={{0,2},{1,3},{2,0},{3,1},{4,6},{5,7},{6,4},{7,5},{8,10},{9,11},{10,... | collective-permute-start | bytes 294920 | tf_op jit(solution)/shard_map/ppermute | solution.py:23
  62.9 7.0 %collective-permute-start.23 = (bf16[192,256]{1,0:T(8,128)(2,1)S(1)}, bf16[192,256]{1,0:T(8,128)(2,1)S(1)}, u32[]{:S(2)}, u32[]{:S(2)}) collective-permute-start(bf16[192,256]{1,0:T(8,128)(2,1)S(1)} %get-tuple-element.41), channel_id=1, source_target_pairs={{0,1},{1,0},{2,3},{3,2},{4,5},{5,4},{6,7},{7,6},{8,9},{9,8},{10,11... | collective-permute-start | bytes 294920 | tf_op jit(solution)/shard_map/ppermute | solution.py:23

commit v2 on v1

--- a/solution.py
+++ b/solution.py
@@ -109,57 +109,54 @@
     return pl.ds(pl.multiple_of((column ^ j) * size, size), size)
 
 
-def prepare(coarse_in, skip_in, counts_in, summed, pair, cross, own, coarse, skip, top, bottom, done):
+def prepare(mp_count, group, coarse_in, skip_in, counts_in, head_in, weight_in, *refs):
+    messages, (pair, cross, weight, coarse, skip, top, bottom, done) = refs[: mp_count - 1], refs[mp_count - 1 :]
     width, length = skip.shape
     rows, tracks = top.shape
-    copies = [
-        pltpu.make_async_copy(source, target, done.at[i])
-        for i, (source, target) in enumerate(
-            (
-                (coarse_in, coarse),
-                (skip_in, skip),
-                (counts_in.at[pl.ds(0, rows)], top),
-                (counts_in.at[pl.ds(length - rows, rows)], bottom),
+    place, column = lax.axis_index("seq"), lax.axis_index("mp")
+    moves = [
+        (coarse_in, coarse),
+        (skip_in, skip),
+        (counts_in.at[pl.ds(0, rows)], top),
+        (counts_in.at[pl.ds(length - rows, rows)], bottom),
+        (weight_in, weight),
+    ]
+    share = width // group
+    for j, message in zip(range(1, mp_count), messages):
+        for i in range(2):
+            start = (column ^ j) * width + ((place >> 1) & (group - 1)) * share + i * (share // 2)
+            moves.append(
+                (
+                    head_in.at[pl.ds(pl.multiple_of(start, 8), share // 2)],
+                    message.at[pl.ds(width, share // 2), pl.ds(i * tracks, tracks)],
+                )
             )
-        )
-    ]
+    copies = [pltpu.make_async_copy(*move, done.at[i]) for i, move in enumerate(moves)]
     for copy in copies:
         copy.start()
-    for copy in copies:
+    for copy in copies[:4]:
         copy.wait()
     pairs = jnp.where(
         iota((coarse.shape[1], length), 0) == iota((coarse.shape[1], length), 1) // 2, 1.0, 0.0
     ).astype(bf16)
     total = (dot(coarse[...], pairs, nn) + skip[...].astype(f32)).astype(bf16)
-    summed[...] = total
+    for message in messages:
+        message[:width, :] = total
     slot = iota((edge_rows, tracks), 0)
     ahead = dot(chosen((edge_rows, length), ((0, length - 2), (1, length - 1))), total, nt)
     behind = dot(chosen((edge_rows, length), ((4, 0), (5, 1))), total, nt)
-    mine = dot(chosen((edge_rows, length), ((2, 0), (3, length - 1))), total, nt)
     first = jnp.where(slot == 7, top[0:1, :].astype(f32), behind[:, :tracks])
     last = jnp.where(slot == 6, bottom[rows - 1 : rows, :].astype(f32), ahead[:, :tracks])
-    even = lax.axis_index("seq") % 2 == 0
-    for out, (left, right) in (
-        (pair, (jnp.where(even, last, first), jnp.where(even, ahead, behind))),
-        (cross, (jnp.where(even, first, last), jnp.where(even, behind, ahead))),
-        (own, (mine[:, :tracks], mine)),
+    even = place % 2 == 0
+    for out, left, right in (
+        (pair, jnp.where(even, last, first), jnp.where(even, ahead, behind)),
+        (cross, jnp.where(even, first, last), jnp.where(even, behind, ahead)),
     ):
         out[...] = jnp.zeros(out.shape, bf16)
         out[:, :tracks] = left.astype(bf16)
         out[:, tracks:width] = right[:, tracks:].astype(bf16)
-
-
-def stage(after, weight_in, weight, done):
-    copy = pltpu.make_async_copy(weight_in, weight, done.at[0])
-    copy.start()
-    copy.wait()
-
-
-def joined(after, *refs):
-    *parts, out = refs
-    rows = parts[0].shape[0]
-    for i, part in enumerate(parts):
-        out[i * rows : (i + 1) * rows, :] = part[...]
+    for copy in copies[4:]:
+        copy.wait()
 
 
 def gelu_parts(inputs):
@@ -172,41 +169,62 @@
     return value, slope
 
 
-def assembled(pieces, whole, column, width, length):
+def assembled(blocks, whole, column, width, length):
     spread = jnp.where(
         iota((edge_rows, edge_lanes), 0) == iota((edge_rows, edge_lanes), 1), 1.0, 0.0
     ).astype(bf16)
-    for j, piece in enumerate(pieces):
+    for j, (block, edges) in enumerate(blocks):
         rows = block_rows(column, j, width)
-        whole[rows, :length] = piece[:width, :]
-        whole[rows, length:] = dot(piece[width:, :width], spread, tn).astype(bf16)
-
-
-def convolve(mp_count, *refs):
-    pieces, (weight, bias, message, slopes, full, whole) = refs[:mp_count], refs[mp_count:]
+        whole[rows, :length] = block
+        whole[rows, length:] = dot(edges, spread, tn).astype(bf16)
+
+
+def regrouped(out, whole, length, halves):
+    if not halves:
+        out[...] = whole[:, :length]
+        return
+    mine = lax.axis_index("seq") & 1
+    chunk = whole.shape[0] // (2 * halves)
+    for q in range(halves):
+        for i, core in enumerate((mine, 1 - mine)):
+            start = pl.multiple_of((2 * q + core) * chunk, 16)
+            at = (i * halves + q) * chunk
+            out[at : at + chunk, :] = whole[pl.ds(start, chunk), :length]
+
+
+def convolve(mp_count, halves, *refs):
+    pieces, edges = refs[:mp_count], refs[mp_count : 2 * mp_count]
+    weight, bias, message, slopes, full, bundle, whole = refs[2 * mp_count :]
     width = weight.shape[0] // 3
     length = message.shape[1]
+    half, tracks = pieces[1].shape[0] - width, bundle.shape[1]
     column = lax.axis_index("mp")
-    assembled(pieces, whole, column, width, length)
-    full[...] = whole[:, :length]
+    for j, piece in enumerate(pieces[1:]):
+        for i in range(2):
+            bundle[(2 * j + i) * half : (2 * j + i + 1) * half, :] = piece[width:, i * tracks : (i + 1) * tracks]
+    blocks = [(piece[:width, :], edge[:, :width]) for piece, edge in zip(pieces, edges)]
+    assembled(blocks, whole, column, width, length)
+    regrouped(full, whole, length, halves)
     taps = [dot(weight[k * width : (k + 1) * width, :], whole[...], nn) for k in range(3)]
     lanes = iota((width, length), 1)
     edge = iota((width, edge_lanes), 1)
+    square = (width, width)
+    shift = jnp.sum(jnp.where(iota(square, 0) == iota(square, 1), bias[...], 0.0), axis=1, keepdims=True)
+
+    def at(tap, lane):
+        return taps[tap][:, lane : lane + 1]
+
     inner = (
         taps[1][:, :length]
-        + jnp.where(lanes == 0, taps[0][:, length + 1 : length + 2], pltpu.roll(taps[0][:, :length], 1, 1))
-        + jnp.where(
-            lanes == length - 1,
-            taps[2][:, length + 4 : length + 5],
-            pltpu.roll(taps[2][:, :length], length - 1, 1),
-        )
-        + bias[...]
-    )
-    outer = [
-        sum(taps[k][:, length + first + k : length + first + k + 1] for k in range(3)) + bias[...]
-        for first in (0, 3)
-    ]
-    outer = jnp.where(edge == 0, outer[0], jnp.where(edge == 1, outer[1], 0.0))
+        + jnp.where(lanes == 0, at(0, length + 1), pltpu.roll(taps[0][:, :length], 1, 1))
+        + jnp.where(lanes == length - 1, at(2, length + 4), pltpu.roll(taps[2][:, :length], length - 1, 1))
+        + shift
+    )
+    outer = jnp.where(
+        edge == 0,
+        at(0, length) + at(1, length + 1) + at(2, 0) + shift,
+        jnp.where(edge == 1, at(0, length - 1) + at(1, length + 4) + at(2, length + 5) + shift, 0.0),
+    )
     own = whole[block_rows(column, 0, width), :].astype(f32)
     beside = jnp.where(edge == 0, own[:, length + 1 : length + 2], own[:, length + 4 : length + 5])
     value, slope = gelu_parts(inner)
@@ -223,12 +241,13 @@
     return jnp.maximum(logits, 0.0) + jnp.log1p(jnp.exp(-jnp.abs(logits))) + pseudo_count
 
 
-def score(mp_count, *refs):
+def score(mp_count, halves, *refs):
     pieces, (head, bias, counts, logits, sums, full, whole) = refs[:mp_count], refs[mp_count:]
     width = head.shape[0] // mp_count
     length = counts.shape[0]
-    assembled(pieces, whole, lax.axis_index("mp"), width, length)
-    full[...] = whole[:, :length]
+    blocks = [(piece[:width, :], piece[width:, :width]) for piece in pieces]
+    assembled(blocks, whole, lax.axis_index("mp"), width, length)
+    regrouped(full, whole, length, halves)
     scores = dot(whole[...], head[...], tn) + bias[...]
     logits[...] = scores[: length + edge_rows, :]
     tracks = head.shape[1]
@@ -254,13 +273,13 @@
     slope[length:, :] = slope_of(logits[length:, :], beside)
 
 
-def packed(out, base, source, start, chunk, both):
-    tiles, half = both // 128, chunk // 2
+def packed(out, base, value, start, chunk):
+    tiles, half = value.shape[1] // 128, chunk // 2
     for t in range(tiles):
-        rows = source[pl.ds(start, chunk), t * 128 : (t + 1) * 128]
+        rows = value[start : start + chunk, t * 128 : (t + 1) * 128]
         out[base + t * chunk : base + (t + 1) * chunk, :] = rows.astype(out.dtype)
-    if both % 128:
-        pair = [source[pl.ds(start + i * half, half), tiles * 128 :] for i in range(2)]
+    if value.shape[1] % 128:
+        pair = [value[start + i * half : start + (i + 1) * half, tiles * 128 :] for i in range(2)]
         at = base + tiles * chunk
         out[at : at + half, :] = jnp.concatenate(pair, axis=1).astype(out.dtype)
 
@@ -295,18 +314,22 @@
     stacked[:width, :] = jnp.where(lanes == length - 1, high, pltpu.roll(middle, length - 1, 1)).astype(bf16)
     stacked[width : 2 * width, :] = middle.astype(bf16)
     stacked[2 * width :, :] = jnp.where(lanes == 0, low, pltpu.roll(middle, 1, 1)).astype(bf16)
-    grads, total = outs[-4], outs[-2]
-    grads[:, :tracks] = dot(hidden[...], slopes[0][:length, :], nn)
-    grads[:, tracks:] = dot(full[...], stacked[...], nt)
+    total = outs[-2]
+    own_slope = slopes[0][:length, :]
     if split:
-        kept, sent = outs[:2]
-        both = grads.shape[1]
+        rows = full.shape[0] // 2
         chunk = full.shape[0] // seq_count
-        mine = place & 1
-        for q in range(seq_count // 2):
-            base = q * packed_rows(chunk, both)
-            packed(kept, base, grads, pl.multiple_of((2 * q + mine) * chunk, 8), chunk, both)
-            packed(sent, base, grads, pl.multiple_of((2 * q + 1 - mine) * chunk, 8), chunk, both)
+        for i, out in ((1, outs[1]), (0, outs[0])):
+            at = slice(i * rows, (i + 1) * rows)
+            value = jnp.concatenate(
+                [dot(hidden[at, :], own_slope, nn), dot(full[at, :], stacked[...], nt)], axis=1
+            )
+            for q in range(seq_count // 2):
+                packed(out, q * packed_rows(chunk, value.shape[1]), value, q * chunk, chunk)
+    else:
+        grads = outs[0]
+        grads[:, :tracks] = dot(hidden[...], own_slope, nn)
+        grads[:, tracks:] = dot(full[...], stacked[...], nt)
     total[...] = dot(weight[...], stacked[...], tn)
     own[...] = inner + total[block_rows(column, 0, width), :]
     for j, out in zip(range(1, mp_count), carry):
@@ -363,47 +386,45 @@
     channels, tracks = head_weight.shape
     scale_back = 1.0 / math.sqrt(length * seq_count)
     place, column = lax.axis_index("seq"), lax.axis_index("mp")
-    weight = conv_weight.reshape(taps * width, channels)
+    group = min(4, seq_count // 2)
+    share = width // group
+    chunk = channels // seq_count
+    both = tracks + taps * width
+    split = chunk % 32 == 0 and both % 64 == 0 and len(list(staged(0, seq_count.bit_length() - 1))) == 2
+    halves = seq_count // 2 if split else 0
     tall = width + edge_rows
-
     tile = ((edge_rows, length), bf16)
-    summed, pair, cross, own = call(
-        prepare, [((width, length), bf16), tile, tile, tile], coarse, skip, counts,
+    *messages, pair, cross, weight = call(
+        functools.partial(prepare, mp_count, group),
+        [((width + share // 2, length), bf16)] * (mp_count - 1) + [tile, tile, ((taps * width, channels), bf16)],
+        coarse, skip, counts, head_weight, conv_weight.reshape(taps * width, channels),
         scratch=[
-            (coarse.shape, bf16), (skip.shape, bf16), ((8, tracks), jnp.int32), ((8, tracks), jnp.int32), ((4,), None),
+            (coarse.shape, bf16), (skip.shape, bf16), ((8, tracks), jnp.int32), ((8, tracks), jnp.int32),
+            ((5 + 2 * (mp_count - 1),), None),
         ],
-        outside=(0, 1, 2),
-    )
+        outside=range(5),
+    )
+    pieces = [messages[0]]
+    for j, message in zip(range(1, mp_count), messages):
+        pieces.append(swap(message, "mp", j))
     cross = crossed(cross, "seq")
     pair = swap(pair, "seq", 1)
-    edges = cross + pair + own
-    group = min(4, seq_count // 2)
-    head_parts = head_weight.reshape(mp_count, group, width // group, tracks)
+    edges = cross + pair
+    wide = length + edge_lanes
+    message, gelu, full_in, bundle = call(
+        functools.partial(convolve, mp_count, halves),
+        [((tall, length), bf16), ((width, wide), f32), ((channels, length), bf16)]
+        + [(((mp_count - 1) * share, tracks), bf16)],
+        *pieces, *gathered(edges, "mp"), weight, conv_bias[None, :],
+        scratch=[((channels, wide), bf16)],
+    )
+    pieces = gathered(message, "mp")
+    bundles = [bundle]
+    for r in range(1, group):
+        bundles.append(swap(bundle, "seq", 2 * r))
     head_own = lax.dynamic_index_in_dim(head_weight.reshape(mp_count, width, tracks), column, 0, keepdims=False)
-    shares = []
-    for j in range(1, mp_count):
-        share = lax.dynamic_slice(
-            head_parts, (column ^ j, (place >> 1) & (group - 1), 0, 0), (1, 1, width // group, tracks)
-        )
-        shares.append(swap(share.reshape(width // group, tracks), "mp", j))
-    pieces = gathered(jnp.concatenate([summed, edges], axis=0), "mp")
-    (weight,) = call(
-        stage, [(weight.shape, bf16)], pieces[0], weight, scratch=[((1,), None)], outside=(1,)
-    )
-    wide = length + edge_lanes
-    message, gelu, full_in = call(
-        functools.partial(convolve, mp_count),
-        [((tall, length), bf16), ((width, wide), f32), ((channels, length), bf16)],
-        *pieces, weight, conv_bias[:, None],
-        scratch=[((channels, wide), bf16)],
-    )
-    pieces = gathered(message, "mp")
-    (share,) = call(joined, [((width // group * (mp_count - 1), tracks), bf16)], message, *shares)
-    bundles = [share]
-    for r in range(1, group):
-        bundles.append(swap(share, "seq", 2 * r))
     logits, sums, full = call(
-        functools.partial(score, mp_count),
+        functools.partial(score, mp_count, halves),
         [((length + edge_rows, tracks), f32), ((8, tracks), f32), ((channels, length), bf16)],
         *pieces, head_weight, head_bias[None, :], counts,
         scratch=[((channels, wide), bf16)],
@@ -415,9 +436,6 @@
         differentiate, [((length + edge_rows, tracks), bf16)], logits, counts, edges, totals, mask_row
     )
     slopes = gathered(slope, "mp")
-    chunk = channels // seq_count
-    both = tracks + taps * width
-    split = chunk % (2 * edge_rows) == 0 and both % 64 == 0 and len(list(staged(0, seq_count.bit_length() - 1))) == 2
     quarter = (packed_rows(chunk, both), 128)
     half = (seq_count // 2 * quarter[0], 128)
     grads_at = ((channels, both), f32)
@@ -429,7 +447,7 @@
         + [((width, length), bf16)] * (mp_count - 1)
         + ([(half, f32), (half, bf16)] if split else [grads_at]),
         *slopes, head_own, *bundles, gelu, full_in, full, weight,
-        scratch=([grads_at] if split else []) + head_at + scratch,
+        scratch=head_at + scratch,
     )
     carry, grads = outs[: mp_count - 1], outs[mp_count - 1 :]
     if split:

time: 71.1 us -> 69.7 us (0.980)
  waiting for transfers between devices: 24.5 us -> 27.1 us
  starting transfers between devices: 36.5 us -> 34.7 us
  Pallas kernels: 8.23 us -> 6.88 us
  local copies, waits for them, and re-layouts: 0.82 us -> 0.03 us
    ppermute x27, waiting for transfers between devices: 24.5 us -> 27.1 us  [swap(): return lax.ppermute(block, axis, [(i, i ^ mask) for i in range(count)])]
    ppermute x27, starting transfers between devices: 35.8 us -> 34.1 us  [swap(): return lax.ppermute(block, axis, [(i, i ^ mask) for i in range(count)])]
    pallas_call x10 -> x8, Pallas kernels: 8.23 us -> 6.88 us  [call(): pl.pallas_call(body, out_shape=[jax.ShapeDtypeStruct(shape, kind) if last...]
    broadcast_in_dim x1 -> x0, local copies, waits for them, and re-layouts: 0.79 us -> none  [shards(): conv_bias[:, None]]
  transfers between devices with their start and end apart: 28 -> 28, of which waited for: 13 -> 14; matrix products, arithmetic and copies ran while one was open for 1% -> 0% of each run, Pallas kernels for 4% -> 1%
where the time goes in v2:
time: 69.7 us; the launch traced here: 69.5 us
  starting transfers between devices  34.7 us (50%)
  waiting for transfers between devices  27.1 us (39%)
  Pallas kernels  6.88 us (10%)
  between operations  0.77 us (1%)
    ppermute x27, starting transfers between devices, swap(): return lax.ppermute(block, axis, [(i, i ^ mask) for i in range(count)])  34.1 us
    ppermute x27, waiting for transfers between devices, swap(): return lax.ppermute(block, axis, [(i, i ^ mask) for i in range(count)])  27.1 us
    pallas_call x8, Pallas kernels, call(): pl.pallas_call(body, out_shape=[jax.ShapeDtypeStruct(shape, kind) if last...  6.88 us
  transfers between devices with their start and end apart: 28, of which 14 were waited for; matrix products, arithmetic and copies ran while one was open for 0% of the time, Pallas kernels for 1%

profile of v2, /device:TPU:0, one launch (start us, length us, event | category | flops | bytes accessed | tf_op | source)
XLA Modules:
  0.0 69.5 jit_solution(10770945748823084955)
XLA Ops:
  0.7 1.4 %shard_map.111 = (bf16[216,256]{1,0:T(8,128)(2,1)S(1)}, bf16[216,256]{1,0:T(8,128)(2,1)S(1)}, bf16[216,256]{1,0:T(8,128)(2,1)S(1)}, bf16[8,256]{1,0:T(8,128)(2,1...) custom-call(bf16[192,128]{1,0:T(8,128)(2,1)} %coarse_in.1, bf16[192,256]{1,0:T(8,128)(2,1)} %skip_in.1, ...), custom_call_target="tpu_custom_call" | custom-call | tf_op jit(solution)/shard_map/pallas_call | solution.py:92
  2.1 0.0 copy-start.4
  2.1 4.1 %collective-permute-start.1 = (bf16[216,256]{1,0:T(8,128)(2,1)S(1)}, bf16[216,256]{1,0:T(8,128)(2,1)S(1)}, u32[]{:S(2)}, u32[]{:S(2)}) collective-permute-start(bf16[216,256]{1,0:T(8,128)(2,1)S(1)} %get-tuple-element.32), channel_id=1, source_target_pairs={{0,2},{1,3},{2,0},{3,1},{4,6},{5,7},{6,4},{7,5},{8,10},{9,11},{10,... | collective-permute-start | bytes 331784 | tf_op jit(solution)/shard_map/ppermute | solution.py:23
  6.3 1.3 %collective-permute-start.2 = (bf16[216,256]{1,0:T(8,128)(2,1)S(1)}, bf16[216,256]{1,0:T(8,128)(2,1)S(1)}, u32[]{:S(2)}, u32[]{:S(2)}) collective-permute-start(bf16[216,256]{1,0:T(8,128)(2,1)S(1)} %get-tuple-element.33), channel_id=1, source_target_pairs={{0,3},{1,2},{2,1},{3,0},{4,7},{5,6},{6,5},{7,4},{8,11},{9,10},{10,... | collective-permute-start | bytes 331784 | tf_op jit(solution)/shard_map/ppermute | solution.py:23
  7.6 0.2 collective-permute-start
  7.8 0.6 collective-permute-start.3
  8.5 2.9 %collective-permute-start.4 = (bf16[8,256]{1,0:T(8,128)(2,1)S(1)}, bf16[8,256]{1,0:T(8,128)(2,1)S(1)}, u32[]{:S(2)}, u32[]{:S(2)}) collective-permute-start(bf16[8,256]{1,0:T(8,128)(2,1)S(1)} %get-tuple-element.35), channel_id=1, source_target_pairs={{0,4},{4,0},{8,12},{12,8},{16,20},{20,16},{24,28},{28,24},{1,5},{5... | collective-permute-start | bytes 12296 | tf_op jit(solution)/shard_map/ppermute | solution.py:23
  11.4 0.0 collective-permute-done.3
  11.4 0.8 %collective-permute-done.4 = bf16[8,256]{1,0:T(8,128)(2,1)S(1)} collective-permute-done((bf16[8,256]{1,0:T(8,128)(2,1)S(1)}, bf16[8,256]{1,0:T(8,128)(2,1)S(1)}, u32[]{:S(2)}, u32[]{:S(2)}) %collective-permute-start.4) | collective-permute-done | bytes 4128 | tf_op jit(solution)/shard_map/ppermute | solution.py:23
  12.2 2.9 %collective-permute-start.7 = (bf16[8,256]{1,0:T(8,128)(2,1)S(1)}, bf16[8,256]{1,0:T(8,128)(2,1)S(1)}, u32[]{:S(2)}, u32[]{:S(2)}) collective-permute-start(bf16[8,256]{1,0:T(8,128)(2,1)S(1)} %add.21.refs_4_.edges), channel_id=1, source_target_pairs={{0,3},{1,2},{2,1},{3,0},{4,7},{5,6},{6,5},{7,4},{8,11},{9,10},{10,... | collective-permute-start | bytes 12296 | tf_op jit(solution)/shard_map/ppermute | solution.py:23
  15.2 0.3 collective-permute-start.6
  15.5 2.1 %collective-permute-done.7.refs_7_ = bf16[8,256]{1,0:T(8,128)(2,1)S(1)} collective-permute-done((bf16[8,256]{1,0:T(8,128)(2,1)S(1)}, bf16[8,256]{1,0:T(8,128)(2,1)S(1)}, u32[]{:S(2)}, u32[]{:S(2)}) %collective-permute-start.7) | collective-permute-done | bytes 4128 | tf_op jit(solution)/shard_map/ppermute | solution.py:23
  17.6 0.0 collective-permute-start.5
  17.7 2.0 %collective-permute-done.6.refs_6_ = bf16[8,256]{1,0:T(8,128)(2,1)S(1)} collective-permute-done((bf16[8,256]{1,0:T(8,128)(2,1)S(1)}, bf16[8,256]{1,0:T(8,128)(2,1)S(1)}, u32[]{:S(2)}, u32[]{:S(2)}) %collective-permute-start.6) | collective-permute-done | bytes 4128 | tf_op jit(solution)/shard_map/ppermute | solution.py:23
  19.7 1.6 %collective-permute-done.5.refs_5_ = bf16[8,256]{1,0:T(8,128)(2,1)S(1)} collective-permute-done((bf16[8,256]{1,0:T(8,128)(2,1)S(1)}, bf16[8,256]{1,0:T(8,128)(2,1)S(1)}, u32[]{:S(2)}, u32[]{:S(2)}) %collective-permute-start.5) | collective-permute-done | bytes 4128 | tf_op jit(solution)/shard_map/ppermute | solution.py:23
  21.3 0.0 collective-permute-done.1.refs_2_
  21.3 0.0 collective-permute-done.2.refs_3_
  21.3 0.0 collective-permute-done.refs_1_
  21.3 1.3 %shard_map.112 = (bf16[200,256]{1,0:T(8,128)(2,1)S(1)}, f32[192,384]{1,0:T(8,128)S(1)}, bf16[768,256]{1,0:T(8,128)(2,1)S(1)}, bf16[144,128]{1,0:T(8,128)(2,1)S(1)}) custom-call(bf16[216,256]{1,0:T(8,128)(2,1)S(1)} %get-tuple-element.31.refs_0_, bf16[216,256]{1,0:T(8,128)(2,1)S(1)} %collective-permute-done.refs_1_, ...), custom_call_target="tpu_custom_call" | custom-call | tf_op jit(solution)/shard_map/pallas_call | solution.py:92
  22.6 2.9 %collective-permute-start.10 = (bf16[200,256]{1,0:T(8,128)(2,1)S(1)}, bf16[200,256]{1,0:T(8,128)(2,1)S(1)}, u32[]{:S(2)}, u32[]{:S(2)}) collective-permute-start(bf16[200,256]{1,0:T(8,128)(2,1)S(1)} %get-tuple-element.37.refs_0_), channel_id=1, source_target_pairs={{0,3},{1,2},{2,1},{3,0},{4,7},{5,6},{6,5},{7,4},{8,11},{9,10},{10,... | collective-permute-start | bytes 307208 | tf_op jit(solution)/shard_map/ppermute | solution.py:23
  25.5 0.0 collective-permute-start.9
  25.5 1.5 %collective-permute-start.8 = (bf16[200,256]{1,0:T(8,128)(2,1)S(1)}, bf16[200,256]{1,0:T(8,128)(2,1)S(1)}, u32[]{:S(2)}, u32[]{:S(2)}) collective-permute-start(bf16[200,256]{1,0:T(8,128)(2,1)S(1)} %get-tuple-element.37.refs_0_), channel_id=1, source_target_pairs={{0,1},{1,0},{2,3},{3,2},{4,5},{5,4},{6,7},{7,6},{8,9},{9,8},{10,11... | collective-permute-start | bytes 307208 | tf_op jit(solution)/shard_map/ppermute | solution.py:23
  27.0 2.8 %collective-permute-done.10.refs_3_ = bf16[200,256]{1,0:T(8,128)(2,1)S(1)} collective-permute-done((bf16[200,256]{1,0:T(8,128)(2,1)S(1)}, bf16[200,256]{1,0:T(8,128)(2,1)S(1)}, u32[]{:S(2)}, u32[]{:S(2)}) %collective-permute-start.10) | collective-permute-done | bytes 102432 | tf_op jit(solution)/shard_map/ppermute | solution.py:23
  29.8 3.5 %collective-permute-done.9.refs_2_ = bf16[200,256]{1,0:T(8,128)(2,1)S(1)} collective-permute-done((bf16[200,256]{1,0:T(8,128)(2,1)S(1)}, bf16[200,256]{1,0:T(8,128)(2,1)S(1)}, u32[]{:S(2)}, u32[]{:S(2)}) %collective-permute-start.9) | collective-permute-done | bytes 102432 | tf_op jit(solution)/shard_map/ppermute | solution.py:23
  33.2 0.0 collective-permute-done.8.refs_1_
  33.2 0.7 shard_map.113
  33.9 0.1 collective-permute-start.11
  34.0 1.2 %collective-permute-done.11 = f32[8,128]{1,0:T(8,128)S(1)} collective-permute-done((f32[8,128]{1,0:T(8,128)S(1)}, f32[8,128]{1,0:T(8,128)S(1)}, u32[]{:S(2)}, u32[]{:S(2)}) %collective-permute-start.11) | collective-permute-done | bytes 4128 | tf_op jit(solution)/shard_map/ppermute | solution.py:23
  35.1 2.0 %collective-permute-start.14 = (f32[8,128]{1,0:T(8,128)S(1)}, f32[8,128]{1,0:T(8,128)S(1)}, u32[]{:S(2)}, u32[]{:S(2)}) collective-permute-start(f32[8,128]{1,0:T(8,128)S(1)} %add.22), channel_id=1, source_target_pairs={{0,24},{4,28},{8,16},{12,20},{16,8},{20,12},{24,0},{28,4},{1,25},{... | collective-permute-start | bytes 12296 | tf_op jit(solution)/shard_map/ppermute | solution.py:23
  37.1 1.5 %collective-permute-start.13 = (f32[8,128]{1,0:T(8,128)S(1)}, f32[8,128]{1,0:T(8,128)S(1)}, u32[]{:S(2)}, u32[]{:S(2)}) collective-permute-start(f32[8,128]{1,0:T(8,128)S(1)} %add.22), channel_id=1, source_target_pairs={{0,16},{4,20},{8,24},{12,28},{16,0},{20,4},{24,8},{28,12},{1,17},{... | collective-permute-start | bytes 12296 | tf_op jit(solution)/shard_map/ppermute | solution.py:23
  38.6 0.0 collective-permute-start.12
  38.6 2.0 %collective-permute-start.20 = (bf16[144,128]{1,0:T(8,128)(2,1)S(1)}, bf16[144,128]{1,0:T(8,128)(2,1)S(1)}, u32[]{:S(2)}, u32[]{:S(2)}) collective-permute-start(bf16[144,128]{1,0:T(8,128)(2,1)S(1)} %get-tuple-element.40.refs_5_), channel_id=1, source_target_pairs={{0,24},{4,28},{8,16},{12,20},{16,8},{20,12},{24,0},{28,4},{1,25},{... | collective-permute-start | bytes 110600 | tf_op jit(solution)/shard_map/ppermute | solution.py:23
  40.6 1.5 %collective-permute-start.19 = (bf16[144,128]{1,0:T(8,128)(2,1)S(1)}, bf16[144,128]{1,0:T(8,128)(2,1)S(1)}, u32[]{:S(2)}, u32[]{:S(2)}) collective-permute-start(bf16[144,128]{1,0:T(8,128)(2,1)S(1)} %get-tuple-element.40.refs_5_), channel_id=1, source_target_pairs={{0,16},{4,20},{8,24},{12,28},{16,0},{20,4},{24,8},{28,12},{1,17},{... | collective-permute-start | bytes 110600 | tf_op jit(solution)/shard_map/ppermute | solution.py:23
  42.1 0.0 collective-permute-done.14
  42.1 0.1 collective-permute-start.18
  42.2 0.0 collective-permute-done.13
  42.2 0.0 collective-permute-done.12
  42.2 0.1 shard_map.114.refs_0_
  42.3 2.6 %collective-permute-start.17 = (bf16[264,128]{1,0:T(8,128)(2,1)S(1)}, bf16[264,128]{1,0:T(8,128)(2,1)S(1)}, u32[]{:S(2)}, u32[]{:S(2)}) collective-permute-start(bf16[264,128]{1,0:T(8,128)(2,1)S(1)} %shard_map.114.refs_0_), channel_id=1, source_target_pairs={{0,3},{1,2},{2,1},{3,0},{4,7},{5,6},{6,5},{7,4},{8,11},{9,10},{10,... | collective-permute-start | bytes 202760 | tf_op jit(solution)/shard_map/ppermute | solution.py:23
  45.0 0.0 collective-permute-start.16
  45.0 0.0 collective-permute-done.20.refs_8_
  45.0 1.8 %collective-permute-start.15 = (bf16[264,128]{1,0:T(8,128)(2,1)S(1)}, bf16[264,128]{1,0:T(8,128)(2,1)S(1)}, u32[]{:S(2)}, u32[]{:S(2)}) collective-permute-start(bf16[264,128]{1,0:T(8,128)(2,1)S(1)} %shard_map.114.refs_0_), channel_id=1, source_target_pairs={{0,1},{1,0},{2,3},{3,2},{4,5},{5,4},{6,7},{7,6},{8,9},{9,8},{10,11... | collective-permute-start | bytes 202760 | tf_op jit(solution)/shard_map/ppermute | solution.py:23
  46.8 0.0 collective-permute-done.19.refs_7_
  46.8 0.0 collective-permute-done.18.refs_6_
  46.8 2.3 %collective-permute-done.17.refs_3_ = bf16[264,128]{1,0:T(8,128)(2,1)S(1)} collective-permute-done((bf16[264,128]{1,0:T(8,128)(2,1)S(1)}, bf16[264,128]{1,0:T(8,128)(2,1)S(1)}, u32[]{:S(2)}, u32[]{:S(2)}) %collective-permute-start.17) | collective-permute-done | bytes 67616 | tf_op jit(solution)/shard_map/ppermute | solution.py:23
  49.1 1.6 %collective-permute-done.16.refs_2_ = bf16[264,128]{1,0:T(8,128)(2,1)S(1)} collective-permute-done((bf16[264,128]{1,0:T(8,128)(2,1)S(1)}, bf16[264,128]{1,0:T(8,128)(2,1)S(1)}, u32[]{:S(2)}, u32[]{:S(2)}) %collective-permute-start.16) | collective-permute-done | bytes 67616 | tf_op jit(solution)/shard_map/ppermute | solution.py:23
  50.7 0.0 collective-permute-done.15.refs_1_
  50.7 1.3 %shard_map.115 = (f32[192,256]{1,0:T(8,128)S(1)}, bf16[192,256]{1,0:T(8,128)(2,1)S(1)}, bf16[192,256]{1,0:T(8,128)(2,1)S(1)}, bf16[192,256]{1,0:T(8,128)(2,1)S(1...) custom-call(bf16[264,128]{1,0:T(8,128)(2,1)S(1)} %shard_map.114.refs_0_, ...), custom_call_target="tpu_custom_call" | custom-call | tf_op jit(solution)/shard_map/pallas_call | solution.py:92
  52.0 0.1 collective-permute-start.24
  52.1 1.9 %collective-permute-done.24.got = bf16[2112,128]{1,0:T(8,128)(2,1)S(1)} collective-permute-done((bf16[2112,128]{1,0:T(8,128)(2,1)S(1)}, bf16[2112,128]{1,0:T(8,128)(2,1)S(1)}, u32[]{:S(2)}, u32[]{:S(2)}) %collective-permute-start.24) | collective-permute-done | bytes 540704 | tf_op jit(solution)/shard_map/ppermute | solution.py:23
  54.0 0.2 shard_map.116
  54.2 2.0 %collective-permute-start.25 = (bf16[528,128]{1,0:T(8,128)(2,1)S(1)}, bf16[528,128]{1,0:T(8,128)(2,1)S(1)}, u32[]{:S(2)}, u32[]{:S(2)}) collective-permute-start(bf16[528,128]{1,0:T(8,128)(2,1)S(1)} %get-tuple-element.51), channel_id=1, source_target_pairs={{0,24},{4,28},{8,16},{12,20},{16,8},{20,12},{24,0},{28,4},{1,25},{... | collective-permute-start | bytes 405512 | tf_op jit(solution)/shard_map/ppermute | solution.py:23
  56.2 1.4 %collective-permute-start.26 = (bf16[528,128]{1,0:T(8,128)(2,1)S(1)}, bf16[528,128]{1,0:T(8,128)(2,1)S(1)}, u32[]{:S(2)}, u32[]{:S(2)}) collective-permute-start(bf16[528,128]{1,0:T(8,128)(2,1)S(1)} %get-tuple-element.52), channel_id=1, source_target_pairs={{0,16},{4,20},{8,24},{12,28},{16,0},{20,4},{24,8},{28,12},{1,17},{... | collective-permute-start | bytes 405512 | tf_op jit(solution)/shard_map/ppermute | solution.py:23
  57.5 0.2 collective-permute-start.27
  57.8 2.1 %collective-permute-start.21 = (bf16[192,256]{1,0:T(8,128)(2,1)S(1)}, bf16[192,256]{1,0:T(8,128)(2,1)S(1)}, u32[]{:S(2)}, u32[]{:S(2)}) collective-permute-start(bf16[192,256]{1,0:T(8,128)(2,1)S(1)} %get-tuple-element.45), channel_id=1, source_target_pairs={{0,3},{1,2},{2,1},{3,0},{4,7},{5,6},{6,5},{7,4},{8,11},{9,10},{10,... | collective-permute-start | bytes 294920 | tf_op jit(solution)/shard_map/ppermute | solution.py:23
  59.8 0.0 collective-permute-start.22
  59.9 1.8 %collective-permute-done.25.refs_0_ = bf16[528,128]{1,0:T(8,128)(2,1)S(1)} collective-permute-done((bf16[528,128]{1,0:T(8,128)(2,1)S(1)}, bf16[528,128]{1,0:T(8,128)(2,1)S(1)}, u32[]{:S(2)}, u32[]{:S(2)}) %collective-permute-start.25) | collective-permute-done | bytes 135200 | tf_op jit(solution)/shard_map/ppermute | solution.py:23
  61.6 0.5 collective-permute-start.23
  62.2 1.5 %collective-permute-done.26.refs_1_ = bf16[528,128]{1,0:T(8,128)(2,1)S(1)} collective-permute-done((bf16[528,128]{1,0:T(8,128)(2,1)S(1)}, bf16[528,128]{1,0:T(8,128)(2,1)S(1)}, u32[]{:S(2)}, u32[]{:S(2)}) %collective-permute-start.26) | collective-permute-done | bytes 135200 | tf_op jit(solution)/shard_map/ppermute | solution.py:23
  63.7 0.0 collective-permute-done.27.refs_2_
  63.7 0.8 %shard_map.117 = (f32[96,128]{1,0:T(8,128)}, f32[3,96,192]{2,1,0:T(8,128)}) custom-call(f32[528,128]{1,0:T(8,128)S(1)} %get-tuple-element.50.own, bf16[528,128]{1,0:T(8,128)(2,1)S(1)} %collective-permute-done.25.refs_0_, bf16[528,128]{1,0:T(8,128)(2,1)S(1)} %collective-permute-done.26.refs_1_, bf16[528,128]{1,0:T(8,128)(2,1)S(1)} %collective-permute-done.27.refs_2_), custom_call_target="tpu_custom_call" | custom-call | tf_op jit(solution)/shard_map/pallas_call | solution.py:92
  64.5 0.7 %collective-permute-done.21.refs_1_ = bf16[192,256]{1,0:T(8,128)(2,1)S(1)} collective-permute-done((bf16[192,256]{1,0:T(8,128)(2,1)S(1)}, bf16[192,256]{1,0:T(8,128)(2,1)S(1)}, u32[]{:S(2)}, u32[]{:S(2)}) %collective-permute-start.21) | collective-permute-done | bytes 98336 | tf_op jit(solution)/shard_map/ppermute | solution.py:23
  65.2 3.3 %collective-permute-done.22.refs_2_ = bf16[192,256]{1,0:T(8,128)(2,1)S(1)} collective-permute-done((bf16[192,256]{1,0:T(8,128)(2,1)S(1)}, bf16[192,256]{1,0:T(8,128)(2,1)S(1)}, u32[]{:S(2)}, u32[]{:S(2)}) %collective-permute-start.22) | collective-permute-done | bytes 98336 | tf_op jit(solution)/shard_map/ppermute | solution.py:23
  68.6 1.0 %shard_map.118 = (bf16[192,256]{1,0:T(8,128)(2,1)}, bf16[192,128]{1,0:T(8,128)(2,1)}) custom-call(f32[192,256]{1,0:T(8,128)S(1)} %get-tuple-element.44.refs_0_, bf16[192,256]{1,0:T(8,128)(2,1)S(1)} %collective-permute-done.21.refs_1_, bf16[192,256]{1,0:T(8,128)(2,1)S(1)} %collective-permute-done.22.refs_2_, ...), custom_call_target="tpu_custom_call" | custom-call | tf_op jit(solution)/shard_map/pallas_call | solution.py:92
  (15 shorter events, 0.0 us)
Async XLA Ops:
  0.6 20.6 %copy-start.2 = (f32[192]{0:T(256)S(1)}, f32[192]{0:T(256)}, u32[]{:S(2)}) copy-start(f32[192]{0:T(256)} %param.11) | copy-start | bytes 2308
  0.6 32.6 %copy-start = (s32[256,128]{1,0:T(8,128)S(1)}, s32[256,128]{1,0:T(8,128)}, u32[]{:S(2)}) copy-start(s32[256,128]{1,0:T(8,128)} %counts.1) | copy-start | bytes 393220
  0.7 32.6 %copy-start.1 = (bf16[768,128]{1,0:T(8,128)(2,1)S(1)}, bf16[768,128]{1,0:T(8,128)(2,1)}, u32[]{:S(2)}) copy-start(bf16[768,128]{1,0:T(8,128)(2,1)} %refs_4_.1) | copy-start | bytes 589828
  0.7 32.6 %copy-start.3 = (f32[128]{0:T(128)S(1)}, f32[128]{0:T(128)}, u32[]{:S(2)}) copy-start(f32[128]{0:T(128)} %param.13) | copy-start | bytes 1540
  2.1 36.5 %copy-start.4 = (s32[1,128]{1,0:T(1,128)S(1)}, s32[1,128]{1,0:T(1,128)}, u32[]{:S(2)}) copy-start(s32[1,128]{1,0:T(1,128)} %param.15) | copy-start | bytes 1540
  2.1 19.1 %collective-permute-start.1 = (bf16[216,256]{1,0:T(8,128)(2,1)S(1)}, bf16[216,256]{1,0:T(8,128)(2,1)S(1)}, u32[]{:S(2)}, u32[]{:S(2)}) collective-permute-start(bf16[216,256]{1,0:T(8,128)(2,1)S(1)} %get-tuple-element.32), channel_id=1, source_target_pairs={{0,2},{1,3},{2,0},{3,1},{4,6},{5,7},{6,4},{7,5},{8,10},{9,11},{10,... | collective-permute-start | bytes 331784 | tf_op jit(solution)/shard_map/ppermute | solution.py:23
  6.3 15.0 %collective-permute-start.2 = (bf16[216,256]{1,0:T(8,128)(2,1)S(1)}, bf16[216,256]{1,0:T(8,128)(2,1)S(1)}, u32[]{:S(2)}, u32[]{:S(2)}) collective-permute-start(bf16[216,256]{1,0:T(8,128)(2,1)S(1)} %get-tuple-element.33), channel_id=1, source_target_pairs={{0,3},{1,2},{2,1},{3,0},{4,7},{5,6},{6,5},{7,4},{8,11},{9,10},{10,... | collective-permute-start | bytes 331784 | tf_op jit(solution)/shard_map/ppermute | solution.py:23
  7.6 13.7 %collective-permute-start = (bf16[216,256]{1,0:T(8,128)(2,1)S(1)}, bf16[216,256]{1,0:T(8,128)(2,1)S(1)}, u32[]{:S(2)}, u32[]{:S(2)}) collective-permute-start(bf16[216,256]{1,0:T(8,128)(2,1)S(1)} %get-tuple-element.31.refs_0_), channel_id=1, source_target_pairs={{0,1},{1,0},{2,3},{3,2},{4,5},{5,4},{6,7},{7,6},{8,9},{9,8},{10,11... | collective-permute-start | bytes 331784 | tf_op jit(solution)/shard_map/ppermute | solution.py:23
  7.8 3.6 %collective-permute-start.3 = (bf16[8,256]{1,0:T(8,128)(2,1)S(1)}, bf16[8,256]{1,0:T(8,128)(2,1)S(1)}, u32[]{:S(2)}, u32[]{:S(2)}) collective-permute-start(bf16[8,256]{1,0:T(8,128)(2,1)S(1)} %get-tuple-element.34), channel_id=1, source_target_pairs={{4,8},{12,16},{20,24},{8,4},{16,12},{24,20},{5,9},{13,17},{21,25},... | collective-permute-start | bytes 12296 | tf_op jit(solution)/shard_map/ppermute | solution.py:29
  8.5 3.7 %collective-permute-start.4 = (bf16[8,256]{1,0:T(8,128)(2,1)S(1)}, bf16[8,256]{1,0:T(8,128)(2,1)S(1)}, u32[]{:S(2)}, u32[]{:S(2)}) collective-permute-start(bf16[8,256]{1,0:T(8,128)(2,1)S(1)} %get-tuple-element.35), channel_id=1, source_target_pairs={{0,4},{4,0},{8,12},{12,8},{16,20},{20,16},{24,28},{28,24},{1,5},{5... | collective-permute-start | bytes 12296 | tf_op jit(solution)/shard_map/ppermute | solution.py:23
  12.2 5.4 %collective-permute-start.7 = (bf16[8,256]{1,0:T(8,128)(2,1)S(1)}, bf16[8,256]{1,0:T(8,128)(2,1)S(1)}, u32[]{:S(2)}, u32[]{:S(2)}) collective-permute-start(bf16[8,256]{1,0:T(8,128)(2,1)S(1)} %add.21.refs_4_.edges), channel_id=1, source_target_pairs={{0,3},{1,2},{2,1},{3,0},{4,7},{5,6},{6,5},{7,4},{8,11},{9,10},{10,... | collective-permute-start | bytes 12296 | tf_op jit(solution)/shard_map/ppermute | solution.py:23
  15.2 4.5 %collective-permute-start.6 = (bf16[8,256]{1,0:T(8,128)(2,1)S(1)}, bf16[8,256]{1,0:T(8,128)(2,1)S(1)}, u32[]{:S(2)}, u32[]{:S(2)}) collective-permute-start(bf16[8,256]{1,0:T(8,128)(2,1)S(1)} %add.21.refs_4_.edges), channel_id=1, source_target_pairs={{0,2},{1,3},{2,0},{3,1},{4,6},{5,7},{6,4},{7,5},{8,10},{9,11},{10,... | collective-permute-start | bytes 12296 | tf_op jit(solution)/shard_map/ppermute | solution.py:23
  17.6 3.6 %collective-permute-start.5 = (bf16[8,256]{1,0:T(8,128)(2,1)S(1)}, bf16[8,256]{1,0:T(8,128)(2,1)S(1)}, u32[]{:S(2)}, u32[]{:S(2)}) collective-permute-start(bf16[8,256]{1,0:T(8,128)(2,1)S(1)} %add.21.refs_4_.edges), channel_id=1, source_target_pairs={{0,1},{1,0},{2,3},{3,2},{4,5},{5,4},{6,7},{7,6},{8,9},{9,8},{10,11... | collective-permute-start | bytes 12296 | tf_op jit(solution)/shard_map/ppermute | solution.py:23
  22.6 7.2 %collective-permute-start.10 = (bf16[200,256]{1,0:T(8,128)(2,1)S(1)}, bf16[200,256]{1,0:T(8,128)(2,1)S(1)}, u32[]{:S(2)}, u32[]{:S(2)}) collective-permute-start(bf16[200,256]{1,0:T(8,128)(2,1)S(1)} %get-tuple-element.37.refs_0_), channel_id=1, source_target_pairs={{0,3},{1,2},{2,1},{3,0},{4,7},{5,6},{6,5},{7,4},{8,11},{9,10},{10,... | collective-permute-start | bytes 307208 | tf_op jit(solution)/shard_map/ppermute | solution.py:23
  25.5 7.7 %collective-permute-start.9 = (bf16[200,256]{1,0:T(8,128)(2,1)S(1)}, bf16[200,256]{1,0:T(8,128)(2,1)S(1)}, u32[]{:S(2)}, u32[]{:S(2)}) collective-permute-start(bf16[200,256]{1,0:T(8,128)(2,1)S(1)} %get-tuple-element.37.refs_0_), channel_id=1, source_target_pairs={{0,2},{1,3},{2,0},{3,1},{4,6},{5,7},{6,4},{7,5},{8,10},{9,11},{10,... | collective-permute-start | bytes 307208 | tf_op jit(solution)/shard_map/ppermute | solution.py:23
  25.5 7.7 %collective-permute-start.8 = (bf16[200,256]{1,0:T(8,128)(2,1)S(1)}, bf16[200,256]{1,0:T(8,128)(2,1)S(1)}, u32[]{:S(2)}, u32[]{:S(2)}) collective-permute-start(bf16[200,256]{1,0:T(8,128)(2,1)S(1)} %get-tuple-element.37.refs_0_), channel_id=1, source_target_pairs={{0,1},{1,0},{2,3},{3,2},{4,5},{5,4},{6,7},{7,6},{8,9},{9,8},{10,11... | collective-permute-start | bytes 307208 | tf_op jit(solution)/shard_map/ppermute | solution.py:23
  33.9 1.2 %collective-permute-start.11 = (f32[8,128]{1,0:T(8,128)S(1)}, f32[8,128]{1,0:T(8,128)S(1)}, u32[]{:S(2)}, u32[]{:S(2)}) collective-permute-start(f32[8,128]{1,0:T(8,128)S(1)} %get-tuple-element.39), channel_id=1, source_target_pairs={{0,4},{4,0},{8,12},{12,8},{16,20},{20,16},{24,28},{28,24},{1,5},{5... | collective-permute-start | bytes 12296 | tf_op jit(solution)/shard_map/ppermute | solution.py:23
  35.1 7.0 %collective-permute-start.14 = (f32[8,128]{1,0:T(8,128)S(1)}, f32[8,128]{1,0:T(8,128)S(1)}, u32[]{:S(2)}, u32[]{:S(2)}) collective-permute-start(f32[8,128]{1,0:T(8,128)S(1)} %add.22), channel_id=1, source_target_pairs={{0,24},{4,28},{8,16},{12,20},{16,8},{20,12},{24,0},{28,4},{1,25},{... | collective-permute-start | bytes 12296 | tf_op jit(solution)/shard_map/ppermute | solution.py:23
  37.1 5.1 %collective-permute-start.13 = (f32[8,128]{1,0:T(8,128)S(1)}, f32[8,128]{1,0:T(8,128)S(1)}, u32[]{:S(2)}, u32[]{:S(2)}) collective-permute-start(f32[8,128]{1,0:T(8,128)S(1)} %add.22), channel_id=1, source_target_pairs={{0,16},{4,20},{8,24},{12,28},{16,0},{20,4},{24,8},{28,12},{1,17},{... | collective-permute-start | bytes 12296 | tf_op jit(solution)/shard_map/ppermute | solution.py:23
  38.6 3.6 %collective-permute-start.12 = (f32[8,128]{1,0:T(8,128)S(1)}, f32[8,128]{1,0:T(8,128)S(1)}, u32[]{:S(2)}, u32[]{:S(2)}) collective-permute-start(f32[8,128]{1,0:T(8,128)S(1)} %add.22), channel_id=1, source_target_pairs={{0,8},{4,12},{8,0},{12,4},{16,24},{20,28},{24,16},{28,20},{1,9},{5... | collective-permute-start | bytes 12296 | tf_op jit(solution)/shard_map/ppermute | solution.py:23
  38.6 6.4 %collective-permute-start.20 = (bf16[144,128]{1,0:T(8,128)(2,1)S(1)}, bf16[144,128]{1,0:T(8,128)(2,1)S(1)}, u32[]{:S(2)}, u32[]{:S(2)}) collective-permute-start(bf16[144,128]{1,0:T(8,128)(2,1)S(1)} %get-tuple-element.40.refs_5_), channel_id=1, source_target_pairs={{0,24},{4,28},{8,16},{12,20},{16,8},{20,12},{24,0},{28,4},{1,25},{... | collective-permute-start | bytes 110600 | tf_op jit(solution)/shard_map/ppermute | solution.py:23
  40.6 6.2 %collective-permute-start.19 = (bf16[144,128]{1,0:T(8,128)(2,1)S(1)}, bf16[144,128]{1,0:T(8,128)(2,1)S(1)}, u32[]{:S(2)}, u32[]{:S(2)}) collective-permute-start(bf16[144,128]{1,0:T(8,128)(2,1)S(1)} %get-tuple-element.40.refs_5_), channel_id=1, source_target_pairs={{0,16},{4,20},{8,24},{12,28},{16,0},{20,4},{24,8},{28,12},{1,17},{... | collective-permute-start | bytes 110600 | tf_op jit(solution)/shard_map/ppermute | solution.py:23
  42.1 4.7 %collective-permute-start.18 = (bf16[144,128]{1,0:T(8,128)(2,1)S(1)}, bf16[144,128]{1,0:T(8,128)(2,1)S(1)}, u32[]{:S(2)}, u32[]{:S(2)}) collective-permute-start(bf16[144,128]{1,0:T(8,128)(2,1)S(1)} %get-tuple-element.40.refs_5_), channel_id=1, source_target_pairs={{0,8},{4,12},{8,0},{12,4},{16,24},{20,28},{24,16},{28,20},{1,9},{5... | collective-permute-start | bytes 110600 | tf_op jit(solution)/shard_map/ppermute | solution.py:23
  42.3 6.7 %collective-permute-start.17 = (bf16[264,128]{1,0:T(8,128)(2,1)S(1)}, bf16[264,128]{1,0:T(8,128)(2,1)S(1)}, u32[]{:S(2)}, u32[]{:S(2)}) collective-permute-start(bf16[264,128]{1,0:T(8,128)(2,1)S(1)} %shard_map.114.refs_0_), channel_id=1, source_target_pairs={{0,3},{1,2},{2,1},{3,0},{4,7},{5,6},{6,5},{7,4},{8,11},{9,10},{10,... | collective-permute-start | bytes 202760 | tf_op jit(solution)/shard_map/ppermute | solution.py:23
  45.0 5.7 %collective-permute-start.16 = (bf16[264,128]{1,0:T(8,128)(2,1)S(1)}, bf16[264,128]{1,0:T(8,128)(2,1)S(1)}, u32[]{:S(2)}, u32[]{:S(2)}) collective-permute-start(bf16[264,128]{1,0:T(8,128)(2,1)S(1)} %shard_map.114.refs_0_), channel_id=1, source_target_pairs={{0,2},{1,3},{2,0},{3,1},{4,6},{5,7},{6,4},{7,5},{8,10},{9,11},{10,... | collective-permute-start | bytes 202760 | tf_op jit(solution)/shard_map/ppermute | solution.py:23
  45.0 5.7 %collective-permute-start.15 = (bf16[264,128]{1,0:T(8,128)(2,1)S(1)}, bf16[264,128]{1,0:T(8,128)(2,1)S(1)}, u32[]{:S(2)}, u32[]{:S(2)}) collective-permute-start(bf16[264,128]{1,0:T(8,128)(2,1)S(1)} %shard_map.114.refs_0_), channel_id=1, source_target_pairs={{0,1},{1,0},{2,3},{3,2},{4,5},{5,4},{6,7},{7,6},{8,9},{9,8},{10,11... | collective-permute-start | bytes 202760 | tf_op jit(solution)/shard_map/ppermute | solution.py:23
  52.0 2.0 %collective-permute-start.24 = (bf16[2112,128]{1,0:T(8,128)(2,1)S(1)}, bf16[2112,128]{1,0:T(8,128)(2,1)S(1)}, u32[]{:S(2)}, u32[]{:S(2)}) collective-permute-start(bf16[2112,128]{1,0:T(8,128)(2,1)S(1)} %get-tuple-element.49), channel_id=1, source_target_pairs={{0,4},{4,0},{8,12},{12,8},{16,20},{20,16},{24,28},{28,24},{1,5},{5... | collective-permute-start | bytes 1622024 | tf_op jit(solution)/shard_map/ppermute | solution.py:23
  54.2 7.4 %collective-permute-start.25 = (bf16[528,128]{1,0:T(8,128)(2,1)S(1)}, bf16[528,128]{1,0:T(8,128)(2,1)S(1)}, u32[]{:S(2)}, u32[]{:S(2)}) collective-permute-start(bf16[528,128]{1,0:T(8,128)(2,1)S(1)} %get-tuple-element.51), channel_id=1, source_target_pairs={{0,24},{4,28},{8,16},{12,20},{16,8},{20,12},{24,0},{28,4},{1,25},{... | collective-permute-start | bytes 405512 | tf_op jit(solution)/shard_map/ppermute | solution.py:23
  56.2 7.5 %collective-permute-start.26 = (bf16[528,128]{1,0:T(8,128)(2,1)S(1)}, bf16[528,128]{1,0:T(8,128)(2,1)S(1)}, u32[]{:S(2)}, u32[]{:S(2)}) collective-permute-start(bf16[528,128]{1,0:T(8,128)(2,1)S(1)} %get-tuple-element.52), channel_id=1, source_target_pairs={{0,16},{4,20},{8,24},{12,28},{16,0},{20,4},{24,8},{28,12},{1,17},{... | collective-permute-start | bytes 405512 | tf_op jit(solution)/shard_map/ppermute | solution.py:23
  57.5 6.2 %collective-permute-start.27 = (bf16[528,128]{1,0:T(8,128)(2,1)S(1)}, bf16[528,128]{1,0:T(8,128)(2,1)S(1)}, u32[]{:S(2)}, u32[]{:S(2)}) collective-permute-start(bf16[528,128]{1,0:T(8,128)(2,1)S(1)} %get-tuple-element.53), channel_id=1, source_target_pairs={{0,8},{4,12},{8,0},{12,4},{16,24},{20,28},{24,16},{28,20},{1,9},{5... | collective-permute-start | bytes 405512 | tf_op jit(solution)/shard_map/ppermute | solution.py:23
  57.8 7.5 %collective-permute-start.21 = (bf16[192,256]{1,0:T(8,128)(2,1)S(1)}, bf16[192,256]{1,0:T(8,128)(2,1)S(1)}, u32[]{:S(2)}, u32[]{:S(2)}) collective-permute-start(bf16[192,256]{1,0:T(8,128)(2,1)S(1)} %get-tuple-element.45), channel_id=1, source_target_pairs={{0,3},{1,2},{2,1},{3,0},{4,7},{5,6},{6,5},{7,4},{8,11},{9,10},{10,... | collective-permute-start | bytes 294920 | tf_op jit(solution)/shard_map/ppermute | solution.py:23
  59.8 8.7 %collective-permute-start.22 = (bf16[192,256]{1,0:T(8,128)(2,1)S(1)}, bf16[192,256]{1,0:T(8,128)(2,1)S(1)}, u32[]{:S(2)}, u32[]{:S(2)}) collective-permute-start(bf16[192,256]{1,0:T(8,128)(2,1)S(1)} %get-tuple-element.46), channel_id=1, source_target_pairs={{0,2},{1,3},{2,0},{3,1},{4,6},{5,7},{6,4},{7,5},{8,10},{9,11},{10,... | collective-permute-start | bytes 294920 | tf_op jit(solution)/shard_map/ppermute | solution.py:23
  61.6 6.9 %collective-permute-start.23 = (bf16[192,256]{1,0:T(8,128)(2,1)S(1)}, bf16[192,256]{1,0:T(8,128)(2,1)S(1)}, u32[]{:S(2)}, u32[]{:S(2)}) collective-permute-start(bf16[192,256]{1,0:T(8,128)(2,1)S(1)} %get-tuple-element.47), channel_id=1, source_target_pairs={{0,1},{1,0},{2,3},{3,2},{4,5},{5,4},{6,7},{7,6},{8,9},{9,8},{10,11... | collective-permute-start | bytes 294920 | tf_op jit(solution)/shard_map/ppermute | solution.py:23

commit v3 on v2

--- a/solution.py
+++ b/solution.py
@@ -96,7 +96,7 @@
             for shape, kind in outs
         ],
         in_specs=[pl.BlockSpec(memory_space=space) for space in spaces],
-        out_specs=[pl.BlockSpec(memory_space=pltpu.VMEM)] * len(outs),
+        out_specs=[pl.BlockSpec(memory_space=pltpu.HBM if last else pltpu.VMEM)] * len(outs),
         scratch_shapes=[
             pltpu.SemaphoreType.DMA(shape) if kind is None else pltpu.VMEM(shape, kind)
             for shape, kind in scratch
@@ -346,37 +346,50 @@
         out[...] = total[pl.ds(pl.multiple_of((at ^ j) * rows, 8), rows), :].astype(bf16)
 
 
-def summed_up(scale, own, *refs):
-    *parts, grad_head, grad_conv, whole = refs
-    total = own[...]
-    for part in parts:
-        total = total + part[...].astype(f32)
-    total = total * scale
+def unpacked(whole, total):
     chunk, both = whole.shape
     if total.shape == whole.shape:
         whole[...] = total
-    else:
-        tiles, half = both // 128, chunk // 2
-        for t in range(tiles):
-            whole[:, t * 128 : (t + 1) * 128] = total[t * chunk : (t + 1) * chunk, :]
-        for i in range(2 if both % 128 else 0):
-            at = tiles * chunk
-            whole[i * half : (i + 1) * half, tiles * 128 :] = total[at : at + half, i * 64 : (i + 1) * 64]
+        return
+    tiles, half = both // 128, chunk // 2
+    for t in range(tiles):
+        whole[:, t * 128 : (t + 1) * 128] = total[t * chunk : (t + 1) * chunk, :]
+    for i in range(2 if both % 128 else 0):
+        at = tiles * chunk
+        whole[i * half : (i + 1) * half, tiles * 128 :] = total[at : at + half, i * 64 : (i + 1) * 64]
+
+
+def finish(mp_count, scale, *refs):
+    carried, rest = refs[:mp_count], refs[mp_count:]
+    *summands, grad_skip, grad_coarse, grad_head, grad_conv, skip, coarse, whole, conv, done = rest
+    total = summands[0][...]
+    for part in summands[1:]:
+        total = total + part[...].astype(f32)
+    unpacked(whole, total * scale)
     tracks, wide = grad_head.shape[1], grad_conv.shape[2]
-    grad_head[...] = whole[:, :tracks]
+    copies = [pltpu.make_async_copy(whole.at[:, pl.ds(0, tracks)], grad_head, done.at[0])]
+    copies[0].start()
     for k in range(grad_conv.shape[0]):
-        grad_conv[k] = whole[:, tracks + k * wide : tracks + (k + 1) * wide]
-
-
-def finish(mp_count, *refs):
-    own, parts, (_, grad_skip, grad_coarse) = refs[0], refs[1:mp_count], refs[mp_count:]
-    total = own[...]
-    for part in parts:
+        conv[k] = whole[:, tracks + k * wide : tracks + (k + 1) * wide]
+    copies.append(pltpu.make_async_copy(conv, grad_conv, done.at[1]))
+    copies[1].start()
+    total = carried[0][...]
+    for part in carried[1:]:
         total = total + part[...].astype(f32)
-    grad_skip[...] = total.astype(bf16)
+    skip[...] = total.astype(bf16)
+    copies.append(pltpu.make_async_copy(skip, grad_skip, done.at[2]))
+    copies[2].start()
     length, half = grad_skip.shape[1], grad_coarse.shape[1]
-    pairs = jnp.where(iota((length, half), 0) // 2 == iota((length, half), 1), 1.0, 0.0)
-    grad_coarse[...] = dot(total, pairs, nn, lax.Precision.HIGHEST).astype(bf16)
+    pairs = jnp.where(iota((length, half), 0) // 2 == iota((length, half), 1), 1.0, 0.0).astype(bf16)
+    terms, left = [], total
+    for _ in range(3):
+        terms.append(left.astype(bf16))
+        left = left - terms[-1].astype(f32)
+    coarse[...] = sum(dot(term, pairs, nn) for term in terms).astype(bf16)
+    copies.append(pltpu.make_async_copy(coarse, grad_coarse, done.at[3]))
+    copies[3].start()
+    for copy in copies:
+        copy.wait()
 
 
 def shards(coarse, skip, conv_weight, conv_bias, head_weight, head_bias, counts, seg_mask):
@@ -468,15 +481,13 @@
             gots.append(swap(sends[j - 1], "seq", 2 * j))
     else:
         grad_own, gots = scattered(grads[0].reshape(seq_count, chunk, both), "seq"), []
-    grad_head, grad_conv = call(
-        functools.partial(summed_up, scale_back),
-        [((chunk, tracks), f32), ((taps, chunk, width), f32)],
-        grad_own, *gots, scratch=[((chunk, both), f32)], last=True,
-    )
-    grad_skip, grad_coarse = call(
-        functools.partial(finish, mp_count),
-        [((width, length), bf16), ((width, length // 2), bf16)],
-        own, *parts, grad_head, outside=(mp_count,), last=True,
+    outs = [((width, length), bf16), ((width, length // 2), bf16), ((chunk, tracks), f32), ((taps, chunk, width), f32)]
+    grad_skip, grad_coarse, grad_head, grad_conv = call(
+        functools.partial(finish, mp_count, scale_back),
+        outs,
+        own, *parts, grad_own, *gots,
+        scratch=outs[:2] + [((chunk, both), f32), outs[3], ((len(outs),), None)],
+        last=True,
     )
     return (grad_skip, grad_coarse, grad_head, grad_conv.transpose(1, 0, 2))
 

time: 69.7 us -> 66.7 us (0.957)
  waiting for transfers between devices: 27.1 us -> 22.9 us
  starting transfers between devices: 34.7 us -> 36.7 us
  Pallas kernels: 6.88 us -> 6.12 us
    ppermute x27, waiting for transfers between devices: 27.1 us -> 22.9 us  [swap(): return lax.ppermute(block, axis, [(i, i ^ mask) for i in range(count)])]
    ppermute x27, starting transfers between devices: 34.1 us -> 36 us  [swap(): return lax.ppermute(block, axis, [(i, i ^ mask) for i in range(count)])]
    pallas_call x8 -> x7, Pallas kernels: 6.88 us -> 6.12 us  [call(): pl.pallas_call(body, out_shape=[jax.ShapeDtypeStruct(shape, kind) if last...]
  transfers between devices with their start and end apart: 28 -> 28, of which waited for: 14 -> 11; matrix products, arithmetic and copies ran while one was open for 0% -> 0% of each run, Pallas kernels for 1% -> 0%
where the time goes in v3:
time: 66.7 us; the launch traced here: 66.5 us
  starting transfers between devices  36.7 us (55%)
  waiting for transfers between devices  22.9 us (34%)
  Pallas kernels  6.12 us (9%)
  between operations  0.78 us (1%)
    ppermute x27, starting transfers between devices, swap(): return lax.ppermute(block, axis, [(i, i ^ mask) for i in range(count)])  36 us
    ppermute x27, waiting for transfers between devices, swap(): return lax.ppermute(block, axis, [(i, i ^ mask) for i in range(count)])  22.9 us
    pallas_call x7, Pallas kernels, call(): pl.pallas_call(body, out_shape=[jax.ShapeDtypeStruct(shape, kind) if last...  6.12 us
  transfers between devices with their start and end apart: 28, of which 11 were waited for; matrix products, arithmetic and copies ran while one was open for 0% of the time, Pallas kernels for 0%

profile of v3, /device:TPU:0, one launch (start us, length us, event | category | flops | bytes accessed | tf_op | source)
XLA Modules:
  0.0 66.5 jit_solution(1179752735459526093)
XLA Ops:
  0.7 1.4 %shard_map.111 = (bf16[216,256]{1,0:T(8,128)(2,1)S(1)}, bf16[216,256]{1,0:T(8,128)(2,1)S(1)}, bf16[216,256]{1,0:T(8,128)(2,1)S(1)}, bf16[8,256]{1,0:T(8,128)(2,1...) custom-call(bf16[192,128]{1,0:T(8,128)(2,1)} %coarse_in.1, bf16[192,256]{1,0:T(8,128)(2,1)} %skip_in.1, ...), custom_call_target="tpu_custom_call" | custom-call | tf_op jit(solution)/shard_map/pallas_call | solution.py:92
  2.1 0.0 copy-start.4
  2.1 4.1 %collective-permute-start.1 = (bf16[216,256]{1,0:T(8,128)(2,1)S(1)}, bf16[216,256]{1,0:T(8,128)(2,1)S(1)}, u32[]{:S(2)}, u32[]{:S(2)}) collective-permute-start(bf16[216,256]{1,0:T(8,128)(2,1)S(1)} %get-tuple-element.32), channel_id=1, source_target_pairs={{0,2},{1,3},{2,0},{3,1},{4,6},{5,7},{6,4},{7,5},{8,10},{9,11},{10,... | collective-permute-start | bytes 331784 | tf_op jit(solution)/shard_map/ppermute | solution.py:23
  6.3 1.3 %collective-permute-start.2 = (bf16[216,256]{1,0:T(8,128)(2,1)S(1)}, bf16[216,256]{1,0:T(8,128)(2,1)S(1)}, u32[]{:S(2)}, u32[]{:S(2)}) collective-permute-start(bf16[216,256]{1,0:T(8,128)(2,1)S(1)} %get-tuple-element.33), channel_id=1, source_target_pairs={{0,3},{1,2},{2,1},{3,0},{4,7},{5,6},{6,5},{7,4},{8,11},{9,10},{10,... | collective-permute-start | bytes 331784 | tf_op jit(solution)/shard_map/ppermute | solution.py:23
  7.6 0.2 collective-permute-start
  7.8 0.6 collective-permute-start.3
  8.5 2.9 %collective-permute-start.4 = (bf16[8,256]{1,0:T(8,128)(2,1)S(1)}, bf16[8,256]{1,0:T(8,128)(2,1)S(1)}, u32[]{:S(2)}, u32[]{:S(2)}) collective-permute-start(bf16[8,256]{1,0:T(8,128)(2,1)S(1)} %get-tuple-element.35), channel_id=1, source_target_pairs={{0,4},{4,0},{8,12},{12,8},{16,20},{20,16},{24,28},{28,24},{1,5},{5... | collective-permute-start | bytes 12296 | tf_op jit(solution)/shard_map/ppermute | solution.py:23
  11.4 0.0 collective-permute-done.3
  11.4 0.8 %collective-permute-done.4 = bf16[8,256]{1,0:T(8,128)(2,1)S(1)} collective-permute-done((bf16[8,256]{1,0:T(8,128)(2,1)S(1)}, bf16[8,256]{1,0:T(8,128)(2,1)S(1)}, u32[]{:S(2)}, u32[]{:S(2)}) %collective-permute-start.4) | collective-permute-done | bytes 4128 | tf_op jit(solution)/shard_map/ppermute | solution.py:23
  12.2 2.9 %collective-permute-start.7 = (bf16[8,256]{1,0:T(8,128)(2,1)S(1)}, bf16[8,256]{1,0:T(8,128)(2,1)S(1)}, u32[]{:S(2)}, u32[]{:S(2)}) collective-permute-start(bf16[8,256]{1,0:T(8,128)(2,1)S(1)} %add.21.refs_4_.edges), channel_id=1, source_target_pairs={{0,3},{1,2},{2,1},{3,0},{4,7},{5,6},{6,5},{7,4},{8,11},{9,10},{10,... | collective-permute-start | bytes 12296 | tf_op jit(solution)/shard_map/ppermute | solution.py:23
  15.2 0.3 collective-permute-start.6
  15.5 2.1 %collective-permute-done.7.refs_7_ = bf16[8,256]{1,0:T(8,128)(2,1)S(1)} collective-permute-done((bf16[8,256]{1,0:T(8,128)(2,1)S(1)}, bf16[8,256]{1,0:T(8,128)(2,1)S(1)}, u32[]{:S(2)}, u32[]{:S(2)}) %collective-permute-start.7) | collective-permute-done | bytes 4128 | tf_op jit(solution)/shard_map/ppermute | solution.py:23
  17.6 0.0 collective-permute-start.5
  17.7 2.0 %collective-permute-done.6.refs_6_ = bf16[8,256]{1,0:T(8,128)(2,1)S(1)} collective-permute-done((bf16[8,256]{1,0:T(8,128)(2,1)S(1)}, bf16[8,256]{1,0:T(8,128)(2,1)S(1)}, u32[]{:S(2)}, u32[]{:S(2)}) %collective-permute-start.6) | collective-permute-done | bytes 4128 | tf_op jit(solution)/shard_map/ppermute | solution.py:23
  19.7 1.6 %collective-permute-done.5.refs_5_ = bf16[8,256]{1,0:T(8,128)(2,1)S(1)} collective-permute-done((bf16[8,256]{1,0:T(8,128)(2,1)S(1)}, bf16[8,256]{1,0:T(8,128)(2,1)S(1)}, u32[]{:S(2)}, u32[]{:S(2)}) %collective-permute-start.5) | collective-permute-done | bytes 4128 | tf_op jit(solution)/shard_map/ppermute | solution.py:23
  21.3 0.0 collective-permute-done.1.refs_2_
  21.3 0.0 collective-permute-done.2.refs_3_
  21.3 0.0 collective-permute-done.refs_1_
  21.3 1.3 %shard_map.112 = (bf16[200,256]{1,0:T(8,128)(2,1)S(1)}, f32[192,384]{1,0:T(8,128)S(1)}, bf16[768,256]{1,0:T(8,128)(2,1)S(1)}, bf16[144,128]{1,0:T(8,128)(2,1)S(1)}) custom-call(bf16[216,256]{1,0:T(8,128)(2,1)S(1)} %get-tuple-element.31.refs_0_, bf16[216,256]{1,0:T(8,128)(2,1)S(1)} %collective-permute-done.refs_1_, ...), custom_call_target="tpu_custom_call" | custom-call | tf_op jit(solution)/shard_map/pallas_call | solution.py:92
  22.6 2.9 %collective-permute-start.10 = (bf16[200,256]{1,0:T(8,128)(2,1)S(1)}, bf16[200,256]{1,0:T(8,128)(2,1)S(1)}, u32[]{:S(2)}, u32[]{:S(2)}) collective-permute-start(bf16[200,256]{1,0:T(8,128)(2,1)S(1)} %get-tuple-element.37.refs_0_), channel_id=1, source_target_pairs={{0,3},{1,2},{2,1},{3,0},{4,7},{5,6},{6,5},{7,4},{8,11},{9,10},{10,... | collective-permute-start | bytes 307208 | tf_op jit(solution)/shard_map/ppermute | solution.py:23
  25.5 0.0 collective-permute-start.9
  25.5 1.5 %collective-permute-start.8 = (bf16[200,256]{1,0:T(8,128)(2,1)S(1)}, bf16[200,256]{1,0:T(8,128)(2,1)S(1)}, u32[]{:S(2)}, u32[]{:S(2)}) collective-permute-start(bf16[200,256]{1,0:T(8,128)(2,1)S(1)} %get-tuple-element.37.refs_0_), channel_id=1, source_target_pairs={{0,1},{1,0},{2,3},{3,2},{4,5},{5,4},{6,7},{7,6},{8,9},{9,8},{10,11... | collective-permute-start | bytes 307208 | tf_op jit(solution)/shard_map/ppermute | solution.py:23
  27.0 2.8 %collective-permute-done.10.refs_3_ = bf16[200,256]{1,0:T(8,128)(2,1)S(1)} collective-permute-done((bf16[200,256]{1,0:T(8,128)(2,1)S(1)}, bf16[200,256]{1,0:T(8,128)(2,1)S(1)}, u32[]{:S(2)}, u32[]{:S(2)}) %collective-permute-start.10) | collective-permute-done | bytes 102432 | tf_op jit(solution)/shard_map/ppermute | solution.py:23
  29.8 3.5 %collective-permute-done.9.refs_2_ = bf16[200,256]{1,0:T(8,128)(2,1)S(1)} collective-permute-done((bf16[200,256]{1,0:T(8,128)(2,1)S(1)}, bf16[200,256]{1,0:T(8,128)(2,1)S(1)}, u32[]{:S(2)}, u32[]{:S(2)}) %collective-permute-start.9) | collective-permute-done | bytes 102432 | tf_op jit(solution)/shard_map/ppermute | solution.py:23
  33.2 0.0 collective-permute-done.8.refs_1_
  33.2 0.7 shard_map.113
  33.9 0.1 collective-permute-start.11
  34.0 1.2 %collective-permute-done.11 = f32[8,128]{1,0:T(8,128)S(1)} collective-permute-done((f32[8,128]{1,0:T(8,128)S(1)}, f32[8,128]{1,0:T(8,128)S(1)}, u32[]{:S(2)}, u32[]{:S(2)}) %collective-permute-start.11) | collective-permute-done | bytes 4128 | tf_op jit(solution)/shard_map/ppermute | solution.py:23
  35.1 2.0 %collective-permute-start.14 = (f32[8,128]{1,0:T(8,128)S(1)}, f32[8,128]{1,0:T(8,128)S(1)}, u32[]{:S(2)}, u32[]{:S(2)}) collective-permute-start(f32[8,128]{1,0:T(8,128)S(1)} %add.22), channel_id=1, source_target_pairs={{0,24},{4,28},{8,16},{12,20},{16,8},{20,12},{24,0},{28,4},{1,25},{... | collective-permute-start | bytes 12296 | tf_op jit(solution)/shard_map/ppermute | solution.py:23
  37.1 1.5 %collective-permute-start.13 = (f32[8,128]{1,0:T(8,128)S(1)}, f32[8,128]{1,0:T(8,128)S(1)}, u32[]{:S(2)}, u32[]{:S(2)}) collective-permute-start(f32[8,128]{1,0:T(8,128)S(1)} %add.22), channel_id=1, source_target_pairs={{0,16},{4,20},{8,24},{12,28},{16,0},{20,4},{24,8},{28,12},{1,17},{... | collective-permute-start | bytes 12296 | tf_op jit(solution)/shard_map/ppermute | solution.py:23
  38.6 0.0 collective-permute-start.12
  38.6 2.0 %collective-permute-start.20 = (bf16[144,128]{1,0:T(8,128)(2,1)S(1)}, bf16[144,128]{1,0:T(8,128)(2,1)S(1)}, u32[]{:S(2)}, u32[]{:S(2)}) collective-permute-start(bf16[144,128]{1,0:T(8,128)(2,1)S(1)} %get-tuple-element.40.refs_5_), channel_id=1, source_target_pairs={{0,24},{4,28},{8,16},{12,20},{16,8},{20,12},{24,0},{28,4},{1,25},{... | collective-permute-start | bytes 110600 | tf_op jit(solution)/shard_map/ppermute | solution.py:23
  40.6 1.5 %collective-permute-start.19 = (bf16[144,128]{1,0:T(8,128)(2,1)S(1)}, bf16[144,128]{1,0:T(8,128)(2,1)S(1)}, u32[]{:S(2)}, u32[]{:S(2)}) collective-permute-start(bf16[144,128]{1,0:T(8,128)(2,1)S(1)} %get-tuple-element.40.refs_5_), channel_id=1, source_target_pairs={{0,16},{4,20},{8,24},{12,28},{16,0},{20,4},{24,8},{28,12},{1,17},{... | collective-permute-start | bytes 110600 | tf_op jit(solution)/shard_map/ppermute | solution.py:23
  42.1 0.0 collective-permute-done.14
  42.1 0.1 collective-permute-start.18
  42.2 0.0 collective-permute-done.13
  42.2 0.0 collective-permute-done.12
  42.2 0.1 shard_map.114.refs_0_
  42.3 2.6 %collective-permute-start.17 = (bf16[264,128]{1,0:T(8,128)(2,1)S(1)}, bf16[264,128]{1,0:T(8,128)(2,1)S(1)}, u32[]{:S(2)}, u32[]{:S(2)}) collective-permute-start(bf16[264,128]{1,0:T(8,128)(2,1)S(1)} %shard_map.114.refs_0_), channel_id=1, source_target_pairs={{0,3},{1,2},{2,1},{3,0},{4,7},{5,6},{6,5},{7,4},{8,11},{9,10},{10,... | collective-permute-start | bytes 202760 | tf_op jit(solution)/shard_map/ppermute | solution.py:23
  45.0 0.0 collective-permute-start.16
  45.0 0.0 collective-permute-done.20.refs_8_
  45.0 1.8 %collective-permute-start.15 = (bf16[264,128]{1,0:T(8,128)(2,1)S(1)}, bf16[264,128]{1,0:T(8,128)(2,1)S(1)}, u32[]{:S(2)}, u32[]{:S(2)}) collective-permute-start(bf16[264,128]{1,0:T(8,128)(2,1)S(1)} %shard_map.114.refs_0_), channel_id=1, source_target_pairs={{0,1},{1,0},{2,3},{3,2},{4,5},{5,4},{6,7},{7,6},{8,9},{9,8},{10,11... | collective-permute-start | bytes 202760 | tf_op jit(solution)/shard_map/ppermute | solution.py:23
  46.8 0.0 collective-permute-done.19.refs_7_
  46.8 0.0 collective-permute-done.18.refs_6_
  46.8 2.3 %collective-permute-done.17.refs_3_ = bf16[264,128]{1,0:T(8,128)(2,1)S(1)} collective-permute-done((bf16[264,128]{1,0:T(8,128)(2,1)S(1)}, bf16[264,128]{1,0:T(8,128)(2,1)S(1)}, u32[]{:S(2)}, u32[]{:S(2)}) %collective-permute-start.17) | collective-permute-done | bytes 67616 | tf_op jit(solution)/shard_map/ppermute | solution.py:23
  49.1 1.6 %collective-permute-done.16.refs_2_ = bf16[264,128]{1,0:T(8,128)(2,1)S(1)} collective-permute-done((bf16[264,128]{1,0:T(8,128)(2,1)S(1)}, bf16[264,128]{1,0:T(8,128)(2,1)S(1)}, u32[]{:S(2)}, u32[]{:S(2)}) %collective-permute-start.16) | collective-permute-done | bytes 67616 | tf_op jit(solution)/shard_map/ppermute | solution.py:23
  50.7 0.0 collective-permute-done.15.refs_1_
  50.7 1.3 %shard_map.115 = (f32[192,256]{1,0:T(8,128)S(1)}, bf16[192,256]{1,0:T(8,128)(2,1)S(1)}, bf16[192,256]{1,0:T(8,128)(2,1)S(1)}, bf16[192,256]{1,0:T(8,128)(2,1)S(1...) custom-call(bf16[264,128]{1,0:T(8,128)(2,1)S(1)} %shard_map.114.refs_0_, ...), custom_call_target="tpu_custom_call" | custom-call | tf_op jit(solution)/shard_map/pallas_call | solution.py:92
  52.0 0.1 collective-permute-start.24
  52.1 2.1 %collective-permute-start.21 = (bf16[192,256]{1,0:T(8,128)(2,1)S(1)}, bf16[192,256]{1,0:T(8,128)(2,1)S(1)}, u32[]{:S(2)}, u32[]{:S(2)}) collective-permute-start(bf16[192,256]{1,0:T(8,128)(2,1)S(1)} %get-tuple-element.45), channel_id=1, source_target_pairs={{0,3},{1,2},{2,1},{3,0},{4,7},{5,6},{6,5},{7,4},{8,11},{9,10},{10,... | collective-permute-start | bytes 294920 | tf_op jit(solution)/shard_map/ppermute | solution.py:23
  54.2 0.0 collective-permute-done.24.got
  54.2 0.2 shard_map.116
  54.4 2.1 %collective-permute-start.25 = (bf16[528,128]{1,0:T(8,128)(2,1)S(1)}, bf16[528,128]{1,0:T(8,128)(2,1)S(1)}, u32[]{:S(2)}, u32[]{:S(2)}) collective-permute-start(bf16[528,128]{1,0:T(8,128)(2,1)S(1)} %get-tuple-element.51), channel_id=1, source_target_pairs={{0,24},{4,28},{8,16},{12,20},{16,8},{20,12},{24,0},{28,4},{1,25},{... | collective-permute-start | bytes 405512 | tf_op jit(solution)/shard_map/ppermute | solution.py:23
  56.6 1.0 %collective-permute-start.26 = (bf16[528,128]{1,0:T(8,128)(2,1)S(1)}, bf16[528,128]{1,0:T(8,128)(2,1)S(1)}, u32[]{:S(2)}, u32[]{:S(2)}) collective-permute-start(bf16[528,128]{1,0:T(8,128)(2,1)S(1)} %get-tuple-element.52), channel_id=1, source_target_pairs={{0,16},{4,20},{8,24},{12,28},{16,0},{20,4},{24,8},{28,12},{1,17},{... | collective-permute-start | bytes 405512 | tf_op jit(solution)/shard_map/ppermute | solution.py:23
  57.5 0.5 collective-permute-start.27
  58.0 1.3 %collective-permute-start.22 = (bf16[192,256]{1,0:T(8,128)(2,1)S(1)}, bf16[192,256]{1,0:T(8,128)(2,1)S(1)}, u32[]{:S(2)}, u32[]{:S(2)}) collective-permute-start(bf16[192,256]{1,0:T(8,128)(2,1)S(1)} %get-tuple-element.46), channel_id=1, source_target_pairs={{0,2},{1,3},{2,0},{3,1},{4,6},{5,7},{6,4},{7,5},{8,10},{9,11},{10,... | collective-permute-start | bytes 294920 | tf_op jit(solution)/shard_map/ppermute | solution.py:23
  59.3 0.0 collective-permute-done.21.refs_1_
  59.3 1.1 %collective-permute-start.23 = (bf16[192,256]{1,0:T(8,128)(2,1)S(1)}, bf16[192,256]{1,0:T(8,128)(2,1)S(1)}, u32[]{:S(2)}, u32[]{:S(2)}) collective-permute-start(bf16[192,256]{1,0:T(8,128)(2,1)S(1)} %get-tuple-element.47), channel_id=1, source_target_pairs={{0,1},{1,0},{2,3},{3,2},{4,5},{5,4},{6,7},{7,6},{8,9},{9,8},{10,11... | collective-permute-start | bytes 294920 | tf_op jit(solution)/shard_map/ppermute | solution.py:23
  60.4 4.4 %collective-permute-done.22.refs_2_ = bf16[192,256]{1,0:T(8,128)(2,1)S(1)} collective-permute-done((bf16[192,256]{1,0:T(8,128)(2,1)S(1)}, bf16[192,256]{1,0:T(8,128)(2,1)S(1)}, u32[]{:S(2)}, u32[]{:S(2)}) %collective-permute-start.22) | collective-permute-done | bytes 98336 | tf_op jit(solution)/shard_map/ppermute | solution.py:23
  64.8 0.7 collective-permute-done.23.refs_3_
  65.5 0.0 collective-permute-done.25.refs_5_
  65.5 0.0 collective-permute-done.26.refs_6_
  65.5 0.0 collective-permute-done.27.refs_7_
  65.5 1.1 %shard_map.117 = (bf16[192,256]{1,0:T(8,128)(2,1)}, bf16[192,128]{1,0:T(8,128)(2,1)}, f32[96,128]{1,0:T(8,128)}, f32[3,96,192]{2,1,0:T(8,128)}) custom-call(f32[192,256]{1,0:T(8,128)S(1)} %get-tuple-element.44.refs_0_, bf16[192,256]{1,0:T(8,128)(2,1)S(1)} %collective-permute-done.21.refs_1_, bf16[192,256]{1,0:T(8,128)(2,1)S(1)} %collective-permute-done.22.refs_2_, ...), custom_call_target="tpu_custom_call" | custom-call | tf_op jit(solution)/shard_map/pallas_call | solution.py:92
  (14 shorter events, 0.0 us)
Async XLA Ops:
  0.6 20.6 %copy-start.2 = (f32[192]{0:T(256)S(1)}, f32[192]{0:T(256)}, u32[]{:S(2)}) copy-start(f32[192]{0:T(256)} %param.11) | copy-start | bytes 2308
  0.6 32.6 %copy-start = (s32[256,128]{1,0:T(8,128)S(1)}, s32[256,128]{1,0:T(8,128)}, u32[]{:S(2)}) copy-start(s32[256,128]{1,0:T(8,128)} %counts.1) | copy-start | bytes 393220
  0.7 32.6 %copy-start.1 = (bf16[768,128]{1,0:T(8,128)(2,1)S(1)}, bf16[768,128]{1,0:T(8,128)(2,1)}, u32[]{:S(2)}) copy-start(bf16[768,128]{1,0:T(8,128)(2,1)} %refs_4_.1) | copy-start | bytes 589828
  0.7 32.6 %copy-start.3 = (f32[128]{0:T(128)S(1)}, f32[128]{0:T(128)}, u32[]{:S(2)}) copy-start(f32[128]{0:T(128)} %param.13) | copy-start | bytes 1540
  2.1 36.5 %copy-start.4 = (s32[1,128]{1,0:T(1,128)S(1)}, s32[1,128]{1,0:T(1,128)}, u32[]{:S(2)}) copy-start(s32[1,128]{1,0:T(1,128)} %param.15) | copy-start | bytes 1540
  2.1 19.1 %collective-permute-start.1 = (bf16[216,256]{1,0:T(8,128)(2,1)S(1)}, bf16[216,256]{1,0:T(8,128)(2,1)S(1)}, u32[]{:S(2)}, u32[]{:S(2)}) collective-permute-start(bf16[216,256]{1,0:T(8,128)(2,1)S(1)} %get-tuple-element.32), channel_id=1, source_target_pairs={{0,2},{1,3},{2,0},{3,1},{4,6},{5,7},{6,4},{7,5},{8,10},{9,11},{10,... | collective-permute-start | bytes 331784 | tf_op jit(solution)/shard_map/ppermute | solution.py:23
  6.3 15.0 %collective-permute-start.2 = (bf16[216,256]{1,0:T(8,128)(2,1)S(1)}, bf16[216,256]{1,0:T(8,128)(2,1)S(1)}, u32[]{:S(2)}, u32[]{:S(2)}) collective-permute-start(bf16[216,256]{1,0:T(8,128)(2,1)S(1)} %get-tuple-element.33), channel_id=1, source_target_pairs={{0,3},{1,2},{2,1},{3,0},{4,7},{5,6},{6,5},{7,4},{8,11},{9,10},{10,... | collective-permute-start | bytes 331784 | tf_op jit(solution)/shard_map/ppermute | solution.py:23
  7.6 13.7 %collective-permute-start = (bf16[216,256]{1,0:T(8,128)(2,1)S(1)}, bf16[216,256]{1,0:T(8,128)(2,1)S(1)}, u32[]{:S(2)}, u32[]{:S(2)}) collective-permute-start(bf16[216,256]{1,0:T(8,128)(2,1)S(1)} %get-tuple-element.31.refs_0_), channel_id=1, source_target_pairs={{0,1},{1,0},{2,3},{3,2},{4,5},{5,4},{6,7},{7,6},{8,9},{9,8},{10,11... | collective-permute-start | bytes 331784 | tf_op jit(solution)/shard_map/ppermute | solution.py:23
  7.8 3.6 %collective-permute-start.3 = (bf16[8,256]{1,0:T(8,128)(2,1)S(1)}, bf16[8,256]{1,0:T(8,128)(2,1)S(1)}, u32[]{:S(2)}, u32[]{:S(2)}) collective-permute-start(bf16[8,256]{1,0:T(8,128)(2,1)S(1)} %get-tuple-element.34), channel_id=1, source_target_pairs={{4,8},{12,16},{20,24},{8,4},{16,12},{24,20},{5,9},{13,17},{21,25},... | collective-permute-start | bytes 12296 | tf_op jit(solution)/shard_map/ppermute | solution.py:29
  8.5 3.7 %collective-permute-start.4 = (bf16[8,256]{1,0:T(8,128)(2,1)S(1)}, bf16[8,256]{1,0:T(8,128)(2,1)S(1)}, u32[]{:S(2)}, u32[]{:S(2)}) collective-permute-start(bf16[8,256]{1,0:T(8,128)(2,1)S(1)} %get-tuple-element.35), channel_id=1, source_target_pairs={{0,4},{4,0},{8,12},{12,8},{16,20},{20,16},{24,28},{28,24},{1,5},{5... | collective-permute-start | bytes 12296 | tf_op jit(solution)/shard_map/ppermute | solution.py:23
  12.2 5.4 %collective-permute-start.7 = (bf16[8,256]{1,0:T(8,128)(2,1)S(1)}, bf16[8,256]{1,0:T(8,128)(2,1)S(1)}, u32[]{:S(2)}, u32[]{:S(2)}) collective-permute-start(bf16[8,256]{1,0:T(8,128)(2,1)S(1)} %add.21.refs_4_.edges), channel_id=1, source_target_pairs={{0,3},{1,2},{2,1},{3,0},{4,7},{5,6},{6,5},{7,4},{8,11},{9,10},{10,... | collective-permute-start | bytes 12296 | tf_op jit(solution)/shard_map/ppermute | solution.py:23
  15.2 4.5 %collective-permute-start.6 = (bf16[8,256]{1,0:T(8,128)(2,1)S(1)}, bf16[8,256]{1,0:T(8,128)(2,1)S(1)}, u32[]{:S(2)}, u32[]{:S(2)}) collective-permute-start(bf16[8,256]{1,0:T(8,128)(2,1)S(1)} %add.21.refs_4_.edges), channel_id=1, source_target_pairs={{0,2},{1,3},{2,0},{3,1},{4,6},{5,7},{6,4},{7,5},{8,10},{9,11},{10,... | collective-permute-start | bytes 12296 | tf_op jit(solution)/shard_map/ppermute | solution.py:23
  17.6 3.6 %collective-permute-start.5 = (bf16[8,256]{1,0:T(8,128)(2,1)S(1)}, bf16[8,256]{1,0:T(8,128)(2,1)S(1)}, u32[]{:S(2)}, u32[]{:S(2)}) collective-permute-start(bf16[8,256]{1,0:T(8,128)(2,1)S(1)} %add.21.refs_4_.edges), channel_id=1, source_target_pairs={{0,1},{1,0},{2,3},{3,2},{4,5},{5,4},{6,7},{7,6},{8,9},{9,8},{10,11... | collective-permute-start | bytes 12296 | tf_op jit(solution)/shard_map/ppermute | solution.py:23
  22.6 7.2 %collective-permute-start.10 = (bf16[200,256]{1,0:T(8,128)(2,1)S(1)}, bf16[200,256]{1,0:T(8,128)(2,1)S(1)}, u32[]{:S(2)}, u32[]{:S(2)}) collective-permute-start(bf16[200,256]{1,0:T(8,128)(2,1)S(1)} %get-tuple-element.37.refs_0_), channel_id=1, source_target_pairs={{0,3},{1,2},{2,1},{3,0},{4,7},{5,6},{6,5},{7,4},{8,11},{9,10},{10,... | collective-permute-start | bytes 307208 | tf_op jit(solution)/shard_map/ppermute | solution.py:23
  25.5 7.7 %collective-permute-start.9 = (bf16[200,256]{1,0:T(8,128)(2,1)S(1)}, bf16[200,256]{1,0:T(8,128)(2,1)S(1)}, u32[]{:S(2)}, u32[]{:S(2)}) collective-permute-start(bf16[200,256]{1,0:T(8,128)(2,1)S(1)} %get-tuple-element.37.refs_0_), channel_id=1, source_target_pairs={{0,2},{1,3},{2,0},{3,1},{4,6},{5,7},{6,4},{7,5},{8,10},{9,11},{10,... | collective-permute-start | bytes 307208 | tf_op jit(solution)/shard_map/ppermute | solution.py:23
  25.5 7.7 %collective-permute-start.8 = (bf16[200,256]{1,0:T(8,128)(2,1)S(1)}, bf16[200,256]{1,0:T(8,128)(2,1)S(1)}, u32[]{:S(2)}, u32[]{:S(2)}) collective-permute-start(bf16[200,256]{1,0:T(8,128)(2,1)S(1)} %get-tuple-element.37.refs_0_), channel_id=1, source_target_pairs={{0,1},{1,0},{2,3},{3,2},{4,5},{5,4},{6,7},{7,6},{8,9},{9,8},{10,11... | collective-permute-start | bytes 307208 | tf_op jit(solution)/shard_map/ppermute | solution.py:23
  33.9 1.2 %collective-permute-start.11 = (f32[8,128]{1,0:T(8,128)S(1)}, f32[8,128]{1,0:T(8,128)S(1)}, u32[]{:S(2)}, u32[]{:S(2)}) collective-permute-start(f32[8,128]{1,0:T(8,128)S(1)} %get-tuple-element.39), channel_id=1, source_target_pairs={{0,4},{4,0},{8,12},{12,8},{16,20},{20,16},{24,28},{28,24},{1,5},{5... | collective-permute-start | bytes 12296 | tf_op jit(solution)/shard_map/ppermute | solution.py:23
  35.1 7.0 %collective-permute-start.14 = (f32[8,128]{1,0:T(8,128)S(1)}, f32[8,128]{1,0:T(8,128)S(1)}, u32[]{:S(2)}, u32[]{:S(2)}) collective-permute-start(f32[8,128]{1,0:T(8,128)S(1)} %add.22), channel_id=1, source_target_pairs={{0,24},{4,28},{8,16},{12,20},{16,8},{20,12},{24,0},{28,4},{1,25},{... | collective-permute-start | bytes 12296 | tf_op jit(solution)/shard_map/ppermute | solution.py:23
  37.1 5.1 %collective-permute-start.13 = (f32[8,128]{1,0:T(8,128)S(1)}, f32[8,128]{1,0:T(8,128)S(1)}, u32[]{:S(2)}, u32[]{:S(2)}) collective-permute-start(f32[8,128]{1,0:T(8,128)S(1)} %add.22), channel_id=1, source_target_pairs={{0,16},{4,20},{8,24},{12,28},{16,0},{20,4},{24,8},{28,12},{1,17},{... | collective-permute-start | bytes 12296 | tf_op jit(solution)/shard_map/ppermute | solution.py:23
  38.6 3.6 %collective-permute-start.12 = (f32[8,128]{1,0:T(8,128)S(1)}, f32[8,128]{1,0:T(8,128)S(1)}, u32[]{:S(2)}, u32[]{:S(2)}) collective-permute-start(f32[8,128]{1,0:T(8,128)S(1)} %add.22), channel_id=1, source_target_pairs={{0,8},{4,12},{8,0},{12,4},{16,24},{20,28},{24,16},{28,20},{1,9},{5... | collective-permute-start | bytes 12296 | tf_op jit(solution)/shard_map/ppermute | solution.py:23
  38.6 6.4 %collective-permute-start.20 = (bf16[144,128]{1,0:T(8,128)(2,1)S(1)}, bf16[144,128]{1,0:T(8,128)(2,1)S(1)}, u32[]{:S(2)}, u32[]{:S(2)}) collective-permute-start(bf16[144,128]{1,0:T(8,128)(2,1)S(1)} %get-tuple-element.40.refs_5_), channel_id=1, source_target_pairs={{0,24},{4,28},{8,16},{12,20},{16,8},{20,12},{24,0},{28,4},{1,25},{... | collective-permute-start | bytes 110600 | tf_op jit(solution)/shard_map/ppermute | solution.py:23
  40.6 6.2 %collective-permute-start.19 = (bf16[144,128]{1,0:T(8,128)(2,1)S(1)}, bf16[144,128]{1,0:T(8,128)(2,1)S(1)}, u32[]{:S(2)}, u32[]{:S(2)}) collective-permute-start(bf16[144,128]{1,0:T(8,128)(2,1)S(1)} %get-tuple-element.40.refs_5_), channel_id=1, source_target_pairs={{0,16},{4,20},{8,24},{12,28},{16,0},{20,4},{24,8},{28,12},{1,17},{... | collective-permute-start | bytes 110600 | tf_op jit(solution)/shard_map/ppermute | solution.py:23
  42.1 4.7 %collective-permute-start.18 = (bf16[144,128]{1,0:T(8,128)(2,1)S(1)}, bf16[144,128]{1,0:T(8,128)(2,1)S(1)}, u32[]{:S(2)}, u32[]{:S(2)}) collective-permute-start(bf16[144,128]{1,0:T(8,128)(2,1)S(1)} %get-tuple-element.40.refs_5_), channel_id=1, source_target_pairs={{0,8},{4,12},{8,0},{12,4},{16,24},{20,28},{24,16},{28,20},{1,9},{5... | collective-permute-start | bytes 110600 | tf_op jit(solution)/shard_map/ppermute | solution.py:23
  42.3 6.7 %collective-permute-start.17 = (bf16[264,128]{1,0:T(8,128)(2,1)S(1)}, bf16[264,128]{1,0:T(8,128)(2,1)S(1)}, u32[]{:S(2)}, u32[]{:S(2)}) collective-permute-start(bf16[264,128]{1,0:T(8,128)(2,1)S(1)} %shard_map.114.refs_0_), channel_id=1, source_target_pairs={{0,3},{1,2},{2,1},{3,0},{4,7},{5,6},{6,5},{7,4},{8,11},{9,10},{10,... | collective-permute-start | bytes 202760 | tf_op jit(solution)/shard_map/ppermute | solution.py:23
  45.0 5.7 %collective-permute-start.16 = (bf16[264,128]{1,0:T(8,128)(2,1)S(1)}, bf16[264,128]{1,0:T(8,128)(2,1)S(1)}, u32[]{:S(2)}, u32[]{:S(2)}) collective-permute-start(bf16[264,128]{1,0:T(8,128)(2,1)S(1)} %shard_map.114.refs_0_), channel_id=1, source_target_pairs={{0,2},{1,3},{2,0},{3,1},{4,6},{5,7},{6,4},{7,5},{8,10},{9,11},{10,... | collective-permute-start | bytes 202760 | tf_op jit(solution)/shard_map/ppermute | solution.py:23
  45.0 5.7 %collective-permute-start.15 = (bf16[264,128]{1,0:T(8,128)(2,1)S(1)}, bf16[264,128]{1,0:T(8,128)(2,1)S(1)}, u32[]{:S(2)}, u32[]{:S(2)}) collective-permute-start(bf16[264,128]{1,0:T(8,128)(2,1)S(1)} %shard_map.114.refs_0_), channel_id=1, source_target_pairs={{0,1},{1,0},{2,3},{3,2},{4,5},{5,4},{6,7},{7,6},{8,9},{9,8},{10,11... | collective-permute-start | bytes 202760 | tf_op jit(solution)/shard_map/ppermute | solution.py:23
  52.0 2.2 %collective-permute-start.24 = (bf16[2112,128]{1,0:T(8,128)(2,1)S(1)}, bf16[2112,128]{1,0:T(8,128)(2,1)S(1)}, u32[]{:S(2)}, u32[]{:S(2)}) collective-permute-start(bf16[2112,128]{1,0:T(8,128)(2,1)S(1)} %get-tuple-element.49), channel_id=1, source_target_pairs={{0,4},{4,0},{8,12},{12,8},{16,20},{20,16},{24,28},{28,24},{1,5},{5... | collective-permute-start | bytes 1622024 | tf_op jit(solution)/shard_map/ppermute | solution.py:23
  52.1 7.2 %collective-permute-start.21 = (bf16[192,256]{1,0:T(8,128)(2,1)S(1)}, bf16[192,256]{1,0:T(8,128)(2,1)S(1)}, u32[]{:S(2)}, u32[]{:S(2)}) collective-permute-start(bf16[192,256]{1,0:T(8,128)(2,1)S(1)} %get-tuple-element.45), channel_id=1, source_target_pairs={{0,3},{1,2},{2,1},{3,0},{4,7},{5,6},{6,5},{7,4},{8,11},{9,10},{10,... | collective-permute-start | bytes 294920 | tf_op jit(solution)/shard_map/ppermute | solution.py:23
  54.4 11.0 %collective-permute-start.25 = (bf16[528,128]{1,0:T(8,128)(2,1)S(1)}, bf16[528,128]{1,0:T(8,128)(2,1)S(1)}, u32[]{:S(2)}, u32[]{:S(2)}) collective-permute-start(bf16[528,128]{1,0:T(8,128)(2,1)S(1)} %get-tuple-element.51), channel_id=1, source_target_pairs={{0,24},{4,28},{8,16},{12,20},{16,8},{20,12},{24,0},{28,4},{1,25},{... | collective-permute-start | bytes 405512 | tf_op jit(solution)/shard_map/ppermute | solution.py:23
  56.6 8.9 %collective-permute-start.26 = (bf16[528,128]{1,0:T(8,128)(2,1)S(1)}, bf16[528,128]{1,0:T(8,128)(2,1)S(1)}, u32[]{:S(2)}, u32[]{:S(2)}) collective-permute-start(bf16[528,128]{1,0:T(8,128)(2,1)S(1)} %get-tuple-element.52), channel_id=1, source_target_pairs={{0,16},{4,20},{8,24},{12,28},{16,0},{20,4},{24,8},{28,12},{1,17},{... | collective-permute-start | bytes 405512 | tf_op jit(solution)/shard_map/ppermute | solution.py:23
  57.5 7.9 %collective-permute-start.27 = (bf16[528,128]{1,0:T(8,128)(2,1)S(1)}, bf16[528,128]{1,0:T(8,128)(2,1)S(1)}, u32[]{:S(2)}, u32[]{:S(2)}) collective-permute-start(bf16[528,128]{1,0:T(8,128)(2,1)S(1)} %get-tuple-element.53), channel_id=1, source_target_pairs={{0,8},{4,12},{8,0},{12,4},{16,24},{20,28},{24,16},{28,20},{1,9},{5... | collective-permute-start | bytes 405512 | tf_op jit(solution)/shard_map/ppermute | solution.py:23
  58.0 6.8 %collective-permute-start.22 = (bf16[192,256]{1,0:T(8,128)(2,1)S(1)}, bf16[192,256]{1,0:T(8,128)(2,1)S(1)}, u32[]{:S(2)}, u32[]{:S(2)}) collective-permute-start(bf16[192,256]{1,0:T(8,128)(2,1)S(1)} %get-tuple-element.46), channel_id=1, source_target_pairs={{0,2},{1,3},{2,0},{3,1},{4,6},{5,7},{6,4},{7,5},{8,10},{9,11},{10,... | collective-permute-start | bytes 294920 | tf_op jit(solution)/shard_map/ppermute | solution.py:23
  59.3 6.2 %collective-permute-start.23 = (bf16[192,256]{1,0:T(8,128)(2,1)S(1)}, bf16[192,256]{1,0:T(8,128)(2,1)S(1)}, u32[]{:S(2)}, u32[]{:S(2)}) collective-permute-start(bf16[192,256]{1,0:T(8,128)(2,1)S(1)} %get-tuple-element.47), channel_id=1, source_target_pairs={{0,1},{1,0},{2,3},{3,2},{4,5},{5,4},{6,7},{7,6},{8,9},{9,8},{10,11... | collective-permute-start | bytes 294920 | tf_op jit(solution)/shard_map/ppermute | solution.py:23

commit v4 on v3

--- a/solution.py
+++ b/solution.py
@@ -14,7 +14,6 @@
 multi_weight = 5.0
 pseudo_count = 0.5
 edge_rows = 8
-edge_lanes = 128
 bf16, f32 = jnp.bfloat16, jnp.float32
 
 
@@ -110,7 +109,7 @@
 
 
 def prepare(mp_count, group, coarse_in, skip_in, counts_in, head_in, weight_in, *refs):
-    messages, (pair, cross, weight, coarse, skip, top, bottom, done) = refs[: mp_count - 1], refs[mp_count - 1 :]
+    messages, (pair, cross, own, weight, coarse, skip, top, bottom, done) = refs[: mp_count - 1], refs[mp_count - 1 :]
     width, length = skip.shape
     rows, tracks = top.shape
     place, column = lax.axis_index("seq"), lax.axis_index("mp")
@@ -145,12 +144,14 @@
     slot = iota((edge_rows, tracks), 0)
     ahead = dot(chosen((edge_rows, length), ((0, length - 2), (1, length - 1))), total, nt)
     behind = dot(chosen((edge_rows, length), ((4, 0), (5, 1))), total, nt)
+    mine = dot(chosen((edge_rows, length), ((2, 0), (3, length - 1))), total, nt)
     first = jnp.where(slot == 7, top[0:1, :].astype(f32), behind[:, :tracks])
     last = jnp.where(slot == 6, bottom[rows - 1 : rows, :].astype(f32), ahead[:, :tracks])
     even = place % 2 == 0
     for out, left, right in (
         (pair, jnp.where(even, last, first), jnp.where(even, ahead, behind)),
         (cross, jnp.where(even, first, last), jnp.where(even, behind, ahead)),
+        (own, mine[:, :tracks], mine),
     ):
         out[...] = jnp.zeros(out.shape, bf16)
         out[:, :tracks] = left.astype(bf16)
@@ -169,19 +170,19 @@
     return value, slope
 
 
-def assembled(blocks, whole, column, width, length):
-    spread = jnp.where(
-        iota((edge_rows, edge_lanes), 0) == iota((edge_rows, edge_lanes), 1), 1.0, 0.0
-    ).astype(bf16)
-    for j, (block, edges) in enumerate(blocks):
-        rows = block_rows(column, j, width)
-        whole[rows, :length] = block
-        whole[rows, length:] = dot(edges, spread, tn).astype(bf16)
-
-
-def regrouped(out, whole, length, halves):
+def assembled(blocks, whole, column, width):
+    channels = whole.shape[0]
+    edges = 0.0
+    for j, (block, rows) in enumerate(blocks):
+        whole[block_rows(column, j, width), :] = block
+        wide = jnp.concatenate([rows.astype(f32), jnp.zeros((edge_rows, channels - rows.shape[1]), f32)], axis=1)
+        edges = edges + pltpu.roll(wide, (column ^ j) * width, 1)
+    return edges.astype(bf16)
+
+
+def regrouped(out, whole, halves):
     if not halves:
-        out[...] = whole[:, :length]
+        out[...] = whole[...]
         return
     mine = lax.axis_index("seq") & 1
     chunk = whole.shape[0] // (2 * halves)
@@ -189,12 +190,17 @@
         for i, core in enumerate((mine, 1 - mine)):
             start = pl.multiple_of((2 * q + core) * chunk, 16)
             at = (i * halves + q) * chunk
-            out[at : at + chunk, :] = whole[pl.ds(start, chunk), :length]
+            out[at : at + chunk, :] = whole[pl.ds(start, chunk), :]
+
+
+def two_rows(first, second, shape):
+    row = iota(shape, 0)
+    return jnp.where(row == 0, first, jnp.where(row == 1, second, 0.0))
 
 
 def convolve(mp_count, halves, *refs):
     pieces, edges = refs[:mp_count], refs[mp_count : 2 * mp_count]
-    weight, bias, message, slopes, full, bundle, whole = refs[2 * mp_count :]
+    weight, bias, message, slopes, slopes_beside, full, bundle, whole = refs[2 * mp_count :]
     width = weight.shape[0] // 3
     length = message.shape[1]
     half, tracks = pieces[1].shape[0] - width, bundle.shape[1]
@@ -202,39 +208,44 @@
     for j, piece in enumerate(pieces[1:]):
         for i in range(2):
             bundle[(2 * j + i) * half : (2 * j + i + 1) * half, :] = piece[width:, i * tracks : (i + 1) * tracks]
-    blocks = [(piece[:width, :], edge[:, :width]) for piece, edge in zip(pieces, edges)]
-    assembled(blocks, whole, column, width, length)
-    regrouped(full, whole, length, halves)
-    taps = [dot(weight[k * width : (k + 1) * width, :], whole[...], nn) for k in range(3)]
+    slots = assembled(
+        [(piece[:width, :], edge[...]) for piece, edge in zip(pieces, edges)], whole, column, width
+    )
+    regrouped(full, whole, halves)
+    rows = [weight[k * width : (k + 1) * width, :] for k in range(3)]
+    taps = [dot(row, whole[...], nn) for row in rows]
+    beside = [dot(slots, row, nt) for row in rows]
     lanes = iota((width, length), 1)
-    edge = iota((width, edge_lanes), 1)
-    square = (width, width)
-    shift = jnp.sum(jnp.where(iota(square, 0) == iota(square, 1), bias[...], 0.0), axis=1, keepdims=True)
-
-    def at(tap, lane):
-        return taps[tap][:, lane : lane + 1]
-
+    place = iota((edge_rows, length), 0)
+    lane = iota((edge_rows, length), 1)
+    spread = (place == 0) | ((place == 1) & (lane == 0)) | ((place == 2) & (lane == length - 1))
+    spread = jnp.where(spread, 1.0, 0.0).astype(bf16)
+    row = iota((edge_rows, width), 0)
+    left = jnp.where(
+        row == 0, bias[...], jnp.where(row == 1, beside[0][1:2, :], jnp.where(row == 2, beside[2][4:5, :], 0.0))
+    )
     inner = (
-        taps[1][:, :length]
-        + jnp.where(lanes == 0, at(0, length + 1), pltpu.roll(taps[0][:, :length], 1, 1))
-        + jnp.where(lanes == length - 1, at(2, length + 4), pltpu.roll(taps[2][:, :length], length - 1, 1))
-        + shift
-    )
-    outer = jnp.where(
-        edge == 0,
-        at(0, length) + at(1, length + 1) + at(2, 0) + shift,
-        jnp.where(edge == 1, at(0, length - 1) + at(1, length + 4) + at(2, length + 5) + shift, 0.0),
-    )
+        taps[1]
+        + jnp.where(lanes == 0, 0.0, pltpu.roll(taps[0], 1, 1))
+        + jnp.where(lanes == length - 1, 0.0, pltpu.roll(taps[2], length - 1, 1))
+    )
+    for _ in range(3):
+        term = left.astype(bf16)
+        inner = inner + dot(term, spread, tn)
+        left = left - term.astype(f32)
+    value, slope = gelu_parts(inner)
     own = whole[block_rows(column, 0, width), :].astype(f32)
-    beside = jnp.where(edge == 0, own[:, length + 1 : length + 2], own[:, length + 4 : length + 5])
-    value, slope = gelu_parts(inner)
-    message[:width, :] = (own[:, :length] + value).astype(bf16)
-    slopes[:, :length] = slope
+    message[:width, :] = (own + value).astype(bf16)
+    slopes[...] = slope
+    shape = (edge_rows, width)
+    outer = two_rows(
+        *[sum(beside[k][first + k : first + k + 1, :] for k in range(3)) + bias[...] for first in (0, 3)], shape
+    )
+    near = edges[0][:, :width].astype(f32)
     value, slope = gelu_parts(outer)
-    hidden = (beside + value).astype(bf16)
     message[width:, :] = jnp.zeros((edge_rows, length), bf16)
-    message[width:, :width] = dot(chosen((edge_rows, edge_lanes), ((0, 0), (1, 1))), hidden, nt).astype(bf16)
-    slopes[:, length:] = slope
+    message[width:, :width] = (two_rows(near[1:2, :], near[4:5, :], shape) + value).astype(bf16)
+    slopes_beside[...] = slope
 
 
 def predict(logits):
@@ -244,17 +255,16 @@
 def score(mp_count, halves, *refs):
     pieces, (head, bias, counts, logits, sums, full, whole) = refs[:mp_count], refs[mp_count:]
     width = head.shape[0] // mp_count
-    length = counts.shape[0]
-    blocks = [(piece[:width, :], piece[width:, :width]) for piece in pieces]
-    assembled(blocks, whole, lax.axis_index("mp"), width, length)
-    regrouped(full, whole, length, halves)
+    length, tracks = counts.shape
+    blocks = [(piece[:width, :], piece[width:, :]) for piece in pieces]
+    slots = assembled(blocks, whole, lax.axis_index("mp"), width)
+    regrouped(full, whole, halves)
     scores = dot(whole[...], head[...], tn) + bias[...]
-    logits[...] = scores[: length + edge_rows, :]
-    tracks = head.shape[1]
-    pred = jnp.sum(predict(scores[:length, :]), axis=0, keepdims=True)
+    logits[:length, :] = scores
+    logits[length:, :] = dot(slots, head[...], nn) + bias[...]
+    pred = jnp.sum(predict(scores), axis=0, keepdims=True)
     seen = jnp.sum(counts[...].astype(f32), axis=0, keepdims=True)
-    row = iota((8, tracks), 0)
-    sums[...] = jnp.where(row == 0, pred, jnp.where(row == 1, seen, 0.0))
+    sums[...] = two_rows(pred, seen, (8, tracks))
 
 
 def differentiate(logits, counts, edges, totals, mask, slope):
@@ -290,8 +300,8 @@
 
 def backward(mp_count, seq_count, split, group, *refs):
     slopes, head_own, bundles = refs[:mp_count], refs[mp_count], refs[mp_count + 1 : mp_count + 1 + group]
-    gelu, full, hidden, weight, *outs = refs[mp_count + 1 + group :]
-    head_rows = outs[-3]
+    gelu, gelu_beside, full, hidden, weight, *outs = refs[mp_count + 1 + group :]
+    head_rows, slope_rows = outs[-3], outs[-4]
     own, *outs = outs
     carry, outs = outs[: mp_count - 1], outs[mp_count - 1 :]
     width, length = head_own.shape[0], full.shape[1]
@@ -301,20 +311,27 @@
     for r, bundle in enumerate(bundles):
         at = pl.multiple_of((((place >> 1) & (group - 1)) ^ r) * part, 16)
         for j in range(mp_count - 1):
-            head_rows[j, pl.ds(at, part), :] = bundle[j * part : (j + 1) * part, :]
-    heads = [head_own] + [head_rows.at[j] for j in range(mp_count - 1)]
-    inner = sum(dot(head[...], part[:length, :], nt) for head, part in zip(heads, slopes))
-    outer = sum(dot(head[...], part[length:, :], nt) for head, part in zip(heads, slopes))
-    middle = (inner * gelu[:, :length]).astype(bf16).astype(f32)
-    outer = (outer * gelu[:, length : length + edge_rows]).astype(bf16).astype(f32)
-    low = jnp.where(place == 0, 0.0, outer[:, 0:1])
-    high = jnp.where(place == seq_count - 1, 0.0, outer[:, 1:2])
+            head_rows[pl.ds(at, part), (j + 1) * tracks : (j + 2) * tracks] = bundle[j * part : (j + 1) * part, :]
+    head_rows[:, :tracks] = head_own[...]
+    for j, slope in enumerate(slopes):
+        slope_rows[:, j * tracks : (j + 1) * tracks] = slope[...]
+    inner = dot(head_rows[...], slope_rows[:length, :], nt)
+    outer = dot(slope_rows[length:, :], head_rows[...], nt)
+    middle = (inner * gelu[...]).astype(bf16).astype(f32)
+    row = iota(outer.shape, 0)
+    absent = ((row == 0) & (place == 0)) | ((row == 1) & (place == seq_count - 1))
+    outer = jnp.where(absent, 0.0, outer * gelu_beside[...]).astype(bf16)
+    ends = dot(outer, chosen((edge_rows, length), ((0, 0), (1, length - 1))), tn)
     lanes = iota((width, length), 1)
     stacked = outs[-1]
-    stacked[:width, :] = jnp.where(lanes == length - 1, high, pltpu.roll(middle, length - 1, 1)).astype(bf16)
+    stacked[:width, :] = jnp.where(lanes == length - 1, ends, pltpu.roll(middle, length - 1, 1)).astype(bf16)
     stacked[width : 2 * width, :] = middle.astype(bf16)
-    stacked[2 * width :, :] = jnp.where(lanes == 0, low, pltpu.roll(middle, 1, 1)).astype(bf16)
+    stacked[2 * width :, :] = jnp.where(lanes == 0, ends, pltpu.roll(middle, 1, 1)).astype(bf16)
     total = outs[-2]
+    total[...] = dot(weight[...], stacked[...], tn)
+    own[...] = inner + total[block_rows(column, 0, width), :]
+    for j, out in zip(range(1, mp_count), carry):
+        out[...] = total[block_rows(column, j, width), :].astype(bf16)
     own_slope = slopes[0][:length, :]
     if split:
         rows = full.shape[0] // 2
@@ -330,10 +347,6 @@
         grads = outs[0]
         grads[:, :tracks] = dot(hidden[...], own_slope, nn)
         grads[:, tracks:] = dot(full[...], stacked[...], nt)
-    total[...] = dot(weight[...], stacked[...], tn)
-    own[...] = inner + total[block_rows(column, 0, width), :]
-    for j, out in zip(range(1, mp_count), carry):
-        out[...] = total[block_rows(column, j, width), :].astype(bf16)
 
 
 def quartered(count, kept, got, own, *outs):
@@ -407,9 +420,9 @@
     halves = seq_count // 2 if split else 0
     tall = width + edge_rows
     tile = ((edge_rows, length), bf16)
-    *messages, pair, cross, weight = call(
+    *messages, pair, cross, own, weight = call(
         functools.partial(prepare, mp_count, group),
-        [((width + share // 2, length), bf16)] * (mp_count - 1) + [tile, tile, ((taps * width, channels), bf16)],
+        [((width + share // 2, length), bf16)] * (mp_count - 1) + [tile, tile, tile, ((taps * width, channels), bf16)],
         coarse, skip, counts, head_weight, conv_weight.reshape(taps * width, channels),
         scratch=[
             (coarse.shape, bf16), (skip.shape, bf16), ((8, tracks), jnp.int32), ((8, tracks), jnp.int32),
@@ -422,14 +435,13 @@
         pieces.append(swap(message, "mp", j))
     cross = crossed(cross, "seq")
     pair = swap(pair, "seq", 1)
-    edges = cross + pair
-    wide = length + edge_lanes
-    message, gelu, full_in, bundle = call(
+    edges = cross + pair + own
+    message, gelu, gelu_beside, full_in, bundle = call(
         functools.partial(convolve, mp_count, halves),
-        [((tall, length), bf16), ((width, wide), f32), ((channels, length), bf16)]
+        [((tall, length), bf16), ((width, length), f32), ((edge_rows, width), f32), ((channels, length), bf16)]
         + [(((mp_count - 1) * share, tracks), bf16)],
         *pieces, *gathered(edges, "mp"), weight, conv_bias[None, :],
-        scratch=[((channels, wide), bf16)],
+        scratch=[((channels, length), bf16)],
     )
     pieces = gathered(message, "mp")
     bundles = [bundle]
@@ -440,7 +452,7 @@
         functools.partial(score, mp_count, halves),
         [((length + edge_rows, tracks), f32), ((8, tracks), f32), ((channels, length), bf16)],
         *pieces, head_weight, head_bias[None, :], counts,
-        scratch=[((channels, wide), bf16)],
+        scratch=[((channels, length), bf16)],
     )
     span = seq_count // seg_mask.shape[0]
     totals = totalled(sums, "seq", span)
@@ -453,13 +465,13 @@
     half = (seq_count // 2 * quarter[0], 128)
     grads_at = ((channels, both), f32)
     scratch = [((channels, length), f32), ((taps * width, length), bf16)]
-    head_at = [((mp_count - 1, width, tracks), bf16)]
+    head_at = [((length + edge_rows, mp_count * tracks), bf16), ((width, mp_count * tracks), bf16)]
     own, *outs = call(
         functools.partial(backward, mp_count, seq_count, split, group),
         [((width, length), f32)]
         + [((width, length), bf16)] * (mp_count - 1)
         + ([(half, f32), (half, bf16)] if split else [grads_at]),
-        *slopes, head_own, *bundles, gelu, full_in, full, weight,
+        *slopes, head_own, *bundles, gelu, gelu_beside, full_in, full, weight,
         scratch=head_at + scratch,
     )
     carry, grads = outs[: mp_count - 1], outs[mp_count - 1 :]

time: 66.7 us -> 69.6 us (1.043)
  starting transfers between devices: 36.7 us -> 38.8 us
  waiting for transfers between devices: 22.9 us -> 23.9 us
    ppermute x27, starting transfers between devices: 36 us -> 38.1 us  [swap(): return lax.ppermute(block, axis, [(i, i ^ mask) for i in range(count)])]
    ppermute x27, waiting for transfers between devices: 22.9 us -> 23.9 us  [swap(): return lax.ppermute(block, axis, [(i, i ^ mask) for i in range(count)])]
  transfers between devices with their start and end apart: 28 -> 28, of which waited for: 11 -> 9; matrix products, arithmetic and copies ran while one was open for 0% -> 0% of each run, Pallas kernels for 0% -> 1%
where the time goes in v4:
time: 69.6 us; the launch traced here: 69.4 us
  starting transfers between devices  38.8 us (56%)
  waiting for transfers between devices  23.9 us (34%)
  Pallas kernels  5.84 us (8%)
  between operations  0.78 us (1%)
    ppermute x27, starting transfers between devices, swap(): return lax.ppermute(block, axis, [(i, i ^ mask) for i in range(count)])  38.1 us
    ppermute x27, waiting for transfers between devices, swap(): return lax.ppermute(block, axis, [(i, i ^ mask) for i in range(count)])  23.9 us
    pallas_call x7, Pallas kernels, call(): pl.pallas_call(body, out_shape=[jax.ShapeDtypeStruct(shape, kind) if last...  5.84 us
  transfers between devices with their start and end apart: 28, of which 9 were waited for; matrix products, arithmetic and copies ran while one was open for 0% of the time, Pallas kernels for 1%

profile of v4, /device:TPU:0, one launch (start us, length us, event | category | flops | bytes accessed | tf_op | source)
XLA Modules:
  0.0 69.4 jit_solution(14820299100847080936)
XLA Ops:
  0.7 1.4 %shard_map.111 = (bf16[216,256]{1,0:T(8,128)(2,1)S(1)}, bf16[216,256]{1,0:T(8,128)(2,1)S(1)}, bf16[216,256]{1,0:T(8,128)(2,1)S(1)}, bf16[8,256]{1,0:T(8,128)(2,1...) custom-call(bf16[192,128]{1,0:T(8,128)(2,1)} %coarse_in.1, ...), custom_call_target="tpu_custom_call" | custom-call | tf_op jit(solution)/shard_map/pallas_call | solution.py:91
  2.1 0.0 copy-start.4
  2.1 0.7 collective-permute-start.3
  2.8 4.4 %collective-permute-start.4 = (bf16[8,256]{1,0:T(8,128)(2,1)S(1)}, bf16[8,256]{1,0:T(8,128)(2,1)S(1)}, u32[]{:S(2)}, u32[]{:S(2)}) collective-permute-start(bf16[8,256]{1,0:T(8,128)(2,1)S(1)} %get-tuple-element.37), channel_id=1, source_target_pairs={{0,4},{4,0},{8,12},{12,8},{16,20},{20,16},{24,28},{28,24},{1,5},{5... | collective-permute-start | bytes 12296 | tf_op jit(solution)/shard_map/ppermute | solution.py:22
  7.2 2.6 %collective-permute-start.1 = (bf16[216,256]{1,0:T(8,128)(2,1)S(1)}, bf16[216,256]{1,0:T(8,128)(2,1)S(1)}, u32[]{:S(2)}, u32[]{:S(2)}) collective-permute-start(bf16[216,256]{1,0:T(8,128)(2,1)S(1)} %get-tuple-element.34), channel_id=1, source_target_pairs={{0,2},{1,3},{2,0},{3,1},{4,6},{5,7},{6,4},{7,5},{8,10},{9,11},{10,... | collective-permute-start | bytes 331784 | tf_op jit(solution)/shard_map/ppermute | solution.py:22
  9.8 1.3 %collective-permute-start.2 = (bf16[216,256]{1,0:T(8,128)(2,1)S(1)}, bf16[216,256]{1,0:T(8,128)(2,1)S(1)}, u32[]{:S(2)}, u32[]{:S(2)}) collective-permute-start(bf16[216,256]{1,0:T(8,128)(2,1)S(1)} %get-tuple-element.35), channel_id=1, source_target_pairs={{0,3},{1,2},{2,1},{3,0},{4,7},{5,6},{6,5},{7,4},{8,11},{9,10},{10,... | collective-permute-start | bytes 331784 | tf_op jit(solution)/shard_map/ppermute | solution.py:22
  11.1 0.2 collective-permute-start
  11.4 0.0 collective-permute-done.3
  11.4 0.0 collective-permute-done.4
  11.4 3.0 %collective-permute-start.7 = (bf16[8,256]{1,0:T(8,128)(2,1)S(1)}, bf16[8,256]{1,0:T(8,128)(2,1)S(1)}, u32[]{:S(2)}, u32[]{:S(2)}) collective-permute-start(bf16[8,256]{1,0:T(8,128)(2,1)S(1)} %add_add_fusion.1.refs_4_.edges), channel_id=1, source_target_pairs={{0,3},{1,2},{2,1},{3,0},{4,7},{5,6},{6,5},{7,4},{8,11},{9,10},{10,... | collective-permute-start | bytes 12296 | tf_op jit(solution)/shard_map/ppermute | solution.py:22
  14.4 0.3 collective-permute-start.6
  14.7 4.5 %collective-permute-done.7.refs_7_ = bf16[8,256]{1,0:T(8,128)(2,1)S(1)} collective-permute-done((bf16[8,256]{1,0:T(8,128)(2,1)S(1)}, bf16[8,256]{1,0:T(8,128)(2,1)S(1)}, u32[]{:S(2)}, u32[]{:S(2)}) %collective-permute-start.7) | collective-permute-done | bytes 4128 | tf_op jit(solution)/shard_map/ppermute | solution.py:22
  19.2 2.1 %collective-permute-start.5 = (bf16[8,256]{1,0:T(8,128)(2,1)S(1)}, bf16[8,256]{1,0:T(8,128)(2,1)S(1)}, u32[]{:S(2)}, u32[]{:S(2)}) collective-permute-start(bf16[8,256]{1,0:T(8,128)(2,1)S(1)} %add_add_fusion.1.refs_4_.edges), channel_id=1, source_target_pairs={{0,1},{1,0},{2,3},{3,2},{4,5},{5,4},{6,7},{7,6},{8,9},{9,8},{10,11... | collective-permute-start | bytes 12296 | tf_op jit(solution)/shard_map/ppermute | solution.py:22
  21.3 0.0 collective-permute-done.6.refs_6_
  21.3 1.6 %collective-permute-done.5.refs_5_ = bf16[8,256]{1,0:T(8,128)(2,1)S(1)} collective-permute-done((bf16[8,256]{1,0:T(8,128)(2,1)S(1)}, bf16[8,256]{1,0:T(8,128)(2,1)S(1)}, u32[]{:S(2)}, u32[]{:S(2)}) %collective-permute-start.5) | collective-permute-done | bytes 4128 | tf_op jit(solution)/shard_map/ppermute | solution.py:22
  22.9 0.0 collective-permute-done.1.refs_2_
  22.9 0.0 collective-permute-done.2.refs_3_
  22.9 0.0 collective-permute-done.refs_1_
  22.9 1.1 %shard_map.112 = (bf16[200,256]{1,0:T(8,128)(2,1)S(1)}, f32[192,256]{1,0:T(8,128)S(1)}, f32[8,192]{1,0:T(8,128)S(1)}, bf16[768,256]{1,0:T(8,128)(2,1)S(1)}, bf16[144,128]{1,0:T(8,128)(2,1)S(1)}) custom-call(bf16[216,256]{1,0:T(8,128)(2,1)S(1)} %get-tuple-element.33.refs_0_, bf16[216,256]{1,0:T(8,128)(2,1)S(1)} %collective-permute-done.refs_1_, ...), custom_call_target="tpu_custom_call" | custom-call | tf_op jit(solution)/shard_map/pallas_call | solution.py:91
  24.0 3.4 %collective-permute-start.10 = (bf16[200,256]{1,0:T(8,128)(2,1)S(1)}, bf16[200,256]{1,0:T(8,128)(2,1)S(1)}, u32[]{:S(2)}, u32[]{:S(2)}) collective-permute-start(bf16[200,256]{1,0:T(8,128)(2,1)S(1)} %get-tuple-element.40.refs_0_), channel_id=1, source_target_pairs={{0,3},{1,2},{2,1},{3,0},{4,7},{5,6},{6,5},{7,4},{8,11},{9,10},{10,... | collective-permute-start | bytes 307208 | tf_op jit(solution)/shard_map/ppermute | solution.py:22
  27.4 0.6 collective-permute-start.9
  28.1 0.5 collective-permute-start.8
  28.6 2.6 %collective-permute-done.10.refs_3_ = bf16[200,256]{1,0:T(8,128)(2,1)S(1)} collective-permute-done((bf16[200,256]{1,0:T(8,128)(2,1)S(1)}, bf16[200,256]{1,0:T(8,128)(2,1)S(1)}, u32[]{:S(2)}, u32[]{:S(2)}) %collective-permute-start.10) | collective-permute-done | bytes 102432 | tf_op jit(solution)/shard_map/ppermute | solution.py:22
  31.1 5.2 %collective-permute-done.9.refs_2_ = bf16[200,256]{1,0:T(8,128)(2,1)S(1)} collective-permute-done((bf16[200,256]{1,0:T(8,128)(2,1)S(1)}, bf16[200,256]{1,0:T(8,128)(2,1)S(1)}, u32[]{:S(2)}, u32[]{:S(2)}) %collective-permute-start.9) | collective-permute-done | bytes 102432 | tf_op jit(solution)/shard_map/ppermute | solution.py:22
  36.4 0.0 collective-permute-done.8.refs_1_
  36.4 0.4 shard_map.113
  36.8 0.1 collective-permute-start.11
  36.9 1.2 %collective-permute-done.11 = f32[8,128]{1,0:T(8,128)S(1)} collective-permute-done((f32[8,128]{1,0:T(8,128)S(1)}, f32[8,128]{1,0:T(8,128)S(1)}, u32[]{:S(2)}, u32[]{:S(2)}) %collective-permute-start.11) | collective-permute-done | bytes 4128 | tf_op jit(solution)/shard_map/ppermute | solution.py:22
  38.0 1.3 %collective-permute-start.14 = (f32[8,128]{1,0:T(8,128)S(1)}, f32[8,128]{1,0:T(8,128)S(1)}, u32[]{:S(2)}, u32[]{:S(2)}) collective-permute-start(f32[8,128]{1,0:T(8,128)S(1)} %add.26), channel_id=1, source_target_pairs={{0,24},{4,28},{8,16},{12,20},{16,8},{20,12},{24,0},{28,4},{1,25},{... | collective-permute-start | bytes 12296 | tf_op jit(solution)/shard_map/ppermute | solution.py:22
  39.4 1.6 %collective-permute-start.13 = (f32[8,128]{1,0:T(8,128)S(1)}, f32[8,128]{1,0:T(8,128)S(1)}, u32[]{:S(2)}, u32[]{:S(2)}) collective-permute-start(f32[8,128]{1,0:T(8,128)S(1)} %add.26), channel_id=1, source_target_pairs={{0,16},{4,20},{8,24},{12,28},{16,0},{20,4},{24,8},{28,12},{1,17},{... | collective-permute-start | bytes 12296 | tf_op jit(solution)/shard_map/ppermute | solution.py:22
  41.0 0.5 collective-permute-start.12
  41.5 1.3 %collective-permute-start.20 = (bf16[144,128]{1,0:T(8,128)(2,1)S(1)}, bf16[144,128]{1,0:T(8,128)(2,1)S(1)}, u32[]{:S(2)}, u32[]{:S(2)}) collective-permute-start(bf16[144,128]{1,0:T(8,128)(2,1)S(1)} %get-tuple-element.43.refs_5_), channel_id=1, source_target_pairs={{0,24},{4,28},{8,16},{12,20},{16,8},{20,12},{24,0},{28,4},{1,25},{... | collective-permute-start | bytes 110600 | tf_op jit(solution)/shard_map/ppermute | solution.py:22
  42.9 1.6 %collective-permute-start.19 = (bf16[144,128]{1,0:T(8,128)(2,1)S(1)}, bf16[144,128]{1,0:T(8,128)(2,1)S(1)}, u32[]{:S(2)}, u32[]{:S(2)}) collective-permute-start(bf16[144,128]{1,0:T(8,128)(2,1)S(1)} %get-tuple-element.43.refs_5_), channel_id=1, source_target_pairs={{0,16},{4,20},{8,24},{12,28},{16,0},{20,4},{24,8},{28,12},{1,17},{... | collective-permute-start | bytes 110600 | tf_op jit(solution)/shard_map/ppermute | solution.py:22
  44.5 0.0 collective-permute-done.14
  44.5 0.5 collective-permute-start.18
  45.0 0.0 collective-permute-done.13
  45.0 0.0 collective-permute-done.12
  45.0 0.1 shard_map.114.refs_0_
  45.2 2.8 %collective-permute-start.17 = (bf16[264,128]{1,0:T(8,128)(2,1)S(1)}, bf16[264,128]{1,0:T(8,128)(2,1)S(1)}, u32[]{:S(2)}, u32[]{:S(2)}) collective-permute-start(bf16[264,128]{1,0:T(8,128)(2,1)S(1)} %shard_map.114.refs_0_), channel_id=1, source_target_pairs={{0,3},{1,2},{2,1},{3,0},{4,7},{5,6},{6,5},{7,4},{8,11},{9,10},{10,... | collective-permute-start | bytes 202760 | tf_op jit(solution)/shard_map/ppermute | solution.py:22
  48.0 0.0 collective-permute-start.16
  48.0 0.0 collective-permute-done.20.refs_8_
  48.0 1.6 %collective-permute-start.15 = (bf16[264,128]{1,0:T(8,128)(2,1)S(1)}, bf16[264,128]{1,0:T(8,128)(2,1)S(1)}, u32[]{:S(2)}, u32[]{:S(2)}) collective-permute-start(bf16[264,128]{1,0:T(8,128)(2,1)S(1)} %shard_map.114.refs_0_), channel_id=1, source_target_pairs={{0,1},{1,0},{2,3},{3,2},{4,5},{5,4},{6,7},{7,6},{8,9},{9,8},{10,11... | collective-permute-start | bytes 202760 | tf_op jit(solution)/shard_map/ppermute | solution.py:22
  49.6 0.0 collective-permute-done.19.refs_7_
  49.6 0.0 collective-permute-done.18.refs_6_
  49.7 2.1 %collective-permute-done.17.refs_3_ = bf16[264,128]{1,0:T(8,128)(2,1)S(1)} collective-permute-done((bf16[264,128]{1,0:T(8,128)(2,1)S(1)}, bf16[264,128]{1,0:T(8,128)(2,1)S(1)}, u32[]{:S(2)}, u32[]{:S(2)}) %collective-permute-start.17) | collective-permute-done | bytes 67616 | tf_op jit(solution)/shard_map/ppermute | solution.py:22
  51.8 1.7 %collective-permute-done.16.refs_2_ = bf16[264,128]{1,0:T(8,128)(2,1)S(1)} collective-permute-done((bf16[264,128]{1,0:T(8,128)(2,1)S(1)}, bf16[264,128]{1,0:T(8,128)(2,1)S(1)}, u32[]{:S(2)}, u32[]{:S(2)}) %collective-permute-start.16) | collective-permute-done | bytes 67616 | tf_op jit(solution)/shard_map/ppermute | solution.py:22
  53.5 0.0 collective-permute-done.15.refs_1_
  53.5 1.5 %shard_map.115 = (f32[192,256]{1,0:T(8,128)S(1)}, bf16[192,256]{1,0:T(8,128)(2,1)S(1)}, bf16[192,256]{1,0:T(8,128)(2,1)S(1)}, bf16[192,256]{1,0:T(8,128)(2,1)S(1...) custom-call(bf16[264,128]{1,0:T(8,128)(2,1)S(1)} %shard_map.114.refs_0_, ...), custom_call_target="tpu_custom_call" | custom-call | tf_op jit(solution)/shard_map/pallas_call | solution.py:91
  55.0 0.0 collective-permute-start.24
  55.0 2.1 %collective-permute-start.21 = (bf16[192,256]{1,0:T(8,128)(2,1)S(1)}, bf16[192,256]{1,0:T(8,128)(2,1)S(1)}, u32[]{:S(2)}, u32[]{:S(2)}) collective-permute-start(bf16[192,256]{1,0:T(8,128)(2,1)S(1)} %get-tuple-element.49), channel_id=1, source_target_pairs={{0,3},{1,2},{2,1},{3,0},{4,7},{5,6},{6,5},{7,4},{8,11},{9,10},{10,... | collective-permute-start | bytes 294920 | tf_op jit(solution)/shard_map/ppermute | solution.py:22
  57.1 0.0 collective-permute-done.24.got
  57.1 0.2 shard_map.116
  57.3 1.4 %collective-permute-start.25 = (bf16[528,128]{1,0:T(8,128)(2,1)S(1)}, bf16[528,128]{1,0:T(8,128)(2,1)S(1)}, u32[]{:S(2)}, u32[]{:S(2)}) collective-permute-start(bf16[528,128]{1,0:T(8,128)(2,1)S(1)} %get-tuple-element.55), channel_id=1, source_target_pairs={{0,24},{4,28},{8,16},{12,20},{16,8},{20,12},{24,0},{28,4},{1,25},{... | collective-permute-start | bytes 405512 | tf_op jit(solution)/shard_map/ppermute | solution.py:22
  58.7 1.6 %collective-permute-start.26 = (bf16[528,128]{1,0:T(8,128)(2,1)S(1)}, bf16[528,128]{1,0:T(8,128)(2,1)S(1)}, u32[]{:S(2)}, u32[]{:S(2)}) collective-permute-start(bf16[528,128]{1,0:T(8,128)(2,1)S(1)} %get-tuple-element.56), channel_id=1, source_target_pairs={{0,16},{4,20},{8,24},{12,28},{16,0},{20,4},{24,8},{28,12},{1,17},{... | collective-permute-start | bytes 405512 | tf_op jit(solution)/shard_map/ppermute | solution.py:22
  60.3 0.5 collective-permute-start.27
  60.9 1.5 %collective-permute-start.22 = (bf16[192,256]{1,0:T(8,128)(2,1)S(1)}, bf16[192,256]{1,0:T(8,128)(2,1)S(1)}, u32[]{:S(2)}, u32[]{:S(2)}) collective-permute-start(bf16[192,256]{1,0:T(8,128)(2,1)S(1)} %get-tuple-element.50), channel_id=1, source_target_pairs={{0,2},{1,3},{2,0},{3,1},{4,6},{5,7},{6,4},{7,5},{8,10},{9,11},{10,... | collective-permute-start | bytes 294920 | tf_op jit(solution)/shard_map/ppermute | solution.py:22
  62.4 0.0 collective-permute-done.21.refs_1_
  62.4 0.9 %collective-permute-start.23 = (bf16[192,256]{1,0:T(8,128)(2,1)S(1)}, bf16[192,256]{1,0:T(8,128)(2,1)S(1)}, u32[]{:S(2)}, u32[]{:S(2)}) collective-permute-start(bf16[192,256]{1,0:T(8,128)(2,1)S(1)} %get-tuple-element.51), channel_id=1, source_target_pairs={{0,1},{1,0},{2,3},{3,2},{4,5},{5,4},{6,7},{7,6},{8,9},{9,8},{10,11... | collective-permute-start | bytes 294920 | tf_op jit(solution)/shard_map/ppermute | solution.py:22
  63.3 4.4 %collective-permute-done.22.refs_2_ = bf16[192,256]{1,0:T(8,128)(2,1)S(1)} collective-permute-done((bf16[192,256]{1,0:T(8,128)(2,1)S(1)}, bf16[192,256]{1,0:T(8,128)(2,1)S(1)}, u32[]{:S(2)}, u32[]{:S(2)}) %collective-permute-start.22) | collective-permute-done | bytes 98336 | tf_op jit(solution)/shard_map/ppermute | solution.py:22
  67.7 0.7 %collective-permute-done.23.refs_3_ = bf16[192,256]{1,0:T(8,128)(2,1)S(1)} collective-permute-done((bf16[192,256]{1,0:T(8,128)(2,1)S(1)}, bf16[192,256]{1,0:T(8,128)(2,1)S(1)}, u32[]{:S(2)}, u32[]{:S(2)}) %collective-permute-start.23) | collective-permute-done | bytes 98336 | tf_op jit(solution)/shard_map/ppermute | solution.py:22
  68.4 0.0 collective-permute-done.25.refs_5_
  68.4 0.0 collective-permute-done.26.refs_6_
  68.4 0.0 collective-permute-done.27.refs_7_
  68.4 1.1 %shard_map.117 = (bf16[192,256]{1,0:T(8,128)(2,1)}, bf16[192,128]{1,0:T(8,128)(2,1)}, f32[96,128]{1,0:T(8,128)}, f32[3,96,192]{2,1,0:T(8,128)}) custom-call(f32[192,256]{1,0:T(8,128)S(1)} %get-tuple-element.48.refs_0_, bf16[192,256]{1,0:T(8,128)(2,1)S(1)} %collective-permute-done.21.refs_1_, bf16[192,256]{1,0:T(8,128)(2,1)S(1)} %collective-permute-done.22.refs_2_, ...), custom_call_target="tpu_custom_call" | custom-call | tf_op jit(solution)/shard_map/pallas_call | solution.py:91
  (14 shorter events, 0.0 us)
Async XLA Ops:
  0.6 22.3 %copy-start.2 = (f32[192]{0:T(256)S(1)}, f32[192]{0:T(256)}, u32[]{:S(2)}) copy-start(f32[192]{0:T(256)} %param.11) | copy-start | bytes 2308
  0.6 35.7 %copy-start = (s32[256,128]{1,0:T(8,128)S(1)}, s32[256,128]{1,0:T(8,128)}, u32[]{:S(2)}) copy-start(s32[256,128]{1,0:T(8,128)} %counts.1) | copy-start | bytes 393220
  0.7 35.7 %copy-start.1 = (bf16[768,128]{1,0:T(8,128)(2,1)S(1)}, bf16[768,128]{1,0:T(8,128)(2,1)}, u32[]{:S(2)}) copy-start(bf16[768,128]{1,0:T(8,128)(2,1)} %refs_4_.1) | copy-start | bytes 589828
  0.7 35.7 %copy-start.3 = (f32[128]{0:T(128)S(1)}, f32[128]{0:T(128)}, u32[]{:S(2)}) copy-start(f32[128]{0:T(128)} %param.13) | copy-start | bytes 1540
  2.1 39.4 %copy-start.4 = (s32[1,128]{1,0:T(1,128)S(1)}, s32[1,128]{1,0:T(1,128)}, u32[]{:S(2)}) copy-start(s32[1,128]{1,0:T(1,128)} %param.15) | copy-start | bytes 1540
  2.1 9.2 %collective-permute-start.3 = (bf16[8,256]{1,0:T(8,128)(2,1)S(1)}, bf16[8,256]{1,0:T(8,128)(2,1)S(1)}, u32[]{:S(2)}, u32[]{:S(2)}) collective-permute-start(bf16[8,256]{1,0:T(8,128)(2,1)S(1)} %get-tuple-element.36), channel_id=1, source_target_pairs={{4,8},{12,16},{20,24},{8,4},{16,12},{24,20},{5,9},{13,17},{21,25},... | collective-permute-start | bytes 12296 | tf_op jit(solution)/shard_map/ppermute | solution.py:28
  2.8 8.6 %collective-permute-start.4 = (bf16[8,256]{1,0:T(8,128)(2,1)S(1)}, bf16[8,256]{1,0:T(8,128)(2,1)S(1)}, u32[]{:S(2)}, u32[]{:S(2)}) collective-permute-start(bf16[8,256]{1,0:T(8,128)(2,1)S(1)} %get-tuple-element.37), channel_id=1, source_target_pairs={{0,4},{4,0},{8,12},{12,8},{16,20},{20,16},{24,28},{28,24},{1,5},{5... | collective-permute-start | bytes 12296 | tf_op jit(solution)/shard_map/ppermute | solution.py:22
  7.2 15.7 %collective-permute-start.1 = (bf16[216,256]{1,0:T(8,128)(2,1)S(1)}, bf16[216,256]{1,0:T(8,128)(2,1)S(1)}, u32[]{:S(2)}, u32[]{:S(2)}) collective-permute-start(bf16[216,256]{1,0:T(8,128)(2,1)S(1)} %get-tuple-element.34), channel_id=1, source_target_pairs={{0,2},{1,3},{2,0},{3,1},{4,6},{5,7},{6,4},{7,5},{8,10},{9,11},{10,... | collective-permute-start | bytes 331784 | tf_op jit(solution)/shard_map/ppermute | solution.py:22
  9.8 13.1 %collective-permute-start.2 = (bf16[216,256]{1,0:T(8,128)(2,1)S(1)}, bf16[216,256]{1,0:T(8,128)(2,1)S(1)}, u32[]{:S(2)}, u32[]{:S(2)}) collective-permute-start(bf16[216,256]{1,0:T(8,128)(2,1)S(1)} %get-tuple-element.35), channel_id=1, source_target_pairs={{0,3},{1,2},{2,1},{3,0},{4,7},{5,6},{6,5},{7,4},{8,11},{9,10},{10,... | collective-permute-start | bytes 331784 | tf_op jit(solution)/shard_map/ppermute | solution.py:22
  11.1 11.7 %collective-permute-start = (bf16[216,256]{1,0:T(8,128)(2,1)S(1)}, bf16[216,256]{1,0:T(8,128)(2,1)S(1)}, u32[]{:S(2)}, u32[]{:S(2)}) collective-permute-start(bf16[216,256]{1,0:T(8,128)(2,1)S(1)} %get-tuple-element.33.refs_0_), channel_id=1, source_target_pairs={{0,1},{1,0},{2,3},{3,2},{4,5},{5,4},{6,7},{7,6},{8,9},{9,8},{10,11... | collective-permute-start | bytes 331784 | tf_op jit(solution)/shard_map/ppermute | solution.py:22
  11.4 7.8 %collective-permute-start.7 = (bf16[8,256]{1,0:T(8,128)(2,1)S(1)}, bf16[8,256]{1,0:T(8,128)(2,1)S(1)}, u32[]{:S(2)}, u32[]{:S(2)}) collective-permute-start(bf16[8,256]{1,0:T(8,128)(2,1)S(1)} %add_add_fusion.1.refs_4_.edges), channel_id=1, source_target_pairs={{0,3},{1,2},{2,1},{3,0},{4,7},{5,6},{6,5},{7,4},{8,11},{9,10},{10,... | collective-permute-start | bytes 12296 | tf_op jit(solution)/shard_map/ppermute | solution.py:22
  14.4 6.9 %collective-permute-start.6 = (bf16[8,256]{1,0:T(8,128)(2,1)S(1)}, bf16[8,256]{1,0:T(8,128)(2,1)S(1)}, u32[]{:S(2)}, u32[]{:S(2)}) collective-permute-start(bf16[8,256]{1,0:T(8,128)(2,1)S(1)} %add_add_fusion.1.refs_4_.edges), channel_id=1, source_target_pairs={{0,2},{1,3},{2,0},{3,1},{4,6},{5,7},{6,4},{7,5},{8,10},{9,11},{10,... | collective-permute-start | bytes 12296 | tf_op jit(solution)/shard_map/ppermute | solution.py:22
  19.2 3.7 %collective-permute-start.5 = (bf16[8,256]{1,0:T(8,128)(2,1)S(1)}, bf16[8,256]{1,0:T(8,128)(2,1)S(1)}, u32[]{:S(2)}, u32[]{:S(2)}) collective-permute-start(bf16[8,256]{1,0:T(8,128)(2,1)S(1)} %add_add_fusion.1.refs_4_.edges), channel_id=1, source_target_pairs={{0,1},{1,0},{2,3},{3,2},{4,5},{5,4},{6,7},{7,6},{8,9},{9,8},{10,11... | collective-permute-start | bytes 12296 | tf_op jit(solution)/shard_map/ppermute | solution.py:22
  24.0 7.1 %collective-permute-start.10 = (bf16[200,256]{1,0:T(8,128)(2,1)S(1)}, bf16[200,256]{1,0:T(8,128)(2,1)S(1)}, u32[]{:S(2)}, u32[]{:S(2)}) collective-permute-start(bf16[200,256]{1,0:T(8,128)(2,1)S(1)} %get-tuple-element.40.refs_0_), channel_id=1, source_target_pairs={{0,3},{1,2},{2,1},{3,0},{4,7},{5,6},{6,5},{7,4},{8,11},{9,10},{10,... | collective-permute-start | bytes 307208 | tf_op jit(solution)/shard_map/ppermute | solution.py:22
  27.4 8.9 %collective-permute-start.9 = (bf16[200,256]{1,0:T(8,128)(2,1)S(1)}, bf16[200,256]{1,0:T(8,128)(2,1)S(1)}, u32[]{:S(2)}, u32[]{:S(2)}) collective-permute-start(bf16[200,256]{1,0:T(8,128)(2,1)S(1)} %get-tuple-element.40.refs_0_), channel_id=1, source_target_pairs={{0,2},{1,3},{2,0},{3,1},{4,6},{5,7},{6,4},{7,5},{8,10},{9,11},{10,... | collective-permute-start | bytes 307208 | tf_op jit(solution)/shard_map/ppermute | solution.py:22
  28.1 8.3 %collective-permute-start.8 = (bf16[200,256]{1,0:T(8,128)(2,1)S(1)}, bf16[200,256]{1,0:T(8,128)(2,1)S(1)}, u32[]{:S(2)}, u32[]{:S(2)}) collective-permute-start(bf16[200,256]{1,0:T(8,128)(2,1)S(1)} %get-tuple-element.40.refs_0_), channel_id=1, source_target_pairs={{0,1},{1,0},{2,3},{3,2},{4,5},{5,4},{6,7},{7,6},{8,9},{9,8},{10,11... | collective-permute-start | bytes 307208 | tf_op jit(solution)/shard_map/ppermute | solution.py:22
  36.8 1.2 %collective-permute-start.11 = (f32[8,128]{1,0:T(8,128)S(1)}, f32[8,128]{1,0:T(8,128)S(1)}, u32[]{:S(2)}, u32[]{:S(2)}) collective-permute-start(f32[8,128]{1,0:T(8,128)S(1)} %get-tuple-element.42), channel_id=1, source_target_pairs={{0,4},{4,0},{8,12},{12,8},{16,20},{20,16},{24,28},{28,24},{1,5},{5... | collective-permute-start | bytes 12296 | tf_op jit(solution)/shard_map/ppermute | solution.py:22
  38.0 6.5 %collective-permute-start.14 = (f32[8,128]{1,0:T(8,128)S(1)}, f32[8,128]{1,0:T(8,128)S(1)}, u32[]{:S(2)}, u32[]{:S(2)}) collective-permute-start(f32[8,128]{1,0:T(8,128)S(1)} %add.26), channel_id=1, source_target_pairs={{0,24},{4,28},{8,16},{12,20},{16,8},{20,12},{24,0},{28,4},{1,25},{... | collective-permute-start | bytes 12296 | tf_op jit(solution)/shard_map/ppermute | solution.py:22
  39.4 5.7 %collective-permute-start.13 = (f32[8,128]{1,0:T(8,128)S(1)}, f32[8,128]{1,0:T(8,128)S(1)}, u32[]{:S(2)}, u32[]{:S(2)}) collective-permute-start(f32[8,128]{1,0:T(8,128)S(1)} %add.26), channel_id=1, source_target_pairs={{0,16},{4,20},{8,24},{12,28},{16,0},{20,4},{24,8},{28,12},{1,17},{... | collective-permute-start | bytes 12296 | tf_op jit(solution)/shard_map/ppermute | solution.py:22
  41.0 4.0 %collective-permute-start.12 = (f32[8,128]{1,0:T(8,128)S(1)}, f32[8,128]{1,0:T(8,128)S(1)}, u32[]{:S(2)}, u32[]{:S(2)}) collective-permute-start(f32[8,128]{1,0:T(8,128)S(1)} %add.26), channel_id=1, source_target_pairs={{0,8},{4,12},{8,0},{12,4},{16,24},{20,28},{24,16},{28,20},{1,9},{5... | collective-permute-start | bytes 12296 | tf_op jit(solution)/shard_map/ppermute | solution.py:22
  41.5 6.5 %collective-permute-start.20 = (bf16[144,128]{1,0:T(8,128)(2,1)S(1)}, bf16[144,128]{1,0:T(8,128)(2,1)S(1)}, u32[]{:S(2)}, u32[]{:S(2)}) collective-permute-start(bf16[144,128]{1,0:T(8,128)(2,1)S(1)} %get-tuple-element.43.refs_5_), channel_id=1, source_target_pairs={{0,24},{4,28},{8,16},{12,20},{16,8},{20,12},{24,0},{28,4},{1,25},{... | collective-permute-start | bytes 110600 | tf_op jit(solution)/shard_map/ppermute | solution.py:22
  42.9 6.8 %collective-permute-start.19 = (bf16[144,128]{1,0:T(8,128)(2,1)S(1)}, bf16[144,128]{1,0:T(8,128)(2,1)S(1)}, u32[]{:S(2)}, u32[]{:S(2)}) collective-permute-start(bf16[144,128]{1,0:T(8,128)(2,1)S(1)} %get-tuple-element.43.refs_5_), channel_id=1, source_target_pairs={{0,16},{4,20},{8,24},{12,28},{16,0},{20,4},{24,8},{28,12},{1,17},{... | collective-permute-start | bytes 110600 | tf_op jit(solution)/shard_map/ppermute | solution.py:22
  44.5 5.2 %collective-permute-start.18 = (bf16[144,128]{1,0:T(8,128)(2,1)S(1)}, bf16[144,128]{1,0:T(8,128)(2,1)S(1)}, u32[]{:S(2)}, u32[]{:S(2)}) collective-permute-start(bf16[144,128]{1,0:T(8,128)(2,1)S(1)} %get-tuple-element.43.refs_5_), channel_id=1, source_target_pairs={{0,8},{4,12},{8,0},{12,4},{16,24},{20,28},{24,16},{28,20},{1,9},{5... | collective-permute-start | bytes 110600 | tf_op jit(solution)/shard_map/ppermute | solution.py:22
  45.2 6.6 %collective-permute-start.17 = (bf16[264,128]{1,0:T(8,128)(2,1)S(1)}, bf16[264,128]{1,0:T(8,128)(2,1)S(1)}, u32[]{:S(2)}, u32[]{:S(2)}) collective-permute-start(bf16[264,128]{1,0:T(8,128)(2,1)S(1)} %shard_map.114.refs_0_), channel_id=1, source_target_pairs={{0,3},{1,2},{2,1},{3,0},{4,7},{5,6},{6,5},{7,4},{8,11},{9,10},{10,... | collective-permute-start | bytes 202760 | tf_op jit(solution)/shard_map/ppermute | solution.py:22
  48.0 5.5 %collective-permute-start.16 = (bf16[264,128]{1,0:T(8,128)(2,1)S(1)}, bf16[264,128]{1,0:T(8,128)(2,1)S(1)}, u32[]{:S(2)}, u32[]{:S(2)}) collective-permute-start(bf16[264,128]{1,0:T(8,128)(2,1)S(1)} %shard_map.114.refs_0_), channel_id=1, source_target_pairs={{0,2},{1,3},{2,0},{3,1},{4,6},{5,7},{6,4},{7,5},{8,10},{9,11},{10,... | collective-permute-start | bytes 202760 | tf_op jit(solution)/shard_map/ppermute | solution.py:22
  48.0 5.5 %collective-permute-start.15 = (bf16[264,128]{1,0:T(8,128)(2,1)S(1)}, bf16[264,128]{1,0:T(8,128)(2,1)S(1)}, u32[]{:S(2)}, u32[]{:S(2)}) collective-permute-start(bf16[264,128]{1,0:T(8,128)(2,1)S(1)} %shard_map.114.refs_0_), channel_id=1, source_target_pairs={{0,1},{1,0},{2,3},{3,2},{4,5},{5,4},{6,7},{7,6},{8,9},{9,8},{10,11... | collective-permute-start | bytes 202760 | tf_op jit(solution)/shard_map/ppermute | solution.py:22
  55.0 2.1 %collective-permute-start.24 = (bf16[2112,128]{1,0:T(8,128)(2,1)S(1)}, bf16[2112,128]{1,0:T(8,128)(2,1)S(1)}, u32[]{:S(2)}, u32[]{:S(2)}) collective-permute-start(bf16[2112,128]{1,0:T(8,128)(2,1)S(1)} %get-tuple-element.53), channel_id=1, source_target_pairs={{0,4},{4,0},{8,12},{12,8},{16,20},{20,16},{24,28},{28,24},{1,5},{5... | collective-permute-start | bytes 1622024 | tf_op jit(solution)/shard_map/ppermute | solution.py:22
  55.0 7.4 %collective-permute-start.21 = (bf16[192,256]{1,0:T(8,128)(2,1)S(1)}, bf16[192,256]{1,0:T(8,128)(2,1)S(1)}, u32[]{:S(2)}, u32[]{:S(2)}) collective-permute-start(bf16[192,256]{1,0:T(8,128)(2,1)S(1)} %get-tuple-element.49), channel_id=1, source_target_pairs={{0,3},{1,2},{2,1},{3,0},{4,7},{5,6},{6,5},{7,4},{8,11},{9,10},{10,... | collective-permute-start | bytes 294920 | tf_op jit(solution)/shard_map/ppermute | solution.py:22
  57.3 11.1 %collective-permute-start.25 = (bf16[528,128]{1,0:T(8,128)(2,1)S(1)}, bf16[528,128]{1,0:T(8,128)(2,1)S(1)}, u32[]{:S(2)}, u32[]{:S(2)}) collective-permute-start(bf16[528,128]{1,0:T(8,128)(2,1)S(1)} %get-tuple-element.55), channel_id=1, source_target_pairs={{0,24},{4,28},{8,16},{12,20},{16,8},{20,12},{24,0},{28,4},{1,25},{... | collective-permute-start | bytes 405512 | tf_op jit(solution)/shard_map/ppermute | solution.py:22
  58.7 9.6 %collective-permute-start.26 = (bf16[528,128]{1,0:T(8,128)(2,1)S(1)}, bf16[528,128]{1,0:T(8,128)(2,1)S(1)}, u32[]{:S(2)}, u32[]{:S(2)}) collective-permute-start(bf16[528,128]{1,0:T(8,128)(2,1)S(1)} %get-tuple-element.56), channel_id=1, source_target_pairs={{0,16},{4,20},{8,24},{12,28},{16,0},{20,4},{24,8},{28,12},{1,17},{... | collective-permute-start | bytes 405512 | tf_op jit(solution)/shard_map/ppermute | solution.py:22
  60.3 8.0 %collective-permute-start.27 = (bf16[528,128]{1,0:T(8,128)(2,1)S(1)}, bf16[528,128]{1,0:T(8,128)(2,1)S(1)}, u32[]{:S(2)}, u32[]{:S(2)}) collective-permute-start(bf16[528,128]{1,0:T(8,128)(2,1)S(1)} %get-tuple-element.57), channel_id=1, source_target_pairs={{0,8},{4,12},{8,0},{12,4},{16,24},{20,28},{24,16},{28,20},{1,9},{5... | collective-permute-start | bytes 405512 | tf_op jit(solution)/shard_map/ppermute | solution.py:22
  60.9 6.8 %collective-permute-start.22 = (bf16[192,256]{1,0:T(8,128)(2,1)S(1)}, bf16[192,256]{1,0:T(8,128)(2,1)S(1)}, u32[]{:S(2)}, u32[]{:S(2)}) collective-permute-start(bf16[192,256]{1,0:T(8,128)(2,1)S(1)} %get-tuple-element.50), channel_id=1, source_target_pairs={{0,2},{1,3},{2,0},{3,1},{4,6},{5,7},{6,4},{7,5},{8,10},{9,11},{10,... | collective-permute-start | bytes 294920 | tf_op jit(solution)/shard_map/ppermute | solution.py:22
  62.4 6.0 %collective-permute-start.23 = (bf16[192,256]{1,0:T(8,128)(2,1)S(1)}, bf16[192,256]{1,0:T(8,128)(2,1)S(1)}, u32[]{:S(2)}, u32[]{:S(2)}) collective-permute-start(bf16[192,256]{1,0:T(8,128)(2,1)S(1)} %get-tuple-element.51), channel_id=1, source_target_pairs={{0,1},{1,0},{2,3},{3,2},{4,5},{5,4},{6,7},{7,6},{8,9},{9,8},{10,11... | collective-permute-start | bytes 294920 | tf_op jit(solution)/shard_map/ppermute | solution.py:22

commit v5 on v4

--- a/solution.py
+++ b/solution.py
@@ -86,7 +86,7 @@
     return jnp.where(hit, 1.0, 0.0).astype(bf16)
 
 
-def call(body, outs, *args, scratch=(), grant=16 << 20, outside=(), last=False):
+def call(body, outs, *args, scratch=(), grant=16 << 20, outside=(), last=False, aliases={}):
     spaces = [pltpu.HBM if i in outside else pltpu.VMEM for i in range(len(args))]
     return pl.pallas_call(
         body,
@@ -100,6 +100,7 @@
             pltpu.SemaphoreType.DMA(shape) if kind is None else pltpu.VMEM(shape, kind)
             for shape, kind in scratch
         ],
+        input_output_aliases=aliases,
         compiler_params=pltpu.CompilerParams(vmem_limit_bytes=grant),
     )(*[pltpu.with_memory_space_constraint(arg, space) for arg, space in zip(args, spaces)])
 
@@ -160,6 +161,12 @@
         copy.wait()
 
 
+def attach(cross, pair, own, message_in, edges, message):
+    total = cross[...] + pair[...] + own[...]
+    edges[...] = total
+    message[message.shape[0] - edge_rows :, :] = total
+
+
 def gelu_parts(inputs):
     inner = root_two_pi * (inputs + cubic_coef * inputs * inputs * inputs)
     tangent = jnp.tanh(inner)
@@ -199,17 +206,18 @@
 
 
 def convolve(mp_count, halves, *refs):
-    pieces, edges = refs[:mp_count], refs[mp_count : 2 * mp_count]
-    weight, bias, message, slopes, slopes_beside, full, bundle, whole = refs[2 * mp_count :]
+    pieces, (near, *far) = refs[:mp_count], refs[mp_count : 2 * mp_count - 1]
+    weight, bias, message, slopes, slopes_beside, full, bundle, whole = refs[2 * mp_count - 1 :]
     width = weight.shape[0] // 3
     length = message.shape[1]
-    half, tracks = pieces[1].shape[0] - width, bundle.shape[1]
+    half, tracks = pieces[1].shape[0] - edge_rows - width, bundle.shape[1]
+    edges = [near[...], pieces[1][width + half :, :]] + [rows[...] for rows in far]
     column = lax.axis_index("mp")
     for j, piece in enumerate(pieces[1:]):
         for i in range(2):
-            bundle[(2 * j + i) * half : (2 * j + i + 1) * half, :] = piece[width:, i * tracks : (i + 1) * tracks]
+            bundle[(2 * j + i) * half : (2 * j + i + 1) * half, :] = piece[width : width + half, i * tracks : (i + 1) * tracks]
     slots = assembled(
-        [(piece[:width, :], edge[...]) for piece, edge in zip(pieces, edges)], whole, column, width
+        [(piece[:width, :], edge) for piece, edge in zip(pieces, edges)], whole, column, width
     )
     regrouped(full, whole, halves)
     rows = [weight[k * width : (k + 1) * width, :] for k in range(3)]
@@ -241,7 +249,7 @@
     outer = two_rows(
         *[sum(beside[k][first + k : first + k + 1, :] for k in range(3)) + bias[...] for first in (0, 3)], shape
     )
-    near = edges[0][:, :width].astype(f32)
+    near = near[:, :width].astype(f32)
     value, slope = gelu_parts(outer)
     message[width:, :] = jnp.zeros((edge_rows, length), bf16)
     message[width:, :width] = (two_rows(near[1:2, :], near[4:5, :], shape) + value).astype(bf16)
@@ -420,9 +428,11 @@
     halves = seq_count // 2 if split else 0
     tall = width + edge_rows
     tile = ((edge_rows, length), bf16)
+    block = ((width + share // 2, length), bf16)
+    nearest = ((width + share // 2 + edge_rows, length), bf16)
     *messages, pair, cross, own, weight = call(
         functools.partial(prepare, mp_count, group),
-        [((width + share // 2, length), bf16)] * (mp_count - 1) + [tile, tile, tile, ((taps * width, channels), bf16)],
+        [nearest] + [block] * (mp_count - 2) + [tile, tile, tile, ((taps * width, channels), bf16)],
         coarse, skip, counts, head_weight, conv_weight.reshape(taps * width, channels),
         scratch=[
             (coarse.shape, bf16), (skip.shape, bf16), ((8, tracks), jnp.int32), ((8, tracks), jnp.int32),
@@ -430,17 +440,20 @@
         ],
         outside=range(5),
     )
-    pieces = [messages[0]]
+    cross = crossed(cross, "seq")
+    pair = swap(pair, "seq", 1)
+    edges, messages[0] = call(attach, [tile, nearest], cross, pair, own, messages[0], aliases={3: 1})
+    pieces = [messages[-1]]
     for j, message in zip(range(1, mp_count), messages):
         pieces.append(swap(message, "mp", j))
-    cross = crossed(cross, "seq")
-    pair = swap(pair, "seq", 1)
-    edges = cross + pair + own
+    halos = [edges]
+    for j in range(2, mp_count):
+        halos.append(swap(edges, "mp", j))
     message, gelu, gelu_beside, full_in, bundle = call(
         functools.partial(convolve, mp_count, halves),
         [((tall, length), bf16), ((width, length), f32), ((edge_rows, width), f32), ((channels, length), bf16)]
         + [(((mp_count - 1) * share, tracks), bf16)],
-        *pieces, *gathered(edges, "mp"), weight, conv_bias[None, :],
+        *pieces, *halos, weight, conv_bias[None, :],
         scratch=[((channels, length), bf16)],
     )
     pieces = gathered(message, "mp")

time: 69.6 us -> 69.3 us (level)
  starting transfers between devices: 38.8 us -> 37.6 us
  waiting for transfers between devices: 23.9 us -> 24.9 us
    ppermute x27 -> x26, starting transfers between devices: 38.1 us -> 36.8 us  [swap(): return lax.ppermute(block, axis, [(i, i ^ mask) for i in range(count)])]
    ppermute x27 -> x26, waiting for transfers between devices: 23.9 us -> 24.9 us  [swap(): return lax.ppermute(block, axis, [(i, i ^ mask) for i in range(count)])]
    pallas_call x7 -> x8, Pallas kernels: 5.84 us -> 5.79 us  [call(): pl.pallas_call(body, out_shape=[jax.ShapeDtypeStruct(shape, kind) if last...]
  transfers between devices with their start and end apart: 28 -> 27, of which waited for: 9 -> 10; matrix products, arithmetic and copies ran while one was open for 0% -> 0% of each run, Pallas kernels for 1% -> 1%
where the time goes in v5:
time: 69.3 us; the launch traced here: 69.1 us
  starting transfers between devices  37.6 us (54%)
  waiting for transfers between devices  24.9 us (36%)
  Pallas kernels  5.79 us (8%)
  between operations  0.77 us (1%)
    ppermute x26, starting transfers between devices, swap(): return lax.ppermute(block, axis, [(i, i ^ mask) for i in range(count)])  36.8 us
    ppermute x26, waiting for transfers between devices, swap(): return lax.ppermute(block, axis, [(i, i ^ mask) for i in range(count)])  24.9 us
    pallas_call x8, Pallas kernels, call(): pl.pallas_call(body, out_shape=[jax.ShapeDtypeStruct(shape, kind) if last...  5.79 us
  transfers between devices with their start and end apart: 27, of which 10 were waited for; matrix products, arithmetic and copies ran while one was open for 0% of the time, Pallas kernels for 1%

profile of v5, /device:TPU:0, one launch (start us, length us, event | category | flops | bytes accessed | tf_op | source)
XLA Modules:
  0.0 69.1 jit_solution(1477248703701162544)
XLA Ops:
  0.6 1.4 %shard_map.111 = (bf16[224,256]{1,0:T(8,128)(2,1)S(1)}, bf16[216,256]{1,0:T(8,128)(2,1)S(1)}, bf16[216,256]{1,0:T(8,128)(2,1)S(1)}, bf16[8,256]{1,0:T(8,128)(2,1...) custom-call(bf16[192,128]{1,0:T(8,128)(2,1)} %coarse_in.1, ...), custom_call_target="tpu_custom_call" | custom-call | tf_op jit(solution)/shard_map/pallas_call | solution.py:91
  2.0 0.0 copy-start
  2.1 0.0 copy-start.1
  2.1 0.0 copy-start.3
  2.1 0.8 %collective-permute-start = (bf16[8,256]{1,0:T(8,128)(2,1)S(1)}, bf16[8,256]{1,0:T(8,128)(2,1)S(1)}, u32[]{:S(2)}, u32[]{:S(2)}) collective-permute-start(bf16[8,256]{1,0:T(8,128)(2,1)S(1)} %get-tuple-element.36), channel_id=1, source_target_pairs={{4,8},{12,16},{20,24},{8,4},{16,12},{24,20},{5,9},{13,17},{21,25},... | collective-permute-start | bytes 12296 | tf_op jit(solution)/shard_map/ppermute | solution.py:28
  2.9 4.4 %collective-permute-start.1 = (bf16[8,256]{1,0:T(8,128)(2,1)S(1)}, bf16[8,256]{1,0:T(8,128)(2,1)S(1)}, u32[]{:S(2)}, u32[]{:S(2)}) collective-permute-start(bf16[8,256]{1,0:T(8,128)(2,1)S(1)} %get-tuple-element.37), channel_id=1, source_target_pairs={{0,4},{4,0},{8,12},{12,8},{16,20},{20,16},{24,28},{28,24},{1,5},{5... | collective-permute-start | bytes 12296 | tf_op jit(solution)/shard_map/ppermute | solution.py:22
  7.3 0.0 collective-permute-done.cross
  7.3 0.8 %collective-permute-done.1.pair = bf16[8,256]{1,0:T(8,128)(2,1)S(1)} collective-permute-done((bf16[8,256]{1,0:T(8,128)(2,1)S(1)}, bf16[8,256]{1,0:T(8,128)(2,1)S(1)}, u32[]{:S(2)}, u32[]{:S(2)}) %collective-permute-start.1) | collective-permute-done | bytes 4128 | tf_op jit(solution)/shard_map/ppermute | solution.py:22
  8.1 1.6 %collective-permute-start.2 = (bf16[224,256]{1,0:T(8,128)(2,1)S(1)}, bf16[224,256]{1,0:T(8,128)(2,1)S(1)}, u32[]{:S(2)}, u32[]{:S(2)}) collective-permute-start(bf16[224,256]{1,0:T(8,128)(2,1)S(1)} %get-tuple-element.40), channel_id=1, source_target_pairs={{0,1},{1,0},{2,3},{3,2},{4,5},{5,4},{6,7},{7,6},{8,9},{9,8},{10,11... | collective-permute-start | bytes 344072 | tf_op jit(solution)/shard_map/ppermute | solution.py:22
  9.7 2.6 %collective-permute-start.3 = (bf16[216,256]{1,0:T(8,128)(2,1)S(1)}, bf16[216,256]{1,0:T(8,128)(2,1)S(1)}, u32[]{:S(2)}, u32[]{:S(2)}) collective-permute-start(bf16[216,256]{1,0:T(8,128)(2,1)S(1)} %get-tuple-element.41), channel_id=1, source_target_pairs={{0,2},{1,3},{2,0},{3,1},{4,6},{5,7},{6,4},{7,5},{8,10},{9,11},{10,... | collective-permute-start | bytes 331784 | tf_op jit(solution)/shard_map/ppermute | solution.py:22
  12.3 0.2 collective-permute-start.4
  12.5 3.6 %collective-permute-start.6 = (bf16[8,256]{1,0:T(8,128)(2,1)S(1)}, bf16[8,256]{1,0:T(8,128)(2,1)S(1)}, u32[]{:S(2)}, u32[]{:S(2)}) collective-permute-start(bf16[8,256]{1,0:T(8,128)(2,1)S(1)} %get-tuple-element.42.refs_4_.edges), channel_id=1, source_target_pairs={{0,3},{1,2},{2,1},{3,0},{4,7},{5,6},{6,5},{7,4},{8,11},{9,10},{10,... | collective-permute-start | bytes 12296 | tf_op jit(solution)/shard_map/ppermute | solution.py:22
  16.1 0.0 collective-permute-start.5
  16.1 4.5 %collective-permute-done.6.refs_6_ = bf16[8,256]{1,0:T(8,128)(2,1)S(1)} collective-permute-done((bf16[8,256]{1,0:T(8,128)(2,1)S(1)}, bf16[8,256]{1,0:T(8,128)(2,1)S(1)}, u32[]{:S(2)}, u32[]{:S(2)}) %collective-permute-start.6) | collective-permute-done | bytes 4128 | tf_op jit(solution)/shard_map/ppermute | solution.py:22
  20.6 2.6 %collective-permute-done.5.refs_5_ = bf16[8,256]{1,0:T(8,128)(2,1)S(1)} collective-permute-done((bf16[8,256]{1,0:T(8,128)(2,1)S(1)}, bf16[8,256]{1,0:T(8,128)(2,1)S(1)}, u32[]{:S(2)}, u32[]{:S(2)}) %collective-permute-start.5) | collective-permute-done | bytes 4128 | tf_op jit(solution)/shard_map/ppermute | solution.py:22
  23.2 0.0 collective-permute-done.3.refs_2_
  23.2 0.0 collective-permute-done.4.refs_3_
  23.2 0.0 collective-permute-done.2.refs_1_
  23.3 1.1 %shard_map.113 = (bf16[200,256]{1,0:T(8,128)(2,1)S(1)}, f32[192,256]{1,0:T(8,128)S(1)}, f32[8,192]{1,0:T(8,128)S(1)}, bf16[768,256]{1,0:T(8,128)(2,1)S(1)}, bf16[144,128]{1,0:T(8,128)(2,1)S(1)}) custom-call(bf16[216,256]{1,0:T(8,128)(2,1)S(1)} %get-tuple-element.35.refs_0_, bf16[224,256]{1,0:T(8,128)(2,1)S(1)} %collective-permute-done.2.refs_1_, ...), custom_call_target="tpu_custom_call" | custom-call | tf_op jit(solution)/shard_map/pallas_call | solution.py:91
  24.4 2.5 %collective-permute-start.9 = (bf16[200,256]{1,0:T(8,128)(2,1)S(1)}, bf16[200,256]{1,0:T(8,128)(2,1)S(1)}, u32[]{:S(2)}, u32[]{:S(2)}) collective-permute-start(bf16[200,256]{1,0:T(8,128)(2,1)S(1)} %get-tuple-element.44.refs_0_), channel_id=1, source_target_pairs={{0,3},{1,2},{2,1},{3,0},{4,7},{5,6},{6,5},{7,4},{8,11},{9,10},{10,... | collective-permute-start | bytes 307208 | tf_op jit(solution)/shard_map/ppermute | solution.py:22
  26.9 0.0 collective-permute-start.8
  26.9 1.9 %collective-permute-start.7 = (bf16[200,256]{1,0:T(8,128)(2,1)S(1)}, bf16[200,256]{1,0:T(8,128)(2,1)S(1)}, u32[]{:S(2)}, u32[]{:S(2)}) collective-permute-start(bf16[200,256]{1,0:T(8,128)(2,1)S(1)} %get-tuple-element.44.refs_0_), channel_id=1, source_target_pairs={{0,1},{1,0},{2,3},{3,2},{4,5},{5,4},{6,7},{7,6},{8,9},{9,8},{10,11... | collective-permute-start | bytes 307208 | tf_op jit(solution)/shard_map/ppermute | solution.py:22
  28.8 3.2 %collective-permute-done.9.refs_3_ = bf16[200,256]{1,0:T(8,128)(2,1)S(1)} collective-permute-done((bf16[200,256]{1,0:T(8,128)(2,1)S(1)}, bf16[200,256]{1,0:T(8,128)(2,1)S(1)}, u32[]{:S(2)}, u32[]{:S(2)}) %collective-permute-start.9) | collective-permute-done | bytes 102432 | tf_op jit(solution)/shard_map/ppermute | solution.py:22
  32.0 3.5 %collective-permute-done.8.refs_2_ = bf16[200,256]{1,0:T(8,128)(2,1)S(1)} collective-permute-done((bf16[200,256]{1,0:T(8,128)(2,1)S(1)}, bf16[200,256]{1,0:T(8,128)(2,1)S(1)}, u32[]{:S(2)}, u32[]{:S(2)}) %collective-permute-start.8) | collective-permute-done | bytes 102432 | tf_op jit(solution)/shard_map/ppermute | solution.py:22
  35.5 0.0 collective-permute-done.7.refs_1_
  35.6 0.4 shard_map.114
  36.0 0.1 collective-permute-start.10
  36.1 1.2 %collective-permute-done.10 = f32[8,128]{1,0:T(8,128)S(1)} collective-permute-done((f32[8,128]{1,0:T(8,128)S(1)}, f32[8,128]{1,0:T(8,128)S(1)}, u32[]{:S(2)}, u32[]{:S(2)}) %collective-permute-start.10) | collective-permute-done | bytes 4128 | tf_op jit(solution)/shard_map/ppermute | solution.py:22
  37.2 0.2 collective-permute-start.13
  37.4 3.7 %collective-permute-start.12 = (f32[8,128]{1,0:T(8,128)S(1)}, f32[8,128]{1,0:T(8,128)S(1)}, u32[]{:S(2)}, u32[]{:S(2)}) collective-permute-start(f32[8,128]{1,0:T(8,128)S(1)} %add.18), channel_id=1, source_target_pairs={{0,16},{4,20},{8,24},{12,28},{16,0},{20,4},{24,8},{28,12},{1,17},{... | collective-permute-start | bytes 12296 | tf_op jit(solution)/shard_map/ppermute | solution.py:22
  41.2 0.0 collective-permute-start.11
  41.2 1.5 %collective-permute-start.19 = (bf16[144,128]{1,0:T(8,128)(2,1)S(1)}, bf16[144,128]{1,0:T(8,128)(2,1)S(1)}, u32[]{:S(2)}, u32[]{:S(2)}) collective-permute-start(bf16[144,128]{1,0:T(8,128)(2,1)S(1)} %get-tuple-element.47.refs_5_), channel_id=1, source_target_pairs={{0,24},{4,28},{8,16},{12,20},{16,8},{20,12},{24,0},{28,4},{1,25},{... | collective-permute-start | bytes 110600 | tf_op jit(solution)/shard_map/ppermute | solution.py:22
  42.6 2.0 %collective-permute-start.18 = (bf16[144,128]{1,0:T(8,128)(2,1)S(1)}, bf16[144,128]{1,0:T(8,128)(2,1)S(1)}, u32[]{:S(2)}, u32[]{:S(2)}) collective-permute-start(bf16[144,128]{1,0:T(8,128)(2,1)S(1)} %get-tuple-element.47.refs_5_), channel_id=1, source_target_pairs={{0,16},{4,20},{8,24},{12,28},{16,0},{20,4},{24,8},{28,12},{1,17},{... | collective-permute-start | bytes 110600 | tf_op jit(solution)/shard_map/ppermute | solution.py:22
  44.6 0.0 collective-permute-done.13
  44.7 0.1 collective-permute-start.17
  44.7 0.0 collective-permute-done.12
  44.7 0.0 collective-permute-done.11
  44.8 0.1 shard_map.115.refs_0_
  44.9 2.5 %collective-permute-start.16 = (bf16[264,128]{1,0:T(8,128)(2,1)S(1)}, bf16[264,128]{1,0:T(8,128)(2,1)S(1)}, u32[]{:S(2)}, u32[]{:S(2)}) collective-permute-start(bf16[264,128]{1,0:T(8,128)(2,1)S(1)} %shard_map.115.refs_0_), channel_id=1, source_target_pairs={{0,3},{1,2},{2,1},{3,0},{4,7},{5,6},{6,5},{7,4},{8,11},{9,10},{10,... | collective-permute-start | bytes 202760 | tf_op jit(solution)/shard_map/ppermute | solution.py:22
  47.4 0.0 collective-permute-start.15
  47.4 0.0 collective-permute-done.19.refs_8_
  47.4 1.9 %collective-permute-start.14 = (bf16[264,128]{1,0:T(8,128)(2,1)S(1)}, bf16[264,128]{1,0:T(8,128)(2,1)S(1)}, u32[]{:S(2)}, u32[]{:S(2)}) collective-permute-start(bf16[264,128]{1,0:T(8,128)(2,1)S(1)} %shard_map.115.refs_0_), channel_id=1, source_target_pairs={{0,1},{1,0},{2,3},{3,2},{4,5},{5,4},{6,7},{7,6},{8,9},{9,8},{10,11... | collective-permute-start | bytes 202760 | tf_op jit(solution)/shard_map/ppermute | solution.py:22
  49.4 0.0 collective-permute-done.18.refs_7_
  49.4 0.0 collective-permute-done.17.refs_6_
  49.4 2.2 %collective-permute-done.16.refs_3_ = bf16[264,128]{1,0:T(8,128)(2,1)S(1)} collective-permute-done((bf16[264,128]{1,0:T(8,128)(2,1)S(1)}, bf16[264,128]{1,0:T(8,128)(2,1)S(1)}, u32[]{:S(2)}, u32[]{:S(2)}) %collective-permute-start.16) | collective-permute-done | bytes 67616 | tf_op jit(solution)/shard_map/ppermute | solution.py:22
  51.5 1.6 %collective-permute-done.15.refs_2_ = bf16[264,128]{1,0:T(8,128)(2,1)S(1)} collective-permute-done((bf16[264,128]{1,0:T(8,128)(2,1)S(1)}, bf16[264,128]{1,0:T(8,128)(2,1)S(1)}, u32[]{:S(2)}, u32[]{:S(2)}) %collective-permute-start.15) | collective-permute-done | bytes 67616 | tf_op jit(solution)/shard_map/ppermute | solution.py:22
  53.2 0.0 collective-permute-done.14.refs_1_
  53.2 1.5 %shard_map.116 = (f32[192,256]{1,0:T(8,128)S(1)}, bf16[192,256]{1,0:T(8,128)(2,1)S(1)}, bf16[192,256]{1,0:T(8,128)(2,1)S(1)}, bf16[192,256]{1,0:T(8,128)(2,1)S(1...) custom-call(bf16[264,128]{1,0:T(8,128)(2,1)S(1)} %shard_map.115.refs_0_, ...), custom_call_target="tpu_custom_call" | custom-call | tf_op jit(solution)/shard_map/pallas_call | solution.py:91
  54.6 0.0 collective-permute-start.23
  54.6 1.9 %collective-permute-start.20 = (bf16[192,256]{1,0:T(8,128)(2,1)S(1)}, bf16[192,256]{1,0:T(8,128)(2,1)S(1)}, u32[]{:S(2)}, u32[]{:S(2)}) collective-permute-start(bf16[192,256]{1,0:T(8,128)(2,1)S(1)} %get-tuple-element.53), channel_id=1, source_target_pairs={{0,3},{1,2},{2,1},{3,0},{4,7},{5,6},{6,5},{7,4},{8,11},{9,10},{10,... | collective-permute-start | bytes 294920 | tf_op jit(solution)/shard_map/ppermute | solution.py:22
  56.5 0.0 collective-permute-done.23.got
  56.6 0.2 shard_map.117
  56.8 1.4 %collective-permute-start.24 = (bf16[528,128]{1,0:T(8,128)(2,1)S(1)}, bf16[528,128]{1,0:T(8,128)(2,1)S(1)}, u32[]{:S(2)}, u32[]{:S(2)}) collective-permute-start(bf16[528,128]{1,0:T(8,128)(2,1)S(1)} %get-tuple-element.59), channel_id=1, source_target_pairs={{0,24},{4,28},{8,16},{12,20},{16,8},{20,12},{24,0},{28,4},{1,25},{... | collective-permute-start | bytes 405512 | tf_op jit(solution)/shard_map/ppermute | solution.py:22
  58.2 2.1 %collective-permute-start.25 = (bf16[528,128]{1,0:T(8,128)(2,1)S(1)}, bf16[528,128]{1,0:T(8,128)(2,1)S(1)}, u32[]{:S(2)}, u32[]{:S(2)}) collective-permute-start(bf16[528,128]{1,0:T(8,128)(2,1)S(1)} %get-tuple-element.60), channel_id=1, source_target_pairs={{0,16},{4,20},{8,24},{12,28},{16,0},{20,4},{24,8},{28,12},{1,17},{... | collective-permute-start | bytes 405512 | tf_op jit(solution)/shard_map/ppermute | solution.py:22
  60.3 0.0 collective-permute-start.26
  60.3 1.5 %collective-permute-start.21 = (bf16[192,256]{1,0:T(8,128)(2,1)S(1)}, bf16[192,256]{1,0:T(8,128)(2,1)S(1)}, u32[]{:S(2)}, u32[]{:S(2)}) collective-permute-start(bf16[192,256]{1,0:T(8,128)(2,1)S(1)} %get-tuple-element.54), channel_id=1, source_target_pairs={{0,2},{1,3},{2,0},{3,1},{4,6},{5,7},{6,4},{7,5},{8,10},{9,11},{10,... | collective-permute-start | bytes 294920 | tf_op jit(solution)/shard_map/ppermute | solution.py:22
  61.8 0.0 collective-permute-done.20.refs_1_
  61.8 1.0 %collective-permute-start.22 = (bf16[192,256]{1,0:T(8,128)(2,1)S(1)}, bf16[192,256]{1,0:T(8,128)(2,1)S(1)}, u32[]{:S(2)}, u32[]{:S(2)}) collective-permute-start(bf16[192,256]{1,0:T(8,128)(2,1)S(1)} %get-tuple-element.55), channel_id=1, source_target_pairs={{0,1},{1,0},{2,3},{3,2},{4,5},{5,4},{6,7},{7,6},{8,9},{9,8},{10,11... | collective-permute-start | bytes 294920 | tf_op jit(solution)/shard_map/ppermute | solution.py:22
  62.9 4.6 %collective-permute-done.21.refs_2_ = bf16[192,256]{1,0:T(8,128)(2,1)S(1)} collective-permute-done((bf16[192,256]{1,0:T(8,128)(2,1)S(1)}, bf16[192,256]{1,0:T(8,128)(2,1)S(1)}, u32[]{:S(2)}, u32[]{:S(2)}) %collective-permute-start.21) | collective-permute-done | bytes 98336 | tf_op jit(solution)/shard_map/ppermute | solution.py:22
  67.4 0.6 collective-permute-done.22.refs_3_
  68.0 0.0 collective-permute-done.24.refs_5_
  68.0 0.0 collective-permute-done.25.refs_6_
  68.0 0.0 collective-permute-done.26.refs_7_
  68.0 1.1 %shard_map.118 = (bf16[192,256]{1,0:T(8,128)(2,1)}, bf16[192,128]{1,0:T(8,128)(2,1)}, f32[96,128]{1,0:T(8,128)}, f32[3,96,192]{2,1,0:T(8,128)}) custom-call(f32[192,256]{1,0:T(8,128)S(1)} %get-tuple-element.52.refs_0_, bf16[192,256]{1,0:T(8,128)(2,1)S(1)} %collective-permute-done.20.refs_1_, bf16[192,256]{1,0:T(8,128)(2,1)S(1)} %collective-permute-done.21.refs_2_, ...), custom_call_target="tpu_custom_call" | custom-call | tf_op jit(solution)/shard_map/pallas_call | solution.py:91
  (12 shorter events, 0.0 us)
Async XLA Ops:
  0.6 22.6 %copy-start.2 = (f32[192]{0:T(256)S(1)}, f32[192]{0:T(256)}, u32[]{:S(2)}) copy-start(f32[192]{0:T(256)} %param.11) | copy-start | bytes 2308
  2.0 33.5 %copy-start = (s32[256,128]{1,0:T(8,128)S(1)}, s32[256,128]{1,0:T(8,128)}, u32[]{:S(2)}) copy-start(s32[256,128]{1,0:T(8,128)} %counts.1) | copy-start | bytes 393220
  2.1 33.5 %copy-start.1 = (bf16[768,128]{1,0:T(8,128)(2,1)S(1)}, bf16[768,128]{1,0:T(8,128)(2,1)}, u32[]{:S(2)}) copy-start(bf16[768,128]{1,0:T(8,128)(2,1)} %refs_4_.1) | copy-start | bytes 589828
  2.1 33.5 %copy-start.3 = (f32[128]{0:T(128)S(1)}, f32[128]{0:T(128)}, u32[]{:S(2)}) copy-start(f32[128]{0:T(128)} %param.13) | copy-start | bytes 1540
  2.1 5.2 %collective-permute-start = (bf16[8,256]{1,0:T(8,128)(2,1)S(1)}, bf16[8,256]{1,0:T(8,128)(2,1)S(1)}, u32[]{:S(2)}, u32[]{:S(2)}) collective-permute-start(bf16[8,256]{1,0:T(8,128)(2,1)S(1)} %get-tuple-element.36), channel_id=1, source_target_pairs={{4,8},{12,16},{20,24},{8,4},{16,12},{24,20},{5,9},{13,17},{21,25},... | collective-permute-start | bytes 12296 | tf_op jit(solution)/shard_map/ppermute | solution.py:28
  2.9 5.2 %collective-permute-start.1 = (bf16[8,256]{1,0:T(8,128)(2,1)S(1)}, bf16[8,256]{1,0:T(8,128)(2,1)S(1)}, u32[]{:S(2)}, u32[]{:S(2)}) collective-permute-start(bf16[8,256]{1,0:T(8,128)(2,1)S(1)} %get-tuple-element.37), channel_id=1, source_target_pairs={{0,4},{4,0},{8,12},{12,8},{16,20},{20,16},{24,28},{28,24},{1,5},{5... | collective-permute-start | bytes 12296 | tf_op jit(solution)/shard_map/ppermute | solution.py:22
  8.1 33.1 %copy-start.4 = (s32[1,128]{1,0:T(1,128)S(1)}, s32[1,128]{1,0:T(1,128)}, u32[]{:S(2)}) copy-start(s32[1,128]{1,0:T(1,128)} %param.15) | copy-start | bytes 1540
  8.1 15.1 %collective-permute-start.2 = (bf16[224,256]{1,0:T(8,128)(2,1)S(1)}, bf16[224,256]{1,0:T(8,128)(2,1)S(1)}, u32[]{:S(2)}, u32[]{:S(2)}) collective-permute-start(bf16[224,256]{1,0:T(8,128)(2,1)S(1)} %get-tuple-element.40), channel_id=1, source_target_pairs={{0,1},{1,0},{2,3},{3,2},{4,5},{5,4},{6,7},{7,6},{8,9},{9,8},{10,11... | collective-permute-start | bytes 344072 | tf_op jit(solution)/shard_map/ppermute | solution.py:22
  9.7 13.6 %collective-permute-start.3 = (bf16[216,256]{1,0:T(8,128)(2,1)S(1)}, bf16[216,256]{1,0:T(8,128)(2,1)S(1)}, u32[]{:S(2)}, u32[]{:S(2)}) collective-permute-start(bf16[216,256]{1,0:T(8,128)(2,1)S(1)} %get-tuple-element.41), channel_id=1, source_target_pairs={{0,2},{1,3},{2,0},{3,1},{4,6},{5,7},{6,4},{7,5},{8,10},{9,11},{10,... | collective-permute-start | bytes 331784 | tf_op jit(solution)/shard_map/ppermute | solution.py:22
  12.3 11.0 %collective-permute-start.4 = (bf16[216,256]{1,0:T(8,128)(2,1)S(1)}, bf16[216,256]{1,0:T(8,128)(2,1)S(1)}, u32[]{:S(2)}, u32[]{:S(2)}) collective-permute-start(bf16[216,256]{1,0:T(8,128)(2,1)S(1)} %get-tuple-element.35.refs_0_), channel_id=1, source_target_pairs={{0,3},{1,2},{2,1},{3,0},{4,7},{5,6},{6,5},{7,4},{8,11},{9,10},{10,... | collective-permute-start | bytes 331784 | tf_op jit(solution)/shard_map/ppermute | solution.py:22
  12.5 8.1 %collective-permute-start.6 = (bf16[8,256]{1,0:T(8,128)(2,1)S(1)}, bf16[8,256]{1,0:T(8,128)(2,1)S(1)}, u32[]{:S(2)}, u32[]{:S(2)}) collective-permute-start(bf16[8,256]{1,0:T(8,128)(2,1)S(1)} %get-tuple-element.42.refs_4_.edges), channel_id=1, source_target_pairs={{0,3},{1,2},{2,1},{3,0},{4,7},{5,6},{6,5},{7,4},{8,11},{9,10},{10,... | collective-permute-start | bytes 12296 | tf_op jit(solution)/shard_map/ppermute | solution.py:22
  16.1 7.1 %collective-permute-start.5 = (bf16[8,256]{1,0:T(8,128)(2,1)S(1)}, bf16[8,256]{1,0:T(8,128)(2,1)S(1)}, u32[]{:S(2)}, u32[]{:S(2)}) collective-permute-start(bf16[8,256]{1,0:T(8,128)(2,1)S(1)} %get-tuple-element.42.refs_4_.edges), channel_id=1, source_target_pairs={{0,2},{1,3},{2,0},{3,1},{4,6},{5,7},{6,4},{7,5},{8,10},{9,11},{10,... | collective-permute-start | bytes 12296 | tf_op jit(solution)/shard_map/ppermute | solution.py:22
  24.4 7.6 %collective-permute-start.9 = (bf16[200,256]{1,0:T(8,128)(2,1)S(1)}, bf16[200,256]{1,0:T(8,128)(2,1)S(1)}, u32[]{:S(2)}, u32[]{:S(2)}) collective-permute-start(bf16[200,256]{1,0:T(8,128)(2,1)S(1)} %get-tuple-element.44.refs_0_), channel_id=1, source_target_pairs={{0,3},{1,2},{2,1},{3,0},{4,7},{5,6},{6,5},{7,4},{8,11},{9,10},{10,... | collective-permute-start | bytes 307208 | tf_op jit(solution)/shard_map/ppermute | solution.py:22
  26.9 8.6 %collective-permute-start.8 = (bf16[200,256]{1,0:T(8,128)(2,1)S(1)}, bf16[200,256]{1,0:T(8,128)(2,1)S(1)}, u32[]{:S(2)}, u32[]{:S(2)}) collective-permute-start(bf16[200,256]{1,0:T(8,128)(2,1)S(1)} %get-tuple-element.44.refs_0_), channel_id=1, source_target_pairs={{0,2},{1,3},{2,0},{3,1},{4,6},{5,7},{6,4},{7,5},{8,10},{9,11},{10,... | collective-permute-start | bytes 307208 | tf_op jit(solution)/shard_map/ppermute | solution.py:22
  26.9 8.6 %collective-permute-start.7 = (bf16[200,256]{1,0:T(8,128)(2,1)S(1)}, bf16[200,256]{1,0:T(8,128)(2,1)S(1)}, u32[]{:S(2)}, u32[]{:S(2)}) collective-permute-start(bf16[200,256]{1,0:T(8,128)(2,1)S(1)} %get-tuple-element.44.refs_0_), channel_id=1, source_target_pairs={{0,1},{1,0},{2,3},{3,2},{4,5},{5,4},{6,7},{7,6},{8,9},{9,8},{10,11... | collective-permute-start | bytes 307208 | tf_op jit(solution)/shard_map/ppermute | solution.py:22
  36.0 1.2 %collective-permute-start.10 = (f32[8,128]{1,0:T(8,128)S(1)}, f32[8,128]{1,0:T(8,128)S(1)}, u32[]{:S(2)}, u32[]{:S(2)}) collective-permute-start(f32[8,128]{1,0:T(8,128)S(1)} %get-tuple-element.46), channel_id=1, source_target_pairs={{0,4},{4,0},{8,12},{12,8},{16,20},{20,16},{24,28},{28,24},{1,5},{5... | collective-permute-start | bytes 12296 | tf_op jit(solution)/shard_map/ppermute | solution.py:22
  37.2 7.4 %collective-permute-start.13 = (f32[8,128]{1,0:T(8,128)S(1)}, f32[8,128]{1,0:T(8,128)S(1)}, u32[]{:S(2)}, u32[]{:S(2)}) collective-permute-start(f32[8,128]{1,0:T(8,128)S(1)} %add.18), channel_id=1, source_target_pairs={{0,24},{4,28},{8,16},{12,20},{16,8},{20,12},{24,0},{28,4},{1,25},{... | collective-permute-start | bytes 12296 | tf_op jit(solution)/shard_map/ppermute | solution.py:22
  37.4 7.3 %collective-permute-start.12 = (f32[8,128]{1,0:T(8,128)S(1)}, f32[8,128]{1,0:T(8,128)S(1)}, u32[]{:S(2)}, u32[]{:S(2)}) collective-permute-start(f32[8,128]{1,0:T(8,128)S(1)} %add.18), channel_id=1, source_target_pairs={{0,16},{4,20},{8,24},{12,28},{16,0},{20,4},{24,8},{28,12},{1,17},{... | collective-permute-start | bytes 12296 | tf_op jit(solution)/shard_map/ppermute | solution.py:22
  41.2 3.6 %collective-permute-start.11 = (f32[8,128]{1,0:T(8,128)S(1)}, f32[8,128]{1,0:T(8,128)S(1)}, u32[]{:S(2)}, u32[]{:S(2)}) collective-permute-start(f32[8,128]{1,0:T(8,128)S(1)} %add.18), channel_id=1, source_target_pairs={{0,8},{4,12},{8,0},{12,4},{16,24},{20,28},{24,16},{28,20},{1,9},{5... | collective-permute-start | bytes 12296 | tf_op jit(solution)/shard_map/ppermute | solution.py:22
  41.2 6.3 %collective-permute-start.19 = (bf16[144,128]{1,0:T(8,128)(2,1)S(1)}, bf16[144,128]{1,0:T(8,128)(2,1)S(1)}, u32[]{:S(2)}, u32[]{:S(2)}) collective-permute-start(bf16[144,128]{1,0:T(8,128)(2,1)S(1)} %get-tuple-element.47.refs_5_), channel_id=1, source_target_pairs={{0,24},{4,28},{8,16},{12,20},{16,8},{20,12},{24,0},{28,4},{1,25},{... | collective-permute-start | bytes 110600 | tf_op jit(solution)/shard_map/ppermute | solution.py:22
  42.6 6.7 %collective-permute-start.18 = (bf16[144,128]{1,0:T(8,128)(2,1)S(1)}, bf16[144,128]{1,0:T(8,128)(2,1)S(1)}, u32[]{:S(2)}, u32[]{:S(2)}) collective-permute-start(bf16[144,128]{1,0:T(8,128)(2,1)S(1)} %get-tuple-element.47.refs_5_), channel_id=1, source_target_pairs={{0,16},{4,20},{8,24},{12,28},{16,0},{20,4},{24,8},{28,12},{1,17},{... | collective-permute-start | bytes 110600 | tf_op jit(solution)/shard_map/ppermute | solution.py:22
  44.7 4.7 %collective-permute-start.17 = (bf16[144,128]{1,0:T(8,128)(2,1)S(1)}, bf16[144,128]{1,0:T(8,128)(2,1)S(1)}, u32[]{:S(2)}, u32[]{:S(2)}) collective-permute-start(bf16[144,128]{1,0:T(8,128)(2,1)S(1)} %get-tuple-element.47.refs_5_), channel_id=1, source_target_pairs={{0,8},{4,12},{8,0},{12,4},{16,24},{20,28},{24,16},{28,20},{1,9},{5... | collective-permute-start | bytes 110600 | tf_op jit(solution)/shard_map/ppermute | solution.py:22
  44.9 6.6 %collective-permute-start.16 = (bf16[264,128]{1,0:T(8,128)(2,1)S(1)}, bf16[264,128]{1,0:T(8,128)(2,1)S(1)}, u32[]{:S(2)}, u32[]{:S(2)}) collective-permute-start(bf16[264,128]{1,0:T(8,128)(2,1)S(1)} %shard_map.115.refs_0_), channel_id=1, source_target_pairs={{0,3},{1,2},{2,1},{3,0},{4,7},{5,6},{6,5},{7,4},{8,11},{9,10},{10,... | collective-permute-start | bytes 202760 | tf_op jit(solution)/shard_map/ppermute | solution.py:22
  47.4 5.7 %collective-permute-start.15 = (bf16[264,128]{1,0:T(8,128)(2,1)S(1)}, bf16[264,128]{1,0:T(8,128)(2,1)S(1)}, u32[]{:S(2)}, u32[]{:S(2)}) collective-permute-start(bf16[264,128]{1,0:T(8,128)(2,1)S(1)} %shard_map.115.refs_0_), channel_id=1, source_target_pairs={{0,2},{1,3},{2,0},{3,1},{4,6},{5,7},{6,4},{7,5},{8,10},{9,11},{10,... | collective-permute-start | bytes 202760 | tf_op jit(solution)/shard_map/ppermute | solution.py:22
  47.4 5.7 %collective-permute-start.14 = (bf16[264,128]{1,0:T(8,128)(2,1)S(1)}, bf16[264,128]{1,0:T(8,128)(2,1)S(1)}, u32[]{:S(2)}, u32[]{:S(2)}) collective-permute-start(bf16[264,128]{1,0:T(8,128)(2,1)S(1)} %shard_map.115.refs_0_), channel_id=1, source_target_pairs={{0,1},{1,0},{2,3},{3,2},{4,5},{5,4},{6,7},{7,6},{8,9},{9,8},{10,11... | collective-permute-start | bytes 202760 | tf_op jit(solution)/shard_map/ppermute | solution.py:22
  54.6 1.9 %collective-permute-start.23 = (bf16[2112,128]{1,0:T(8,128)(2,1)S(1)}, bf16[2112,128]{1,0:T(8,128)(2,1)S(1)}, u32[]{:S(2)}, u32[]{:S(2)}) collective-permute-start(bf16[2112,128]{1,0:T(8,128)(2,1)S(1)} %get-tuple-element.57), channel_id=1, source_target_pairs={{0,4},{4,0},{8,12},{12,8},{16,20},{20,16},{24,28},{28,24},{1,5},{5... | collective-permute-start | bytes 1622024 | tf_op jit(solution)/shard_map/ppermute | solution.py:22
  54.6 7.2 %collective-permute-start.20 = (bf16[192,256]{1,0:T(8,128)(2,1)S(1)}, bf16[192,256]{1,0:T(8,128)(2,1)S(1)}, u32[]{:S(2)}, u32[]{:S(2)}) collective-permute-start(bf16[192,256]{1,0:T(8,128)(2,1)S(1)} %get-tuple-element.53), channel_id=1, source_target_pairs={{0,3},{1,2},{2,1},{3,0},{4,7},{5,6},{6,5},{7,4},{8,11},{9,10},{10,... | collective-permute-start | bytes 294920 | tf_op jit(solution)/shard_map/ppermute | solution.py:22
  56.8 11.2 %collective-permute-start.24 = (bf16[528,128]{1,0:T(8,128)(2,1)S(1)}, bf16[528,128]{1,0:T(8,128)(2,1)S(1)}, u32[]{:S(2)}, u32[]{:S(2)}) collective-permute-start(bf16[528,128]{1,0:T(8,128)(2,1)S(1)} %get-tuple-element.59), channel_id=1, source_target_pairs={{0,24},{4,28},{8,16},{12,20},{16,8},{20,12},{24,0},{28,4},{1,25},{... | collective-permute-start | bytes 405512 | tf_op jit(solution)/shard_map/ppermute | solution.py:22
  58.2 9.8 %collective-permute-start.25 = (bf16[528,128]{1,0:T(8,128)(2,1)S(1)}, bf16[528,128]{1,0:T(8,128)(2,1)S(1)}, u32[]{:S(2)}, u32[]{:S(2)}) collective-permute-start(bf16[528,128]{1,0:T(8,128)(2,1)S(1)} %get-tuple-element.60), channel_id=1, source_target_pairs={{0,16},{4,20},{8,24},{12,28},{16,0},{20,4},{24,8},{28,12},{1,17},{... | collective-permute-start | bytes 405512 | tf_op jit(solution)/shard_map/ppermute | solution.py:22
  60.3 7.7 %collective-permute-start.26 = (bf16[528,128]{1,0:T(8,128)(2,1)S(1)}, bf16[528,128]{1,0:T(8,128)(2,1)S(1)}, u32[]{:S(2)}, u32[]{:S(2)}) collective-permute-start(bf16[528,128]{1,0:T(8,128)(2,1)S(1)} %get-tuple-element.61), channel_id=1, source_target_pairs={{0,8},{4,12},{8,0},{12,4},{16,24},{20,28},{24,16},{28,20},{1,9},{5... | collective-permute-start | bytes 405512 | tf_op jit(solution)/shard_map/ppermute | solution.py:22
  60.3 7.1 %collective-permute-start.21 = (bf16[192,256]{1,0:T(8,128)(2,1)S(1)}, bf16[192,256]{1,0:T(8,128)(2,1)S(1)}, u32[]{:S(2)}, u32[]{:S(2)}) collective-permute-start(bf16[192,256]{1,0:T(8,128)(2,1)S(1)} %get-tuple-element.54), channel_id=1, source_target_pairs={{0,2},{1,3},{2,0},{3,1},{4,6},{5,7},{6,4},{7,5},{8,10},{9,11},{10,... | collective-permute-start | bytes 294920 | tf_op jit(solution)/shard_map/ppermute | solution.py:22
  61.8 6.2 %collective-permute-start.22 = (bf16[192,256]{1,0:T(8,128)(2,1)S(1)}, bf16[192,256]{1,0:T(8,128)(2,1)S(1)}, u32[]{:S(2)}, u32[]{:S(2)}) collective-permute-start(bf16[192,256]{1,0:T(8,128)(2,1)S(1)} %get-tuple-element.55), channel_id=1, source_target_pairs={{0,1},{1,0},{2,3},{3,2},{4,5},{5,4},{6,7},{7,6},{8,9},{9,8},{10,11... | collective-permute-start | bytes 294920 | tf_op jit(solution)/shard_map/ppermute | solution.py:22

commit v6 on v5

--- a/solution.py
+++ b/solution.py
@@ -306,21 +306,26 @@
     return chunk * both // 128
 
 
-def backward(mp_count, seq_count, split, group, *refs):
-    slopes, head_own, bundles = refs[:mp_count], refs[mp_count], refs[mp_count + 1 : mp_count + 1 + group]
-    gelu, gelu_beside, full, hidden, weight, *outs = refs[mp_count + 1 + group :]
-    head_rows, slope_rows = outs[-3], outs[-4]
+def ranked(group, after, head_own, *refs):
+    *bundles, out = refs
+    width, tracks = head_own.shape
+    part = width // group
+    out[:, :tracks] = head_own[...]
+    for r, bundle in enumerate(bundles):
+        at = pl.multiple_of((((lax.axis_index("seq") >> 1) & (group - 1)) ^ r) * part, 16)
+        for j in range(out.shape[1] // tracks - 1):
+            out[pl.ds(at, part), (j + 1) * tracks : (j + 2) * tracks] = bundle[j * part : (j + 1) * part, :]
+
+
+def backward(mp_count, seq_count, split, *refs):
+    slopes, head_rows = refs[:mp_count], refs[mp_count]
+    gelu, gelu_beside, full, hidden, weight, *outs = refs[mp_count + 1 :]
+    slope_rows = outs[-3]
     own, *outs = outs
     carry, outs = outs[: mp_count - 1], outs[mp_count - 1 :]
-    width, length = head_own.shape[0], full.shape[1]
-    tracks = head_own.shape[1]
+    width, length = head_rows.shape[0], full.shape[1]
+    tracks = head_rows.shape[1] // mp_count
     place, column = lax.axis_index("seq"), lax.axis_index("mp")
-    part = width // group
-    for r, bundle in enumerate(bundles):
-        at = pl.multiple_of((((place >> 1) & (group - 1)) ^ r) * part, 16)
-        for j in range(mp_count - 1):
-            head_rows[pl.ds(at, part), (j + 1) * tracks : (j + 2) * tracks] = bundle[j * part : (j + 1) * part, :]
-    head_rows[:, :tracks] = head_own[...]
     for j, slope in enumerate(slopes):
         slope_rows[:, j * tracks : (j + 1) * tracks] = slope[...]
     inner = dot(head_rows[...], slope_rows[:length, :], nt)
@@ -474,17 +479,20 @@
         differentiate, [((length + edge_rows, tracks), bf16)], logits, counts, edges, totals, mask_row
     )
     slopes = gathered(slope, "mp")
+    (head_rows,) = call(
+        functools.partial(ranked, group), [((width, mp_count * tracks), bf16)], slope, head_own, *bundles
+    )
     quarter = (packed_rows(chunk, both), 128)
     half = (seq_count // 2 * quarter[0], 128)
     grads_at = ((channels, both), f32)
     scratch = [((channels, length), f32), ((taps * width, length), bf16)]
-    head_at = [((length + edge_rows, mp_count * tracks), bf16), ((width, mp_count * tracks), bf16)]
+    head_at = [((length + edge_rows, mp_count * tracks), bf16)]
     own, *outs = call(
-        functools.partial(backward, mp_count, seq_count, split, group),
+        functools.partial(backward, mp_count, seq_count, split),
         [((width, length), f32)]
         + [((width, length), bf16)] * (mp_count - 1)
         + ([(half, f32), (half, bf16)] if split else [grads_at]),
-        *slopes, head_own, *bundles, gelu, gelu_beside, full_in, full, weight,
+        *slopes, head_rows, gelu, gelu_beside, full_in, full, weight,
         scratch=head_at + scratch,
     )
     carry, grads = outs[: mp_count - 1], outs[mp_count - 1 :]

time: 69.3 us -> 69.2 us (level)
    pallas_call x8 -> x9, Pallas kernels: 5.79 us -> 5.78 us  [call(): pl.pallas_call(body, out_shape=[jax.ShapeDtypeStruct(shape, kind) if last...]
where the time goes in v6:
time: 69.2 us; the launch traced here: 69 us
  starting transfers between devices  37.6 us (54%)
  waiting for transfers between devices  24.8 us (36%)
  Pallas kernels  5.78 us (8%)
  between operations  0.77 us (1%)
    ppermute x26, starting transfers between devices, swap(): return lax.ppermute(block, axis, [(i, i ^ mask) for i in range(count)])  36.8 us
    ppermute x26, waiting for transfers between devices, swap(): return lax.ppermute(block, axis, [(i, i ^ mask) for i in range(count)])  24.8 us
    pallas_call x9, Pallas kernels, call(): pl.pallas_call(body, out_shape=[jax.ShapeDtypeStruct(shape, kind) if last...  5.78 us
  transfers between devices with their start and end apart: 27, of which 10 were waited for; matrix products, arithmetic and copies ran while one was open for 0% of the time, Pallas kernels for 1%

profile of v6, /device:TPU:0, one launch (start us, length us, event | category | flops | bytes accessed | tf_op | source)
XLA Modules:
  0.0 69.0 jit_solution(2441737123173452193)
XLA Ops:
  0.6 1.4 %shard_map.111 = (bf16[224,256]{1,0:T(8,128)(2,1)S(1)}, bf16[216,256]{1,0:T(8,128)(2,1)S(1)}, bf16[216,256]{1,0:T(8,128)(2,1)S(1)}, bf16[8,256]{1,0:T(8,128)(2,1...) custom-call(bf16[192,128]{1,0:T(8,128)(2,1)} %coarse_in.1, ...), custom_call_target="tpu_custom_call" | custom-call | tf_op jit(solution)/shard_map/pallas_call | solution.py:91
  2.0 0.0 copy-start
  2.1 0.0 copy-start.1
  2.1 0.0 copy-start.3
  2.1 0.8 %collective-permute-start = (bf16[8,256]{1,0:T(8,128)(2,1)S(1)}, bf16[8,256]{1,0:T(8,128)(2,1)S(1)}, u32[]{:S(2)}, u32[]{:S(2)}) collective-permute-start(bf16[8,256]{1,0:T(8,128)(2,1)S(1)} %get-tuple-element.36), channel_id=1, source_target_pairs={{4,8},{12,16},{20,24},{8,4},{16,12},{24,20},{5,9},{13,17},{21,25},... | collective-permute-start | bytes 12296 | tf_op jit(solution)/shard_map/ppermute | solution.py:28
  2.9 4.4 %collective-permute-start.1 = (bf16[8,256]{1,0:T(8,128)(2,1)S(1)}, bf16[8,256]{1,0:T(8,128)(2,1)S(1)}, u32[]{:S(2)}, u32[]{:S(2)}) collective-permute-start(bf16[8,256]{1,0:T(8,128)(2,1)S(1)} %get-tuple-element.37), channel_id=1, source_target_pairs={{0,4},{4,0},{8,12},{12,8},{16,20},{20,16},{24,28},{28,24},{1,5},{5... | collective-permute-start | bytes 12296 | tf_op jit(solution)/shard_map/ppermute | solution.py:22
  7.3 0.0 collective-permute-done.cross
  7.3 0.8 %collective-permute-done.1.pair = bf16[8,256]{1,0:T(8,128)(2,1)S(1)} collective-permute-done((bf16[8,256]{1,0:T(8,128)(2,1)S(1)}, bf16[8,256]{1,0:T(8,128)(2,1)S(1)}, u32[]{:S(2)}, u32[]{:S(2)}) %collective-permute-start.1) | collective-permute-done | bytes 4128 | tf_op jit(solution)/shard_map/ppermute | solution.py:22
  8.1 1.6 %collective-permute-start.2 = (bf16[224,256]{1,0:T(8,128)(2,1)S(1)}, bf16[224,256]{1,0:T(8,128)(2,1)S(1)}, u32[]{:S(2)}, u32[]{:S(2)}) collective-permute-start(bf16[224,256]{1,0:T(8,128)(2,1)S(1)} %get-tuple-element.40), channel_id=1, source_target_pairs={{0,1},{1,0},{2,3},{3,2},{4,5},{5,4},{6,7},{7,6},{8,9},{9,8},{10,11... | collective-permute-start | bytes 344072 | tf_op jit(solution)/shard_map/ppermute | solution.py:22
  9.7 2.6 %collective-permute-start.3 = (bf16[216,256]{1,0:T(8,128)(2,1)S(1)}, bf16[216,256]{1,0:T(8,128)(2,1)S(1)}, u32[]{:S(2)}, u32[]{:S(2)}) collective-permute-start(bf16[216,256]{1,0:T(8,128)(2,1)S(1)} %get-tuple-element.41), channel_id=1, source_target_pairs={{0,2},{1,3},{2,0},{3,1},{4,6},{5,7},{6,4},{7,5},{8,10},{9,11},{10,... | collective-permute-start | bytes 331784 | tf_op jit(solution)/shard_map/ppermute | solution.py:22
  12.3 0.2 collective-permute-start.4
  12.5 3.6 %collective-permute-start.6 = (bf16[8,256]{1,0:T(8,128)(2,1)S(1)}, bf16[8,256]{1,0:T(8,128)(2,1)S(1)}, u32[]{:S(2)}, u32[]{:S(2)}) collective-permute-start(bf16[8,256]{1,0:T(8,128)(2,1)S(1)} %get-tuple-element.42.refs_4_.edges), channel_id=1, source_target_pairs={{0,3},{1,2},{2,1},{3,0},{4,7},{5,6},{6,5},{7,4},{8,11},{9,10},{10,... | collective-permute-start | bytes 12296 | tf_op jit(solution)/shard_map/ppermute | solution.py:22
  16.1 0.0 collective-permute-start.5
  16.1 4.5 %collective-permute-done.6.refs_6_ = bf16[8,256]{1,0:T(8,128)(2,1)S(1)} collective-permute-done((bf16[8,256]{1,0:T(8,128)(2,1)S(1)}, bf16[8,256]{1,0:T(8,128)(2,1)S(1)}, u32[]{:S(2)}, u32[]{:S(2)}) %collective-permute-start.6) | collective-permute-done | bytes 4128 | tf_op jit(solution)/shard_map/ppermute | solution.py:22
  20.6 2.6 %collective-permute-done.5.refs_5_ = bf16[8,256]{1,0:T(8,128)(2,1)S(1)} collective-permute-done((bf16[8,256]{1,0:T(8,128)(2,1)S(1)}, bf16[8,256]{1,0:T(8,128)(2,1)S(1)}, u32[]{:S(2)}, u32[]{:S(2)}) %collective-permute-start.5) | collective-permute-done | bytes 4128 | tf_op jit(solution)/shard_map/ppermute | solution.py:22
  23.2 0.0 collective-permute-done.3.refs_2_
  23.2 0.0 collective-permute-done.4.refs_3_
  23.2 0.0 collective-permute-done.2.refs_1_
  23.3 1.1 %shard_map.113 = (bf16[200,256]{1,0:T(8,128)(2,1)S(1)}, f32[192,256]{1,0:T(8,128)S(1)}, f32[8,192]{1,0:T(8,128)S(1)}, bf16[768,256]{1,0:T(8,128)(2,1)S(1)}, bf16[144,128]{1,0:T(8,128)(2,1)S(1)}) custom-call(bf16[216,256]{1,0:T(8,128)(2,1)S(1)} %get-tuple-element.35.refs_0_, bf16[224,256]{1,0:T(8,128)(2,1)S(1)} %collective-permute-done.2.refs_1_, ...), custom_call_target="tpu_custom_call" | custom-call | tf_op jit(solution)/shard_map/pallas_call | solution.py:91
  24.4 2.5 %collective-permute-start.9 = (bf16[200,256]{1,0:T(8,128)(2,1)S(1)}, bf16[200,256]{1,0:T(8,128)(2,1)S(1)}, u32[]{:S(2)}, u32[]{:S(2)}) collective-permute-start(bf16[200,256]{1,0:T(8,128)(2,1)S(1)} %get-tuple-element.44.refs_0_), channel_id=1, source_target_pairs={{0,3},{1,2},{2,1},{3,0},{4,7},{5,6},{6,5},{7,4},{8,11},{9,10},{10,... | collective-permute-start | bytes 307208 | tf_op jit(solution)/shard_map/ppermute | solution.py:22
  26.9 0.0 collective-permute-start.8
  26.9 1.9 %collective-permute-start.7 = (bf16[200,256]{1,0:T(8,128)(2,1)S(1)}, bf16[200,256]{1,0:T(8,128)(2,1)S(1)}, u32[]{:S(2)}, u32[]{:S(2)}) collective-permute-start(bf16[200,256]{1,0:T(8,128)(2,1)S(1)} %get-tuple-element.44.refs_0_), channel_id=1, source_target_pairs={{0,1},{1,0},{2,3},{3,2},{4,5},{5,4},{6,7},{7,6},{8,9},{9,8},{10,11... | collective-permute-start | bytes 307208 | tf_op jit(solution)/shard_map/ppermute | solution.py:22
  28.8 3.2 %collective-permute-done.9.refs_3_ = bf16[200,256]{1,0:T(8,128)(2,1)S(1)} collective-permute-done((bf16[200,256]{1,0:T(8,128)(2,1)S(1)}, bf16[200,256]{1,0:T(8,128)(2,1)S(1)}, u32[]{:S(2)}, u32[]{:S(2)}) %collective-permute-start.9) | collective-permute-done | bytes 102432 | tf_op jit(solution)/shard_map/ppermute | solution.py:22
  32.0 3.5 %collective-permute-done.8.refs_2_ = bf16[200,256]{1,0:T(8,128)(2,1)S(1)} collective-permute-done((bf16[200,256]{1,0:T(8,128)(2,1)S(1)}, bf16[200,256]{1,0:T(8,128)(2,1)S(1)}, u32[]{:S(2)}, u32[]{:S(2)}) %collective-permute-start.8) | collective-permute-done | bytes 102432 | tf_op jit(solution)/shard_map/ppermute | solution.py:22
  35.5 0.0 collective-permute-done.7.refs_1_
  35.6 0.4 shard_map.114
  36.0 0.1 collective-permute-start.10
  36.1 1.2 %collective-permute-done.10 = f32[8,128]{1,0:T(8,128)S(1)} collective-permute-done((f32[8,128]{1,0:T(8,128)S(1)}, f32[8,128]{1,0:T(8,128)S(1)}, u32[]{:S(2)}, u32[]{:S(2)}) %collective-permute-start.10) | collective-permute-done | bytes 4128 | tf_op jit(solution)/shard_map/ppermute | solution.py:22
  37.2 0.2 collective-permute-start.13
  37.4 3.7 %collective-permute-start.12 = (f32[8,128]{1,0:T(8,128)S(1)}, f32[8,128]{1,0:T(8,128)S(1)}, u32[]{:S(2)}, u32[]{:S(2)}) collective-permute-start(f32[8,128]{1,0:T(8,128)S(1)} %add.18), channel_id=1, source_target_pairs={{0,16},{4,20},{8,24},{12,28},{16,0},{20,4},{24,8},{28,12},{1,17},{... | collective-permute-start | bytes 12296 | tf_op jit(solution)/shard_map/ppermute | solution.py:22
  41.2 0.0 collective-permute-start.11
  41.2 1.5 %collective-permute-start.19 = (bf16[144,128]{1,0:T(8,128)(2,1)S(1)}, bf16[144,128]{1,0:T(8,128)(2,1)S(1)}, u32[]{:S(2)}, u32[]{:S(2)}) collective-permute-start(bf16[144,128]{1,0:T(8,128)(2,1)S(1)} %get-tuple-element.47.refs_0_), channel_id=1, source_target_pairs={{0,24},{4,28},{8,16},{12,20},{16,8},{20,12},{24,0},{28,4},{1,25},{... | collective-permute-start | bytes 110600 | tf_op jit(solution)/shard_map/ppermute | solution.py:22
  42.6 2.0 %collective-permute-start.18 = (bf16[144,128]{1,0:T(8,128)(2,1)S(1)}, bf16[144,128]{1,0:T(8,128)(2,1)S(1)}, u32[]{:S(2)}, u32[]{:S(2)}) collective-permute-start(bf16[144,128]{1,0:T(8,128)(2,1)S(1)} %get-tuple-element.47.refs_0_), channel_id=1, source_target_pairs={{0,16},{4,20},{8,24},{12,28},{16,0},{20,4},{24,8},{28,12},{1,17},{... | collective-permute-start | bytes 110600 | tf_op jit(solution)/shard_map/ppermute | solution.py:22
  44.6 0.0 collective-permute-done.13
  44.7 0.1 collective-permute-start.17
  44.7 0.0 collective-permute-done.12
  44.7 0.0 collective-permute-done.11
  44.8 0.1 shard_map.115.after.refs_0_
  44.9 2.5 %collective-permute-start.16 = (bf16[264,128]{1,0:T(8,128)(2,1)S(1)}, bf16[264,128]{1,0:T(8,128)(2,1)S(1)}, u32[]{:S(2)}, u32[]{:S(2)}) collective-permute-start(bf16[264,128]{1,0:T(8,128)(2,1)S(1)} %shard_map.115.after.refs_0_), channel_id=1, source_target_pairs={{0,3},{1,2},{2,1},{3,0},{4,7},{5,6},{6,5},{7,4},{8,11},{9,10},{10,... | collective-permute-start | bytes 202760 | tf_op jit(solution)/shard_map/ppermute | solution.py:22
  47.4 0.0 collective-permute-start.15
  47.4 0.0 collective-permute-done.19.refs_3_
  47.4 1.9 %collective-permute-start.14 = (bf16[264,128]{1,0:T(8,128)(2,1)S(1)}, bf16[264,128]{1,0:T(8,128)(2,1)S(1)}, u32[]{:S(2)}, u32[]{:S(2)}) collective-permute-start(bf16[264,128]{1,0:T(8,128)(2,1)S(1)} %shard_map.115.after.refs_0_), channel_id=1, source_target_pairs={{0,1},{1,0},{2,3},{3,2},{4,5},{5,4},{6,7},{7,6},{8,9},{9,8},{10,11... | collective-permute-start | bytes 202760 | tf_op jit(solution)/shard_map/ppermute | solution.py:22
  49.4 0.0 collective-permute-done.18.refs_2_
  49.4 0.0 collective-permute-done.17.refs_1_
  49.4 2.1 %collective-permute-done.16.refs_3_ = bf16[264,128]{1,0:T(8,128)(2,1)S(1)} collective-permute-done((bf16[264,128]{1,0:T(8,128)(2,1)S(1)}, bf16[264,128]{1,0:T(8,128)(2,1)S(1)}, u32[]{:S(2)}, u32[]{:S(2)}) %collective-permute-start.16) | collective-permute-done | bytes 67616 | tf_op jit(solution)/shard_map/ppermute | solution.py:22
  51.5 1.6 %collective-permute-done.15.refs_2_ = bf16[264,128]{1,0:T(8,128)(2,1)S(1)} collective-permute-done((bf16[264,128]{1,0:T(8,128)(2,1)S(1)}, bf16[264,128]{1,0:T(8,128)(2,1)S(1)}, u32[]{:S(2)}, u32[]{:S(2)}) %collective-permute-start.15) | collective-permute-done | bytes 67616 | tf_op jit(solution)/shard_map/ppermute | solution.py:22
  53.2 0.0 collective-permute-done.14.refs_1_
  53.2 1.4 %shard_map.117 = (f32[192,256]{1,0:T(8,128)S(1)}, bf16[192,256]{1,0:T(8,128)(2,1)S(1)}, bf16[192,256]{1,0:T(8,128)(2,1)S(1)}, bf16[192,256]{1,0:T(8,128)(2,1)S(1...) custom-call(bf16[264,128]{1,0:T(8,128)(2,1)S(1)} %shard_map.115.after.refs_0_, ...), custom_call_target="tpu_custom_call" | custom-call | tf_op jit(solution)/shard_map/pallas_call | solution.py:91
  54.6 0.0 collective-permute-start.23
  54.6 1.9 %collective-permute-start.20 = (bf16[192,256]{1,0:T(8,128)(2,1)S(1)}, bf16[192,256]{1,0:T(8,128)(2,1)S(1)}, u32[]{:S(2)}, u32[]{:S(2)}) collective-permute-start(bf16[192,256]{1,0:T(8,128)(2,1)S(1)} %get-tuple-element.53), channel_id=1, source_target_pairs={{0,3},{1,2},{2,1},{3,0},{4,7},{5,6},{6,5},{7,4},{8,11},{9,10},{10,... | collective-permute-start | bytes 294920 | tf_op jit(solution)/shard_map/ppermute | solution.py:22
  56.5 0.0 collective-permute-done.23.got
  56.5 0.2 shard_map.118
  56.7 1.4 %collective-permute-start.24 = (bf16[528,128]{1,0:T(8,128)(2,1)S(1)}, bf16[528,128]{1,0:T(8,128)(2,1)S(1)}, u32[]{:S(2)}, u32[]{:S(2)}) collective-permute-start(bf16[528,128]{1,0:T(8,128)(2,1)S(1)} %get-tuple-element.59), channel_id=1, source_target_pairs={{0,24},{4,28},{8,16},{12,20},{16,8},{20,12},{24,0},{28,4},{1,25},{... | collective-permute-start | bytes 405512 | tf_op jit(solution)/shard_map/ppermute | solution.py:22
  58.2 2.1 %collective-permute-start.25 = (bf16[528,128]{1,0:T(8,128)(2,1)S(1)}, bf16[528,128]{1,0:T(8,128)(2,1)S(1)}, u32[]{:S(2)}, u32[]{:S(2)}) collective-permute-start(bf16[528,128]{1,0:T(8,128)(2,1)S(1)} %get-tuple-element.60), channel_id=1, source_target_pairs={{0,16},{4,20},{8,24},{12,28},{16,0},{20,4},{24,8},{28,12},{1,17},{... | collective-permute-start | bytes 405512 | tf_op jit(solution)/shard_map/ppermute | solution.py:22
  60.3 0.0 collective-permute-start.26
  60.3 1.5 %collective-permute-start.21 = (bf16[192,256]{1,0:T(8,128)(2,1)S(1)}, bf16[192,256]{1,0:T(8,128)(2,1)S(1)}, u32[]{:S(2)}, u32[]{:S(2)}) collective-permute-start(bf16[192,256]{1,0:T(8,128)(2,1)S(1)} %get-tuple-element.54), channel_id=1, source_target_pairs={{0,2},{1,3},{2,0},{3,1},{4,6},{5,7},{6,4},{7,5},{8,10},{9,11},{10,... | collective-permute-start | bytes 294920 | tf_op jit(solution)/shard_map/ppermute | solution.py:22
  61.8 0.0 collective-permute-done.20.refs_1_
  61.8 1.0 %collective-permute-start.22 = (bf16[192,256]{1,0:T(8,128)(2,1)S(1)}, bf16[192,256]{1,0:T(8,128)(2,1)S(1)}, u32[]{:S(2)}, u32[]{:S(2)}) collective-permute-start(bf16[192,256]{1,0:T(8,128)(2,1)S(1)} %get-tuple-element.55), channel_id=1, source_target_pairs={{0,1},{1,0},{2,3},{3,2},{4,5},{5,4},{6,7},{7,6},{8,9},{9,8},{10,11... | collective-permute-start | bytes 294920 | tf_op jit(solution)/shard_map/ppermute | solution.py:22
  62.8 4.6 %collective-permute-done.21.refs_2_ = bf16[192,256]{1,0:T(8,128)(2,1)S(1)} collective-permute-done((bf16[192,256]{1,0:T(8,128)(2,1)S(1)}, bf16[192,256]{1,0:T(8,128)(2,1)S(1)}, u32[]{:S(2)}, u32[]{:S(2)}) %collective-permute-start.21) | collective-permute-done | bytes 98336 | tf_op jit(solution)/shard_map/ppermute | solution.py:22
  67.4 0.6 collective-permute-done.22.refs_3_
  68.0 0.0 collective-permute-done.24.refs_5_
  68.0 0.0 collective-permute-done.25.refs_6_
  68.0 0.0 collective-permute-done.26.refs_7_
  68.0 1.0 %shard_map.119 = (bf16[192,256]{1,0:T(8,128)(2,1)}, bf16[192,128]{1,0:T(8,128)(2,1)}, f32[96,128]{1,0:T(8,128)}, f32[3,96,192]{2,1,0:T(8,128)}) custom-call(f32[192,256]{1,0:T(8,128)S(1)} %get-tuple-element.52.refs_0_, bf16[192,256]{1,0:T(8,128)(2,1)S(1)} %collective-permute-done.20.refs_1_, bf16[192,256]{1,0:T(8,128)(2,1)S(1)} %collective-permute-done.21.refs_2_, ...), custom_call_target="tpu_custom_call" | custom-call | tf_op jit(solution)/shard_map/pallas_call | solution.py:91
  (13 shorter events, 0.1 us)
Async XLA Ops:
  0.6 22.6 %copy-start.2 = (f32[192]{0:T(256)S(1)}, f32[192]{0:T(256)}, u32[]{:S(2)}) copy-start(f32[192]{0:T(256)} %param.11) | copy-start | bytes 2308
  2.0 33.5 %copy-start = (s32[256,128]{1,0:T(8,128)S(1)}, s32[256,128]{1,0:T(8,128)}, u32[]{:S(2)}) copy-start(s32[256,128]{1,0:T(8,128)} %counts.1) | copy-start | bytes 393220
  2.1 33.5 %copy-start.1 = (bf16[768,128]{1,0:T(8,128)(2,1)S(1)}, bf16[768,128]{1,0:T(8,128)(2,1)}, u32[]{:S(2)}) copy-start(bf16[768,128]{1,0:T(8,128)(2,1)} %refs_4_.1) | copy-start | bytes 589828
  2.1 33.5 %copy-start.3 = (f32[128]{0:T(128)S(1)}, f32[128]{0:T(128)}, u32[]{:S(2)}) copy-start(f32[128]{0:T(128)} %param.13) | copy-start | bytes 1540
  2.1 5.2 %collective-permute-start = (bf16[8,256]{1,0:T(8,128)(2,1)S(1)}, bf16[8,256]{1,0:T(8,128)(2,1)S(1)}, u32[]{:S(2)}, u32[]{:S(2)}) collective-permute-start(bf16[8,256]{1,0:T(8,128)(2,1)S(1)} %get-tuple-element.36), channel_id=1, source_target_pairs={{4,8},{12,16},{20,24},{8,4},{16,12},{24,20},{5,9},{13,17},{21,25},... | collective-permute-start | bytes 12296 | tf_op jit(solution)/shard_map/ppermute | solution.py:28
  2.9 5.2 %collective-permute-start.1 = (bf16[8,256]{1,0:T(8,128)(2,1)S(1)}, bf16[8,256]{1,0:T(8,128)(2,1)S(1)}, u32[]{:S(2)}, u32[]{:S(2)}) collective-permute-start(bf16[8,256]{1,0:T(8,128)(2,1)S(1)} %get-tuple-element.37), channel_id=1, source_target_pairs={{0,4},{4,0},{8,12},{12,8},{16,20},{20,16},{24,28},{28,24},{1,5},{5... | collective-permute-start | bytes 12296 | tf_op jit(solution)/shard_map/ppermute | solution.py:22
  8.1 33.1 %copy-start.4 = (s32[1,128]{1,0:T(1,128)S(1)}, s32[1,128]{1,0:T(1,128)}, u32[]{:S(2)}) copy-start(s32[1,128]{1,0:T(1,128)} %param.15) | copy-start | bytes 1540
  8.1 15.1 %collective-permute-start.2 = (bf16[224,256]{1,0:T(8,128)(2,1)S(1)}, bf16[224,256]{1,0:T(8,128)(2,1)S(1)}, u32[]{:S(2)}, u32[]{:S(2)}) collective-permute-start(bf16[224,256]{1,0:T(8,128)(2,1)S(1)} %get-tuple-element.40), channel_id=1, source_target_pairs={{0,1},{1,0},{2,3},{3,2},{4,5},{5,4},{6,7},{7,6},{8,9},{9,8},{10,11... | collective-permute-start | bytes 344072 | tf_op jit(solution)/shard_map/ppermute | solution.py:22
  9.7 13.6 %collective-permute-start.3 = (bf16[216,256]{1,0:T(8,128)(2,1)S(1)}, bf16[216,256]{1,0:T(8,128)(2,1)S(1)}, u32[]{:S(2)}, u32[]{:S(2)}) collective-permute-start(bf16[216,256]{1,0:T(8,128)(2,1)S(1)} %get-tuple-element.41), channel_id=1, source_target_pairs={{0,2},{1,3},{2,0},{3,1},{4,6},{5,7},{6,4},{7,5},{8,10},{9,11},{10,... | collective-permute-start | bytes 331784 | tf_op jit(solution)/shard_map/ppermute | solution.py:22
  12.3 11.0 %collective-permute-start.4 = (bf16[216,256]{1,0:T(8,128)(2,1)S(1)}, bf16[216,256]{1,0:T(8,128)(2,1)S(1)}, u32[]{:S(2)}, u32[]{:S(2)}) collective-permute-start(bf16[216,256]{1,0:T(8,128)(2,1)S(1)} %get-tuple-element.35.refs_0_), channel_id=1, source_target_pairs={{0,3},{1,2},{2,1},{3,0},{4,7},{5,6},{6,5},{7,4},{8,11},{9,10},{10,... | collective-permute-start | bytes 331784 | tf_op jit(solution)/shard_map/ppermute | solution.py:22
  12.5 8.1 %collective-permute-start.6 = (bf16[8,256]{1,0:T(8,128)(2,1)S(1)}, bf16[8,256]{1,0:T(8,128)(2,1)S(1)}, u32[]{:S(2)}, u32[]{:S(2)}) collective-permute-start(bf16[8,256]{1,0:T(8,128)(2,1)S(1)} %get-tuple-element.42.refs_4_.edges), channel_id=1, source_target_pairs={{0,3},{1,2},{2,1},{3,0},{4,7},{5,6},{6,5},{7,4},{8,11},{9,10},{10,... | collective-permute-start | bytes 12296 | tf_op jit(solution)/shard_map/ppermute | solution.py:22
  16.1 7.1 %collective-permute-start.5 = (bf16[8,256]{1,0:T(8,128)(2,1)S(1)}, bf16[8,256]{1,0:T(8,128)(2,1)S(1)}, u32[]{:S(2)}, u32[]{:S(2)}) collective-permute-start(bf16[8,256]{1,0:T(8,128)(2,1)S(1)} %get-tuple-element.42.refs_4_.edges), channel_id=1, source_target_pairs={{0,2},{1,3},{2,0},{3,1},{4,6},{5,7},{6,4},{7,5},{8,10},{9,11},{10,... | collective-permute-start | bytes 12296 | tf_op jit(solution)/shard_map/ppermute | solution.py:22
  24.4 7.6 %collective-permute-start.9 = (bf16[200,256]{1,0:T(8,128)(2,1)S(1)}, bf16[200,256]{1,0:T(8,128)(2,1)S(1)}, u32[]{:S(2)}, u32[]{:S(2)}) collective-permute-start(bf16[200,256]{1,0:T(8,128)(2,1)S(1)} %get-tuple-element.44.refs_0_), channel_id=1, source_target_pairs={{0,3},{1,2},{2,1},{3,0},{4,7},{5,6},{6,5},{7,4},{8,11},{9,10},{10,... | collective-permute-start | bytes 307208 | tf_op jit(solution)/shard_map/ppermute | solution.py:22
  26.9 8.6 %collective-permute-start.8 = (bf16[200,256]{1,0:T(8,128)(2,1)S(1)}, bf16[200,256]{1,0:T(8,128)(2,1)S(1)}, u32[]{:S(2)}, u32[]{:S(2)}) collective-permute-start(bf16[200,256]{1,0:T(8,128)(2,1)S(1)} %get-tuple-element.44.refs_0_), channel_id=1, source_target_pairs={{0,2},{1,3},{2,0},{3,1},{4,6},{5,7},{6,4},{7,5},{8,10},{9,11},{10,... | collective-permute-start | bytes 307208 | tf_op jit(solution)/shard_map/ppermute | solution.py:22
  26.9 8.6 %collective-permute-start.7 = (bf16[200,256]{1,0:T(8,128)(2,1)S(1)}, bf16[200,256]{1,0:T(8,128)(2,1)S(1)}, u32[]{:S(2)}, u32[]{:S(2)}) collective-permute-start(bf16[200,256]{1,0:T(8,128)(2,1)S(1)} %get-tuple-element.44.refs_0_), channel_id=1, source_target_pairs={{0,1},{1,0},{2,3},{3,2},{4,5},{5,4},{6,7},{7,6},{8,9},{9,8},{10,11... | collective-permute-start | bytes 307208 | tf_op jit(solution)/shard_map/ppermute | solution.py:22
  36.0 1.2 %collective-permute-start.10 = (f32[8,128]{1,0:T(8,128)S(1)}, f32[8,128]{1,0:T(8,128)S(1)}, u32[]{:S(2)}, u32[]{:S(2)}) collective-permute-start(f32[8,128]{1,0:T(8,128)S(1)} %get-tuple-element.46), channel_id=1, source_target_pairs={{0,4},{4,0},{8,12},{12,8},{16,20},{20,16},{24,28},{28,24},{1,5},{5... | collective-permute-start | bytes 12296 | tf_op jit(solution)/shard_map/ppermute | solution.py:22
  37.2 7.4 %collective-permute-start.13 = (f32[8,128]{1,0:T(8,128)S(1)}, f32[8,128]{1,0:T(8,128)S(1)}, u32[]{:S(2)}, u32[]{:S(2)}) collective-permute-start(f32[8,128]{1,0:T(8,128)S(1)} %add.18), channel_id=1, source_target_pairs={{0,24},{4,28},{8,16},{12,20},{16,8},{20,12},{24,0},{28,4},{1,25},{... | collective-permute-start | bytes 12296 | tf_op jit(solution)/shard_map/ppermute | solution.py:22
  37.4 7.3 %collective-permute-start.12 = (f32[8,128]{1,0:T(8,128)S(1)}, f32[8,128]{1,0:T(8,128)S(1)}, u32[]{:S(2)}, u32[]{:S(2)}) collective-permute-start(f32[8,128]{1,0:T(8,128)S(1)} %add.18), channel_id=1, source_target_pairs={{0,16},{4,20},{8,24},{12,28},{16,0},{20,4},{24,8},{28,12},{1,17},{... | collective-permute-start | bytes 12296 | tf_op jit(solution)/shard_map/ppermute | solution.py:22
  41.2 3.6 %collective-permute-start.11 = (f32[8,128]{1,0:T(8,128)S(1)}, f32[8,128]{1,0:T(8,128)S(1)}, u32[]{:S(2)}, u32[]{:S(2)}) collective-permute-start(f32[8,128]{1,0:T(8,128)S(1)} %add.18), channel_id=1, source_target_pairs={{0,8},{4,12},{8,0},{12,4},{16,24},{20,28},{24,16},{28,20},{1,9},{5... | collective-permute-start | bytes 12296 | tf_op jit(solution)/shard_map/ppermute | solution.py:22
  41.2 6.3 %collective-permute-start.19 = (bf16[144,128]{1,0:T(8,128)(2,1)S(1)}, bf16[144,128]{1,0:T(8,128)(2,1)S(1)}, u32[]{:S(2)}, u32[]{:S(2)}) collective-permute-start(bf16[144,128]{1,0:T(8,128)(2,1)S(1)} %get-tuple-element.47.refs_0_), channel_id=1, source_target_pairs={{0,24},{4,28},{8,16},{12,20},{16,8},{20,12},{24,0},{28,4},{1,25},{... | collective-permute-start | bytes 110600 | tf_op jit(solution)/shard_map/ppermute | solution.py:22
  42.6 6.7 %collective-permute-start.18 = (bf16[144,128]{1,0:T(8,128)(2,1)S(1)}, bf16[144,128]{1,0:T(8,128)(2,1)S(1)}, u32[]{:S(2)}, u32[]{:S(2)}) collective-permute-start(bf16[144,128]{1,0:T(8,128)(2,1)S(1)} %get-tuple-element.47.refs_0_), channel_id=1, source_target_pairs={{0,16},{4,20},{8,24},{12,28},{16,0},{20,4},{24,8},{28,12},{1,17},{... | collective-permute-start | bytes 110600 | tf_op jit(solution)/shard_map/ppermute | solution.py:22
  44.7 4.7 %collective-permute-start.17 = (bf16[144,128]{1,0:T(8,128)(2,1)S(1)}, bf16[144,128]{1,0:T(8,128)(2,1)S(1)}, u32[]{:S(2)}, u32[]{:S(2)}) collective-permute-start(bf16[144,128]{1,0:T(8,128)(2,1)S(1)} %get-tuple-element.47.refs_0_), channel_id=1, source_target_pairs={{0,8},{4,12},{8,0},{12,4},{16,24},{20,28},{24,16},{28,20},{1,9},{5... | collective-permute-start | bytes 110600 | tf_op jit(solution)/shard_map/ppermute | solution.py:22
  44.9 6.6 %collective-permute-start.16 = (bf16[264,128]{1,0:T(8,128)(2,1)S(1)}, bf16[264,128]{1,0:T(8,128)(2,1)S(1)}, u32[]{:S(2)}, u32[]{:S(2)}) collective-permute-start(bf16[264,128]{1,0:T(8,128)(2,1)S(1)} %shard_map.115.after.refs_0_), channel_id=1, source_target_pairs={{0,3},{1,2},{2,1},{3,0},{4,7},{5,6},{6,5},{7,4},{8,11},{9,10},{10,... | collective-permute-start | bytes 202760 | tf_op jit(solution)/shard_map/ppermute | solution.py:22
  47.4 5.7 %collective-permute-start.15 = (bf16[264,128]{1,0:T(8,128)(2,1)S(1)}, bf16[264,128]{1,0:T(8,128)(2,1)S(1)}, u32[]{:S(2)}, u32[]{:S(2)}) collective-permute-start(bf16[264,128]{1,0:T(8,128)(2,1)S(1)} %shard_map.115.after.refs_0_), channel_id=1, source_target_pairs={{0,2},{1,3},{2,0},{3,1},{4,6},{5,7},{6,4},{7,5},{8,10},{9,11},{10,... | collective-permute-start | bytes 202760 | tf_op jit(solution)/shard_map/ppermute | solution.py:22
  47.4 5.7 %collective-permute-start.14 = (bf16[264,128]{1,0:T(8,128)(2,1)S(1)}, bf16[264,128]{1,0:T(8,128)(2,1)S(1)}, u32[]{:S(2)}, u32[]{:S(2)}) collective-permute-start(bf16[264,128]{1,0:T(8,128)(2,1)S(1)} %shard_map.115.after.refs_0_), channel_id=1, source_target_pairs={{0,1},{1,0},{2,3},{3,2},{4,5},{5,4},{6,7},{7,6},{8,9},{9,8},{10,11... | collective-permute-start | bytes 202760 | tf_op jit(solution)/shard_map/ppermute | solution.py:22
  54.6 1.9 %collective-permute-start.23 = (bf16[2112,128]{1,0:T(8,128)(2,1)S(1)}, bf16[2112,128]{1,0:T(8,128)(2,1)S(1)}, u32[]{:S(2)}, u32[]{:S(2)}) collective-permute-start(bf16[2112,128]{1,0:T(8,128)(2,1)S(1)} %get-tuple-element.57), channel_id=1, source_target_pairs={{0,4},{4,0},{8,12},{12,8},{16,20},{20,16},{24,28},{28,24},{1,5},{5... | collective-permute-start | bytes 1622024 | tf_op jit(solution)/shard_map/ppermute | solution.py:22
  54.6 7.2 %collective-permute-start.20 = (bf16[192,256]{1,0:T(8,128)(2,1)S(1)}, bf16[192,256]{1,0:T(8,128)(2,1)S(1)}, u32[]{:S(2)}, u32[]{:S(2)}) collective-permute-start(bf16[192,256]{1,0:T(8,128)(2,1)S(1)} %get-tuple-element.53), channel_id=1, source_target_pairs={{0,3},{1,2},{2,1},{3,0},{4,7},{5,6},{6,5},{7,4},{8,11},{9,10},{10,... | collective-permute-start | bytes 294920 | tf_op jit(solution)/shard_map/ppermute | solution.py:22
  56.7 11.2 %collective-permute-start.24 = (bf16[528,128]{1,0:T(8,128)(2,1)S(1)}, bf16[528,128]{1,0:T(8,128)(2,1)S(1)}, u32[]{:S(2)}, u32[]{:S(2)}) collective-permute-start(bf16[528,128]{1,0:T(8,128)(2,1)S(1)} %get-tuple-element.59), channel_id=1, source_target_pairs={{0,24},{4,28},{8,16},{12,20},{16,8},{20,12},{24,0},{28,4},{1,25},{... | collective-permute-start | bytes 405512 | tf_op jit(solution)/shard_map/ppermute | solution.py:22
  58.2 9.8 %collective-permute-start.25 = (bf16[528,128]{1,0:T(8,128)(2,1)S(1)}, bf16[528,128]{1,0:T(8,128)(2,1)S(1)}, u32[]{:S(2)}, u32[]{:S(2)}) collective-permute-start(bf16[528,128]{1,0:T(8,128)(2,1)S(1)} %get-tuple-element.60), channel_id=1, source_target_pairs={{0,16},{4,20},{8,24},{12,28},{16,0},{20,4},{24,8},{28,12},{1,17},{... | collective-permute-start | bytes 405512 | tf_op jit(solution)/shard_map/ppermute | solution.py:22
  60.3 7.7 %collective-permute-start.26 = (bf16[528,128]{1,0:T(8,128)(2,1)S(1)}, bf16[528,128]{1,0:T(8,128)(2,1)S(1)}, u32[]{:S(2)}, u32[]{:S(2)}) collective-permute-start(bf16[528,128]{1,0:T(8,128)(2,1)S(1)} %get-tuple-element.61), channel_id=1, source_target_pairs={{0,8},{4,12},{8,0},{12,4},{16,24},{20,28},{24,16},{28,20},{1,9},{5... | collective-permute-start | bytes 405512 | tf_op jit(solution)/shard_map/ppermute | solution.py:22
  60.3 7.1 %collective-permute-start.21 = (bf16[192,256]{1,0:T(8,128)(2,1)S(1)}, bf16[192,256]{1,0:T(8,128)(2,1)S(1)}, u32[]{:S(2)}, u32[]{:S(2)}) collective-permute-start(bf16[192,256]{1,0:T(8,128)(2,1)S(1)} %get-tuple-element.54), channel_id=1, source_target_pairs={{0,2},{1,3},{2,0},{3,1},{4,6},{5,7},{6,4},{7,5},{8,10},{9,11},{10,... | collective-permute-start | bytes 294920 | tf_op jit(solution)/shard_map/ppermute | solution.py:22
  61.8 6.2 %collective-permute-start.22 = (bf16[192,256]{1,0:T(8,128)(2,1)S(1)}, bf16[192,256]{1,0:T(8,128)(2,1)S(1)}, u32[]{:S(2)}, u32[]{:S(2)}) collective-permute-start(bf16[192,256]{1,0:T(8,128)(2,1)S(1)} %get-tuple-element.55), channel_id=1, source_target_pairs={{0,1},{1,0},{2,3},{3,2},{4,5},{5,4},{6,7},{7,6},{8,9},{9,8},{10,11... | collective-permute-start | bytes 294920 | tf_op jit(solution)/shard_map/ppermute | solution.py:22

commit v7 on v6

--- a/solution.py
+++ b/solution.py
@@ -109,8 +109,14 @@
     return pl.ds(pl.multiple_of((column ^ j) * size, size), size)
 
 
-def prepare(mp_count, group, coarse_in, skip_in, counts_in, head_in, weight_in, *refs):
-    messages, (pair, cross, own, weight, coarse, skip, top, bottom, done) = refs[: mp_count - 1], refs[mp_count - 1 :]
+def stage(after, weight_in, weight, done):
+    copy = pltpu.make_async_copy(weight_in, weight, done.at[0])
+    copy.start()
+    copy.wait()
+
+
+def prepare(mp_count, group, coarse_in, skip_in, counts_in, head_in, *refs):
+    messages, (pair, cross, own, coarse, skip, top, bottom, done) = refs[: mp_count - 1], refs[mp_count - 1 :]
     width, length = skip.shape
     rows, tracks = top.shape
     place, column = lax.axis_index("seq"), lax.axis_index("mp")
@@ -119,7 +125,6 @@
         (skip_in, skip),
         (counts_in.at[pl.ds(0, rows)], top),
         (counts_in.at[pl.ds(length - rows, rows)], bottom),
-        (weight_in, weight),
     ]
     share = width // group
     for j, message in zip(range(1, mp_count), messages):
@@ -408,7 +413,7 @@
     length, half = grad_skip.shape[1], grad_coarse.shape[1]
     pairs = jnp.where(iota((length, half), 0) // 2 == iota((length, half), 1), 1.0, 0.0).astype(bf16)
     terms, left = [], total
-    for _ in range(3):
+    for _ in range(2):
         terms.append(left.astype(bf16))
         left = left - terms[-1].astype(f32)
     coarse[...] = sum(dot(term, pairs, nn) for term in terms).astype(bf16)
@@ -435,15 +440,15 @@
     tile = ((edge_rows, length), bf16)
     block = ((width + share // 2, length), bf16)
     nearest = ((width + share // 2 + edge_rows, length), bf16)
-    *messages, pair, cross, own, weight = call(
+    *messages, pair, cross, own = call(
         functools.partial(prepare, mp_count, group),
-        [nearest] + [block] * (mp_count - 2) + [tile, tile, tile, ((taps * width, channels), bf16)],
-        coarse, skip, counts, head_weight, conv_weight.reshape(taps * width, channels),
+        [nearest] + [block] * (mp_count - 2) + [tile, tile, tile],
+        coarse, skip, counts, head_weight,
         scratch=[
             (coarse.shape, bf16), (skip.shape, bf16), ((8, tracks), jnp.int32), ((8, tracks), jnp.int32),
-            ((5 + 2 * (mp_count - 1),), None),
+            ((4 + 2 * (mp_count - 1),), None),
         ],
-        outside=range(5),
+        outside=range(4),
     )
     cross = crossed(cross, "seq")
     pair = swap(pair, "seq", 1)
@@ -454,6 +459,10 @@
     halos = [edges]
     for j in range(2, mp_count):
         halos.append(swap(edges, "mp", j))
+    (weight,) = call(
+        stage, [((taps * width, channels), bf16)], edges, conv_weight.reshape(taps * width, channels),
+        scratch=[((1,), None)], outside=(1,),
+    )
     message, gelu, gelu_beside, full_in, bundle = call(
         functools.partial(convolve, mp_count, halves),
         [((tall, length), bf16), ((width, length), f32), ((edge_rows, width), f32), ((channels, length), bf16)]

time: 69.2 us -> 68.9 us (level)
  waiting for transfers between devices: 24.8 us -> 23.4 us
  Pallas kernels: 5.78 us -> 6.9 us
    ppermute x26, waiting for transfers between devices: 24.8 us -> 23.4 us  [swap(): return lax.ppermute(block, axis, [(i, i ^ mask) for i in range(count)])]
    pallas_call x9 -> x10, Pallas kernels: 5.78 us -> 6.9 us  [call(): pl.pallas_call(body, out_shape=[jax.ShapeDtypeStruct(shape, kind) if last...]
  transfers between devices with their start and end apart: 27 -> 27, of which waited for: 10 -> 10; matrix products, arithmetic and copies ran while one was open for 0% -> 0% of each run, Pallas kernels for 1% -> 2%
where the time goes in v7:
time: 68.9 us; the launch traced here: 68.7 us
  starting transfers between devices  37.6 us (55%)
  waiting for transfers between devices  23.4 us (34%)
  Pallas kernels  6.9 us (10%)
  between operations  0.79 us (1%)
    ppermute x26, starting transfers between devices, swap(): return lax.ppermute(block, axis, [(i, i ^ mask) for i in range(count)])  36.9 us
    ppermute x26, waiting for transfers between devices, swap(): return lax.ppermute(block, axis, [(i, i ^ mask) for i in range(count)])  23.4 us
    pallas_call x10, Pallas kernels, call(): pl.pallas_call(body, out_shape=[jax.ShapeDtypeStruct(shape, kind) if last...  6.9 us
  transfers between devices with their start and end apart: 27, of which 10 were waited for; matrix products, arithmetic and copies ran while one was open for 0% of the time, Pallas kernels for 2%

profile of v7, /device:TPU:0, one launch (start us, length us, event | category | flops | bytes accessed | tf_op | source)
XLA Modules:
  0.0 68.7 jit_solution(1512635627737721944)
XLA Ops:
  0.6 1.4 %shard_map.111 = (bf16[224,256]{1,0:T(8,128)(2,1)S(1)}, bf16[216,256]{1,0:T(8,128)(2,1)S(1)}, bf16[216,256]{1,0:T(8,128)(2,1)S(1)}, bf16[8,256]{1,0:T(8,128)(2,1...) custom-call(bf16[192,128]{1,0:T(8,128)(2,1)} %coarse_in.1, bf16[192,256]{1,0:T(8,128)(2,1)} %skip_in.1, ...), custom_call_target="tpu_custom_call" | custom-call | tf_op jit(solution)/shard_map/pallas_call | solution.py:91
  2.0 0.7 collective-permute-start
  2.7 4.4 %collective-permute-start.1 = (bf16[8,256]{1,0:T(8,128)(2,1)S(1)}, bf16[8,256]{1,0:T(8,128)(2,1)S(1)}, u32[]{:S(2)}, u32[]{:S(2)}) collective-permute-start(bf16[8,256]{1,0:T(8,128)(2,1)S(1)} %get-tuple-element.36), channel_id=1, source_target_pairs={{0,4},{4,0},{8,12},{12,8},{16,20},{20,16},{24,28},{28,24},{1,5},{5... | collective-permute-start | bytes 12296 | tf_op jit(solution)/shard_map/ppermute | solution.py:22
  7.1 0.0 collective-permute-done.cross
  7.1 0.8 %collective-permute-done.1.pair = bf16[8,256]{1,0:T(8,128)(2,1)S(1)} collective-permute-done((bf16[8,256]{1,0:T(8,128)(2,1)S(1)}, bf16[8,256]{1,0:T(8,128)(2,1)S(1)}, u32[]{:S(2)}, u32[]{:S(2)}) %collective-permute-start.1) | collective-permute-done | bytes 4128 | tf_op jit(solution)/shard_map/ppermute | solution.py:22
  7.9 1.6 %collective-permute-start.2 = (bf16[224,256]{1,0:T(8,128)(2,1)S(1)}, bf16[224,256]{1,0:T(8,128)(2,1)S(1)}, u32[]{:S(2)}, u32[]{:S(2)}) collective-permute-start(bf16[224,256]{1,0:T(8,128)(2,1)S(1)} %get-tuple-element.39), channel_id=1, source_target_pairs={{0,1},{1,0},{2,3},{3,2},{4,5},{5,4},{6,7},{7,6},{8,9},{9,8},{10,11... | collective-permute-start | bytes 344072 | tf_op jit(solution)/shard_map/ppermute | solution.py:22
  9.5 2.6 %collective-permute-start.3 = (bf16[216,256]{1,0:T(8,128)(2,1)S(1)}, bf16[216,256]{1,0:T(8,128)(2,1)S(1)}, u32[]{:S(2)}, u32[]{:S(2)}) collective-permute-start(bf16[216,256]{1,0:T(8,128)(2,1)S(1)} %get-tuple-element.40), channel_id=1, source_target_pairs={{0,2},{1,3},{2,0},{3,1},{4,6},{5,7},{6,4},{7,5},{8,10},{9,11},{10,... | collective-permute-start | bytes 331784 | tf_op jit(solution)/shard_map/ppermute | solution.py:22
  12.1 0.2 collective-permute-start.4
  12.3 3.6 %collective-permute-start.6 = (bf16[8,256]{1,0:T(8,128)(2,1)S(1)}, bf16[8,256]{1,0:T(8,128)(2,1)S(1)}, u32[]{:S(2)}, u32[]{:S(2)}) collective-permute-start(bf16[8,256]{1,0:T(8,128)(2,1)S(1)} %get-tuple-element.41.after.refs_4_.edges), channel_id=1, source_target_pairs={{0,3},{1,2},{2,1},{3,0},{4,7},{5,6},{6,5},{7,4},{8,11},{9,10},{10,... | collective-permute-start | bytes 12296 | tf_op jit(solution)/shard_map/ppermute | solution.py:22
  15.9 0.0 collective-permute-start.5
  15.9 1.2 %shard_map.113.refs_7_.refs_9_ = bf16[576,768]{1,0:T(8,128)(2,1)S(1)} custom-call(bf16[8,256]{1,0:T(8,128)(2,1)S(1)} %get-tuple-element.41.after.refs_4_.edges, bf16[576,768]{1,0:T(8,128)(2,1)} %bitcast.10), custom_call_target="tpu_custom_call" | custom-call | tf_op jit(solution)/shard_map/pallas_call | solution.py:91
  17.1 0.0 copy-start
  17.1 0.0 copy-start.1
  17.1 0.0 copy-start.3
  17.1 0.0 copy-start.4
  17.2 3.2 %collective-permute-done.6.refs_6_ = bf16[8,256]{1,0:T(8,128)(2,1)S(1)} collective-permute-done((bf16[8,256]{1,0:T(8,128)(2,1)S(1)}, bf16[8,256]{1,0:T(8,128)(2,1)S(1)}, u32[]{:S(2)}, u32[]{:S(2)}) %collective-permute-start.6) | collective-permute-done | bytes 4128 | tf_op jit(solution)/shard_map/ppermute | solution.py:22
  20.4 2.6 %collective-permute-done.5.refs_5_ = bf16[8,256]{1,0:T(8,128)(2,1)S(1)} collective-permute-done((bf16[8,256]{1,0:T(8,128)(2,1)S(1)}, bf16[8,256]{1,0:T(8,128)(2,1)S(1)}, u32[]{:S(2)}, u32[]{:S(2)}) %collective-permute-start.5) | collective-permute-done | bytes 4128 | tf_op jit(solution)/shard_map/ppermute | solution.py:22
  23.0 0.0 collective-permute-done.3.refs_2_
  23.0 0.0 collective-permute-done.4.refs_3_
  23.0 0.0 collective-permute-done.2.refs_1_
  23.0 1.1 %shard_map.114 = (bf16[200,256]{1,0:T(8,128)(2,1)S(1)}, f32[192,256]{1,0:T(8,128)S(1)}, f32[8,192]{1,0:T(8,128)S(1)}, bf16[768,256]{1,0:T(8,128)(2,1)S(1)}, bf16[144,128]{1,0:T(8,128)(2,1)S(1)}) custom-call(bf16[216,256]{1,0:T(8,128)(2,1)S(1)} %get-tuple-element.34.refs_0_, bf16[224,256]{1,0:T(8,128)(2,1)S(1)} %collective-permute-done.2.refs_1_, ...), custom_call_target="tpu_custom_call" | custom-call | tf_op jit(solution)/shard_map/pallas_call | solution.py:91
  24.1 2.5 %collective-permute-start.9 = (bf16[200,256]{1,0:T(8,128)(2,1)S(1)}, bf16[200,256]{1,0:T(8,128)(2,1)S(1)}, u32[]{:S(2)}, u32[]{:S(2)}) collective-permute-start(bf16[200,256]{1,0:T(8,128)(2,1)S(1)} %get-tuple-element.42.refs_0_), channel_id=1, source_target_pairs={{0,3},{1,2},{2,1},{3,0},{4,7},{5,6},{6,5},{7,4},{8,11},{9,10},{10,... | collective-permute-start | bytes 307208 | tf_op jit(solution)/shard_map/ppermute | solution.py:22
  26.7 0.0 collective-permute-start.8
  26.7 1.9 %collective-permute-start.7 = (bf16[200,256]{1,0:T(8,128)(2,1)S(1)}, bf16[200,256]{1,0:T(8,128)(2,1)S(1)}, u32[]{:S(2)}, u32[]{:S(2)}) collective-permute-start(bf16[200,256]{1,0:T(8,128)(2,1)S(1)} %get-tuple-element.42.refs_0_), channel_id=1, source_target_pairs={{0,1},{1,0},{2,3},{3,2},{4,5},{5,4},{6,7},{7,6},{8,9},{9,8},{10,11... | collective-permute-start | bytes 307208 | tf_op jit(solution)/shard_map/ppermute | solution.py:22
  28.6 3.2 %collective-permute-done.9.refs_3_ = bf16[200,256]{1,0:T(8,128)(2,1)S(1)} collective-permute-done((bf16[200,256]{1,0:T(8,128)(2,1)S(1)}, bf16[200,256]{1,0:T(8,128)(2,1)S(1)}, u32[]{:S(2)}, u32[]{:S(2)}) %collective-permute-start.9) | collective-permute-done | bytes 102432 | tf_op jit(solution)/shard_map/ppermute | solution.py:22
  31.7 3.5 %collective-permute-done.8.refs_2_ = bf16[200,256]{1,0:T(8,128)(2,1)S(1)} collective-permute-done((bf16[200,256]{1,0:T(8,128)(2,1)S(1)}, bf16[200,256]{1,0:T(8,128)(2,1)S(1)}, u32[]{:S(2)}, u32[]{:S(2)}) %collective-permute-start.8) | collective-permute-done | bytes 102432 | tf_op jit(solution)/shard_map/ppermute | solution.py:22
  35.2 0.0 collective-permute-done.7.refs_1_
  35.2 0.4 shard_map.115
  35.7 0.1 collective-permute-start.10
  35.8 1.2 %collective-permute-done.10 = f32[8,128]{1,0:T(8,128)S(1)} collective-permute-done((f32[8,128]{1,0:T(8,128)S(1)}, f32[8,128]{1,0:T(8,128)S(1)}, u32[]{:S(2)}, u32[]{:S(2)}) %collective-permute-start.10) | collective-permute-done | bytes 4128 | tf_op jit(solution)/shard_map/ppermute | solution.py:22
  36.9 0.4 collective-permute-start.13
  37.3 3.6 %collective-permute-start.12 = (f32[8,128]{1,0:T(8,128)S(1)}, f32[8,128]{1,0:T(8,128)S(1)}, u32[]{:S(2)}, u32[]{:S(2)}) collective-permute-start(f32[8,128]{1,0:T(8,128)S(1)} %add.18), channel_id=1, source_target_pairs={{0,16},{4,20},{8,24},{12,28},{16,0},{20,4},{24,8},{28,12},{1,17},{... | collective-permute-start | bytes 12296 | tf_op jit(solution)/shard_map/ppermute | solution.py:22
  40.9 0.0 collective-permute-start.11
  40.9 1.5 %collective-permute-start.19 = (bf16[144,128]{1,0:T(8,128)(2,1)S(1)}, bf16[144,128]{1,0:T(8,128)(2,1)S(1)}, u32[]{:S(2)}, u32[]{:S(2)}) collective-permute-start(bf16[144,128]{1,0:T(8,128)(2,1)S(1)} %get-tuple-element.45.refs_0_), channel_id=1, source_target_pairs={{0,24},{4,28},{8,16},{12,20},{16,8},{20,12},{24,0},{28,4},{1,25},{... | collective-permute-start | bytes 110600 | tf_op jit(solution)/shard_map/ppermute | solution.py:22
  42.4 2.0 %collective-permute-start.18 = (bf16[144,128]{1,0:T(8,128)(2,1)S(1)}, bf16[144,128]{1,0:T(8,128)(2,1)S(1)}, u32[]{:S(2)}, u32[]{:S(2)}) collective-permute-start(bf16[144,128]{1,0:T(8,128)(2,1)S(1)} %get-tuple-element.45.refs_0_), channel_id=1, source_target_pairs={{0,16},{4,20},{8,24},{12,28},{16,0},{20,4},{24,8},{28,12},{1,17},{... | collective-permute-start | bytes 110600 | tf_op jit(solution)/shard_map/ppermute | solution.py:22
  44.4 0.1 collective-permute-start.17
  44.5 0.0 collective-permute-done.12
  44.5 0.0 collective-permute-done.11
  44.5 0.1 shard_map.116.after.refs_0_
  44.6 2.5 %collective-permute-start.16 = (bf16[264,128]{1,0:T(8,128)(2,1)S(1)}, bf16[264,128]{1,0:T(8,128)(2,1)S(1)}, u32[]{:S(2)}, u32[]{:S(2)}) collective-permute-start(bf16[264,128]{1,0:T(8,128)(2,1)S(1)} %shard_map.116.after.refs_0_), channel_id=1, source_target_pairs={{0,3},{1,2},{2,1},{3,0},{4,7},{5,6},{6,5},{7,4},{8,11},{9,10},{10,... | collective-permute-start | bytes 202760 | tf_op jit(solution)/shard_map/ppermute | solution.py:22
  47.2 0.0 collective-permute-start.15
  47.2 0.0 collective-permute-done.19.refs_3_
  47.2 1.9 %collective-permute-start.14 = (bf16[264,128]{1,0:T(8,128)(2,1)S(1)}, bf16[264,128]{1,0:T(8,128)(2,1)S(1)}, u32[]{:S(2)}, u32[]{:S(2)}) collective-permute-start(bf16[264,128]{1,0:T(8,128)(2,1)S(1)} %shard_map.116.after.refs_0_), channel_id=1, source_target_pairs={{0,1},{1,0},{2,3},{3,2},{4,5},{5,4},{6,7},{7,6},{8,9},{9,8},{10,11... | collective-permute-start | bytes 202760 | tf_op jit(solution)/shard_map/ppermute | solution.py:22
  49.1 0.0 collective-permute-done.18.refs_2_
  49.1 0.0 collective-permute-done.17.refs_1_
  49.2 2.1 %collective-permute-done.16.refs_3_ = bf16[264,128]{1,0:T(8,128)(2,1)S(1)} collective-permute-done((bf16[264,128]{1,0:T(8,128)(2,1)S(1)}, bf16[264,128]{1,0:T(8,128)(2,1)S(1)}, u32[]{:S(2)}, u32[]{:S(2)}) %collective-permute-start.16) | collective-permute-done | bytes 67616 | tf_op jit(solution)/shard_map/ppermute | solution.py:22
  51.3 1.6 %collective-permute-done.15.refs_2_ = bf16[264,128]{1,0:T(8,128)(2,1)S(1)} collective-permute-done((bf16[264,128]{1,0:T(8,128)(2,1)S(1)}, bf16[264,128]{1,0:T(8,128)(2,1)S(1)}, u32[]{:S(2)}, u32[]{:S(2)}) %collective-permute-start.15) | collective-permute-done | bytes 67616 | tf_op jit(solution)/shard_map/ppermute | solution.py:22
  52.9 0.0 collective-permute-done.14.refs_1_
  52.9 1.4 %shard_map.118 = (f32[192,256]{1,0:T(8,128)S(1)}, bf16[192,256]{1,0:T(8,128)(2,1)S(1)}, bf16[192,256]{1,0:T(8,128)(2,1)S(1)}, bf16[192,256]{1,0:T(8,128)(2,1)S(1...) custom-call(bf16[264,128]{1,0:T(8,128)(2,1)S(1)} %shard_map.116.after.refs_0_, ...), custom_call_target="tpu_custom_call" | custom-call | tf_op jit(solution)/shard_map/pallas_call | solution.py:91
  54.3 0.0 collective-permute-start.23
  54.3 1.9 %collective-permute-start.20 = (bf16[192,256]{1,0:T(8,128)(2,1)S(1)}, bf16[192,256]{1,0:T(8,128)(2,1)S(1)}, u32[]{:S(2)}, u32[]{:S(2)}) collective-permute-start(bf16[192,256]{1,0:T(8,128)(2,1)S(1)} %get-tuple-element.51), channel_id=1, source_target_pairs={{0,3},{1,2},{2,1},{3,0},{4,7},{5,6},{6,5},{7,4},{8,11},{9,10},{10,... | collective-permute-start | bytes 294920 | tf_op jit(solution)/shard_map/ppermute | solution.py:22
  56.2 0.0 collective-permute-done.23.got
  56.3 0.2 shard_map.119
  56.5 1.4 %collective-permute-start.24 = (bf16[528,128]{1,0:T(8,128)(2,1)S(1)}, bf16[528,128]{1,0:T(8,128)(2,1)S(1)}, u32[]{:S(2)}, u32[]{:S(2)}) collective-permute-start(bf16[528,128]{1,0:T(8,128)(2,1)S(1)} %get-tuple-element.57), channel_id=1, source_target_pairs={{0,24},{4,28},{8,16},{12,20},{16,8},{20,12},{24,0},{28,4},{1,25},{... | collective-permute-start | bytes 405512 | tf_op jit(solution)/shard_map/ppermute | solution.py:22
  57.9 2.1 %collective-permute-start.25 = (bf16[528,128]{1,0:T(8,128)(2,1)S(1)}, bf16[528,128]{1,0:T(8,128)(2,1)S(1)}, u32[]{:S(2)}, u32[]{:S(2)}) collective-permute-start(bf16[528,128]{1,0:T(8,128)(2,1)S(1)} %get-tuple-element.58), channel_id=1, source_target_pairs={{0,16},{4,20},{8,24},{12,28},{16,0},{20,4},{24,8},{28,12},{1,17},{... | collective-permute-start | bytes 405512 | tf_op jit(solution)/shard_map/ppermute | solution.py:22
  60.0 0.0 collective-permute-start.26
  60.0 1.5 %collective-permute-start.21 = (bf16[192,256]{1,0:T(8,128)(2,1)S(1)}, bf16[192,256]{1,0:T(8,128)(2,1)S(1)}, u32[]{:S(2)}, u32[]{:S(2)}) collective-permute-start(bf16[192,256]{1,0:T(8,128)(2,1)S(1)} %get-tuple-element.52), channel_id=1, source_target_pairs={{0,2},{1,3},{2,0},{3,1},{4,6},{5,7},{6,4},{7,5},{8,10},{9,11},{10,... | collective-permute-start | bytes 294920 | tf_op jit(solution)/shard_map/ppermute | solution.py:22
  61.5 1.0 %collective-permute-start.22 = (bf16[192,256]{1,0:T(8,128)(2,1)S(1)}, bf16[192,256]{1,0:T(8,128)(2,1)S(1)}, u32[]{:S(2)}, u32[]{:S(2)}) collective-permute-start(bf16[192,256]{1,0:T(8,128)(2,1)S(1)} %get-tuple-element.53), channel_id=1, source_target_pairs={{0,1},{1,0},{2,3},{3,2},{4,5},{5,4},{6,7},{7,6},{8,9},{9,8},{10,11... | collective-permute-start | bytes 294920 | tf_op jit(solution)/shard_map/ppermute | solution.py:22
  62.6 4.6 %collective-permute-done.21.refs_2_ = bf16[192,256]{1,0:T(8,128)(2,1)S(1)} collective-permute-done((bf16[192,256]{1,0:T(8,128)(2,1)S(1)}, bf16[192,256]{1,0:T(8,128)(2,1)S(1)}, u32[]{:S(2)}, u32[]{:S(2)}) %collective-permute-start.21) | collective-permute-done | bytes 98336 | tf_op jit(solution)/shard_map/ppermute | solution.py:22
  67.1 0.6 collective-permute-done.22.refs_3_
  67.7 0.0 collective-permute-done.24.refs_5_
  67.7 0.0 collective-permute-done.25.refs_6_
  67.7 0.0 collective-permute-done.26.refs_7_
  67.7 1.0 %shard_map.120 = (bf16[192,256]{1,0:T(8,128)(2,1)}, bf16[192,128]{1,0:T(8,128)(2,1)}, f32[96,128]{1,0:T(8,128)}, f32[3,96,192]{2,1,0:T(8,128)}) custom-call(f32[192,256]{1,0:T(8,128)S(1)} %get-tuple-element.50.refs_0_, bf16[192,256]{1,0:T(8,128)(2,1)S(1)} %collective-permute-done.20.refs_1_, bf16[192,256]{1,0:T(8,128)(2,1)S(1)} %collective-permute-done.21.refs_2_, ...), custom_call_target="tpu_custom_call" | custom-call | tf_op jit(solution)/shard_map/pallas_call | solution.py:91
  (14 shorter events, 0.1 us)
Async XLA Ops:
  0.6 22.4 %copy-start.2 = (f32[192]{0:T(256)S(1)}, f32[192]{0:T(256)}, u32[]{:S(2)}) copy-start(f32[192]{0:T(256)} %param.11) | copy-start | bytes 2308
  2.0 5.1 %collective-permute-start = (bf16[8,256]{1,0:T(8,128)(2,1)S(1)}, bf16[8,256]{1,0:T(8,128)(2,1)S(1)}, u32[]{:S(2)}, u32[]{:S(2)}) collective-permute-start(bf16[8,256]{1,0:T(8,128)(2,1)S(1)} %get-tuple-element.35), channel_id=1, source_target_pairs={{4,8},{12,16},{20,24},{8,4},{16,12},{24,20},{5,9},{13,17},{21,25},... | collective-permute-start | bytes 12296 | tf_op jit(solution)/shard_map/ppermute | solution.py:28
  2.7 5.2 %collective-permute-start.1 = (bf16[8,256]{1,0:T(8,128)(2,1)S(1)}, bf16[8,256]{1,0:T(8,128)(2,1)S(1)}, u32[]{:S(2)}, u32[]{:S(2)}) collective-permute-start(bf16[8,256]{1,0:T(8,128)(2,1)S(1)} %get-tuple-element.36), channel_id=1, source_target_pairs={{0,4},{4,0},{8,12},{12,8},{16,20},{20,16},{24,28},{28,24},{1,5},{5... | collective-permute-start | bytes 12296 | tf_op jit(solution)/shard_map/ppermute | solution.py:22
  7.9 15.1 %collective-permute-start.2 = (bf16[224,256]{1,0:T(8,128)(2,1)S(1)}, bf16[224,256]{1,0:T(8,128)(2,1)S(1)}, u32[]{:S(2)}, u32[]{:S(2)}) collective-permute-start(bf16[224,256]{1,0:T(8,128)(2,1)S(1)} %get-tuple-element.39), channel_id=1, source_target_pairs={{0,1},{1,0},{2,3},{3,2},{4,5},{5,4},{6,7},{7,6},{8,9},{9,8},{10,11... | collective-permute-start | bytes 344072 | tf_op jit(solution)/shard_map/ppermute | solution.py:22
  9.5 13.5 %collective-permute-start.3 = (bf16[216,256]{1,0:T(8,128)(2,1)S(1)}, bf16[216,256]{1,0:T(8,128)(2,1)S(1)}, u32[]{:S(2)}, u32[]{:S(2)}) collective-permute-start(bf16[216,256]{1,0:T(8,128)(2,1)S(1)} %get-tuple-element.40), channel_id=1, source_target_pairs={{0,2},{1,3},{2,0},{3,1},{4,6},{5,7},{6,4},{7,5},{8,10},{9,11},{10,... | collective-permute-start | bytes 331784 | tf_op jit(solution)/shard_map/ppermute | solution.py:22
  12.1 10.9 %collective-permute-start.4 = (bf16[216,256]{1,0:T(8,128)(2,1)S(1)}, bf16[216,256]{1,0:T(8,128)(2,1)S(1)}, u32[]{:S(2)}, u32[]{:S(2)}) collective-permute-start(bf16[216,256]{1,0:T(8,128)(2,1)S(1)} %get-tuple-element.34.refs_0_), channel_id=1, source_target_pairs={{0,3},{1,2},{2,1},{3,0},{4,7},{5,6},{6,5},{7,4},{8,11},{9,10},{10,... | collective-permute-start | bytes 331784 | tf_op jit(solution)/shard_map/ppermute | solution.py:22
  12.3 8.0 %collective-permute-start.6 = (bf16[8,256]{1,0:T(8,128)(2,1)S(1)}, bf16[8,256]{1,0:T(8,128)(2,1)S(1)}, u32[]{:S(2)}, u32[]{:S(2)}) collective-permute-start(bf16[8,256]{1,0:T(8,128)(2,1)S(1)} %get-tuple-element.41.after.refs_4_.edges), channel_id=1, source_target_pairs={{0,3},{1,2},{2,1},{3,0},{4,7},{5,6},{6,5},{7,4},{8,11},{9,10},{10,... | collective-permute-start | bytes 12296 | tf_op jit(solution)/shard_map/ppermute | solution.py:22
  15.9 7.1 %collective-permute-start.5 = (bf16[8,256]{1,0:T(8,128)(2,1)S(1)}, bf16[8,256]{1,0:T(8,128)(2,1)S(1)}, u32[]{:S(2)}, u32[]{:S(2)}) collective-permute-start(bf16[8,256]{1,0:T(8,128)(2,1)S(1)} %get-tuple-element.41.after.refs_4_.edges), channel_id=1, source_target_pairs={{0,2},{1,3},{2,0},{3,1},{4,6},{5,7},{6,4},{7,5},{8,10},{9,11},{10,... | collective-permute-start | bytes 12296 | tf_op jit(solution)/shard_map/ppermute | solution.py:22
  17.1 18.1 %copy-start = (s32[256,128]{1,0:T(8,128)S(1)}, s32[256,128]{1,0:T(8,128)}, u32[]{:S(2)}) copy-start(s32[256,128]{1,0:T(8,128)} %counts.1) | copy-start | bytes 393220
  17.1 18.1 %copy-start.1 = (bf16[768,128]{1,0:T(8,128)(2,1)S(1)}, bf16[768,128]{1,0:T(8,128)(2,1)}, u32[]{:S(2)}) copy-start(bf16[768,128]{1,0:T(8,128)(2,1)} %refs_4_.1) | copy-start | bytes 589828
  17.1 18.1 %copy-start.3 = (f32[128]{0:T(128)S(1)}, f32[128]{0:T(128)}, u32[]{:S(2)}) copy-start(f32[128]{0:T(128)} %param.13) | copy-start | bytes 1540
  17.1 23.8 %copy-start.4 = (s32[1,128]{1,0:T(1,128)S(1)}, s32[1,128]{1,0:T(1,128)}, u32[]{:S(2)}) copy-start(s32[1,128]{1,0:T(1,128)} %param.15) | copy-start | bytes 1540
  24.1 7.6 %collective-permute-start.9 = (bf16[200,256]{1,0:T(8,128)(2,1)S(1)}, bf16[200,256]{1,0:T(8,128)(2,1)S(1)}, u32[]{:S(2)}, u32[]{:S(2)}) collective-permute-start(bf16[200,256]{1,0:T(8,128)(2,1)S(1)} %get-tuple-element.42.refs_0_), channel_id=1, source_target_pairs={{0,3},{1,2},{2,1},{3,0},{4,7},{5,6},{6,5},{7,4},{8,11},{9,10},{10,... | collective-permute-start | bytes 307208 | tf_op jit(solution)/shard_map/ppermute | solution.py:22
  26.7 8.6 %collective-permute-start.8 = (bf16[200,256]{1,0:T(8,128)(2,1)S(1)}, bf16[200,256]{1,0:T(8,128)(2,1)S(1)}, u32[]{:S(2)}, u32[]{:S(2)}) collective-permute-start(bf16[200,256]{1,0:T(8,128)(2,1)S(1)} %get-tuple-element.42.refs_0_), channel_id=1, source_target_pairs={{0,2},{1,3},{2,0},{3,1},{4,6},{5,7},{6,4},{7,5},{8,10},{9,11},{10,... | collective-permute-start | bytes 307208 | tf_op jit(solution)/shard_map/ppermute | solution.py:22
  26.7 8.6 %collective-permute-start.7 = (bf16[200,256]{1,0:T(8,128)(2,1)S(1)}, bf16[200,256]{1,0:T(8,128)(2,1)S(1)}, u32[]{:S(2)}, u32[]{:S(2)}) collective-permute-start(bf16[200,256]{1,0:T(8,128)(2,1)S(1)} %get-tuple-element.42.refs_0_), channel_id=1, source_target_pairs={{0,1},{1,0},{2,3},{3,2},{4,5},{5,4},{6,7},{7,6},{8,9},{9,8},{10,11... | collective-permute-start | bytes 307208 | tf_op jit(solution)/shard_map/ppermute | solution.py:22
  35.7 1.2 %collective-permute-start.10 = (f32[8,128]{1,0:T(8,128)S(1)}, f32[8,128]{1,0:T(8,128)S(1)}, u32[]{:S(2)}, u32[]{:S(2)}) collective-permute-start(f32[8,128]{1,0:T(8,128)S(1)} %get-tuple-element.44), channel_id=1, source_target_pairs={{0,4},{4,0},{8,12},{12,8},{16,20},{20,16},{24,28},{28,24},{1,5},{5... | collective-permute-start | bytes 12296 | tf_op jit(solution)/shard_map/ppermute | solution.py:22
  36.9 7.5 %collective-permute-start.13 = (f32[8,128]{1,0:T(8,128)S(1)}, f32[8,128]{1,0:T(8,128)S(1)}, u32[]{:S(2)}, u32[]{:S(2)}) collective-permute-start(f32[8,128]{1,0:T(8,128)S(1)} %add.18), channel_id=1, source_target_pairs={{0,24},{4,28},{8,16},{12,20},{16,8},{20,12},{24,0},{28,4},{1,25},{... | collective-permute-start | bytes 12296 | tf_op jit(solution)/shard_map/ppermute | solution.py:22
  37.3 7.2 %collective-permute-start.12 = (f32[8,128]{1,0:T(8,128)S(1)}, f32[8,128]{1,0:T(8,128)S(1)}, u32[]{:S(2)}, u32[]{:S(2)}) collective-permute-start(f32[8,128]{1,0:T(8,128)S(1)} %add.18), channel_id=1, source_target_pairs={{0,16},{4,20},{8,24},{12,28},{16,0},{20,4},{24,8},{28,12},{1,17},{... | collective-permute-start | bytes 12296 | tf_op jit(solution)/shard_map/ppermute | solution.py:22
  40.9 3.6 %collective-permute-start.11 = (f32[8,128]{1,0:T(8,128)S(1)}, f32[8,128]{1,0:T(8,128)S(1)}, u32[]{:S(2)}, u32[]{:S(2)}) collective-permute-start(f32[8,128]{1,0:T(8,128)S(1)} %add.18), channel_id=1, source_target_pairs={{0,8},{4,12},{8,0},{12,4},{16,24},{20,28},{24,16},{28,20},{1,9},{5... | collective-permute-start | bytes 12296 | tf_op jit(solution)/shard_map/ppermute | solution.py:22
  40.9 6.3 %collective-permute-start.19 = (bf16[144,128]{1,0:T(8,128)(2,1)S(1)}, bf16[144,128]{1,0:T(8,128)(2,1)S(1)}, u32[]{:S(2)}, u32[]{:S(2)}) collective-permute-start(bf16[144,128]{1,0:T(8,128)(2,1)S(1)} %get-tuple-element.45.refs_0_), channel_id=1, source_target_pairs={{0,24},{4,28},{8,16},{12,20},{16,8},{20,12},{24,0},{28,4},{1,25},{... | collective-permute-start | bytes 110600 | tf_op jit(solution)/shard_map/ppermute | solution.py:22
  42.4 6.7 %collective-permute-start.18 = (bf16[144,128]{1,0:T(8,128)(2,1)S(1)}, bf16[144,128]{1,0:T(8,128)(2,1)S(1)}, u32[]{:S(2)}, u32[]{:S(2)}) collective-permute-start(bf16[144,128]{1,0:T(8,128)(2,1)S(1)} %get-tuple-element.45.refs_0_), channel_id=1, source_target_pairs={{0,16},{4,20},{8,24},{12,28},{16,0},{20,4},{24,8},{28,12},{1,17},{... | collective-permute-start | bytes 110600 | tf_op jit(solution)/shard_map/ppermute | solution.py:22
  44.4 4.7 %collective-permute-start.17 = (bf16[144,128]{1,0:T(8,128)(2,1)S(1)}, bf16[144,128]{1,0:T(8,128)(2,1)S(1)}, u32[]{:S(2)}, u32[]{:S(2)}) collective-permute-start(bf16[144,128]{1,0:T(8,128)(2,1)S(1)} %get-tuple-element.45.refs_0_), channel_id=1, source_target_pairs={{0,8},{4,12},{8,0},{12,4},{16,24},{20,28},{24,16},{28,20},{1,9},{5... | collective-permute-start | bytes 110600 | tf_op jit(solution)/shard_map/ppermute | solution.py:22
  44.6 6.6 %collective-permute-start.16 = (bf16[264,128]{1,0:T(8,128)(2,1)S(1)}, bf16[264,128]{1,0:T(8,128)(2,1)S(1)}, u32[]{:S(2)}, u32[]{:S(2)}) collective-permute-start(bf16[264,128]{1,0:T(8,128)(2,1)S(1)} %shard_map.116.after.refs_0_), channel_id=1, source_target_pairs={{0,3},{1,2},{2,1},{3,0},{4,7},{5,6},{6,5},{7,4},{8,11},{9,10},{10,... | collective-permute-start | bytes 202760 | tf_op jit(solution)/shard_map/ppermute | solution.py:22
  47.2 5.7 %collective-permute-start.15 = (bf16[264,128]{1,0:T(8,128)(2,1)S(1)}, bf16[264,128]{1,0:T(8,128)(2,1)S(1)}, u32[]{:S(2)}, u32[]{:S(2)}) collective-permute-start(bf16[264,128]{1,0:T(8,128)(2,1)S(1)} %shard_map.116.after.refs_0_), channel_id=1, source_target_pairs={{0,2},{1,3},{2,0},{3,1},{4,6},{5,7},{6,4},{7,5},{8,10},{9,11},{10,... | collective-permute-start | bytes 202760 | tf_op jit(solution)/shard_map/ppermute | solution.py:22
  47.2 5.7 %collective-permute-start.14 = (bf16[264,128]{1,0:T(8,128)(2,1)S(1)}, bf16[264,128]{1,0:T(8,128)(2,1)S(1)}, u32[]{:S(2)}, u32[]{:S(2)}) collective-permute-start(bf16[264,128]{1,0:T(8,128)(2,1)S(1)} %shard_map.116.after.refs_0_), channel_id=1, source_target_pairs={{0,1},{1,0},{2,3},{3,2},{4,5},{5,4},{6,7},{7,6},{8,9},{9,8},{10,11... | collective-permute-start | bytes 202760 | tf_op jit(solution)/shard_map/ppermute | solution.py:22
  54.3 1.9 %collective-permute-start.23 = (bf16[2112,128]{1,0:T(8,128)(2,1)S(1)}, bf16[2112,128]{1,0:T(8,128)(2,1)S(1)}, u32[]{:S(2)}, u32[]{:S(2)}) collective-permute-start(bf16[2112,128]{1,0:T(8,128)(2,1)S(1)} %get-tuple-element.55), channel_id=1, source_target_pairs={{0,4},{4,0},{8,12},{12,8},{16,20},{20,16},{24,28},{28,24},{1,5},{5... | collective-permute-start | bytes 1622024 | tf_op jit(solution)/shard_map/ppermute | solution.py:22
  54.3 7.2 %collective-permute-start.20 = (bf16[192,256]{1,0:T(8,128)(2,1)S(1)}, bf16[192,256]{1,0:T(8,128)(2,1)S(1)}, u32[]{:S(2)}, u32[]{:S(2)}) collective-permute-start(bf16[192,256]{1,0:T(8,128)(2,1)S(1)} %get-tuple-element.51), channel_id=1, source_target_pairs={{0,3},{1,2},{2,1},{3,0},{4,7},{5,6},{6,5},{7,4},{8,11},{9,10},{10,... | collective-permute-start | bytes 294920 | tf_op jit(solution)/shard_map/ppermute | solution.py:22
  56.5 11.2 %collective-permute-start.24 = (bf16[528,128]{1,0:T(8,128)(2,1)S(1)}, bf16[528,128]{1,0:T(8,128)(2,1)S(1)}, u32[]{:S(2)}, u32[]{:S(2)}) collective-permute-start(bf16[528,128]{1,0:T(8,128)(2,1)S(1)} %get-tuple-element.57), channel_id=1, source_target_pairs={{0,24},{4,28},{8,16},{12,20},{16,8},{20,12},{24,0},{28,4},{1,25},{... | collective-permute-start | bytes 405512 | tf_op jit(solution)/shard_map/ppermute | solution.py:22
  57.9 9.8 %collective-permute-start.25 = (bf16[528,128]{1,0:T(8,128)(2,1)S(1)}, bf16[528,128]{1,0:T(8,128)(2,1)S(1)}, u32[]{:S(2)}, u32[]{:S(2)}) collective-permute-start(bf16[528,128]{1,0:T(8,128)(2,1)S(1)} %get-tuple-element.58), channel_id=1, source_target_pairs={{0,16},{4,20},{8,24},{12,28},{16,0},{20,4},{24,8},{28,12},{1,17},{... | collective-permute-start | bytes 405512 | tf_op jit(solution)/shard_map/ppermute | solution.py:22
  60.0 7.7 %collective-permute-start.26 = (bf16[528,128]{1,0:T(8,128)(2,1)S(1)}, bf16[528,128]{1,0:T(8,128)(2,1)S(1)}, u32[]{:S(2)}, u32[]{:S(2)}) collective-permute-start(bf16[528,128]{1,0:T(8,128)(2,1)S(1)} %get-tuple-element.59), channel_id=1, source_target_pairs={{0,8},{4,12},{8,0},{12,4},{16,24},{20,28},{24,16},{28,20},{1,9},{5... | collective-permute-start | bytes 405512 | tf_op jit(solution)/shard_map/ppermute | solution.py:22
  60.0 7.1 %collective-permute-start.21 = (bf16[192,256]{1,0:T(8,128)(2,1)S(1)}, bf16[192,256]{1,0:T(8,128)(2,1)S(1)}, u32[]{:S(2)}, u32[]{:S(2)}) collective-permute-start(bf16[192,256]{1,0:T(8,128)(2,1)S(1)} %get-tuple-element.52), channel_id=1, source_target_pairs={{0,2},{1,3},{2,0},{3,1},{4,6},{5,7},{6,4},{7,5},{8,10},{9,11},{10,... | collective-permute-start | bytes 294920 | tf_op jit(solution)/shard_map/ppermute | solution.py:22
  61.5 6.2 %collective-permute-start.22 = (bf16[192,256]{1,0:T(8,128)(2,1)S(1)}, bf16[192,256]{1,0:T(8,128)(2,1)S(1)}, u32[]{:S(2)}, u32[]{:S(2)}) collective-permute-start(bf16[192,256]{1,0:T(8,128)(2,1)S(1)} %get-tuple-element.53), channel_id=1, source_target_pairs={{0,1},{1,0},{2,3},{3,2},{4,5},{5,4},{6,7},{7,6},{8,9},{9,8},{10,11... | collective-permute-start | bytes 294920 | tf_op jit(solution)/shard_map/ppermute | solution.py:22
